TPU v7x, 32 devices: a whole 2x2x4 slice. The times are simulated.
32 devices in a mesh: dp: 16 (over z, y, x), expert: 2 (over core).
Axes of the slice: x: 2, y: 2, z: 4, core: 2. Of those that a mesh axis runs over, the one named last changes fastest.
Arguments:
- tokens: bfloat16 [16384, 1536], P(('dp', 'expert')), may hold values from -6 to 6
- cotangent: bfloat16 [16384, 1536], P(('dp', 'expert')), may hold values from -6 to 6
- permutation: int32 [16384], P(('dp', 'expert')), may hold values from 0 to 16383, as said below
- lengths: int32 [64, 4], P(('dp', 'expert')), may hold values from 1 to 128, 256 in all within a row
- expert_ids: int32 [16384, 8], P(('dp', 'expert')), may hold values from 0 to 15, all different within a row
- gate_weights: float32 [16384, 8], P(('dp', 'expert')), may hold values from 0.05 to 0.25
- attn_gain: bfloat16 [1536], P(('dp', 'expert')), may hold values from 0.099609375 to 1.8984375
- qkv_weight: bfloat16 [1536, 2560], P(('dp', 'expert')), may hold values from -0.15625 to 0.15625
- out_weight: bfloat16 [1536, 1536], P(('dp', 'expert')), may hold values from -0.625 to 0.625
- ffn_gain: bfloat16 [1536], P(('dp', 'expert')), may hold values from 0.099609375 to 1.8984375
- expert_in: bfloat16 [1536, 2, 8192], P(None, None, ('dp', 'expert')), may hold values from -0.15625 to 0.15625
- expert_out: bfloat16 [8192, 1536], P(('dp', 'expert')), may hold values from -1 to 1
Outputs:
- output: bfloat16 [16384, 1536], P(('dp', 'expert'))
- input_grad: bfloat16 [16384, 1536], P(('dp', 'expert'))
- attn_gain_grad: float32 [1536], P(('dp', 'expert'))
- qkv_grad: float32 [1536, 2560], P(('dp', 'expert'))
- out_grad: float32 [1536, 1536], P(('dp', 'expert'))
- ffn_gain_grad: float32 [1536], P(('dp', 'expert'))
- expert_in_grad: float32 [1536, 2, 8192], P(None, None, ('dp', 'expert'))
- expert_out_grad: float32 [8192, 1536], P(('dp', 'expert'))
Inputs may be any that keep to these rules, and one draw needn't show every extreme that they name: permutation holds each of 0 to 16383 once; each aligned block of 512 positions takes exactly 16 values from each aligned block of 512 values. `lengths`: each row sums to 256. `expert_ids`: each row names 8 different experts.
All inputs are finite; a program needn't handle non-finite values.
Results may differ from a plain program's by a relative error of at most 0.017.
Values may be sent and summed in bfloat16 or wider, within the bound.
A program may use at most 320 MiB of HBM per device.

v0:
```python
import jax
import jax.numpy as jnp
from jax import lax
from jax.sharding import PartitionSpec as P

HEADS = 24
KV_HEADS = 8
HEAD = 64
FF_E = 512
TOPK = 8
MB = 2
SEQS = 4
TOK_MB = 256


epsilon = 1e-05
theta_base = 10000.0


def layout_rows(length_rows):
    seq_ends = jnp.cumsum(length_rows, axis=1, dtype=jnp.int32)
    starts = seq_ends - length_rows
    within = jnp.arange(TOK_MB, dtype=jnp.int32)
    segment = jnp.sum(
        (within[None, :, None] >= seq_ends[:, None, :]).astype(jnp.int32), axis=2, dtype=jnp.int32
    )
    chosen = segment[:, :, None] == jnp.arange(SEQS, dtype=jnp.int32)[None, None, :]
    seq_begin = jnp.sum(jnp.where(chosen, starts[:, None, :], 0), axis=2, dtype=jnp.int32)
    position = within[None, :] - seq_begin
    segment = segment + jnp.arange(MB, dtype=jnp.int32)[:, None] * SEQS
    return (segment.reshape(-1), position.reshape(-1))


def rope_tables(position):
    half_width = HEAD // 2
    frequency = theta_base ** (-(2.0 / HEAD) * jnp.arange(half_width, dtype=jnp.float32))
    angles = position.astype(jnp.float32)[:, None] * frequency[None, :]
    return (jnp.cos(angles), jnp.sin(angles))


def rotate(values, cosine_table, sine_table):
    half_width = HEAD // 2
    front_half = values[..., :half_width]
    behind = values[..., half_width:]
    cosine_part = cosine_table[:, None, :]
    sine_part = sine_table[:, None, :]
    return jnp.concatenate(
        [
            front_half * cosine_part - behind * sine_part,
            behind * cosine_part + front_half * sine_part,
        ],
        axis=-1,
    )


def assign(picked, expert_count, capacity):
    per_mb = picked.reshape(MB, TOK_MB * TOPK)
    onehot = (
        per_mb[:, :, None] == jnp.arange(expert_count, dtype=jnp.int32)[None, None, :]
    ).astype(jnp.int32)
    earlier = jnp.cumsum(onehot, axis=1, dtype=jnp.int32) - onehot
    slot_index = jnp.sum(earlier * onehot, axis=2, dtype=jnp.int32)
    micro_index = jnp.arange(MB, dtype=jnp.int32)[:, None]
    slots_all = expert_count * MB * capacity
    target = jnp.where(
        slot_index < capacity,
        per_mb * (MB * capacity) + micro_index * capacity + slot_index,
        slots_all,
    )
    target = target.reshape(MB * TOK_MB, TOPK)
    row_ids = jnp.broadcast_to(jnp.arange(MB * TOK_MB, dtype=jnp.int32)[:, None], target.shape)
    slot_row = (
        jnp.full((slots_all,), MB * TOK_MB, jnp.int32)
        .at[target.reshape(-1)]
        .set(row_ids.reshape(-1), mode="drop")
    )
    return (target, slot_row)


def block_scores(queries, key_rows, segment, position):
    row_count = queries.shape[0]
    grouped = queries.reshape(row_count, KV_HEADS, HEADS // KV_HEADS, HEAD)
    scores = jnp.einsum(
        "qhgd,khd->hgqk", grouped, key_rows, preferred_element_type=jnp.float32
    ) * HEAD ** (-0.5)
    allowed = (segment[:, None] == segment[None, :]) & (position[:, None] >= position[None, :])
    return (jnp.where(allowed, scores, -1e30), grouped)


def attend_block(queries, key_rows, value_rows, segment, position):
    row_count = queries.shape[0]
    masked, grouped = block_scores(queries, key_rows, segment, position)
    row_peak = jnp.max(masked, axis=-1, keepdims=True)
    weights_exp = jnp.exp(masked - row_peak)
    row_total = jnp.sum(weights_exp, axis=-1, keepdims=True)
    probabilities = (weights_exp / row_total).astype(jnp.bfloat16)
    mixed_rows = jnp.einsum(
        "hgqk,khd->qhgd", probabilities, value_rows, preferred_element_type=jnp.float32
    )
    return (mixed_rows.reshape(row_count, HEADS * HEAD), row_peak + jnp.log(row_total))


def attend_back(queries, key_rows, value_rows, segment, position, logsum, grad_mixed):
    row_count = queries.shape[0]
    masked, grouped = block_scores(queries, key_rows, segment, position)
    exact_probs = jnp.exp(masked - logsum)
    probabilities = exact_probs.astype(jnp.bfloat16)
    grad_heads = grad_mixed.reshape(row_count, KV_HEADS, HEADS // KV_HEADS, HEAD)
    grad_probs = jnp.einsum(
        "qhgd,khd->hgqk", grad_heads, value_rows, preferred_element_type=jnp.float32
    )
    grad_values = jnp.einsum(
        "hgqk,qhgd->khd", probabilities, grad_heads, preferred_element_type=jnp.float32
    )
    grad_scores = (
        exact_probs * (grad_probs - jnp.sum(grad_probs * exact_probs, axis=-1, keepdims=True))
    ).astype(jnp.bfloat16)
    grad_queries = jnp.einsum(
        "hgqk,khd->qhgd", grad_scores, key_rows, preferred_element_type=jnp.float32
    ) * HEAD ** (-0.5)
    grad_keys = jnp.einsum(
        "hgqk,qhgd->khd", grad_scores, grouped, preferred_element_type=jnp.float32
    ) * HEAD ** (-0.5)
    return (grad_queries.reshape(row_count, HEADS, HEAD), grad_keys, grad_values)


def norm_back(values, scale, gain, grad_normed):
    scaled_grad = grad_normed * gain
    grad_gain = jnp.sum(grad_normed * values * scale, axis=0)
    grad_values = scale * scaled_grad - values * scale * scale * scale * jnp.mean(
        scaled_grad * values, axis=1, keepdims=True
    )
    return (grad_gain, grad_values)


def shards(
    tokens,
    cotangent,
    permutation,
    lengths,
    expert_ids,
    gate_weights,
    attn_gain,
    qkv_weight,
    out_weight,
    ffn_gain,
    expert_in,
    expert_out,
):
    device_count = lax.axis_size(("dp", "expert"))
    dp_count = lax.axis_size("dp")
    tok_dev = permutation.shape[0]
    model_width = tokens.shape[1]
    peer_rows = tok_dev // device_count
    q_dim = HEADS * HEAD
    kv_dim = KV_HEADS * HEAD
    positions = jnp.arange(tok_dev, dtype=jnp.int32)
    expert_count = expert_in.shape[2] * device_count // FF_E
    capacity = TOK_MB * TOPK // expert_count
    source = permutation // tok_dev
    local_row = permutation % tok_dev
    from_source = (source[:, None] == jnp.arange(device_count, dtype=jnp.int32)[None, :]).astype(
        jnp.int32
    )
    earlier = jnp.cumsum(from_source, axis=0, dtype=jnp.int32) - from_source
    arrival = source * peer_rows + jnp.sum(earlier * from_source, axis=1, dtype=jnp.int32)
    arrival_match = arrival[:, None] == positions[None, :]
    wanted = jnp.sum(jnp.where(arrival_match, local_row[:, None], 0), axis=0, dtype=jnp.int32)
    by_arrival = jnp.sum(jnp.where(arrival_match, positions[:, None], 0), axis=0, dtype=jnp.int32)
    asked_rows = lax.all_to_all(
        wanted.reshape(device_count, peer_rows),
        ("dp", "expert"),
        split_axis=0,
        concat_axis=0,
        tiled=True,
    ).reshape(tok_dev)
    asked_match = asked_rows[:, None] == positions[None, :]
    by_asked = jnp.sum(jnp.where(asked_match, positions[:, None], 0), axis=0, dtype=jnp.int32)
    outgoing = (
        jnp.take(tokens, asked_rows, axis=0).reshape(device_count, peer_rows, model_width),
        jnp.take(cotangent, asked_rows, axis=0).reshape(device_count, peer_rows, model_width),
    )
    got_rows, got_grad = (
        lax.all_to_all(outgoing[0], ("dp", "expert"), split_axis=0, concat_axis=0, tiled=True),
        lax.all_to_all(outgoing[1], ("dp", "expert"), split_axis=0, concat_axis=0, tiled=True),
    )
    rows_in = jnp.take(got_rows.reshape(tok_dev, model_width), arrival, axis=0).astype(jnp.float32)
    grad_output = jnp.take(got_grad.reshape(tok_dev, model_width), arrival, axis=0).astype(
        jnp.float32
    )
    gain_part, qkv_full, out_full, ffn_part = (
        lax.all_gather(attn_gain, ("dp", "expert"), axis=0, tiled=True),
        lax.all_gather(qkv_weight, ("dp", "expert"), axis=0, tiled=True),
        lax.all_gather(out_weight, ("dp", "expert"), axis=0, tiled=True),
        lax.all_gather(ffn_gain, ("dp", "expert"), axis=0, tiled=True),
    )
    gain_one = gain_part.astype(jnp.float32)
    gain_two = ffn_part.astype(jnp.float32)
    full_in, full_out = (
        lax.all_gather(expert_in, "expert", axis=2, tiled=True),
        lax.all_gather(expert_out, "expert", axis=0, tiled=True),
    )
    local_experts = full_in.shape[2] // FF_E
    weights_in = full_in.reshape(model_width, 2, local_experts, FF_E)
    weights_out = full_out.reshape(local_experts, FF_E, model_width)
    segment, position = layout_rows(lengths)
    scale_one = lax.rsqrt(jnp.mean(rows_in * rows_in, axis=1, keepdims=True) + epsilon)
    normed = (rows_in * scale_one * gain_one).astype(jnp.bfloat16)
    projected = jnp.dot(normed, qkv_full, preferred_element_type=jnp.float32)
    cosine_table, sine_table = rope_tables(position)
    queries = rotate(
        projected[:, :q_dim].reshape(tok_dev, HEADS, HEAD), cosine_table, sine_table
    ).astype(jnp.bfloat16)
    key_rows = rotate(
        projected[:, q_dim : q_dim + kv_dim].reshape(tok_dev, KV_HEADS, HEAD),
        cosine_table,
        sine_table,
    ).astype(jnp.bfloat16)
    value_rows = (
        projected[:, q_dim + kv_dim :].reshape(tok_dev, KV_HEADS, HEAD).astype(jnp.bfloat16)
    )
    block_rows = min(tok_dev, max(TOK_MB, 512))
    mixed_part, logsum = attend_block(queries, key_rows, value_rows, segment, position)
    logsums = [logsum]
    mixed_rows = mixed_part.astype(jnp.bfloat16)
    attended = jnp.dot(mixed_rows, out_full, preferred_element_type=jnp.float32)
    residual = rows_in + attended
    scale_two = lax.rsqrt(jnp.mean(residual * residual, axis=1, keepdims=True) + epsilon)
    normed_two = (residual * scale_two * gain_two).astype(jnp.bfloat16)
    target, slot_row = assign(expert_ids, expert_count, capacity)
    padded = jnp.concatenate([normed_two, jnp.zeros((1, model_width), jnp.bfloat16)], axis=0)
    dispatched = jnp.take(padded, slot_row, axis=0).reshape(dp_count, -1, model_width)
    received = lax.all_to_all(dispatched, "dp", split_axis=0, concat_axis=0, tiled=True)
    per_expert = received.shape[1] // local_experts
    expert_rows = received.reshape(dp_count, local_experts, per_expert, model_width)
    gate_up = jnp.einsum(
        "sepd,dgef->sepgf", expert_rows, weights_in, preferred_element_type=jnp.float32
    )
    hidden = (jax.nn.silu(gate_up[:, :, :, 0]) * gate_up[:, :, :, 1]).astype(jnp.bfloat16)
    produced = jnp.einsum(
        "sepf,efd->sepd", hidden, weights_out, preferred_element_type=jnp.float32
    ).astype(jnp.bfloat16)
    returned = lax.all_to_all(
        produced.reshape(dp_count, -1, model_width), "dp", split_axis=0, concat_axis=0, tiled=True
    )
    padded_back = jnp.concatenate(
        [returned.reshape(-1, model_width), jnp.zeros((1, model_width), jnp.bfloat16)], axis=0
    )
    combined = jnp.sum(
        gate_weights[:, :, None] * jnp.take(padded_back, target, axis=0).astype(jnp.float32), axis=1
    )
    output_rows = (residual + combined).astype(jnp.bfloat16)
    slots_all = expert_count * MB * capacity
    slot_gate = (
        jnp.zeros((slots_all,), jnp.float32)
        .at[target.reshape(-1)]
        .set(gate_weights.reshape(-1), mode="drop")
    )
    grad_padded = jnp.concatenate([grad_output, jnp.zeros((1, model_width), jnp.float32)], axis=0)
    grad_slots = (
        (jnp.take(grad_padded, slot_row, axis=0) * slot_gate[:, None])
        .astype(jnp.bfloat16)
        .reshape(dp_count, -1, model_width)
    )
    grad_received, rows_again = (
        lax.all_to_all(grad_slots, "dp", split_axis=0, concat_axis=0, tiled=True),
        lax.all_to_all(dispatched, "dp", split_axis=0, concat_axis=0, tiled=True),
    )
    expert_rows = rows_again.reshape(dp_count, local_experts, per_expert, model_width)
    gate_up = jnp.einsum(
        "sepd,dgef->sepgf", expert_rows, weights_in, preferred_element_type=jnp.float32
    )
    hidden = (jax.nn.silu(gate_up[:, :, :, 0]) * gate_up[:, :, :, 1]).astype(jnp.bfloat16)
    grad_expert = grad_received.reshape(dp_count, local_experts, per_expert, model_width)
    gate_part = gate_up[:, :, :, 0]
    up_part = gate_up[:, :, :, 1]
    sigmoid_gate = jax.nn.sigmoid(gate_part)
    grad_hidden = jnp.einsum(
        "sepd,efd->sepf", grad_expert, weights_out, preferred_element_type=jnp.float32
    )
    grad_weights_out = jnp.einsum(
        "sepf,sepd->efd", hidden, grad_expert, preferred_element_type=jnp.float32
    )
    grad_gate = grad_hidden * up_part * sigmoid_gate * (1.0 + gate_part * (1.0 - sigmoid_gate))
    grad_up = grad_hidden * (gate_part * sigmoid_gate)
    grad_gate_up = jnp.stack([grad_gate, grad_up], axis=3).astype(jnp.bfloat16)
    grad_weights_in = jnp.einsum(
        "sepd,sepgf->dgef", expert_rows, grad_gate_up, preferred_element_type=jnp.float32
    )
    grad_expert_rows = jnp.einsum(
        "sepgf,dgef->sepd", grad_gate_up, weights_in, preferred_element_type=jnp.float32
    ).astype(jnp.bfloat16)
    grad_returned = lax.all_to_all(
        grad_expert_rows.reshape(dp_count, -1, model_width),
        "dp",
        split_axis=0,
        concat_axis=0,
        tiled=True,
    )
    grad_in_flat = grad_weights_in.reshape(model_width, 2, local_experts * FF_E)
    grad_out_flat = grad_weights_out.reshape(local_experts * FF_E, model_width)
    shard_in, shard_out = (
        lax.psum_scatter(
            grad_in_flat.astype(jnp.bfloat16), "expert", scatter_dimension=2, tiled=True
        ).astype(jnp.float32),
        lax.psum_scatter(
            grad_out_flat.astype(jnp.bfloat16), "expert", scatter_dimension=0, tiled=True
        ).astype(jnp.float32),
    )
    grad_back_pad = jnp.concatenate(
        [grad_returned.reshape(-1, model_width), jnp.zeros((1, model_width), jnp.bfloat16)], axis=0
    )
    grad_normed_two = jnp.sum(jnp.take(grad_back_pad, target, axis=0).astype(jnp.float32), axis=1)
    grad_gain_two, grad_from_norm = norm_back(residual, scale_two, gain_two, grad_normed_two)
    grad_residual = grad_output + grad_from_norm
    grad_attended = grad_residual.astype(jnp.bfloat16)
    grad_out_weight = jnp.einsum(
        "nq,nd->qd", mixed_rows, grad_attended, preferred_element_type=jnp.float32
    )
    grad_mixed = jnp.einsum(
        "nd,qd->nq", grad_attended, out_full, preferred_element_type=jnp.float32
    ).astype(jnp.bfloat16)
    grad_query_parts = []
    grad_key_parts = []
    grad_value_parts = []
    for block_number, block_start in enumerate(range(0, tok_dev, block_rows)):
        grad_q, grad_k, grad_v = attend_back(
            queries, key_rows, value_rows, segment, position, logsums[block_number], grad_mixed
        )
        grad_query_parts.append(grad_q)
        grad_key_parts.append(grad_k)
        grad_value_parts.append(grad_v)
    grad_queries = rotate(grad_query_parts[0], cosine_table, -sine_table)
    grad_keys = rotate(grad_key_parts[0], cosine_table, -sine_table)
    grad_values = grad_value_parts[0]
    grad_projected = jnp.concatenate(
        [
            grad_queries.reshape(tok_dev, q_dim),
            grad_keys.reshape(tok_dev, kv_dim),
            grad_values.reshape(tok_dev, kv_dim),
        ],
        axis=1,
    ).astype(jnp.bfloat16)
    grad_qkv_weight = jnp.einsum(
        "nd,nc->dc", normed, grad_projected, preferred_element_type=jnp.float32
    )
    grad_normed = jnp.einsum(
        "nc,dc->nd", grad_projected, qkv_full, preferred_element_type=jnp.float32
    )
    grad_gain_one, grad_from_first = norm_back(rows_in, scale_one, gain_one, grad_normed)
    grad_input = (grad_residual + grad_from_first).astype(jnp.bfloat16)
    shard_gain_one, shard_qkv, shard_attn_out, shard_gain_two = (
        lax.psum_scatter(grad_gain_one, ("dp", "expert"), scatter_dimension=0, tiled=True),
        lax.psum_scatter(grad_qkv_weight, ("dp", "expert"), scatter_dimension=0, tiled=True),
        lax.psum_scatter(grad_out_weight, ("dp", "expert"), scatter_dimension=0, tiled=True),
        lax.psum_scatter(grad_gain_two, ("dp", "expert"), scatter_dimension=0, tiled=True),
    )
    leaving = (
        jnp.take(output_rows, by_arrival, axis=0).reshape(device_count, peer_rows, model_width),
        jnp.take(grad_input, by_arrival, axis=0).reshape(device_count, peer_rows, model_width),
    )
    home_out, home_grad = (
        lax.all_to_all(leaving[0], ("dp", "expert"), split_axis=0, concat_axis=0, tiled=True),
        lax.all_to_all(leaving[1], ("dp", "expert"), split_axis=0, concat_axis=0, tiled=True),
    )
    output = jnp.take(home_out.reshape(tok_dev, model_width), by_asked, axis=0)
    input_grad = jnp.take(home_grad.reshape(tok_dev, model_width), by_asked, axis=0)
    return (
        output,
        input_grad,
        shard_gain_one,
        shard_qkv,
        shard_attn_out,
        shard_gain_two,
        shard_in,
        shard_out,
    )


def solution(mesh):
    return jax.shard_map(
        shards,
        mesh=mesh,
        in_specs=(
            P(("dp", "expert"), None),
            P(("dp", "expert"), None),
            P(("dp", "expert")),
            P(("dp", "expert"), None),
            P(("dp", "expert"), None),
            P(("dp", "expert"), None),
            P(("dp", "expert")),
            P(("dp", "expert"), None),
            P(("dp", "expert"), None),
            P(("dp", "expert")),
            P(None, None, ("dp", "expert")),
            P(("dp", "expert"), None),
        ),
        out_specs=(
            P(("dp", "expert"), None),
            P(("dp", "expert"), None),
            P(("dp", "expert")),
            P(("dp", "expert"), None),
            P(("dp", "expert"), None),
            P(("dp", "expert")),
            P(None, None, ("dp", "expert")),
            P(("dp", "expert"), None),
        ),
        check_vma=False,
    )
```

profile of v0, /device:TPU:12, one launch (start us, length us, event | category | flops | bytes accessed | tf_op | source)
XLA Modules:
  0.0 1836.3 jit_solution(65367306263986578)
XLA Ops:
  13.1 6.0 all-to-all-start
  25.4 2.9 gather_fusion.7
  28.3 2.9 gather_fusion.2
  31.3 3.4 broadcast_select_fusion.6
  34.7 5.2 all-to-all-start.1
  40.7 84.5 %all-reduce.9 = (bf16[1536]{0:T(1024)(128)(2,1)S(1)}, bf16[1536]{0:T(1024)(128)(2,1)S(1)}) all-reduce(bf16[1536]{0:T(1024)(128)(2,1)S(1)} %dynamic-update-slice, bf16[1536]{0:T(1024)(128)(2,1)S(1)} %dynamic-update-slice.1), channel_id=1, replica_groups=mesh['dp'=16,'expert'=2] {'dp','expert'}, use_global_device_ids=true, to_apply=%add.4 | all-reduce | flops 3072 | bytes 12288
  125.2 9.1 reduce-window.16
  136.2 15.5 scatter_custom_fusion
  153.1 4.4 all-to-all-start.5
  157.5 2.9 gather_fusion.3
  162.5 7.3 fusion.86
  172.8 3.6 copy.95
  179.1 2.6 subtract_convert_fusion.1
  181.7 10.6 fusion.13
  192.3 11.2 fusion.3
  204.1 13.2 fusion.67
  217.4 5.6 multiply_reduce_fusion.3
  225.0 19.2 %gather_fusion = bf16[4096,1536]{1,0:T(8,128)(2,1)} fusion(bf16[513,1536]{1,0:T(8,128)(2,1)S(1)} %concatenate.46, s32[4096]{0:T(1024)S(1)} %fusion.96), kind=kCustom, calls=%fused_computation.10 | custom fusion | bytes 25182208 | tf_op jit(solution)/shard_map/jit(_take)/gather | solution.py:232
  244.3 10.7 broadcast_select_fusion
  255.0 7.1 all-to-all-start.2
  262.4 15.5 scatter_custom_fusion.1
  278.0 2.1 gather_fusion.8
  281.8 20.8 %gather_fusion.1 = f32[4096,1536]{1,0:T(8,128)} fusion(f32[513,1536]{1,0:T(8,128)S(1)} %concatenate.48, s32[4096]{0:T(1024)S(1)} %fusion.96), kind=kCustom, calls=%fused_computation.11 | custom fusion | bytes 50348032 | tf_op jit(solution)/shard_map/jit(_take)/gather | solution.py:261
  302.7 13.7 multiply_convert_fusion
  316.3 230.5 %all-to-all-done.2 = bf16[16,256,1536]{2,1,0:T(8,128)(2,1)} async-done(((bf16[16,256,1536]{2,1,0:T(8,128)(2,1)}), bf16[16,256,1536]{2,1,0:T(8,128)(2,1)}, u32[]{:S(2)}, u32[]{:S(2)}) %all-to-all-start.2) | async-done | bytes 12582944 | tf_op jit(solution)/shard_map/all_to_all | solution.py:233
  546.8 7.5 all-to-all-start.6
  556.4 13.1 all-gather.9.cloned.1.call-done
  569.5 20.7 %fusion.14 = f32[16,1,256,2,512]{4,2,3,0,1:T(8,128)} fusion(bf16[16,256,1536]{2,1,0:T(8,128)(2,1)} %all-to-all-done.2, bf16[1536,2,512]{2,0,1:T(8,128)(2,1)} %all-gather.9.cloned.1.call-done), kind=kOutput, calls=%fused_computation.41 | convolution fusion | flops 12884901888 | bytes 32505856 | tf_op jit(solution)/shard_map/sepd,dgef->sepgf/dot_general | solution.py:236
  590.2 13.7 convolution_convert_fusion
  603.9 231.8 %all-to-all-done.6 = bf16[16,256,1536]{2,1,0:T(8,128)(2,1)} async-done(((bf16[16,256,1536]{2,1,0:T(8,128)(2,1)}), bf16[16,256,1536]{2,1,0:T(8,128)(2,1)}, u32[]{:S(2)}, u32[]{:S(2)}) %all-to-all-start.6) | async-done | bytes 12582944 | tf_op jit(solution)/shard_map/all_to_all | solution.py:266
  835.7 9.0 all-to-all-start.3
  844.7 18.7 %fusion.41 = (bf16[16,256,1,512]{3,1,0,2:T(8,128)(2,1)}, bf16[16,256,1,512]{3,1,0,2:T(8,128)(2,1)}) fusion(f32[16,1,256,2,512]{4,2,3,0,1:T(8,128)} %fusion.14, bf16[16,256,1536]{2,1,0:T(8,128)(2,1)} %all-to-all-done.6, bf16[512,1536]{1,0:T(8,128)(2,1)S(1)} %copy-done.63), kind=kOutput, calls=%fused_computation.79 | convolution fusion | flops 6469713920 | bytes 39321600 | tf_op jit(solution)/shard_map/sepd,efd->sepf/dot_general | solution.py:278
  863.4 19.3 %bitcast_convert_fusion = bf16[16,256,1536]{2,1,0:T(8,128)(2,1)} fusion(bf16[16,256,1,512]{3,1,0,2:T(8,128)(2,1)} %get-tuple-element.59, bf16[16,256,1,512]{3,1,0,2:T(8,128)(2,1)} %get-tuple-element.58, bf16[1536,2,512]{2,0,1:T(8,128)(2,1)S(1)} %copy-done.62), kind=kOutput, calls=%fused_computation.19 | convolution fusion | flops 12895387648 | bytes 24117248 | tf_op jit(solution)/shard_map/sepgf,dgef->sepd/dot_general | solution.py:290
  882.7 238.5 %all-to-all-done.3 = bf16[16,256,1536]{2,1,0:T(8,128)(2,1)} async-done(((bf16[16,256,1536]{2,1,0:T(8,128)(2,1)}), bf16[16,256,1536]{2,1,0:T(8,128)(2,1)}, u32[]{:S(2)}, u32[]{:S(2)}) %all-to-all-start.3) | async-done | bytes 12582944 | tf_op jit(solution)/shard_map/all_to_all | solution.py:243
  1121.2 10.8 all-to-all-start.7
  1132.0 15.0 fusion.64
  1147.0 19.6 %fusion.49 = bf16[1536,2,512]{0,2,1:T(8,128)(2,1)} fusion(bf16[16,256,1536]{2,1,0:T(8,128)(2,1)} %all-to-all-done.2, bf16[16,256,1,512]{3,1,0,2:T(8,128)(2,1)} %get-tuple-element.59, bf16[16,256,1,512]{3,1,0,2:T(8,128)(2,1)} %get-tuple-element.58), kind=kOutput, calls=%fused_computation.83 | convolution fusion | flops 12890669056 | bytes 24117248 | tf_op jit(solution)/shard_map/sepd,sepgf->dgef/dot_general | solution.py:287
  1167.9 10.7 concatenate.47
  1178.6 31.5 %gather_fusion.4 = bf16[4096,1536]{1,0:T(8,128)(2,1)} fusion(bf16[4097,1536]{1,0:T(8,128)(2,1)} %concatenate.47, s32[4096]{0:T(1024)S(1)} %broadcast_clamp_fusion), kind=kCustom, calls=%fused_computation.1.clone | custom fusion | bytes 25182208 | tf_op jit(solution)/shard_map/jit(_take)/gather | solution.py:250
  1210.2 195.7 %all-to-all-done.7 = bf16[16,256,1536]{2,1,0:T(8,128)(2,1)} async-done(((bf16[16,256,1536]{2,1,0:T(8,128)(2,1)}), bf16[16,256,1536]{2,1,0:T(8,128)(2,1)}, u32[]{:S(2)}, u32[]{:S(2)}) %all-to-all-start.7) | async-done | bytes 12582944 | tf_op jit(solution)/shard_map/all_to_all | solution.py:293
  1405.8 10.6 concatenate.49
  1416.4 31.5 %gather_fusion.9 = bf16[4096,1536]{1,0:T(8,128)(2,1)} fusion(bf16[4097,1536]{1,0:T(8,128)(2,1)} %concatenate.49, s32[4096]{0:T(1024)S(1)} %broadcast_clamp_fusion), kind=kCustom, calls=%fused_computation.9.clone | custom fusion | bytes 25182208 | tf_op jit(solution)/shard_map/jit(_take)/gather | solution.py:313
  1448.0 45.1 %convert_reduce_fusion = (f32[512,1536]{1,0:T(8,128)S(1)}, f32[512,1536]{1,0:T(8,128)S(1)}) fusion(bf16[4096,1536]{1,0:T(8,128)(2,1)} %gather_fusion.9, pred[512,8]{1,0:T(8,128)(4,1)S(1)} %get-tuple-element.54, bf16[4096,1536]{1,0:T(8,128)(2,1)} %gather_fusion.4, f32[512,8]{1,0:T(8,128)S(1)} %copy-done.24), kind=kLoop, calls=%fused_computation.22 | loop fusion | flops 42467328 | bytes 31477760 | tf_op jit(solution)/shard_map/reduce_sum | solution.py:313
  1497.8 5.0 fusion.82
  1503.7 7.1 convolution_convert_fusion.1
  1512.7 22.7 %fusion = (f32[8,3,512]{2,1,0:T(4,128)S(1)}, f32[8,512,512,3]{2,1,3,0:T(8,128)}) fusion(f32[8,3,512]{2,1,0:T(4,128)S(1)} %log_add_fusion, f32[8,512,512,3]{2,1,3,0:T(8,128)} %get-tuple-element.82, pred[512,512]{0,1:T(8,128)(4,1)S(1)} %copy-done.18, bf16[512,8,64,1]{0,2,3,1:T(8,128)(2,1)} %bitcast.339, bf16[512,8,3,64]{0,3,2,1:T(8,128)(2,1)S(1)} %bitcast.327), kind=kOutput, calls=%fused_computation.16 | convolution fusion | flops 836751360 | bytes 52789248 | tf_op jit(solution)/shard_map/qhgd,khd->hgqk/dot_general | solution.py:109
  1535.4 24.0 %fusion.2 = bf16[8,3,512,512]{2,3,1,0:T(8,128)(2,1)} fusion(f32[8,512,512,3]{2,1,3,0:T(8,128)} %get-tuple-element.86, f32[8,3,512]{2,1,0:T(4,128)S(1)} %get-tuple-element.85, f32[8,3,512]{2,1,0:T(4,128)S(1)} %log_add_fusion, f32[8,512,512,3]{2,1,3,0:T(8,128)} %get-tuple-element.82, pred[512,512]{0,1:T(8,128)(4,1)S(1)} %copy-done.18), kind=kLoop, calls=%fused_computation.18 | loop fusion | flops 37748736 | bytes 63275008 | tf_op jit(solution)/shard_map/convert_element_type | solution.py:117
  1559.4 8.6 fusion.75
  1568.3 7.2 convolution_multiply_fusion
  1576.9 12.4 fusion.76
  1590.1 10.0 fusion.79
  1600.8 2.9 gather_fusion.5
  1603.7 9.3 fusion.61
  1614.6 2.9 gather_fusion.10
  1617.5 2.9 broadcast_select_fusion.3
  1620.4 50.5 %all_to_all.50 = bf16[32,16,1536]{2,1,0:T(8,128)(2,1)S(1)} all-to-all(bf16[32,16,1536]{2,1,0:T(8,128)(2,1)S(1)} %bitcast.331), channel_id=1, replica_groups=mesh['dp'=16,'expert'=2] {'dp','expert'}, dimensions={0} | all-to-all | bytes 3145728 | tf_op jit(solution)/shard_map/all_to_all | solution.py:363
  1670.9 4.4 all-to-all-start.8
  1675.6 2.5 convert_element_type.178
  1678.2 5.1 copy.111
  1683.3 50.8 %all-reduce.8 = (f32[1536]{0:T(1024)S(1)}, f32[1536]{0:T(1024)S(1)}) all-reduce(f32[1536]{0:T(1024)S(1)} %get-tuple-element.44, f32[1536]{0:T(1024)S(1)} %get-tuple-element.42), channel_id=2, replica_groups=mesh['dp'=16,'expert'=2] {'dp','expert'}, use_global_device_ids=true, to_apply=%region_24.27.clone | all-reduce | flops 3072 | bytes 24576
  1735.3 2.9 gather_fusion.6
  1738.2 2.9 gather_fusion.11
  1741.1 3.9 broadcast_select_fusion.1
  1745.1 83.5 %reduce-scatter.5.cloned.1.call-done = f32[48,2560]{1,0:T(8,128)} async-done(((f32[1536,2560]{1,0:T(8,128)}), f32[48,2560]{1,0:T(8,128)}) %reduce-scatter.5.cloned.1.call-update) | async-done | bytes 491536 | tf_op jit(solution)/shard_map/reduce_scatter | solution.py:354
  (261 shorter events, 44.2 us)
Async XLA Ops:
  8.0 17.4 copy-start
  8.0 154.5 %all-gather.5.cloned.1.call-start = ((), (), s32[]{:S(2)}) async-start(), calls=%async_computation.13 | async-start | bytes 8110080 | tf_op jit(solution)/shard_map/all_gather | solution.py:193
  13.1 11.0 all-to-all-start
  19.1 198.3 %all-gather.7.cloned.1.call-start = ((), (), s32[]{:S(2)}) async-start(), calls=%async_computation.14 | async-start | bytes 4866048 | tf_op jit(solution)/shard_map/all_gather | solution.py:194
  22.4 113.4 %copy-start.11 = (s32[512,8]{1,0:T(8,128)}, s32[512,8]{1,0:T(8,128)S(1)}, u32[]{:S(2)}) copy-start(s32[512,8]{1,0:T(8,128)S(1)} %copy.98) | copy-start | bytes 49156
  25.3 3.0 copy-start.51
  25.4 3.0 copy-start.2
  34.7 5.5 copy-start.64
  34.7 5.7 copy-start.65
  34.7 90.6 %copy-start.35 = (s32[2,16,16,128]{3,2,1,0:T(8,128)S(1)}, s32[2,16,16,128]{3,2,1,0:T(8,128)}, u32[]{:S(2)}) copy-start(s32[2,16,16,128]{3,2,1,0:T(8,128)} %fusion.90) | copy-start | bytes 786436
  34.7 118.4 %all-to-all-start.1 = ((bf16[32,16,1536]{2,1,0:T(8,128)(2,1)}), bf16[32,16,1536]{2,1,0:T(8,128)(2,1)S(1)}, u32[]{:S(2)}, u32[]{:S(2)}) async-start(bf16[32,16,1536]{2,1,0:T(8,128)(2,1)} %bitcast.3), calls=%async_computation.1 | async-start | bytes 3145728 | tf_op jit(solution)/shard_map/all_to_all | solution.py:184
  125.2 37.3 %copy-start.49 = (f32[1536]{0:T(1024)}, f32[1536]{0:T(1024)S(1)}, u32[]{:S(2)}) copy-start(f32[1536]{0:T(1024)S(1)} %convert_element_type.144) | copy-start | bytes 18436
  125.2 97.8 %copy-start.45 = (f32[1536]{0:T(1024)}, f32[1536]{0:T(1024)S(1)}, u32[]{:S(2)}) copy-start(f32[1536]{0:T(1024)S(1)} %convert_element_type.155) | copy-start | bytes 18436
  135.7 17.4 copy-start.43
  152.7 26.4 %copy-start.27 = (f32[512,32]{0,1:T(8,128)}, f32[512,32]{0,1:T(8,128)S(1)}, u32[]{:S(2)}) copy-start(f32[512,32]{0,1:T(8,128)S(1)} %get-tuple-element.72) | copy-start | bytes 196612
  153.0 50.5 %copy-start.17 = (pred[512,512]{0,1:T(8,128)(4,1)}, pred[512,512]{0,1:T(8,128)(4,1)S(1)}, u32[]{:S(2)}) copy-start(pred[512,512]{0,1:T(8,128)(4,1)S(1)} %compare_and_fusion) | copy-start | bytes 786436
  153.1 102.0 %all-to-all-start.5 = ((bf16[32,16,1536]{2,1,0:T(8,128)(2,1)}), bf16[32,16,1536]{2,1,0:T(8,128)(2,1)S(1)}, u32[]{:S(2)}, u32[]{:S(2)}) async-start(bf16[32,16,1536]{2,1,0:T(8,128)(2,1)} %bitcast.329), calls=%async_computation.5 | async-start | bytes 3145728 | tf_op jit(solution)/shard_map/all_to_all | solution.py:185
  157.5 3.0 copy-start.55
  162.5 7.3 copy-start.58
  172.8 4.9 copy-start.37
  179.1 13.2 copy-start.31
  179.1 13.2 copy-start.33
  181.7 10.6 copy-start.19
  181.7 10.6 copy-start.21
  192.3 11.2 copy-start.39
  192.3 11.8 copy-start.26
  204.1 13.2 copy-start.9
  255.0 7.1 copy-start.54
  255.0 291.8 %all-to-all-start.2 = ((bf16[16,256,1536]{2,1,0:T(8,128)(2,1)}), bf16[16,256,1536]{2,1,0:T(8,128)(2,1)}, u32[]{:S(2)}, u32[]{:S(2)}) async-start(bf16[16,256,1536]{2,1,0:T(8,128)(2,1)} %broadcast_select_fusion), calls=%async_computation.2 | async-start | bytes 25165824 | tf_op jit(solution)/shard_map/all_to_all | solution.py:233
  262.3 15.7 copy-start.23
  278.0 3.3 copy-start.56
  316.3 238.1 %copy-start.29 = (bf16[1536,2,256]{2,1,0:T(2,128)(2,1)S(1)}, bf16[1536,2,256]{2,1,0:T(2,128)(2,1)}, u32[]{:S(2)}) copy-start(bf16[1536,2,256]{2,1,0:T(2,128)(2,1)} %param.26) | copy-start | bytes 4718596
  546.8 288.8 %all-to-all-start.6 = ((bf16[16,256,1536]{2,1,0:T(8,128)(2,1)}), bf16[16,256,1536]{2,1,0:T(8,128)(2,1)}, u32[]{:S(2)}, u32[]{:S(2)}) async-start(bf16[16,256,1536]{2,1,0:T(8,128)(2,1)} %multiply_convert_fusion), calls=%async_computation.6 | async-start | bytes 25165824 | tf_op jit(solution)/shard_map/all_to_all | solution.py:266
  554.3 15.1 all-gather.9.cloned.1.call-start
  555.8 34.4 %all-gather.11.cloned.1.call-start = ((), (), s32[]{:S(2)}) async-start(), calls=%async_computation.16 | async-start | bytes 2359296 | tf_op jit(solution)/shard_map/all_gather | solution.py:201
  603.9 240.8 %copy-start.63 = (bf16[512,1536]{1,0:T(8,128)(2,1)S(1)}, bf16[512,1536]{1,0:T(8,128)(2,1)}, u32[]{:S(2)}) copy-start(bf16[512,1536]{1,0:T(8,128)(2,1)} %all-gather.11.cloned.1.call-done) | copy-start | bytes 4718596
  835.7 285.5 %all-to-all-start.3 = ((bf16[16,256,1536]{2,1,0:T(8,128)(2,1)}), bf16[16,256,1536]{2,1,0:T(8,128)(2,1)}, u32[]{:S(2)}, u32[]{:S(2)}) async-start(bf16[16,256,1536]{2,1,0:T(8,128)(2,1)} %convolution_convert_fusion), calls=%async_computation.3 | async-start | bytes 25165824 | tf_op jit(solution)/shard_map/all_to_all | solution.py:243
  844.7 18.7 %copy-start.62 = (bf16[1536,2,512]{2,0,1:T(8,128)(2,1)S(1)}, bf16[1536,2,512]{2,0,1:T(8,128)(2,1)}, u32[]{:S(2)}) copy-start(bf16[1536,2,512]{2,0,1:T(8,128)(2,1)} %all-gather.9.cloned.1.call-done) | copy-start | bytes 9437188
  1121.2 284.7 %all-to-all-start.7 = ((bf16[16,256,1536]{2,1,0:T(8,128)(2,1)}), bf16[16,256,1536]{2,1,0:T(8,128)(2,1)}, u32[]{:S(2)}, u32[]{:S(2)}) async-start(bf16[16,256,1536]{2,1,0:T(8,128)(2,1)} %bitcast_convert_fusion), calls=%async_computation.7 | async-start | bytes 25165824 | tf_op jit(solution)/shard_map/all_to_all | solution.py:293
  1131.9 543.7 %reduce-scatter.11.cloned.1.call-start = ((), (), s32[]{:S(2)}) async-start(), calls=%async_computation.20 | async-start | bytes 2359296 | tf_op jit(solution)/shard_map/reduce_scatter | solution.py:306
  1147.0 531.2 %reduce-scatter.9.cloned.1.call-start = ((), (), s32[]{:S(2)}) async-start(), calls=%async_computation.19 | async-start | bytes 4718592 | tf_op jit(solution)/shard_map/reduce_scatter | solution.py:303
  1166.6 578.5 %reduce-scatter.7.cloned.1.call-start = ((), (), s32[]{:S(2)}) async-start(), calls=%async_computation.18 | async-start | bytes 9732096 | tf_op jit(solution)/shard_map/reduce_scatter | solution.py:355
  1416.4 31.5 %copy-start.24 = (f32[512,8]{1,0:T(8,128)S(1)}, f32[512,8]{1,0:T(8,128)}, u32[]{:S(2)}) copy-start(f32[512,8]{1,0:T(8,128)} %copy-done.23) | copy-start | bytes 49156
  1447.9 45.1 %copy-start.4 = (f32[512,1536]{1,0:T(8,128)S(1)}, f32[512,1536]{1,0:T(8,128)}, u32[]{:S(2)}) copy-start(f32[512,1536]{1,0:T(8,128)} %copy-done.3) | copy-start | bytes 9437188
  1447.9 45.1 %copy-start.46 = (f32[1536]{0:T(1024)S(1)}, f32[1536]{0:T(1024)}, u32[]{:S(2)}) copy-start(f32[1536]{0:T(1024)} %copy-done.45) | copy-start | bytes 18436
  1447.9 45.1 %copy-start.48 = (f32[512]{0:T(512)S(1)}, f32[512]{0:T(512)}, u32[]{:S(2)}) copy-start(f32[512]{0:T(512)} %copy-done.47) | copy-start | bytes 6148
  1494.5 3.3 copy-start.25
  1502.8 325.7 %reduce-scatter.5.cloned.1.call-start = ((), (), s32[]{:S(2)}) async-start(), calls=%async_computation.17 | async-start | bytes 16220160 | tf_op jit(solution)/shard_map/reduce_scatter | solution.py:354
  1512.7 22.7 %copy-start.13 = (bf16[512,1536]{0,1:T(8,128)(2,1)}, bf16[512,1536]{0,1:T(8,128)(2,1)S(1)}, u32[]{:S(2)}) copy-start(bf16[512,1536]{0,1:T(8,128)(2,1)S(1)} %copy.105) | copy-start | bytes 4718596
  1535.4 24.0 %copy-start.20 = (bf16[512,24,32]{0,2,1:T(8,128)(2,1)S(1)}, bf16[512,24,32]{0,2,1:T(8,128)(2,1)}, u32[]{:S(2)}) copy-start(bf16[512,24,32]{0,2,1:T(8,128)(2,1)} %copy-done.19) | copy-start | bytes 2359300
  1535.4 24.0 %copy-start.22 = (bf16[512,24,32]{0,2,1:T(8,128)(2,1)S(1)}, bf16[512,24,32]{0,2,1:T(8,128)(2,1)}, u32[]{:S(2)}) copy-start(bf16[512,24,32]{0,2,1:T(8,128)(2,1)} %copy-done.21) | copy-start | bytes 2359300
  1559.4 8.7 copy-start.28
  1559.4 8.7 copy-start.36
  1559.4 8.9 copy-start.32
  1559.4 8.9 copy-start.34
  1568.3 21.0 %copy-start.38 = (bf16[512,8,64]{0,2,1:T(8,128)(2,1)}, bf16[512,8,64]{0,2,1:T(8,128)(2,1)S(1)}, u32[]{:S(2)}) copy-start(bf16[512,8,64]{0,2,1:T(8,128)(2,1)S(1)} %pad_maximum_fusion.14) | copy-start | bytes 1572868
  1576.9 12.4 copy-start.30
  1576.9 13.2 copy-start.10
  1576.9 13.2 copy-start.50
  1576.9 13.2 copy-start.59
  1603.7 9.4 copy-start.6
  1620.4 54.9 %copy-start.52 = (s32[512]{0:T(512)S(1)}, s32[512]{0:T(512)}, u32[]{:S(2)}) copy-start(s32[512]{0:T(512)} %copy-done.51) | copy-start | bytes 6148
  1670.9 67.3 %all-to-all-start.8 = ((bf16[32,16,1536]{2,1,0:T(8,128)(2,1)}), bf16[32,16,1536]{2,1,0:T(8,128)(2,1)S(1)}, u32[]{:S(2)}, u32[]{:S(2)}) async-start(bf16[32,16,1536]{2,1,0:T(8,128)(2,1)} %bitcast.330), calls=%async_computation.8 | async-start | bytes 3145728 | tf_op jit(solution)/shard_map/all_to_all | solution.py:364
  1738.2 90.4 %copy-start.1 = (bf16[512,1536]{1,0:T(8,128)(2,1)S(1)}, bf16[512,1536]{1,0:T(8,128)(2,1)}, u32[]{:S(2)}) copy-start(bf16[512,1536]{1,0:T(8,128)(2,1)} %param.17) | copy-start | bytes 4718596
  (19 other events, 27.7 us)
Sparse Core Ops, SparseCore 0:
  11.7 95.0 all-gather.4
  109.7 79.7 all-gather.6
Sparse Core Ops, SparseCore 1:
  556.9 12.5 all-gather.8
  570.9 10.9 all-gather.10
  1147.0 10.2 reduce-scatter.10
  1166.7 12.3 reduce-scatter.8
  1502.9 143.4 reduce-scatter.6
  1653.0 175.5 reduce-scatter.4
where the time goes:
time: 1850 us; the launch traced here: 1840 us
  waiting for transfers between devices  996 us (54%)
  matrix products  226 us (12%)
  local copies, waits for them, and re-layouts  210 us (11%)
  blocking collectives  186 us (10%)
  other arithmetic  147 us (8%)
  starting transfers between devices  54.8 us (3%)
    all_to_all x1, waiting for transfers between devices, shards(): lax.all_to_all(produced.reshape(dp_count, -1, model_width), 'dp', split_a...  238 us
    all_to_all x1, waiting for transfers between devices, shards(): lax.all_to_all(grad_slots, 'dp', split_axis=0, concat_axis=0, tiled=True)  232 us
    all_to_all x1, waiting for transfers between devices, shards(): lax.all_to_all(dispatched, 'dp', split_axis=0, concat_axis=0, tiled=True)  230 us
    all_to_all x1, waiting for transfers between devices, shards(): lax.all_to_all(grad_expert_rows.reshape(dp_count, -1, model_width), 'dp',...  196 us
    unnamed x2, blocking collectives  135 us
    reduce_scatter x1, waiting for transfers between devices, shards(): lax.psum_scatter(grad_qkv_weight, ('dp', 'expert'), scatter_dimension=0,...  83.5 us
    all_to_all x1, blocking collectives, shards(): lax.all_to_all(leaving[0], ('dp', 'expert'), split_axis=0, concat_axis=0,...  50.5 us
    reduce_sum x1, other arithmetic, shards(): jnp.sum(jnp.take(grad_back_pad, target, axis=0).astype(jnp.float32), axis=1)  45.1 us
  transfers between devices with their start and end apart: 16, of which 7 were waited for; matrix products, arithmetic and copies ran while one was open for 31% of the time, Pallas kernels for 0%

commit v1 on v0

v1 whole, which is shorter than its diff:
```python
import jax
import jax.numpy as jnp
from jax import lax
from jax.sharding import PartitionSpec as P

HEADS = 24
KV_HEADS = 8
HEAD = 64
FF_E = 512
TOPK = 8
MB = 2
SEQS = 4
TOK_MB = 256
ALL = ("hi", "lo", "core")


epsilon = 1e-05
theta_base = 10000.0


def layout_rows(length_rows):
    seq_ends = jnp.cumsum(length_rows, axis=1, dtype=jnp.int32)
    starts = seq_ends - length_rows
    within = jnp.arange(TOK_MB, dtype=jnp.int32)
    segment = jnp.sum(
        (within[None, :, None] >= seq_ends[:, None, :]).astype(jnp.int32), axis=2, dtype=jnp.int32
    )
    chosen = segment[:, :, None] == jnp.arange(SEQS, dtype=jnp.int32)[None, None, :]
    seq_begin = jnp.sum(jnp.where(chosen, starts[:, None, :], 0), axis=2, dtype=jnp.int32)
    position = within[None, :] - seq_begin
    segment = segment + jnp.arange(MB, dtype=jnp.int32)[:, None] * SEQS
    return (segment.reshape(-1), position.reshape(-1))


def rope_tables(position):
    half_width = HEAD // 2
    frequency = theta_base ** (-(2.0 / HEAD) * jnp.arange(half_width, dtype=jnp.float32))
    angles = position.astype(jnp.float32)[:, None] * frequency[None, :]
    return (jnp.cos(angles), jnp.sin(angles))


def rotate(values, cosine_table, sine_table):
    half_width = HEAD // 2
    front_half = values[..., :half_width]
    behind = values[..., half_width:]
    cosine_part = cosine_table[:, None, :]
    sine_part = sine_table[:, None, :]
    return jnp.concatenate(
        [
            front_half * cosine_part - behind * sine_part,
            behind * cosine_part + front_half * sine_part,
        ],
        axis=-1,
    )


def slot_tables(ids, gates, experts, capacity):
    count = experts.shape[0]
    named = ids[..., None] == experts
    picked = jnp.any(named, axis=2)
    weight = jnp.sum(jnp.where(named, gates[..., None], 0.0), axis=2)
    rows = jnp.arange(TOK_MB, dtype=jnp.int32)
    below = (rows[:, None] > rows[None, :]).astype(jnp.bfloat16)
    shaped = picked.reshape(-1, TOK_MB, count)
    slot = jnp.einsum(
        "rq,bqe->ber", below, shaped.astype(jnp.bfloat16), preferred_element_type=jnp.float32
    ).astype(jnp.int32)
    kept = jnp.transpose(shaped, (0, 2, 1))
    hit = kept[:, :, None, :] & (
        slot[:, :, None, :] == jnp.arange(capacity, dtype=jnp.int32)[None, None, :, None]
    )
    weight = jnp.transpose(weight.reshape(-1, TOK_MB, count), (0, 2, 1))
    slot_gate = jnp.sum(jnp.where(hit, weight[:, :, None, :], 0.0), axis=3)
    return hit.astype(jnp.bfloat16), slot_gate


def block_scores(queries, key_rows, segment, position):
    row_count = queries.shape[0]
    grouped = queries.reshape(row_count, KV_HEADS, HEADS // KV_HEADS, HEAD)
    scores = jnp.einsum(
        "qhgd,khd->hgqk", grouped, key_rows, preferred_element_type=jnp.float32
    ) * HEAD ** (-0.5)
    allowed = (segment[:, None] == segment[None, :]) & (position[:, None] >= position[None, :])
    return (jnp.where(allowed, scores, -1e30), grouped)


def attend_block(queries, key_rows, value_rows, segment, position):
    row_count = queries.shape[0]
    masked, grouped = block_scores(queries, key_rows, segment, position)
    row_peak = jnp.max(masked, axis=-1, keepdims=True)
    weights_exp = jnp.exp(masked - row_peak)
    row_total = jnp.sum(weights_exp, axis=-1, keepdims=True)
    probabilities = (weights_exp / row_total).astype(jnp.bfloat16)
    mixed_rows = jnp.einsum(
        "hgqk,khd->qhgd", probabilities, value_rows, preferred_element_type=jnp.float32
    )
    return (mixed_rows.reshape(row_count, HEADS * HEAD), row_peak + jnp.log(row_total))


def attend_back(queries, key_rows, value_rows, segment, position, logsum, grad_mixed):
    row_count = queries.shape[0]
    masked, grouped = block_scores(queries, key_rows, segment, position)
    exact_probs = jnp.exp(masked - logsum)
    probabilities = exact_probs.astype(jnp.bfloat16)
    grad_heads = grad_mixed.reshape(row_count, KV_HEADS, HEADS // KV_HEADS, HEAD)
    grad_probs = jnp.einsum(
        "qhgd,khd->hgqk", grad_heads, value_rows, preferred_element_type=jnp.float32
    )
    grad_values = jnp.einsum(
        "hgqk,qhgd->khd", probabilities, grad_heads, preferred_element_type=jnp.float32
    )
    grad_scores = (
        exact_probs * (grad_probs - jnp.sum(grad_probs * exact_probs, axis=-1, keepdims=True))
    ).astype(jnp.bfloat16)
    grad_queries = jnp.einsum(
        "hgqk,khd->qhgd", grad_scores, key_rows, preferred_element_type=jnp.float32
    ) * HEAD ** (-0.5)
    grad_keys = jnp.einsum(
        "hgqk,qhgd->khd", grad_scores, grouped, preferred_element_type=jnp.float32
    ) * HEAD ** (-0.5)
    return (grad_queries.reshape(row_count, HEADS, HEAD), grad_keys, grad_values)


def norm_back(values, scale, gain, grad_normed):
    scaled_grad = grad_normed * gain
    grad_gain = jnp.sum(grad_normed * values * scale, axis=0)
    grad_values = scale * scaled_grad - values * scale * scale * scale * jnp.mean(
        scaled_grad * values, axis=1, keepdims=True
    )
    return (grad_gain, grad_values)


def shards(
    tokens,
    cotangent,
    permutation,
    lengths,
    expert_ids,
    gate_weights,
    attn_gain,
    qkv_weight,
    out_weight,
    ffn_gain,
    expert_in,
    expert_out,
):
    device_count = lax.axis_size(ALL)
    hi_count = lax.axis_size("hi")
    lo_count = lax.axis_size("lo")
    tok_dev = permutation.shape[0]
    model_width = tokens.shape[1]
    peer_rows = tok_dev // device_count
    q_dim = HEADS * HEAD
    kv_dim = KV_HEADS * HEAD
    positions = jnp.arange(tok_dev, dtype=jnp.int32)
    expert_count = expert_in.shape[2] * device_count // FF_E
    capacity = TOK_MB * TOPK // expert_count
    source = permutation // tok_dev
    local_row = permutation % tok_dev
    from_source = (source[:, None] == jnp.arange(device_count, dtype=jnp.int32)[None, :]).astype(
        jnp.int32
    )
    earlier = jnp.cumsum(from_source, axis=0, dtype=jnp.int32) - from_source
    arrival = source * peer_rows + jnp.sum(earlier * from_source, axis=1, dtype=jnp.int32)
    arrival_match = arrival[:, None] == positions[None, :]
    wanted = jnp.sum(jnp.where(arrival_match, local_row[:, None], 0), axis=0, dtype=jnp.int32)
    by_arrival = jnp.sum(jnp.where(arrival_match, positions[:, None], 0), axis=0, dtype=jnp.int32)
    asked_rows = lax.all_to_all(
        wanted.reshape(device_count, peer_rows),
        ALL,
        split_axis=0,
        concat_axis=0,
        tiled=True,
    ).reshape(tok_dev)
    asked_match = asked_rows[:, None] == positions[None, :]
    by_asked = jnp.sum(jnp.where(asked_match, positions[:, None], 0), axis=0, dtype=jnp.int32)
    outgoing = (
        jnp.take(tokens, asked_rows, axis=0).reshape(device_count, peer_rows, model_width),
        jnp.take(cotangent, asked_rows, axis=0).reshape(device_count, peer_rows, model_width),
    )
    got_rows, got_grad = (
        lax.all_to_all(outgoing[0], ALL, split_axis=0, concat_axis=0, tiled=True),
        lax.all_to_all(outgoing[1], ALL, split_axis=0, concat_axis=0, tiled=True),
    )
    rows_in = jnp.take(got_rows.reshape(tok_dev, model_width), arrival, axis=0).astype(jnp.float32)
    grad_bf = jnp.take(got_grad.reshape(tok_dev, model_width), arrival, axis=0)
    grad_output = grad_bf.astype(jnp.float32)
    gains = jnp.concatenate(
        [attn_gain[:, None], ffn_gain[:, None], jnp.zeros((attn_gain.shape[0], 126), jnp.bfloat16)],
        axis=1,
    )
    packed_qkv = lax.all_gather(
        jnp.concatenate([qkv_weight, gains], axis=1), ALL, axis=0, tiled=True
    )
    qkv_full = packed_qkv[:, : qkv_weight.shape[1]]
    gain_pair = packed_qkv[:, qkv_weight.shape[1] :].astype(jnp.float32)
    gain_one = gain_pair[:, 0]
    gain_two = gain_pair[:, 1]
    out_full = lax.all_gather(out_weight, ALL, axis=0, tiled=True)
    shard_cols = expert_in.shape[2]
    weights_in = lax.all_gather(
        expert_in.reshape(model_width, 2 * shard_cols), ("hi", "core"), axis=0
    ).reshape(hi_count, 2, model_width, 2 * shard_cols)
    weights_out = lax.all_gather(expert_out, ("hi", "core"), axis=0).reshape(
        hi_count, 2, shard_cols, model_width
    )
    segment, position = layout_rows(lengths)
    scale_one = lax.rsqrt(jnp.mean(rows_in * rows_in, axis=1, keepdims=True) + epsilon)
    normed = (rows_in * scale_one * gain_one).astype(jnp.bfloat16)
    projected = jnp.dot(normed, qkv_full, preferred_element_type=jnp.float32)
    cosine_table, sine_table = rope_tables(position)
    queries = rotate(
        projected[:, :q_dim].reshape(tok_dev, HEADS, HEAD), cosine_table, sine_table
    ).astype(jnp.bfloat16)
    key_rows = rotate(
        projected[:, q_dim : q_dim + kv_dim].reshape(tok_dev, KV_HEADS, HEAD),
        cosine_table,
        sine_table,
    ).astype(jnp.bfloat16)
    value_rows = (
        projected[:, q_dim + kv_dim :].reshape(tok_dev, KV_HEADS, HEAD).astype(jnp.bfloat16)
    )
    block_rows = min(tok_dev, max(TOK_MB, 512))
    mixed_part, logsum = attend_block(queries, key_rows, value_rows, segment, position)
    logsums = [logsum]
    mixed_rows = mixed_part.astype(jnp.bfloat16)
    attended = jnp.dot(mixed_rows, out_full, preferred_element_type=jnp.float32)
    residual = rows_in + attended
    scale_two = lax.rsqrt(jnp.mean(residual * residual, axis=1, keepdims=True) + epsilon)
    normed_two = (residual * scale_two * gain_two).astype(jnp.bfloat16)
    home = lax.axis_index("lo")

    def spread(block):
        return [block] + [swap(block, step) for step in range(1, lo_count)]

    def swap(block, step):
        return lax.ppermute(block, "lo", [(i, i ^ step) for i in range(lo_count)])

    ids_all = jnp.stack(spread(expert_ids))
    gates_all = jnp.stack(spread(gate_weights))
    choose, slot_gate = slot_tables(
        ids_all.reshape(-1, TOK_MB, TOPK),
        gates_all.reshape(-1, TOK_MB, TOPK),
        home + lo_count * jnp.arange(hi_count, dtype=jnp.int32),
        capacity,
    )
    rows_all = jnp.stack(spread(normed_two)).reshape(lo_count * MB, TOK_MB, model_width)
    grads_all = jnp.stack(spread(grad_bf)).reshape(lo_count * MB, TOK_MB, model_width)
    expert_rows = jnp.einsum(
        "becr,brd->ebcd", choose, rows_all, preferred_element_type=jnp.float32
    ).astype(jnp.bfloat16).reshape(hi_count, -1, model_width)
    gate_up = jnp.einsum(
        "erd,ekdf->ekrf", expert_rows, weights_in, preferred_element_type=jnp.float32
    )
    gate_part = gate_up[..., :shard_cols]
    up_part = gate_up[..., shard_cols:]
    sigmoid_gate = jax.nn.sigmoid(gate_part)
    hidden = (gate_part * sigmoid_gate * up_part).astype(jnp.bfloat16)
    slot_weight = jnp.transpose(slot_gate, (1, 0, 2)).reshape(hi_count, -1, 1)
    produced = (
        jnp.einsum("ekrf,ekfd->erd", hidden, weights_out, preferred_element_type=jnp.float32)
        * slot_weight
    ).astype(jnp.bfloat16)

    def collect(slot_values):
        parts = jnp.einsum(
            "becr,ebcd->brd",
            choose,
            slot_values.reshape(hi_count, lo_count * MB, capacity, model_width),
            preferred_element_type=jnp.float32,
        ).reshape(lo_count, tok_dev, model_width)
        total = parts[0]
        for step in range(1, lo_count):
            total = total + swap(parts[step].astype(jnp.bfloat16), step).astype(jnp.float32)
        return total

    output_rows = (residual + collect(produced)).astype(jnp.bfloat16)
    grad_expert = (
        jnp.einsum("becr,brd->ebcd", choose, grads_all, preferred_element_type=jnp.float32).reshape(
            hi_count, -1, model_width
        )
        * slot_weight
    ).astype(jnp.bfloat16)
    grad_hidden = jnp.einsum(
        "erd,ekfd->ekrf", grad_expert, weights_out, preferred_element_type=jnp.float32
    )
    grad_weights_out = jnp.einsum(
        "ekrf,erd->ekfd", hidden, grad_expert, preferred_element_type=jnp.float32
    )
    grad_gate = grad_hidden * up_part * sigmoid_gate * (1.0 + gate_part * (1.0 - sigmoid_gate))
    grad_up = grad_hidden * (gate_part * sigmoid_gate)
    grad_gate_up = jnp.concatenate([grad_gate, grad_up], axis=-1).astype(jnp.bfloat16)
    grad_weights_in = jnp.einsum(
        "erd,ekrf->ekdf", expert_rows, grad_gate_up, preferred_element_type=jnp.float32
    )
    grad_expert_rows = jnp.einsum(
        "ekrf,ekdf->erd", grad_gate_up, weights_in, preferred_element_type=jnp.float32
    ).astype(jnp.bfloat16)
    grad_normed_two = collect(grad_expert_rows)
    shard_out = lax.psum_scatter(
        grad_weights_out.astype(jnp.bfloat16).reshape(hi_count * 2 * shard_cols, model_width),
        ("hi", "core"),
        scatter_dimension=0,
        tiled=True,
    ).astype(jnp.float32)
    shard_in = (
        lax.psum_scatter(
            grad_weights_in.astype(jnp.bfloat16).reshape(hi_count * 2 * model_width, 2 * shard_cols),
            ("hi", "core"),
            scatter_dimension=0,
            tiled=True,
        )
        .astype(jnp.float32)
        .reshape(model_width, 2, shard_cols)
    )
    grad_gain_two, grad_from_norm = norm_back(residual, scale_two, gain_two, grad_normed_two)
    grad_residual = grad_output + grad_from_norm
    grad_attended = grad_residual.astype(jnp.bfloat16)
    grad_out_weight = jnp.einsum(
        "nq,nd->qd", mixed_rows, grad_attended, preferred_element_type=jnp.float32
    )
    grad_mixed = jnp.einsum(
        "nd,qd->nq", grad_attended, out_full, preferred_element_type=jnp.float32
    ).astype(jnp.bfloat16)
    grad_query_parts = []
    grad_key_parts = []
    grad_value_parts = []
    for block_number, block_start in enumerate(range(0, tok_dev, block_rows)):
        grad_q, grad_k, grad_v = attend_back(
            queries, key_rows, value_rows, segment, position, logsums[block_number], grad_mixed
        )
        grad_query_parts.append(grad_q)
        grad_key_parts.append(grad_k)
        grad_value_parts.append(grad_v)
    grad_queries = rotate(grad_query_parts[0], cosine_table, -sine_table)
    grad_keys = rotate(grad_key_parts[0], cosine_table, -sine_table)
    grad_values = grad_value_parts[0]
    grad_projected = jnp.concatenate(
        [
            grad_queries.reshape(tok_dev, q_dim),
            grad_keys.reshape(tok_dev, kv_dim),
            grad_values.reshape(tok_dev, kv_dim),
        ],
        axis=1,
    ).astype(jnp.bfloat16)
    grad_qkv_weight = jnp.einsum(
        "nd,nc->dc", normed, grad_projected, preferred_element_type=jnp.float32
    )
    grad_normed = jnp.einsum(
        "nc,dc->nd", grad_projected, qkv_full, preferred_element_type=jnp.float32
    )
    grad_gain_one, grad_from_first = norm_back(rows_in, scale_one, gain_one, grad_normed)
    grad_input = (grad_residual + grad_from_first).astype(jnp.bfloat16)
    def gain_column(grad_gain):
        return jnp.pad(grad_gain[:, None], ((0, 0), (0, 127)))

    packed_out = lax.psum_scatter(
        jnp.concatenate([grad_out_weight, gain_column(grad_gain_two)], axis=1),
        ALL,
        scatter_dimension=0,
        tiled=True,
    )
    shard_attn_out = packed_out[:, :model_width]
    shard_gain_two = packed_out[:, model_width]
    packed_grad = lax.psum_scatter(
        jnp.concatenate([grad_qkv_weight, gain_column(grad_gain_one)], axis=1),
        ALL,
        scatter_dimension=0,
        tiled=True,
    )
    shard_qkv = packed_grad[:, : qkv_weight.shape[1]]
    shard_gain_one = packed_grad[:, qkv_weight.shape[1]]
    leaving = (
        jnp.take(output_rows, by_arrival, axis=0).reshape(device_count, peer_rows, model_width),
        jnp.take(grad_input, by_arrival, axis=0).reshape(device_count, peer_rows, model_width),
    )
    home_out, home_grad = (
        lax.all_to_all(leaving[0], ALL, split_axis=0, concat_axis=0, tiled=True),
        lax.all_to_all(leaving[1], ALL, split_axis=0, concat_axis=0, tiled=True),
    )
    output = jnp.take(home_out.reshape(tok_dev, model_width), by_asked, axis=0)
    input_grad = jnp.take(home_grad.reshape(tok_dev, model_width), by_asked, axis=0)
    return (
        output,
        input_grad,
        shard_gain_one,
        shard_qkv,
        shard_attn_out,
        shard_gain_two,
        shard_in,
        shard_out,
    )


def solution(mesh):
    dp_count = mesh.shape["dp"]
    hi_count = 4 if dp_count % 4 == 0 else 1
    split = jax.sharding.Mesh(
        mesh.devices.reshape(hi_count, dp_count // hi_count, mesh.shape["expert"]), ALL
    )
    rows, columns = P(ALL, None), P(None, None, ALL)
    return jax.shard_map(
        shards,
        mesh=split,
        in_specs=(rows, rows, P(ALL), rows, rows, rows, P(ALL), rows, rows, P(ALL), columns, rows),
        out_specs=(rows, rows, P(ALL), rows, rows, P(ALL), columns, rows),
        check_vma=False,
    )
```

time: 1850 us -> 1160 us (0.63)
  waiting for transfers between devices: 996 us -> 565 us
  blocking collectives: 186 us -> 54.6 us
  local copies, waits for them, and re-layouts: 210 us -> 107 us
  other arithmetic: 147 us -> 109 us
  matrix products: 226 us -> 259 us
  starting transfers between devices: 54.8 us -> 35.6 us
    all_to_all x8 -> x3, waiting for transfers between devices: 897 us -> 147 us  [the longest x1 67.3 us: shards(): lax.all_to_all(leaving[1], ALL, split_axis=0, concat_axis=0, tiled=True)]
    ppermute x0 -> x18, waiting for transfers between devices: none -> 209 us  [swap(): return lax.ppermute(block, 'lo', [(i, i ^ step) for i in range(lo_count)])]
    unnamed x2 -> x0, blocking collectives: 135 us -> none
    reduce_scatter x4 -> x3, waiting for transfers between devices: 83.6 us -> 209 us  [the longest x1 125 us: shards(): lax.psum_scatter(grad_weights_in.astype(jnp.bfloat16).reshape(hi_count *...]
    gather x5 -> x1, local copies, waits for them, and re-layouts: 105 us -> 3.13 us  [shards(): grad_bf = jnp.take(got_grad.reshape(tok_dev, model_width), arrival, axis=0)]
    dot_general x6 -> x11, matrix products: 107 us -> 150 us  [the longest x1 25.2 us: shards(): jnp.einsum('erd,ekdf->ekrf', expert_rows, weights_in, preferred_element_t...]
    reduce_sum x2, other arithmetic: 45.2 us -> 4.82 us  [the longest x1 4.65 us: slot_tables(): slot_gate = jnp.sum(jnp.where(hit, weight[:, :, None, :], 0.0), axis=3)]
    all_to_all x8 -> x3, starting transfers between devices: 54.5 us -> 15.8 us  [the longest x1 6.48 us: shards(): lax.all_to_all(outgoing[0], ALL, split_axis=0, concat_axis=0, tiled=True)]
  transfers between devices with their start and end apart: 16 -> 29, of which waited for: 7 -> 16; matrix products, arithmetic and copies ran while one was open for 31% -> 37% of each run, Pallas kernels for 0% -> 0%
where the time goes in v1:
time: 1160 us; the launch traced here: 1150 us
  waiting for transfers between devices  565 us (49%)
  matrix products  259 us (22%)
  other arithmetic  109 us (9%)
  local copies, waits for them, and re-layouts  107 us (9%)
  blocking collectives  54.6 us (5%)
  starting transfers between devices  35.6 us (3%)
  between operations  15.3 us (1%)
    ppermute x18, waiting for transfers between devices, swap(): return lax.ppermute(block, 'lo', [(i, i ^ step) for i in range(lo_count)])  209 us
    reduce_scatter x1, waiting for transfers between devices, shards(): lax.psum_scatter(grad_weights_in.astype(jnp.bfloat16).reshape(hi_count *...  125 us
    reduce_scatter x1, waiting for transfers between devices, shards(): lax.psum_scatter(jnp.concatenate([grad_qkv_weight, gain_column(grad_gain_...  83.2 us
    all_to_all x1, waiting for transfers between devices, shards(): lax.all_to_all(leaving[1], ALL, split_axis=0, concat_axis=0, tiled=True)  67.3 us
    all_to_all x1, waiting for transfers between devices, shards(): lax.all_to_all(outgoing[1], ALL, split_axis=0, concat_axis=0, tiled=True)  56.2 us
    all_to_all x1, blocking collectives, shards(): lax.all_to_all(leaving[0], ALL, split_axis=0, concat_axis=0, tiled=True)  43.8 us
    dot_general x1, matrix products, shards(): jnp.einsum('erd,ekdf->ekrf', expert_rows, weights_in, preferred_element_t...  25.2 us
    convert_element_type x1, other arithmetic, attend_back(): grad_scores = (exact_probs * (grad_probs - jnp.sum(grad_probs * exact_pro...  23.9 us
  transfers between devices with their start and end apart: 29, of which 16 were waited for; matrix products, arithmetic and copies ran while one was open for 37% of the time, Pallas kernels for 0%

profile of v1, /device:TPU:12, one launch (start us, length us, event | category | flops | bytes accessed | tf_op | source)
XLA Modules:
  0.0 1145.6 jit_solution(10371708990704417468)
XLA Ops:
  11.4 3.7 all_gather_reshape.3
  17.7 10.9 all_to_all.29
  29.9 2.9 gather_fusion.4
  35.8 3.4 broadcast_select_fusion.6
  39.2 5.0 all-to-all-start.3
  50.2 56.2 %all-to-all-done.3 = bf16[32,16,1536]{2,1,0:T(8,128)(2,1)S(1)} async-done(((bf16[32,16,1536]{2,1,0:T(8,128)(2,1)}), bf16[32,16,1536]{2,1,0:T(8,128)(2,1)S(1)}, u32[]{:S(2)}, u32[]{:S(2)}) %all-to-all-start.3) | async-done | bytes 1572896 | tf_op jit(solution)/shard_map/all_to_all | solution.py:183
  106.3 6.5 all-to-all-start.1
  116.6 3.1 gather_fusion.5
  127.2 4.7 select_reduce_fusion
  131.8 23.7 %all-to-all-done.1 = bf16[32,16,1536]{2,1,0:T(8,128)(2,1)S(1)} async-done(((bf16[32,16,1536]{2,1,0:T(8,128)(2,1)}), bf16[32,16,1536]{2,1,0:T(8,128)(2,1)S(1)}, u32[]{:S(2)}, u32[]{:S(2)}) %all-to-all-start.1) | async-done | bytes 1572896 | tf_op jit(solution)/shard_map/all_to_all | solution.py:182
  160.7 17.7 %collective-permute-done.12 = bf16[512,1536]{1,0:T(8,128)(2,1)} collective-permute-done((bf16[512,1536]{1,0:T(8,128)(2,1)}, bf16[512,1536]{1,0:T(8,128)(2,1)}, u32[]{:S(2)}, u32[]{:S(2)}) %collective-permute-start.12) | collective-permute-done | bytes 1572896 | tf_op jit(solution)/shard_map/ppermute | solution.py:237
  178.4 36.2 %collective-permute-done.14 = bf16[512,1536]{1,0:T(8,128)(2,1)} collective-permute-done((bf16[512,1536]{1,0:T(8,128)(2,1)}, bf16[512,1536]{1,0:T(8,128)(2,1)}, u32[]{:S(2)}, u32[]{:S(2)}) %collective-permute-start.14) | collective-permute-done | bytes 1572896 | tf_op jit(solution)/shard_map/ppermute | solution.py:237
  214.5 3.3 pad_maximum_fusion.2
  217.9 7.3 convolution_bitcast_fusion
  225.2 9.4 copy.126
  236.4 6.9 fusion.29
  246.3 3.6 copy.116
  253.9 10.4 fusion.21
  264.4 11.5 %fusion.5 = f32[8,3,512]{2,1,0:T(4,128)S(1)} fusion(f32[8,3,512]{2,1,0:T(4,128)S(1)} %get-tuple-element.82, f32[8,512,512,3]{2,1,3,0:T(8,128)} %get-tuple-element.83, pred[512,512]{0,1:T(8,128)(4,1)S(1)} %compare_and_fusion), kind=kLoop, calls=%fused_computation.22 | loop fusion | flops 25153536 | bytes 25526272 | tf_op jit(solution)/shard_map/reduce_sum | solution.py:92
  276.6 12.1 %fusion.71 = bf16[8,64,3,512]{3,1,2,0:T(8,128)(2,1)S(1)} fusion(bf16[512,8,64,1]{0,2,3,1:T(8,128)(2,1)S(1)} %bitcast.282, f32[8,3,512]{2,1,0:T(4,128)S(1)} %fusion.5, f32[8,3,512]{2,1,0:T(4,128)S(1)} %get-tuple-element.82, f32[8,512,512,3]{2,1,3,0:T(8,128)} %get-tuple-element.83, pred[512,512]{0,1:T(8,128)(4,1)S(1)} %compare_and_fusion), kind=kOutput, calls=%fused_computation.109 | convolution fusion | flops 837550080 | bytes 27623424 | tf_op jit(solution)/shard_map/hgqk,khd->qhgd/dot_general | solution.py:94
  288.7 5.4 multiply_reduce_fusion.2
  298.0 13.5 %fusion.3 = bf16[4,1024,1536]{2,1,0:T(8,128)(2,1)} fusion(f32[4,8,128,1536]{3,2,1,0:T(8,128)} %copy.126, f32[4,1024]{1,0:T(4,128)S(1)} %bitcast.299), kind=kLoop, calls=%fused_computation.15 | loop fusion | flops 12582912 | bytes 37765120 | tf_op jit(solution)/shard_map/convert_element_type | solution.py:283
  311.9 19.0 %collective-permute-done.4 = bf16[512,1536]{1,0:T(8,128)(2,1)S(1)} collective-permute-done((bf16[512,1536]{1,0:T(8,128)(2,1)S(1)}, bf16[512,1536]{1,0:T(8,128)(2,1)S(1)}, u32[]{:S(2)}, u32[]{:S(2)}) %collective-permute-start.4) | collective-permute-done | bytes 1572896 | tf_op jit(solution)/shard_map/ppermute | solution.py:237
  332.6 32.3 %collective-permute-done.5 = bf16[512,1536]{1,0:T(8,128)(2,1)S(1)} collective-permute-done((bf16[512,1536]{1,0:T(8,128)(2,1)S(1)}, bf16[512,1536]{1,0:T(8,128)(2,1)S(1)}, u32[]{:S(2)}, u32[]{:S(2)}) %collective-permute-start.5) | collective-permute-done | bytes 1572896 | tf_op jit(solution)/shard_map/ppermute | solution.py:237
  365.8 7.3 fusion.20
  373.1 5.4 copy.121
  378.5 25.2 %convolution_bitcast_fusion.1 = f32[4,2,1024,512]{2,3,1,0:T(8,128)} fusion(bf16[4,1024,1536,1]{2,1,3,0:T(8,128)(2,1)} %bitcast.265, bf16[4,2,1536,512]{3,2,1,0:T(8,128)(2,1)} %bitcast.311), kind=kOutput, calls=%fused_computation.45 | convolution fusion | flops 12884901888 | bytes 41943040 | tf_op jit(solution)/shard_map/erd,ekdf->ekrf/dot_general | solution.py:252
  403.8 18.7 %fusion.24 = (bf16[4,2,1024,256]{2,3,1,0:T(8,128)(2,1)}, bf16[4,2,1024,256]{2,3,1,0:T(8,128)(2,1)}, bf16[4,2,1024,256]{2,3,1,0:T(8,128)(2,1)S(1)}) fusion(f32[4,2,1024,512]{2,3,1,0:T(8,128)} %convolution_bitcast_fusion.1, bf16[4,2,256,1536]{3,2,1,0:T(8,128)(2,1)} %bitcast.313, bf16[4,1024,1536]{2,1,0:T(8,128)(2,1)} %fusion.3), kind=kOutput, calls=%fused_computation.51 | convolution fusion | flops 6473908224 | bytes 48234496 | tf_op jit(solution)/shard_map/erd,ekfd->ekrf/dot_general | solution.py:284
  422.5 14.7 %fusion.37 = bf16[4,2,256,1536]{3,2,1,0:T(8,128)(2,1)} fusion(bf16[4,2,1024,256]{2,3,1,0:T(8,128)(2,1)S(1)} %get-tuple-element.54, bf16[4,1024,1536]{2,1,0:T(8,128)(2,1)} %fusion.3), kind=kOutput, calls=%fused_computation.69 | convolution fusion | flops 6445596672 | bytes 23068672 | tf_op jit(solution)/shard_map/ekrf,erd->ekfd/dot_general | solution.py:287
  437.3 21.5 %bitcast_convert_fusion = bf16[4,1024,1536]{2,1,0:T(8,128)(2,1)} fusion(bf16[4,2,1536,512]{3,2,1,0:T(8,128)(2,1)} %bitcast.312, bf16[4,2,1024,256]{2,3,1,0:T(8,128)(2,1)} %get-tuple-element.53, bf16[4,2,1024,256]{2,3,1,0:T(8,128)(2,1)} %get-tuple-element.52), kind=kOutput, calls=%fused_computation.13 | convolution fusion | flops 12907970560 | bytes 33554432 | tf_op jit(solution)/shard_map/ekrf,ekdf->erd/dot_general | solution.py:296
  458.8 9.8 fusion.111
  474.4 13.1 %fusion.4 = bf16[4,1024,1536]{2,1,0:T(8,128)(2,1)} fusion(bf16[4,2,1024,256]{2,3,1,0:T(8,128)(2,1)} %copy-done.52, bf16[4,2,256,1536]{3,2,1,0:T(8,128)(2,1)} %bitcast.314, f32[4,1024]{1,0:T(4,128)S(1)} %bitcast.300), kind=kOutput, calls=%fused_computation.17 | convolution fusion | flops 6455033856 | bytes 23085056 | tf_op jit(solution)/shard_map/ekrf,ekfd->erd/dot_general | solution.py:261
  487.5 9.8 fusion.112
  501.7 7.6 collective-permute-done.17
  510.5 31.9 %collective-permute-done.15 = bf16[512,1536]{1,0:T(8,128)(2,1)} collective-permute-done((bf16[512,1536]{1,0:T(8,128)(2,1)}, bf16[512,1536]{1,0:T(8,128)(2,1)}, u32[]{:S(2)}, u32[]{:S(2)}) %collective-permute-start.15) | collective-permute-done | bytes 1572896 | tf_op jit(solution)/shard_map/ppermute | solution.py:237
  543.2 3.2 multiply_reduce_fusion
  546.4 30.4 %collective-permute-done.11 = bf16[512,1536]{1,0:T(8,128)(2,1)} collective-permute-done((bf16[512,1536]{1,0:T(8,128)(2,1)}, bf16[512,1536]{1,0:T(8,128)(2,1)}, u32[]{:S(2)}, u32[]{:S(2)}) %collective-permute-start.11) | collective-permute-done | bytes 1572896 | tf_op jit(solution)/shard_map/ppermute | solution.py:237
  576.9 30.0 %collective-permute-done.9 = bf16[512,1536]{1,0:T(8,128)(2,1)} collective-permute-done((bf16[512,1536]{1,0:T(8,128)(2,1)}, bf16[512,1536]{1,0:T(8,128)(2,1)}, u32[]{:S(2)}, u32[]{:S(2)}) %collective-permute-start.9) | collective-permute-done | bytes 1572896 | tf_op jit(solution)/shard_map/ppermute | solution.py:237
  607.7 4.1 subtract_add_fusion
  616.4 4.8 select_maximum_fusion.1
  621.2 11.1 copy.160
  633.2 7.1 convolution_convert_fusion.2
  642.5 22.7 %fusion = (f32[8,3,512]{2,1,0:T(4,128)S(1)}, f32[8,512,512,3]{2,1,3,0:T(8,128)}) fusion(f32[8,3,512]{2,1,0:T(4,128)S(1)} %log_add_fusion, f32[8,512,512,3]{2,1,3,0:T(8,128)} %get-tuple-element.83, pred[512,512]{0,1:T(8,128)(4,1)S(1)} %copy-done.16, bf16[512,8,64,1]{0,2,3,1:T(8,128)(2,1)} %bitcast.281, bf16[512,8,3,64]{0,3,2,1:T(8,128)(2,1)S(1)} %bitcast.268), kind=kOutput, calls=%fused_computation.10 | convolution fusion | flops 836751360 | bytes 52789248 | tf_op jit(solution)/shard_map/qhgd,khd->hgqk/dot_general | solution.py:106
  665.2 23.9 %fusion.2 = bf16[8,3,512,512]{2,3,1,0:T(8,128)(2,1)} fusion(f32[8,512,512,3]{2,1,3,0:T(8,128)} %get-tuple-element.91, f32[8,3,512]{2,1,0:T(4,128)S(1)} %get-tuple-element.90, f32[8,3,512]{2,1,0:T(4,128)S(1)} %log_add_fusion, f32[8,512,512,3]{2,1,3,0:T(8,128)} %get-tuple-element.83, pred[512,512]{0,1:T(8,128)(4,1)S(1)} %copy-done.16), kind=kLoop, calls=%fused_computation.12 | loop fusion | flops 37748736 | bytes 63275008 | tf_op jit(solution)/shard_map/convert_element_type | solution.py:114
  689.1 8.6 fusion.76
  698.0 7.0 convolution_multiply_fusion
  706.4 12.1 %fusion.77 = bf16[8,64,512]{2,1,0:T(8,128)(2,1)S(1)} fusion(bf16[512,8,3,64]{0,3,2,1:T(8,128)(2,1)S(1)} %bitcast.269, f32[8,3,512]{2,1,0:T(4,128)S(1)} %log_add_fusion, f32[8,512,512,3]{2,1,3,0:T(8,128)} %get-tuple-element.83, pred[512,512]{0,1:T(8,128)(4,1)S(1)} %copy-done.16), kind=kOutput, calls=%fused_computation.128 | convolution fusion | flops 830734336 | bytes 27574272 | tf_op jit(solution)/shard_map/hgqk,qhgd->khd/dot_general | solution.py:109
  718.5 9.9 fusion.56
  728.7 4.7 fusion.80
  733.4 6.0 select_maximum_fusion
  739.5 22.2 %fusion.19 = bf16[4,2,1536,512]{2,3,1,0:T(8,128)(2,1)} fusion(bf16[4,1024,1536,1]{2,1,3,0:T(8,128)(2,1)} %bitcast.266, bf16[4,2,1024,256]{2,3,1,0:T(8,128)(2,1)} %get-tuple-element.53, bf16[4,2,1024,256]{2,3,1,0:T(8,128)(2,1)} %get-tuple-element.52), kind=kOutput, calls=%fused_computation.40 | convolution fusion | flops 12907970560 | bytes 33554432 | tf_op jit(solution)/shard_map/erd,ekrf->ekdf/dot_general | solution.py:293
  761.7 16.7 %copy.135 = bf16[4,2,1536,512]{3,2,1,0:T(8,128)(2,1)} copy(bf16[4,2,1536,512]{2,3,1,0:T(8,128)(2,1)} %fusion.19) | data formatting | bytes 25165824 | tf_op jit(solution)/shard_map/convert_element_type | solution.py:308
  779.1 2.9 gather_fusion.2
  782.1 3.5 fusion.52
  785.6 2.9 gather_fusion.6
  788.6 3.0 broadcast_select_fusion.2
  791.6 43.8 %all_to_all.30 = bf16[32,16,1536]{2,1,0:T(8,128)(2,1)S(1)} all-to-all(bf16[32,16,1536]{2,1,0:T(8,128)(2,1)S(1)} %bitcast.273), channel_id=1, replica_groups=mesh['hi'=4,'lo'=4,'core'=2] {'hi','lo','core'}, dimensions={0} | all-to-all | bytes 3145728 | tf_op jit(solution)/shard_map/all_to_all | solution.py:378
  835.4 4.3 all-to-all-start.4
  839.9 2.9 gather_fusion.3
  842.8 67.3 %all-to-all-done.4 = bf16[32,16,1536]{2,1,0:T(8,128)(2,1)S(1)} async-done(((bf16[32,16,1536]{2,1,0:T(8,128)(2,1)}), bf16[32,16,1536]{2,1,0:T(8,128)(2,1)S(1)}, u32[]{:S(2)}, u32[]{:S(2)}) %all-to-all-start.4) | async-done | bytes 1572896 | tf_op jit(solution)/shard_map/all_to_all | solution.py:379
  913.0 3.5 broadcast_select_fusion
  922.0 83.2 %reduce-scatter.7.cloned.1.call-done = f32[48,2688]{1,0:T(8,128)} async-done(((f32[1536,2688]{1,0:T(8,128)}), f32[48,2688]{1,0:T(8,128)}) %reduce-scatter.7.cloned.1.call-update) | async-done | bytes 516112 | tf_op jit(solution)/shard_map/reduce_scatter | solution.py:365
  1008.4 125.5 %reduce-scatter.9.cloned.1.call-done = bf16[1536,512]{1,0:T(8,128)(2,1)} async-done(((bf16[12288,512]{1,0:T(8,128)(2,1)}), bf16[1536,512]{1,0:T(8,128)(2,1)}) %reduce-scatter.9.cloned.1.call-update) | async-done | bytes 1572880 | tf_op jit(solution)/shard_map/reduce_scatter | solution.py:307
  1133.9 4.7 reshape.385
  (246 shorter events, 84.5 us)
Async XLA Ops:
  7.2 22.7 %copy-start = (bf16[512,1536]{1,0:T(8,128)(2,1)S(1)}, bf16[512,1536]{1,0:T(8,128)(2,1)}, u32[]{:S(2)}) copy-start(bf16[512,1536]{1,0:T(8,128)(2,1)} %param.15) | copy-start | bytes 4718596
  7.2 8.0 copy-start.51
  7.2 227.4 %all-gather.6.cloned.1.call-start = ((), (), s32[]{:S(2)}) async-start(), calls=%async_computation.9 | async-start | bytes 8515584 | tf_op jit(solution)/shard_map/all_gather | solution.py:192
  10.6 278.1 %all-gather.8.cloned.1.call-start = ((), (), s32[]{:S(2)}) async-start(), calls=%async_computation.10 | async-start | bytes 4866048 | tf_op jit(solution)/shard_map/all_gather | solution.py:199
  11.4 367.2 %all-gather.10.cloned.1.call-start = ((), (), s32[]{:S(2)}) async-start(), calls=%async_computation.11 | async-start | bytes 14155776 | tf_op jit(solution)/shard_map/all_gather | solution.py:201
  16.8 271.9 %copy-start.43 = (pred[512]{0:T(512)(128)(4,1)}, pred[512]{0:T(512)(128)(4,1)S(1)}, u32[]{:S(2)}) copy-start(pred[512]{0:T(512)(128)(4,1)S(1)} %get-tuple-element.50) | copy-start | bytes 1540
  29.9 5.9 copy-start.41
  39.2 8.6 copy-start.47
  39.2 10.6 copy-start.50
  39.2 67.1 %all-to-all-start.3 = ((bf16[32,16,1536]{2,1,0:T(8,128)(2,1)}), bf16[32,16,1536]{2,1,0:T(8,128)(2,1)S(1)}, u32[]{:S(2)}, u32[]{:S(2)}) async-start(bf16[32,16,1536]{2,1,0:T(8,128)(2,1)} %bitcast.59), calls=%async_computation.3 | async-start | bytes 3145728 | tf_op jit(solution)/shard_map/all_to_all | solution.py:183
  44.2 359.6 %all-gather.12.cloned.1.call-start = ((), (), s32[]{:S(2)}) async-start(), calls=%async_computation.15 | async-start | bytes 7077888 | tf_op jit(solution)/shard_map/all_gather | solution.py:204
  44.3 70.1 %collective-permute-start = (s32[512,8]{0,1:T(8,128)S(1)}, s32[512,8]{0,1:T(8,128)}, u32[]{:S(2)}, u32[]{:S(2)}) collective-permute-start(s32[512,8]{0,1:T(8,128)S(1)} %copy-done.46), channel_id=1, source_target_pairs={{0,2},{2,0},{4,6},{6,4},{1,3},{3,1},{5,7},{7,5},{8,10},{10,8},{12,... | collective-permute-start | bytes 49160 | tf_op jit(solution)/shard_map/ppermute | solution.py:237
  45.8 69.2 %collective-permute-start.2 = (s32[512,8]{0,1:T(8,128)S(1)}, s32[512,8]{0,1:T(8,128)}, u32[]{:S(2)}, u32[]{:S(2)}) collective-permute-start(s32[512,8]{0,1:T(8,128)S(1)} %copy-done.46), channel_id=1, source_target_pairs={{0,6},{2,4},{4,2},{6,0},{1,7},{3,5},{5,3},{7,1},{8,14},{10,12},{12... | collective-permute-start | bytes 49160 | tf_op jit(solution)/shard_map/ppermute | solution.py:237
  46.3 68.7 %collective-permute-start.1 = (s32[512,8]{0,1:T(8,128)S(1)}, s32[512,8]{0,1:T(8,128)}, u32[]{:S(2)}, u32[]{:S(2)}) collective-permute-start(s32[512,8]{0,1:T(8,128)S(1)} %copy-done.46), channel_id=1, source_target_pairs={{0,4},{2,6},{4,0},{6,2},{1,5},{3,7},{5,1},{7,3},{8,12},{10,14},{12... | collective-permute-start | bytes 49160 | tf_op jit(solution)/shard_map/ppermute | solution.py:237
  47.8 77.6 %collective-permute-start.6 = (f32[512,8]{0,1:T(8,128)S(1)}, f32[512,8]{0,1:T(8,128)}, u32[]{:S(2)}, u32[]{:S(2)}) collective-permute-start(f32[512,8]{0,1:T(8,128)S(1)} %copy-done.47), channel_id=1, source_target_pairs={{0,2},{2,0},{4,6},{6,4},{1,3},{3,1},{5,7},{7,5},{8,10},{10,8},{12,... | collective-permute-start | bytes 49160 | tf_op jit(solution)/shard_map/ppermute | solution.py:237
  49.3 76.9 %collective-permute-start.8 = (f32[512,8]{0,1:T(8,128)S(1)}, f32[512,8]{0,1:T(8,128)}, u32[]{:S(2)}, u32[]{:S(2)}) collective-permute-start(f32[512,8]{0,1:T(8,128)S(1)} %copy-done.47), channel_id=1, source_target_pairs={{0,6},{2,4},{4,2},{6,0},{1,7},{3,5},{5,3},{7,1},{8,14},{10,12},{12... | collective-permute-start | bytes 49160 | tf_op jit(solution)/shard_map/ppermute | solution.py:237
  106.3 49.2 %all-to-all-start.1 = ((bf16[32,16,1536]{2,1,0:T(8,128)(2,1)}), bf16[32,16,1536]{2,1,0:T(8,128)(2,1)S(1)}, u32[]{:S(2)}, u32[]{:S(2)}) async-start(bf16[32,16,1536]{2,1,0:T(8,128)(2,1)} %bitcast.271), calls=%async_computation.1 | async-start | bytes 3145728 | tf_op jit(solution)/shard_map/all_to_all | solution.py:182
  112.8 803.7 %reduce-scatter.11.cloned.1.call-start = ((), (), s32[]{:S(2)}) async-start(), calls=%async_computation.14 | async-start | bytes 7077888 | tf_op jit(solution)/shard_map/reduce_scatter | solution.py:300
  114.0 139.7 %copy-start.25 = (f32[512,32]{0,1:T(8,128)}, f32[512,32]{0,1:T(8,128)S(1)}, u32[]{:S(2)}) copy-start(f32[512,32]{0,1:T(8,128)S(1)} %get-tuple-element.73) | copy-start | bytes 196612
  114.3 161.6 %copy-start.15 = (pred[512,512]{0,1:T(8,128)(4,1)}, pred[512,512]{0,1:T(8,128)(4,1)S(1)}, u32[]{:S(2)}) copy-start(pred[512,512]{0,1:T(8,128)(4,1)S(1)} %compare_and_fusion) | copy-start | bytes 786436
  114.4 11.9 %collective-permute-start.7 = (f32[512,8]{0,1:T(8,128)S(1)}, f32[512,8]{0,1:T(8,128)}, u32[]{:S(2)}, u32[]{:S(2)}) collective-permute-start(f32[512,8]{0,1:T(8,128)S(1)} %copy-done.47), channel_id=1, source_target_pairs={{0,4},{2,6},{4,0},{6,2},{1,5},{3,7},{5,1},{7,3},{8,12},{10,14},{12... | collective-permute-start | bytes 49160 | tf_op jit(solution)/shard_map/ppermute | solution.py:237
  119.7 7.3 copy-start.34
  122.5 55.9 %collective-permute-start.12 = (bf16[512,1536]{1,0:T(8,128)(2,1)}, bf16[512,1536]{1,0:T(8,128)(2,1)}, u32[]{:S(2)}, u32[]{:S(2)}) collective-permute-start(bf16[512,1536]{1,0:T(8,128)(2,1)} %broadcast_select_fusion.4), channel_id=1, source_target_pairs={{0,2},{2,0},{4,6},{6,4},{1,3},{3,1},{5,7},{7,5},{8,10},{10,8},{12,... | collective-permute-start | bytes 4718600 | tf_op jit(solution)/shard_map/ppermute | solution.py:237
  124.0 54.4 %collective-permute-start.13 = (bf16[512,1536]{1,0:T(8,128)(2,1)}, bf16[512,1536]{1,0:T(8,128)(2,1)}, u32[]{:S(2)}, u32[]{:S(2)}) collective-permute-start(bf16[512,1536]{1,0:T(8,128)(2,1)} %broadcast_select_fusion.4), channel_id=1, source_target_pairs={{0,4},{2,6},{4,0},{6,2},{1,5},{3,7},{5,1},{7,3},{8,12},{10,14},{12... | collective-permute-start | bytes 4718600 | tf_op jit(solution)/shard_map/ppermute | solution.py:237
  125.4 89.1 %collective-permute-start.14 = (bf16[512,1536]{1,0:T(8,128)(2,1)}, bf16[512,1536]{1,0:T(8,128)(2,1)}, u32[]{:S(2)}, u32[]{:S(2)}) collective-permute-start(bf16[512,1536]{1,0:T(8,128)(2,1)} %broadcast_select_fusion.4), channel_id=1, source_target_pairs={{0,6},{2,4},{4,2},{6,0},{1,7},{3,5},{5,3},{7,1},{8,14},{10,12},{12... | collective-permute-start | bytes 4718600 | tf_op jit(solution)/shard_map/ppermute | solution.py:237
  160.5 75.9 %copy-start.48 = (f32[512]{0:T(512)}, f32[512]{0:T(512)S(1)}, u32[]{:S(2)}) copy-start(f32[512]{0:T(512)S(1)} %add_rsqrt_fusion.1) | copy-start | bytes 6148
  225.2 11.1 copy-start.8
  236.3 6.9 copy-start.39
  253.7 10.7 copy-start.18
  253.7 10.7 copy-start.20
  253.9 10.5 copy-start.27
  253.9 10.5 copy-start.29
  264.4 11.6 %copy-start.35 = (f32[8,3,512]{2,1,0:T(4,128)}, f32[8,3,512]{2,1,0:T(4,128)S(1)}, u32[]{:S(2)}) copy-start(f32[8,3,512]{2,1,0:T(4,128)S(1)} %get-tuple-element.82) | copy-start | bytes 147460
  264.4 12.2 %copy-start.24 = (bf16[512,512]{0,1:T(8,128)(2,1)S(1)}, bf16[512,512]{0,1:T(8,128)(2,1)}, u32[]{:S(2)}) copy-start(bf16[512,512]{0,1:T(8,128)(2,1)} %copy.114) | copy-start | bytes 1572868
  294.1 17.4 %copy-start.3 = (f32[512,1536]{1,0:T(8,128)}, f32[512,1536]{1,0:T(8,128)S(1)}, u32[]{:S(2)}) copy-start(f32[512,1536]{1,0:T(8,128)S(1)} %get-tuple-element.85) | copy-start | bytes 9437188
  294.5 36.4 %collective-permute-start.4 = (bf16[512,1536]{1,0:T(8,128)(2,1)S(1)}, bf16[512,1536]{1,0:T(8,128)(2,1)S(1)}, u32[]{:S(2)}, u32[]{:S(2)}) collective-permute-start(bf16[512,1536]{1,0:T(8,128)(2,1)S(1)} %multiply_convert_fusion.1), channel_id=1, source_target_pairs={{0,4},{2,6},{4,0},{6,2},{1,5},{3,7},{5,1},{7,3},{8,12},{10,14},{12... | collective-permute-start | bytes 4718600 | tf_op jit(solution)/shard_map/ppermute | solution.py:237
  295.4 37.3 %collective-permute-start.3 = (bf16[512,1536]{1,0:T(8,128)(2,1)S(1)}, bf16[512,1536]{1,0:T(8,128)(2,1)S(1)}, u32[]{:S(2)}, u32[]{:S(2)}) collective-permute-start(bf16[512,1536]{1,0:T(8,128)(2,1)S(1)} %multiply_convert_fusion.1), channel_id=1, source_target_pairs={{0,2},{2,0},{4,6},{6,4},{1,3},{3,1},{5,7},{7,5},{8,10},{10,8},{12,... | collective-permute-start | bytes 4718600 | tf_op jit(solution)/shard_map/ppermute | solution.py:237
  296.6 68.3 %collective-permute-start.5 = (bf16[512,1536]{1,0:T(8,128)(2,1)S(1)}, bf16[512,1536]{1,0:T(8,128)(2,1)S(1)}, u32[]{:S(2)}, u32[]{:S(2)}) collective-permute-start(bf16[512,1536]{1,0:T(8,128)(2,1)S(1)} %multiply_convert_fusion.1), channel_id=1, source_target_pairs={{0,6},{2,4},{4,2},{6,0},{1,7},{3,5},{5,3},{7,1},{8,14},{10,12},{12... | collective-permute-start | bytes 4718600 | tf_op jit(solution)/shard_map/ppermute | solution.py:237
  422.5 14.7 %copy-start.52 = (bf16[4,2,1024,256]{2,3,1,0:T(8,128)(2,1)}, bf16[4,2,1024,256]{2,3,1,0:T(8,128)(2,1)S(1)}, u32[]{:S(2)}) copy-start(bf16[4,2,1024,256]{2,3,1,0:T(8,128)(2,1)S(1)} %get-tuple-element.54) | copy-start | bytes 12582916
  437.2 481.7 %reduce-scatter.13.cloned.1.call-start = ((), (), s32[]{:S(2)}) async-start(), calls=%async_computation.16 | async-start | bytes 10543104
  470.9 38.4 %collective-permute-start.17 = (bf16[512,1536]{1,0:T(8,128)(2,1)}, bf16[512,1536]{1,0:T(8,128)(2,1)S(1)}, u32[]{:S(2)}, u32[]{:S(2)}) collective-permute-start(bf16[512,1536]{1,0:T(8,128)(2,1)} %bitcast.82), channel_id=1, source_target_pairs={{0,6},{2,4},{4,2},{6,0},{1,7},{3,5},{5,3},{7,1},{8,14},{10,12},{12... | collective-permute-start | bytes 4718600 | tf_op jit(solution)/shard_map/ppermute | solution.py:237
  472.6 69.8 %collective-permute-start.15 = (bf16[512,1536]{1,0:T(8,128)(2,1)}, bf16[512,1536]{1,0:T(8,128)(2,1)}, u32[]{:S(2)}, u32[]{:S(2)}) collective-permute-start(bf16[512,1536]{1,0:T(8,128)(2,1)} %bitcast.80), channel_id=1, source_target_pairs={{0,2},{2,0},{4,6},{6,4},{1,3},{3,1},{5,7},{7,5},{8,10},{10,8},{12,... | collective-permute-start | bytes 4718600 | tf_op jit(solution)/shard_map/ppermute | solution.py:237
  473.0 70.1 %collective-permute-start.16 = (bf16[512,1536]{1,0:T(8,128)(2,1)}, bf16[512,1536]{1,0:T(8,128)(2,1)}, u32[]{:S(2)}, u32[]{:S(2)}) collective-permute-start(bf16[512,1536]{1,0:T(8,128)(2,1)} %bitcast.81), channel_id=1, source_target_pairs={{0,4},{2,6},{4,0},{6,2},{1,5},{3,7},{5,1},{7,3},{8,12},{10,14},{12... | collective-permute-start | bytes 4718600 | tf_op jit(solution)/shard_map/ppermute | solution.py:237
  499.6 77.3 %collective-permute-start.11 = (bf16[512,1536]{1,0:T(8,128)(2,1)}, bf16[512,1536]{1,0:T(8,128)(2,1)}, u32[]{:S(2)}, u32[]{:S(2)}) collective-permute-start(bf16[512,1536]{1,0:T(8,128)(2,1)} %bitcast.56), channel_id=1, source_target_pairs={{0,6},{2,4},{4,2},{6,0},{1,7},{3,5},{5,3},{7,1},{8,14},{10,12},{12... | collective-permute-start | bytes 4718600 | tf_op jit(solution)/shard_map/ppermute | solution.py:237
  501.2 105.6 %collective-permute-start.9 = (bf16[512,1536]{1,0:T(8,128)(2,1)}, bf16[512,1536]{1,0:T(8,128)(2,1)}, u32[]{:S(2)}, u32[]{:S(2)}) collective-permute-start(bf16[512,1536]{1,0:T(8,128)(2,1)} %bitcast.54), channel_id=1, source_target_pairs={{0,2},{2,0},{4,6},{6,4},{1,3},{3,1},{5,7},{7,5},{8,10},{10,8},{12,... | collective-permute-start | bytes 4718600 | tf_op jit(solution)/shard_map/ppermute | solution.py:237
  509.3 98.4 %collective-permute-start.10 = (bf16[512,1536]{1,0:T(8,128)(2,1)}, bf16[512,1536]{1,0:T(8,128)(2,1)}, u32[]{:S(2)}, u32[]{:S(2)}) collective-permute-start(bf16[512,1536]{1,0:T(8,128)(2,1)} %bitcast.55), channel_id=1, source_target_pairs={{0,4},{2,6},{4,0},{6,2},{1,5},{3,7},{5,1},{7,3},{8,12},{10,14},{12... | collective-permute-start | bytes 4718600 | tf_op jit(solution)/shard_map/ppermute | solution.py:237
  510.2 33.0 %copy-start.4 = (f32[512,1536]{1,0:T(8,128)S(1)}, f32[512,1536]{1,0:T(8,128)}, u32[]{:S(2)}) copy-start(f32[512,1536]{1,0:T(8,128)} %copy-done.3) | copy-start | bytes 9437188
  510.4 97.3 %copy-start.7 = (bf16[512,1536]{1,0:T(8,128)(2,1)S(1)}, bf16[512,1536]{1,0:T(8,128)(2,1)}, u32[]{:S(2)}) copy-start(bf16[512,1536]{1,0:T(8,128)(2,1)} %gather_fusion.5) | copy-start | bytes 4718596
  510.4 97.3 %copy-start.44 = (pred[512]{0:T(512)(128)(4,1)S(1)}, pred[512]{0:T(512)(128)(4,1)}, u32[]{:S(2)}) copy-start(pred[512]{0:T(512)(128)(4,1)} %copy-done.43) | copy-start | bytes 1540
  632.3 372.9 %reduce-scatter.7.cloned.1.call-start = ((), (), s32[]{:S(2)}) async-start(), calls=%async_computation.12 | async-start | bytes 17031168 | tf_op jit(solution)/shard_map/reduce_scatter | solution.py:365
  642.5 22.7 %copy-start.10 = (bf16[512,1536]{0,1:T(8,128)(2,1)}, bf16[512,1536]{0,1:T(8,128)(2,1)S(1)}, u32[]{:S(2)}) copy-start(bf16[512,1536]{0,1:T(8,128)(2,1)S(1)} %copy.130) | copy-start | bytes 4718596
  665.1 23.9 %copy-start.19 = (bf16[512,24,32]{0,2,1:T(8,128)(2,1)S(1)}, bf16[512,24,32]{0,2,1:T(8,128)(2,1)}, u32[]{:S(2)}) copy-start(bf16[512,24,32]{0,2,1:T(8,128)(2,1)} %copy-done.18) | copy-start | bytes 2359300
  665.2 23.9 %copy-start.21 = (bf16[512,24,32]{0,2,1:T(8,128)(2,1)S(1)}, bf16[512,24,32]{0,2,1:T(8,128)(2,1)}, u32[]{:S(2)}) copy-start(bf16[512,24,32]{0,2,1:T(8,128)(2,1)} %copy-done.20) | copy-start | bytes 2359300
  689.1 8.6 copy-start.26
  689.1 8.6 copy-start.31
  689.1 8.9 copy-start.28
  689.1 8.9 copy-start.30
  706.4 12.1 %copy-start.9 = (bf16[512,1536]{1,0:T(8,128)(2,1)S(1)}, bf16[512,1536]{1,0:T(8,128)(2,1)}, u32[]{:S(2)}) copy-start(bf16[512,1536]{1,0:T(8,128)(2,1)} %gather_fusion.1) | copy-start | bytes 4718596
  706.4 12.1 %copy-start.40 = (f32[1536]{0:T(1024)S(1)}, f32[1536]{0:T(1024)}, u32[]{:S(2)}) copy-start(f32[1536]{0:T(1024)} %copy-done.39) | copy-start | bytes 18436
  706.4 12.1 %copy-start.49 = (f32[512]{0:T(512)S(1)}, f32[512]{0:T(512)}, u32[]{:S(2)}) copy-start(f32[512]{0:T(512)} %copy-done.48) | copy-start | bytes 6148
  739.4 394.5 %reduce-scatter.9.cloned.1.call-start = ((), (), s32[]{:S(2)}) async-start(), calls=%async_computation.13 | async-start | bytes 14155776 | tf_op jit(solution)/shard_map/reduce_scatter | solution.py:307
  791.6 48.1 %copy-start.42 = (s32[512]{0:T(512)S(1)}, s32[512]{0:T(512)}, u32[]{:S(2)}) copy-start(s32[512]{0:T(512)} %copy-done.41) | copy-start | bytes 6148
  835.4 74.7 %all-to-all-start.4 = ((bf16[32,16,1536]{2,1,0:T(8,128)(2,1)}), bf16[32,16,1536]{2,1,0:T(8,128)(2,1)S(1)}, u32[]{:S(2)}, u32[]{:S(2)}) async-start(bf16[32,16,1536]{2,1,0:T(8,128)(2,1)} %bitcast.272), calls=%async_computation.4 | async-start | bytes 3145728 | tf_op jit(solution)/shard_map/all_to_all | solution.py:379
  919.7 218.9 %copy-start.1 = (bf16[512,1536]{1,0:T(8,128)(2,1)S(1)}, bf16[512,1536]{1,0:T(8,128)(2,1)}, u32[]{:S(2)}) copy-start(bf16[512,1536]{1,0:T(8,128)(2,1)} %param.15) | copy-start | bytes 4718596
  (18 other events, 49.4 us)
Sparse Core Ops, SparseCore 0:
  11.5 96.0 all-gather.5
  110.5 82.8 all-gather.7
  195.5 112.3 all-gather.9
  309.4 63.5 all-gather.11
  437.4 67.4 reduce-scatter.10
  632.5 140.8 reduce-scatter.12
  779.7 225.4 reduce-scatter.6
  1007.5 126.3 reduce-scatter.8

commit v2 on v1

--- a/solution.py
+++ b/solution.py
@@ -1,6 +1,10 @@
+import functools
+
 import jax
 import jax.numpy as jnp
 from jax import lax
+from jax.experimental import pallas as pl
+from jax.experimental.pallas import tpu as pltpu
 from jax.sharding import PartitionSpec as P
 
 HEADS = 24
@@ -128,6 +132,345 @@
         scaled_grad * values, axis=1, keepdims=True
     )
     return (grad_gain, grad_values)
+
+
+MESH = pl.DeviceIdType.MESH
+
+
+def flip(value, bits):
+    bit = 1
+    while bit <= bits:
+        if bits & bit:
+            value = value + bit * (1 - 2 * ((value // bit) % 2))
+        bit *= 2
+    return value
+
+
+def place():
+    return lax.axis_index("hi"), lax.axis_index("lo"), lax.axis_index("core")
+
+
+def greet_all(sizes):
+    hi_count, lo_count, _ = sizes
+    count = hi_count * lo_count * 2
+    hi, lo, core = place()
+    me = (hi * lo_count + lo) * 2 + core
+    barrier = pltpu.get_barrier_semaphore()
+
+    def greet(step, carry):
+        peer = (me + step) % count
+        pl.semaphore_signal(
+            barrier,
+            inc=1,
+            device_id=(peer // (2 * lo_count), (peer // 2) % lo_count, peer % 2),
+            device_id_type=MESH,
+        )
+        return carry
+
+    lax.fori_loop(1, count, greet, 0)
+    pl.semaphore_wait(barrier, count - 1)
+
+
+def send_rows(sizes, source, target, send_sem, recv_sem):
+    hi_count, lo_count, _ = sizes
+    count = hi_count * lo_count * 2
+    hi, lo, core = place()
+    me = (hi * lo_count + lo) * 2 + core
+
+    def one(step, carry):
+        peer = (me + step) % count
+        pltpu.make_async_remote_copy(
+            src_ref=source.at[peer],
+            dst_ref=target.at[me],
+            send_sem=send_sem,
+            recv_sem=recv_sem,
+            device_id=(peer // (2 * lo_count), (peer // 2) % lo_count, peer % 2),
+            device_id_type=MESH,
+        ).start()
+        return carry
+
+    lax.fori_loop(1, count, one, 0)
+
+
+def wait_rows(source, target, send_sem, recv_sem):
+    rest = pl.ds(0, source.shape[0] - 1)
+    pltpu.make_async_copy(source.at[rest], source.at[rest], send_sem).wait()
+    pltpu.make_async_copy(target.at[rest], target.at[rest], recv_sem).wait()
+
+
+def lo_steps(lo_count, turn):
+    bits = []
+    bit = 1
+    while bit < lo_count:
+        bits.append(bit)
+        bit *= 2
+    if turn:
+        bits = bits[::-1]
+    held, steps = [0], []
+    for bit in bits:
+        steps.append((bit, list(held)))
+        held = held + [offset ^ bit for offset in held]
+    return steps
+
+
+def opening_kernel(
+    sizes, rows_ref, shard_ref, got_ref, full_ref, own_sem, row_sems, hi_sems, lo_sems, core_sems
+):
+    hi_count, lo_count, _ = sizes
+    hi, lo, core = place()
+    me = (hi * lo_count + lo) * 2 + core
+    own = [
+        pltpu.make_async_copy(shard_ref, full_ref.at[hi, lo, core], own_sem.at[0]),
+        pltpu.make_async_copy(rows_ref.at[me], got_ref.at[me], own_sem.at[1]),
+    ]
+    for copy in own:
+        copy.start()
+    greet_all(sizes)
+
+    def hop(source, at, device, sems, *index):
+        return pltpu.make_async_remote_copy(
+            src_ref=source,
+            dst_ref=full_ref.at[at[0], at[1], at[2]],
+            send_sem=sems.at[0, *index],
+            recv_sem=sems.at[1, *index],
+            device_id=device,
+            device_id_type=MESH,
+        )
+
+    along_hi = {}
+    for step in range(1, hi_count):
+        along_hi[step] = hop(
+            shard_ref, (hi, lo, core), (flip(hi, step), lo, core), hi_sems, step - 1
+        )
+        along_hi[step].start()
+    send_rows(sizes, rows_ref, got_ref, row_sems.at[0], row_sems.at[1])
+
+    def across(plane, offset, first):
+        at = (flip(hi, plane), flip(lo, offset), core)
+        source = shard_ref if first else full_ref.at[at[0], at[1], at[2]]
+        copy = hop(source, at, (hi, lo, 1 - core), core_sems, plane, offset)
+        copy.start()
+        return copy
+
+    started, waits = [], []
+    for plane in range(hi_count):
+        if plane:
+            along_hi[plane].wait_recv()
+        started.append(across(plane, 0, plane == 0))
+        number = 0
+        for bit, offsets in lo_steps(lo_count, plane % 2):
+            for offset in offsets:
+                at = (flip(hi, plane), flip(lo, offset), core)
+                source = shard_ref if plane == 0 and offset == 0 else full_ref.at[at[0], at[1], at[2]]
+                copy = hop(source, at, (hi, flip(lo, bit), core), lo_sems, plane, number)
+                number += 1
+                if offset == 0:
+                    copy.start()
+                    started.append(copy)
+                waits.append((copy, plane, offset, bit))
+    arrived = {}
+    for copy, plane, offset, bit in waits:
+        if offset:
+            copy.start()
+            started.append(copy)
+        copy.wait_recv()
+        started.append(across(plane, offset ^ bit, False))
+    for copy in started:
+        copy.wait_send()
+    for step in range(1, hi_count):
+        along_hi[step].wait_send()
+    for plane in range(hi_count):
+        for offset in range(lo_count):
+            at = (flip(hi, plane), flip(lo, offset), core)
+            hop(
+                full_ref.at[at[0], at[1], at[2]], at, (hi, lo, 1 - core), core_sems, plane, offset
+            ).wait_recv()
+    wait_rows(rows_ref, got_ref, row_sems.at[0], row_sems.at[1])
+    for copy in own:
+        copy.wait()
+
+
+def opening(sizes, rows, shard):
+    hi_count, lo_count, _ = sizes
+    anywhere = pl.BlockSpec(memory_space=pl.ANY)
+    return pl.pallas_call(
+        functools.partial(opening_kernel, sizes),
+        out_shape=(
+            jax.ShapeDtypeStruct(rows.shape, rows.dtype),
+            jax.ShapeDtypeStruct(sizes + shard.shape, shard.dtype),
+        ),
+        in_specs=[anywhere] * 2,
+        out_specs=(anywhere, anywhere),
+        scratch_shapes=[
+            pltpu.SemaphoreType.DMA((2,)),
+            pltpu.SemaphoreType.DMA((2,)),
+            pltpu.SemaphoreType.DMA((2, hi_count)),
+            pltpu.SemaphoreType.DMA((2, hi_count, lo_count)),
+            pltpu.SemaphoreType.DMA((2, hi_count, lo_count)),
+        ],
+        compiler_params=pltpu.CompilerParams(collective_id=0, has_side_effects=True),
+        name="opening",
+    )(rows, shard)
+
+
+def add_blocks(target, first, second):
+    rows = target.shape[0]
+    tile = 16 if rows % 16 == 0 else rows
+
+    def one(index, carry):
+        at = pl.ds(index * tile, tile)
+        target[at, :] = (
+            first[at, :].astype(jnp.float32) + second[at, :].astype(jnp.float32)
+        ).astype(target.dtype)
+        return carry
+
+    lax.fori_loop(0, rows // tile, one, 0)
+
+
+def closing_kernel(
+    sizes, out_ref, grad_ref, parts_ref, got_out, got_grad, sum_ref,
+    from_core, from_lo, from_hi, held, own_sem, row_sems, hi_sems, lo_sems, core_sems
+):
+    hi_count, lo_count, _ = sizes
+    hi, lo, core = place()
+    me = (hi * lo_count + lo) * 2 + core
+    own = [
+        pltpu.make_async_copy(out_ref.at[me], got_out.at[me], own_sem.at[0]),
+        pltpu.make_async_copy(grad_ref.at[me], got_grad.at[me], own_sem.at[1]),
+    ]
+    for copy in own:
+        copy.start()
+    greet_all(sizes)
+
+    def hop(source, target, device, sems, *index):
+        return pltpu.make_async_remote_copy(
+            src_ref=source,
+            dst_ref=target,
+            send_sem=sems.at[0, *index],
+            recv_sem=sems.at[1, *index],
+            device_id=device,
+            device_id_type=MESH,
+        )
+
+    planes = [plane for plane in range(1, hi_count)] + [0]
+    across = {}
+    for plane in planes:
+        for offset in reversed(range(lo_count)):
+            across[plane, offset] = hop(
+                parts_ref.at[flip(hi, plane), flip(lo, offset), 1 - core],
+                from_core.at[plane, offset],
+                (hi, lo, 1 - core),
+                core_sems,
+                plane,
+                offset,
+            )
+            across[plane, offset].start()
+    send_rows(sizes, grad_ref, got_grad, row_sems.at[0, 0], row_sems.at[1, 0])
+    send_rows(sizes, out_ref, got_out, row_sems.at[0, 1], row_sems.at[1, 1])
+    started = []
+    plans = {plane: lo_steps(lo_count, plane % 2)[::-1] for plane in planes}
+    moves = {}
+    for depth in range(len(plans[0])):
+        for plane in planes:
+            bit, kept = plans[plane][depth]
+            base = lo_count - 2 * len(kept)
+            if depth == 0:
+                for offset in [keep ^ bit for keep in kept] + kept:
+                    across[plane, offset].wait_recv()
+                    add_blocks(
+                        held.at[plane, offset],
+                        parts_ref.at[flip(hi, plane), flip(lo, offset), core],
+                        from_core.at[plane, offset],
+                    )
+            else:
+                before = plans[plane][depth - 1]
+                for number, offset in enumerate(before[1]):
+                    copy, spot = moves[plane, depth - 1, offset]
+                    copy.wait_recv()
+                    add_blocks(held.at[plane, offset], held.at[plane, offset], from_lo.at[plane, spot])
+            for number, offset in enumerate(kept):
+                spot = base + number
+                copy = hop(
+                    held.at[plane, offset ^ bit],
+                    from_lo.at[plane, spot],
+                    (hi, flip(lo, bit), core),
+                    lo_sems,
+                    plane,
+                    spot,
+                )
+                copy.start()
+                started.append(copy)
+                moves[plane, depth, offset] = (copy, spot)
+    last = len(plans[0]) - 1
+    along = {}
+    for plane in planes:
+        copy, spot = moves[plane, last, 0]
+        copy.wait_recv()
+        add_blocks(held.at[plane, 0], held.at[plane, 0], from_lo.at[plane, spot])
+        if plane:
+            along[plane] = hop(
+                held.at[plane, 0],
+                from_hi.at[plane],
+                (flip(hi, plane), lo, core),
+                hi_sems,
+                plane,
+            )
+            along[plane].start()
+            started.append(along[plane])
+    for plane in range(1, hi_count):
+        along[plane].wait_recv()
+    rows = sum_ref.shape[0]
+    tile = 16 if rows % 16 == 0 else rows
+
+    def total(index, carry):
+        at = pl.ds(index * tile, tile)
+        value = held[0, 0, at, :].astype(jnp.float32)
+        for plane in range(1, hi_count):
+            value = value + from_hi[plane, at, :].astype(jnp.float32)
+        sum_ref[at, :] = value
+        return carry
+
+    lax.fori_loop(0, rows // tile, total, 0)
+    for copy in started:
+        copy.wait_send()
+    for copy in across.values():
+        copy.wait_send()
+    wait_rows(grad_ref, got_grad, row_sems.at[0, 0], row_sems.at[1, 0])
+    wait_rows(out_ref, got_out, row_sems.at[0, 1], row_sems.at[1, 1])
+    for copy in own:
+        copy.wait()
+
+
+def closing(sizes, out_rows, grad_rows, parts):
+    hi_count, lo_count, _ = sizes
+    block = parts.shape[3:]
+    anywhere = pl.BlockSpec(memory_space=pl.ANY)
+    near = pl.BlockSpec(memory_space=pltpu.VMEM)
+    return pl.pallas_call(
+        functools.partial(closing_kernel, sizes),
+        out_shape=(
+            jax.ShapeDtypeStruct(out_rows.shape, out_rows.dtype),
+            jax.ShapeDtypeStruct(grad_rows.shape, grad_rows.dtype),
+            jax.ShapeDtypeStruct(block, jnp.float32),
+        ),
+        in_specs=[anywhere, anywhere, near],
+        out_specs=(anywhere, anywhere, near),
+        scratch_shapes=[
+            pltpu.VMEM((hi_count, lo_count) + block, jnp.bfloat16),
+            pltpu.VMEM((hi_count, lo_count) + block, jnp.bfloat16),
+            pltpu.VMEM((hi_count,) + block, jnp.bfloat16),
+            pltpu.VMEM((hi_count, lo_count) + block, jnp.bfloat16),
+            pltpu.SemaphoreType.DMA((2,)),
+            pltpu.SemaphoreType.DMA((2, 2)),
+            pltpu.SemaphoreType.DMA((2, hi_count)),
+            pltpu.SemaphoreType.DMA((2, hi_count, lo_count)),
+            pltpu.SemaphoreType.DMA((2, hi_count, lo_count)),
+        ],
+        compiler_params=pltpu.CompilerParams(
+            collective_id=1, has_side_effects=True, vmem_limit_bytes=60 << 20
+        ),
+        name="closing",
+    )(out_rows, grad_rows, parts)
 
 
 def shards(
@@ -174,29 +517,33 @@
     ).reshape(tok_dev)
     asked_match = asked_rows[:, None] == positions[None, :]
     by_asked = jnp.sum(jnp.where(asked_match, positions[:, None], 0), axis=0, dtype=jnp.int32)
-    outgoing = (
-        jnp.take(tokens, asked_rows, axis=0).reshape(device_count, peer_rows, model_width),
-        jnp.take(cotangent, asked_rows, axis=0).reshape(device_count, peer_rows, model_width),
-    )
-    got_rows, got_grad = (
-        lax.all_to_all(outgoing[0], ALL, split_axis=0, concat_axis=0, tiled=True),
-        lax.all_to_all(outgoing[1], ALL, split_axis=0, concat_axis=0, tiled=True),
-    )
+    sizes = (hi_count, lo_count, 2)
+    shard_rows = qkv_weight.shape[0]
+    qkv_cols = qkv_weight.shape[1]
+    weight_shard = jnp.concatenate(
+        [
+            qkv_weight,
+            out_weight,
+            attn_gain[:, None],
+            ffn_gain[:, None],
+            jnp.zeros((shard_rows, 126), jnp.bfloat16),
+        ],
+        axis=1,
+    )
+    asked_tokens = jnp.take(tokens, asked_rows, axis=0).reshape(device_count, peer_rows, model_width)
+    asked_grads = jnp.take(cotangent, asked_rows, axis=0).reshape(
+        device_count, peer_rows, model_width
+    )
+    got_rows, packed = opening(sizes, asked_tokens, weight_shard)
+    packed = packed.reshape(model_width, -1)
+    got_rows, asked_grads = lax.optimization_barrier((got_rows, asked_grads))
+    got_grad = lax.all_to_all(asked_grads, ALL, split_axis=0, concat_axis=0, tiled=True)
     rows_in = jnp.take(got_rows.reshape(tok_dev, model_width), arrival, axis=0).astype(jnp.float32)
-    grad_bf = jnp.take(got_grad.reshape(tok_dev, model_width), arrival, axis=0)
-    grad_output = grad_bf.astype(jnp.float32)
-    gains = jnp.concatenate(
-        [attn_gain[:, None], ffn_gain[:, None], jnp.zeros((attn_gain.shape[0], 126), jnp.bfloat16)],
-        axis=1,
-    )
-    packed_qkv = lax.all_gather(
-        jnp.concatenate([qkv_weight, gains], axis=1), ALL, axis=0, tiled=True
-    )
-    qkv_full = packed_qkv[:, : qkv_weight.shape[1]]
-    gain_pair = packed_qkv[:, qkv_weight.shape[1] :].astype(jnp.float32)
+    qkv_full = packed[:, :qkv_cols]
+    out_full = packed[:, qkv_cols : qkv_cols + model_width]
+    gain_pair = packed[:, qkv_cols + model_width :].astype(jnp.float32)
     gain_one = gain_pair[:, 0]
     gain_two = gain_pair[:, 1]
-    out_full = lax.all_gather(out_weight, ALL, axis=0, tiled=True)
     shard_cols = expert_in.shape[2]
     weights_in = lax.all_gather(
         expert_in.reshape(model_width, 2 * shard_cols), ("hi", "core"), axis=0
@@ -228,6 +575,9 @@
     residual = rows_in + attended
     scale_two = lax.rsqrt(jnp.mean(residual * residual, axis=1, keepdims=True) + epsilon)
     normed_two = (residual * scale_two * gain_two).astype(jnp.bfloat16)
+    got_grad, normed_two = lax.optimization_barrier((got_grad, normed_two))
+    grad_bf = jnp.take(got_grad.reshape(tok_dev, model_width), arrival, axis=0)
+    grad_output = grad_bf.astype(jnp.float32)
     home = lax.axis_index("lo")
 
     def spread(block):
@@ -297,15 +647,22 @@
         "ekrf,ekdf->erd", grad_gate_up, weights_in, preferred_element_type=jnp.float32
     ).astype(jnp.bfloat16)
     grad_normed_two = collect(grad_expert_rows)
+    grad_normed_two, grad_weights_in, grad_weights_out = lax.optimization_barrier(
+        (
+            grad_normed_two,
+            grad_weights_in.astype(jnp.bfloat16),
+            grad_weights_out.astype(jnp.bfloat16),
+        )
+    )
     shard_out = lax.psum_scatter(
-        grad_weights_out.astype(jnp.bfloat16).reshape(hi_count * 2 * shard_cols, model_width),
+        grad_weights_out.reshape(hi_count * 2 * shard_cols, model_width),
         ("hi", "core"),
         scatter_dimension=0,
         tiled=True,
     ).astype(jnp.float32)
     shard_in = (
         lax.psum_scatter(
-            grad_weights_in.astype(jnp.bfloat16).reshape(hi_count * 2 * model_width, 2 * shard_cols),
+            grad_weights_in.reshape(hi_count * 2 * model_width, 2 * shard_cols),
             ("hi", "core"),
             scatter_dimension=0,
             tiled=True,
@@ -351,33 +708,25 @@
     )
     grad_gain_one, grad_from_first = norm_back(rows_in, scale_one, gain_one, grad_normed)
     grad_input = (grad_residual + grad_from_first).astype(jnp.bfloat16)
-    def gain_column(grad_gain):
-        return jnp.pad(grad_gain[:, None], ((0, 0), (0, 127)))
-
-    packed_out = lax.psum_scatter(
-        jnp.concatenate([grad_out_weight, gain_column(grad_gain_two)], axis=1),
-        ALL,
-        scatter_dimension=0,
-        tiled=True,
-    )
-    shard_attn_out = packed_out[:, :model_width]
-    shard_gain_two = packed_out[:, model_width]
-    packed_grad = lax.psum_scatter(
-        jnp.concatenate([grad_qkv_weight, gain_column(grad_gain_one)], axis=1),
-        ALL,
-        scatter_dimension=0,
-        tiled=True,
-    )
-    shard_qkv = packed_grad[:, : qkv_weight.shape[1]]
-    shard_gain_one = packed_grad[:, qkv_weight.shape[1]]
-    leaving = (
+    gains = jnp.pad(jnp.stack([grad_gain_one, grad_gain_two], axis=1), ((0, 0), (0, 126)))
+    parts = jnp.concatenate(
+        [
+            grad_qkv_weight.astype(jnp.bfloat16),
+            grad_out_weight.astype(jnp.bfloat16),
+            gains.astype(jnp.bfloat16),
+        ],
+        axis=1,
+    ).reshape(sizes + (shard_rows, -1))
+    home_out, home_grad, sums = closing(
+        sizes,
         jnp.take(output_rows, by_arrival, axis=0).reshape(device_count, peer_rows, model_width),
         jnp.take(grad_input, by_arrival, axis=0).reshape(device_count, peer_rows, model_width),
-    )
-    home_out, home_grad = (
-        lax.all_to_all(leaving[0], ALL, split_axis=0, concat_axis=0, tiled=True),
-        lax.all_to_all(leaving[1], ALL, split_axis=0, concat_axis=0, tiled=True),
-    )
+        parts,
+    )
+    shard_qkv = sums[:, :qkv_cols]
+    shard_attn_out = sums[:, qkv_cols : qkv_cols + model_width]
+    shard_gain_one = sums[:, qkv_cols + model_width]
+    shard_gain_two = sums[:, qkv_cols + model_width + 1]
     output = jnp.take(home_out.reshape(tok_dev, model_width), by_asked, axis=0)
     input_grad = jnp.take(home_grad.reshape(tok_dev, model_width), by_asked, axis=0)
     return (

time: 1160 us -> 1040 us (0.90)
  waiting for transfers between devices: 565 us -> 242 us
  Pallas kernels: 0 us -> 277 us
  blocking collectives: 54.6 us -> 0 us
  other arithmetic: 109 us -> 93.3 us
    pallas_call x0 -> x2, Pallas kernels: none -> 277 us  [the longest x1 147 us: opening(): pl.pallas_call(functools.partial(opening_kernel, sizes), out_shape=(jax.S...]
    reduce_scatter x3 -> x2, waiting for transfers between devices: 209 us -> 0.01 us  [the longest x1 0.01 us: shards(): lax.psum_scatter(grad_weights_out.reshape(hi_count * 2 * shard_cols, mode...]
    all_to_all x3 -> x2, waiting for transfers between devices: 147 us -> 27.2 us  [the longest x1 24.1 us: shards(): lax.all_to_all(asked_grads, ALL, split_axis=0, concat_axis=0, tiled=True)]
    all_to_all x2 -> x0, blocking collectives: 54.6 us -> none  [the longest x1 43.8 us: shards(): lax.all_to_all(leaving[0], ALL, split_axis=0, concat_axis=0, tiled=True)]
    optimization_barrier x0 -> x1, local copies, waits for them, and re-layouts: none -> 17.2 us  [shards(): lax.optimization_barrier((grad_normed_two, grad_weights_in.astype(jnp.bfl...]
    convert_element_type x1 -> x0, local copies, waits for them, and re-layouts: 16.7 us -> none  [shards(): grad_weights_in.astype(jnp.bfloat16)]
  transfers between devices with their start and end apart: 29 -> 24, of which waited for: 16 -> 11; matrix products, arithmetic and copies ran while one was open for 37% -> 35% of each run, Pallas kernels for 0% -> 27%
where the time goes in v2:
time: 1040 us; the launch traced here: 1030 us
  Pallas kernels  277 us (27%)
  matrix products  259 us (25%)
  waiting for transfers between devices  242 us (23%)
  local copies, waits for them, and re-layouts  103 us (10%)
  other arithmetic  93.3 us (9%)
  starting transfers between devices  38.3 us (4%)
  between operations  15.4 us (1%)
    ppermute x18, waiting for transfers between devices, swap(): return lax.ppermute(block, 'lo', [(i, i ^ step) for i in range(lo_count)])  214 us
    pallas_call x1, Pallas kernels, opening(): pl.pallas_call(functools.partial(opening_kernel, sizes), out_shape=(jax.S...  147 us
    pallas_call x1, Pallas kernels, closing(): pl.pallas_call(functools.partial(closing_kernel, sizes), out_shape=(jax.S...  130 us
    dot_general x1, matrix products, shards(): jnp.einsum('erd,ekdf->ekrf', expert_rows, weights_in, preferred_element_t...  25 us
    all_to_all x1, waiting for transfers between devices, shards(): lax.all_to_all(asked_grads, ALL, split_axis=0, concat_axis=0, tiled=True)  24.1 us
    ppermute x18, starting transfers between devices, swap(): return lax.ppermute(block, 'lo', [(i, i ^ step) for i in range(lo_count)])  23.8 us
    convert_element_type x1, other arithmetic, attend_back(): grad_scores = (exact_probs * (grad_probs - jnp.sum(grad_probs * exact_pro...  22.7 us
    dot_general x1, matrix products, shards(): jnp.einsum('erd,ekrf->ekdf', expert_rows, grad_gate_up, preferred_element...  22.1 us
  transfers between devices with their start and end apart: 24, of which 11 were waited for; matrix products, arithmetic and copies ran while one was open for 35% of the time, Pallas kernels for 27%

profile of v2, /device:TPU:12, one launch (start us, length us, event | category | flops | bytes accessed | tf_op | source)
XLA Modules:
  0.0 1027.3 jit_solution(14851866990720871572)
XLA Ops:
  7.3 3.9 all_gather_reshape.3
  17.9 6.0 all-to-all-start
  27.5 3.1 all-to-all-done
  32.5 2.9 gather_fusion
  35.4 2.9 gather_fusion.1
  38.4 3.5 broadcast_select_fusion.6
  41.8 147.3 %opening.1 = (bf16[32,16,1536]{2,1,0:T(8,128)(2,1)}, bf16[4,4,2,48,4224]{4,3,2,1,0:T(8,128)(2,1)}) custom-call(bf16[32,16,1536]{2,1,0:T(8,128)(2,1)} %bitcast.270, bf16[48,4224]{1,0:T(8,128)(2,1)} %concatenate.35.shard_ref), custom_call_target="tpu_custom_call" | custom-call | tf_op jit(solution)/shard_map/opening/pallas_call | solution.py:296
  189.1 5.2 gather_fusion.2
  196.8 6.8 fusion.31
  207.4 3.6 copy.120
  212.3 3.7 subtract_convert_fusion.1
  218.0 8.1 all-to-all-start.1
  226.4 11.7 %fusion.23 = (f32[8,3,512]{2,1,0:T(4,128)S(1)}, f32[8,512,512,3]{2,1,3,0:T(8,128)}) fusion(pred[512,512]{0,1:T(8,128)(4,1)S(1)} %compare_and_fusion, bf16[512,8,3,32]{0,3,2,1:T(8,128)(2,1)} %bitcast.276, bf16[512,8,3,32]{0,3,2,1:T(8,128)(2,1)} %bitcast.274, bf16[512,8,32]{0,2,1:T(8,128)(2,1)} %get-tuple-element.63, bf16[512,8,32]{0,2,1:T(8,128)(2,1)} %get-tuple-element.62), kind=kOutput, calls=%fused_computation.44 | convolution fusion | flops 828362752 | bytes 27574272 | tf_op jit(solution)/shard_map/qhgd,khd->hgqk/dot_general | solution.py:84
  238.1 11.8 %fusion.6 = f32[8,3,512]{2,1,0:T(4,128)S(1)} fusion(f32[8,3,512]{2,1,0:T(4,128)S(1)} %get-tuple-element.75, f32[8,512,512,3]{2,1,3,0:T(8,128)} %get-tuple-element.76, pred[512,512]{0,1:T(8,128)(4,1)S(1)} %compare_and_fusion), kind=kLoop, calls=%fused_computation.24 | loop fusion | flops 25153536 | bytes 25526272 | tf_op jit(solution)/shard_map/reduce_sum | solution.py:96
  250.0 12.2 %fusion.82 = bf16[8,64,3,512]{3,1,2,0:T(8,128)(2,1)S(1)} fusion(bf16[512,8,64,1]{0,2,3,1:T(8,128)(2,1)S(1)} %bitcast.279, f32[8,3,512]{2,1,0:T(4,128)S(1)} %fusion.6, f32[8,3,512]{2,1,0:T(4,128)S(1)} %get-tuple-element.75, f32[8,512,512,3]{2,1,3,0:T(8,128)} %get-tuple-element.76, pred[512,512]{0,1:T(8,128)(4,1)S(1)} %compare_and_fusion), kind=kOutput, calls=%fused_computation.114 | convolution fusion | flops 837550080 | bytes 27623424 | tf_op jit(solution)/shard_map/hgqk,khd->qhgd/dot_general | solution.py:98
  262.4 3.0 multiply_reduce_fusion.2
  268.5 24.1 %all-to-all-done.1 = bf16[32,16,1536]{2,1,0:T(8,128)(2,1)S(1)} async-done(((bf16[32,16,1536]{2,1,0:T(8,128)(2,1)}), bf16[32,16,1536]{2,1,0:T(8,128)(2,1)S(1)}, u32[]{:S(2)}, u32[]{:S(2)}) %all-to-all-start.1) | async-done | bytes 1572896 | tf_op jit(solution)/shard_map/all_to_all | solution.py:540
  292.6 2.1 gather_fusion.4
  301.6 62.1 %collective-permute-done.6 = f32[512,8]{0,1:T(8,128)S(1)} collective-permute-done((f32[512,8]{0,1:T(8,128)S(1)}, f32[512,8]{0,1:T(8,128)S(1)}, u32[]{:S(2)}, u32[]{:S(2)}) %collective-permute-start.6) | collective-permute-done | bytes 16416 | tf_op jit(solution)/shard_map/ppermute | solution.py:587
  363.6 3.5 collective-permute-start.8
  369.0 4.7 select_reduce_fusion
  374.6 2.6 collective-permute-start.4
  378.9 11.4 %convolution_bitcast_fusion = f32[4,8,128,1536]{3,2,0,1:T(8,128)} fusion(bf16[8,256,1536,1]{2,1,3,0:T(8,128)(2,1)S(1)} %bitcast.257, s32[8,4,256]{2,1,0:T(4,128)S(1)} %copy.123, pred[8,4,256]{2,1,0:T(4,128)(4,1)S(1)} %bitcast.299), kind=kOutput, calls=%fused_computation.26 | convolution fusion | flops 3223322624 | bytes 31498240 | tf_op jit(solution)/shard_map/becr,brd->ebcd/dot_general | solution.py:629
  390.3 10.0 copy.130
  400.3 10.8 %collective-permute-done.3 = bf16[512,1536]{1,0:T(8,128)(2,1)S(1)} collective-permute-done((bf16[512,1536]{1,0:T(8,128)(2,1)S(1)}, bf16[512,1536]{1,0:T(8,128)(2,1)S(1)}, u32[]{:S(2)}, u32[]{:S(2)}) %collective-permute-start.3) | collective-permute-done | bytes 1572896 | tf_op jit(solution)/shard_map/ppermute | solution.py:587
  411.1 31.8 %collective-permute-done.4 = bf16[512,1536]{1,0:T(8,128)(2,1)S(1)} collective-permute-done((bf16[512,1536]{1,0:T(8,128)(2,1)S(1)}, bf16[512,1536]{1,0:T(8,128)(2,1)S(1)}, u32[]{:S(2)}, u32[]{:S(2)}) %collective-permute-start.4) | collective-permute-done | bytes 1572896 | tf_op jit(solution)/shard_map/ppermute | solution.py:587
  444.0 3.0 pad_maximum_fusion.1
  446.9 9.3 fusion.22
  456.2 10.7 %copy.125 = bf16[4,8,128,1536]{3,2,1,0:T(8,128)(2,1)} copy(bf16[4,8,128,1536]{3,2,0,1:T(8,128)(2,1)} %fusion.22) | data formatting | bytes 25165824 | tf_op jit(solution)/shard_map/convert_element_type | solution.py:601
  466.9 5.8 fusion.4
  472.7 25.0 %convolution_bitcast_fusion.1 = f32[4,2,1024,512]{2,3,1,0:T(8,128)} fusion(bf16[4,1024,1536,1]{2,1,3,0:T(8,128)(2,1)} %bitcast.262, bf16[4,2,1536,512]{3,2,1,0:T(8,128)(2,1)} %bitcast.324), kind=kOutput, calls=%fused_computation.45 | convolution fusion | flops 12884901888 | bytes 41943040 | tf_op jit(solution)/shard_map/erd,ekdf->ekrf/dot_general | solution.py:602
  497.7 20.0 %fusion.26 = (bf16[4,2,1024,256]{2,3,1,0:T(8,128)(2,1)}, bf16[4,2,1024,256]{2,3,1,0:T(8,128)(2,1)}, bf16[4,2,1024,256]{2,3,1,0:T(8,128)(2,1)}) fusion(f32[4,2,1024,512]{2,3,1,0:T(8,128)} %convolution_bitcast_fusion.1, bf16[4,2,256,1536]{3,2,1,0:T(8,128)(2,1)} %bitcast.326, bf16[4,1024,1536]{2,1,0:T(8,128)(2,1)} %fusion.4), kind=kOutput, calls=%fused_computation.51 | convolution fusion | flops 6473908224 | bytes 48234496 | tf_op jit(solution)/shard_map/erd,ekfd->ekrf/dot_general | solution.py:634
  517.6 22.1 %fusion.21 = bf16[4,2,1536,512]{2,3,1,0:T(8,128)(2,1)} fusion(bf16[4,1024,1536,1]{2,1,3,0:T(8,128)(2,1)} %bitcast.263, bf16[4,2,1024,256]{2,3,1,0:T(8,128)(2,1)} %get-tuple-element.46, bf16[4,2,1024,256]{2,3,1,0:T(8,128)(2,1)} %get-tuple-element.45), kind=kOutput, calls=%fused_computation.42 | convolution fusion | flops 12907970560 | bytes 33554432 | tf_op jit(solution)/shard_map/erd,ekrf->ekdf/dot_general | solution.py:643
  539.7 21.4 %bitcast_convert_fusion = bf16[4,1024,1536]{2,1,0:T(8,128)(2,1)} fusion(bf16[4,2,1536,512]{3,2,1,0:T(8,128)(2,1)} %bitcast.325, bf16[4,2,1024,256]{2,3,1,0:T(8,128)(2,1)} %get-tuple-element.46, bf16[4,2,1024,256]{2,3,1,0:T(8,128)(2,1)} %get-tuple-element.45), kind=kOutput, calls=%fused_computation.15 | convolution fusion | flops 12907970560 | bytes 33554432 | tf_op jit(solution)/shard_map/ekrf,ekdf->erd/dot_general | solution.py:646
  561.1 9.7 fusion.119
  577.4 13.2 %fusion.39 = bf16[4,2,256,1536]{3,2,1,0:T(8,128)(2,1)} fusion(bf16[4,2,1024,256]{2,3,1,0:T(8,128)(2,1)S(1)} %copy-done.66, bf16[4,1024,1536]{2,1,0:T(8,128)(2,1)} %fusion.4), kind=kOutput, calls=%fused_computation.70 | convolution fusion | flops 6445596672 | bytes 23068672 | tf_op jit(solution)/shard_map/ekrf,erd->ekfd/dot_general | solution.py:637
  590.6 18.0 %collective-permute-done.15 = bf16[512,1536]{1,0:T(8,128)(2,1)S(1)} collective-permute-done((bf16[512,1536]{1,0:T(8,128)(2,1)S(1)}, bf16[512,1536]{1,0:T(8,128)(2,1)S(1)}, u32[]{:S(2)}, u32[]{:S(2)}) %collective-permute-start.15) | collective-permute-done | bytes 1572896 | tf_op jit(solution)/shard_map/ppermute | solution.py:587
  608.5 31.0 %collective-permute-done.16 = bf16[512,1536]{1,0:T(8,128)(2,1)S(1)} collective-permute-done((bf16[512,1536]{1,0:T(8,128)(2,1)S(1)}, bf16[512,1536]{1,0:T(8,128)(2,1)S(1)}, u32[]{:S(2)}, u32[]{:S(2)}) %collective-permute-start.16) | collective-permute-done | bytes 1572896 | tf_op jit(solution)/shard_map/ppermute | solution.py:587
  639.5 2.5 fusion.64
  642.0 17.2 %copy.140 = bf16[4,2,1536,512]{3,2,1,0:T(8,128)(2,1)} copy(bf16[4,2,1536,512]{2,3,1,0:T(8,128)(2,1)} %fusion.21) | data formatting | bytes 25165824 | tf_op jit(solution)/shard_map/optimization_barrier | solution.py:650
  661.0 10.5 %fusion.5 = bf16[4,1024,1536]{2,1,0:T(8,128)(2,1)S(1)} fusion(bf16[4,2,1024,256]{2,3,1,0:T(8,128)(2,1)} %get-tuple-element.47, bf16[4,2,256,1536]{3,2,1,0:T(8,128)(2,1)} %bitcast.327, f32[4,1024]{1,0:T(4,128)S(1)} %bitcast.306), kind=kOutput, calls=%fused_computation.19 | convolution fusion | flops 6455033856 | bytes 23085056 | tf_op jit(solution)/shard_map/ekrf,ekfd->erd/dot_general | solution.py:611
  671.5 5.9 fusion.120
  679.1 2.2 collective-permute-start.9
  686.4 56.0 %collective-permute-done.10 = bf16[512,1536]{1,0:T(8,128)(2,1)S(1)} collective-permute-done((bf16[512,1536]{1,0:T(8,128)(2,1)S(1)}, bf16[512,1536]{1,0:T(8,128)(2,1)S(1)}, u32[]{:S(2)}, u32[]{:S(2)}) %collective-permute-start.10) | collective-permute-done | bytes 1572896 | tf_op jit(solution)/shard_map/ppermute | solution.py:587
  744.2 2.5 subtract_add_fusion
  748.4 6.1 fusion.71
  756.3 21.4 %fusion.1 = (f32[8,3,512]{2,1,0:T(4,128)S(1)}, f32[8,512,512,3]{2,1,3,0:T(8,128)}) fusion(f32[8,3,512]{2,1,0:T(4,128)S(1)} %log_add_fusion, f32[8,512,512,3]{2,1,3,0:T(8,128)} %get-tuple-element.76, pred[512,512]{0,1:T(8,128)(4,1)S(1)} %copy-done.20, bf16[512,8,64,1]{0,2,3,1:T(8,128)(2,1)} %bitcast.278, bf16[512,8,3,64]{0,3,2,1:T(8,128)(2,1)S(1)} %bitcast.265), kind=kOutput, calls=%fused_computation.12 | convolution fusion | flops 836751360 | bytes 52789248 | tf_op jit(solution)/shard_map/qhgd,khd->hgqk/dot_general | solution.py:110
  777.7 22.7 %fusion.3 = bf16[8,3,512,512]{2,3,1,0:T(8,128)(2,1)} fusion(f32[8,512,512,3]{2,1,3,0:T(8,128)} %get-tuple-element.84, f32[8,3,512]{2,1,0:T(4,128)S(1)} %get-tuple-element.83, f32[8,3,512]{2,1,0:T(4,128)S(1)} %log_add_fusion, f32[8,512,512,3]{2,1,3,0:T(8,128)} %get-tuple-element.76, pred[512,512]{0,1:T(8,128)(4,1)S(1)} %copy-done.20), kind=kLoop, calls=%fused_computation.14 | loop fusion | flops 37748736 | bytes 63275008 | tf_op jit(solution)/shard_map/convert_element_type | solution.py:118
  800.5 8.7 fusion.87
  809.5 7.2 convolution_multiply_fusion
  817.4 12.1 %fusion.88 = bf16[8,64,512]{2,1,0:T(8,128)(2,1)S(1)} fusion(bf16[512,8,3,64]{0,3,2,1:T(8,128)(2,1)S(1)} %bitcast.266, f32[8,3,512]{2,1,0:T(4,128)S(1)} %log_add_fusion, f32[8,512,512,3]{2,1,3,0:T(8,128)} %get-tuple-element.76, pred[512,512]{0,1:T(8,128)(4,1)S(1)} %copy-done.20), kind=kOutput, calls=%fused_computation.133 | convolution fusion | flops 830734336 | bytes 27574272 | tf_op jit(solution)/shard_map/hgqk,qhgd->khd/dot_general | solution.py:113
  829.6 10.1 fusion.62
  840.0 3.9 fusion.58
  844.0 2.9 gather_fusion.5
  846.9 2.3 gather_fusion.3
  849.3 5.1 convolution_convert_fusion.3
  857.4 6.0 convolution_convert_fusion.2
  863.4 5.4 fusion.8
  868.7 129.9 %closing.1 = (bf16[32,16,1536]{2,1,0:T(8,128)(2,1)}, bf16[32,16,1536]{2,1,0:T(8,128)(2,1)}, f32[48,4224]{1,0:T(8,128)}) custom-call(bf16[32,16,1536]{2,1,0:T(8,128)(2,1)} %bitcast.272, bf16[32,16,1536]{2,1,0:T(8,128)(2,1)} %bitcast.271, bf16[4,4,2,48,4224]{4,3,2,1,0:T(8,128)(2,1)} %bitcast.255), custom_call_target="tpu_custom_call" | custom-call | tf_op jit(solution)/shard_map/closing/pallas_call | solution.py:449
  1002.3 2.9 gather_fusion.6
  1005.2 2.9 gather_fusion.7
  1009.7 3.5 broadcast_select_fusion
  1013.2 2.5 convert_element_type.203
  1015.7 4.7 reshape.393
  (270 shorter events, 66.9 us)
Async XLA Ops:
  7.2 25.3 %copy-start = (bf16[512,1536]{1,0:T(8,128)(2,1)S(1)}, bf16[512,1536]{1,0:T(8,128)(2,1)}, u32[]{:S(2)}) copy-start(bf16[512,1536]{1,0:T(8,128)(2,1)} %param.14) | copy-start | bytes 4718596
  7.2 7.6 copy-start.61
  7.2 17.5 %copy-start.57 = (s32[2,4]{1,0:T(2,128)S(1)}, s32[2,4]{1,0:T(2,128)}, u32[]{:S(2)}) copy-start(s32[2,4]{1,0:T(2,128)} %param.17) | copy-start | bytes 100
  7.2 19.2 %copy-start.62 = (bf16[48]{0:T(256)(128)(2,1)S(1)}, bf16[48]{0:T(256)(128)(2,1)}, u32[]{:S(2)}) copy-start(bf16[48]{0:T(256)(128)(2,1)} %param.20) | copy-start | bytes 292
  7.2 19.3 %copy-start.63 = (bf16[48]{0:T(256)(128)(2,1)S(1)}, bf16[48]{0:T(256)(128)(2,1)}, u32[]{:S(2)}) copy-start(bf16[48]{0:T(256)(128)(2,1)} %param.23) | copy-start | bytes 292
  7.2 19.4 %copy-start.39 = (bf16[48,2560]{1,0:T(8,128)(2,1)S(1)}, bf16[48,2560]{1,0:T(8,128)(2,1)}, u32[]{:S(2)}) copy-start(bf16[48,2560]{1,0:T(8,128)(2,1)} %param.21) | copy-start | bytes 737284
  7.2 19.4 %copy-start.40 = (bf16[48,1536]{1,0:T(8,128)(2,1)S(1)}, bf16[48,1536]{1,0:T(8,128)(2,1)}, u32[]{:S(2)}) copy-start(bf16[48,1536]{1,0:T(8,128)(2,1)} %param.22) | copy-start | bytes 442372
  7.2 465.5 %all-gather.4.cloned.1.call-start = ((), (), s32[]{:S(2)}) async-start(), calls=%async_computation.4 | async-start | bytes 14155776 | tf_op jit(solution)/shard_map/all_gather | solution.py:548
  11.2 285.9 %collective-permute-start = (s32[512,8]{0,1:T(8,128)}, s32[512,8]{0,1:T(8,128)}, u32[]{:S(2)}, u32[]{:S(2)}) collective-permute-start(s32[512,8]{0,1:T(8,128)} %param.18), channel_id=1, source_target_pairs={{0,2},{2,0},{4,6},{6,4},{1,3},{3,1},{5,7},{7,5},{8,10},{10,8},{12,... | collective-permute-start | bytes 49160 | tf_op jit(solution)/shard_map/ppermute | solution.py:587
  12.8 285.8 %collective-permute-start.1 = (s32[512,8]{0,1:T(8,128)}, s32[512,8]{0,1:T(8,128)}, u32[]{:S(2)}, u32[]{:S(2)}) collective-permute-start(s32[512,8]{0,1:T(8,128)} %param.18), channel_id=1, source_target_pairs={{0,4},{2,6},{4,0},{6,2},{1,5},{3,7},{5,1},{7,3},{8,12},{10,14},{12... | collective-permute-start | bytes 49160 | tf_op jit(solution)/shard_map/ppermute | solution.py:587
  13.3 285.5 %collective-permute-start.2 = (s32[512,8]{0,1:T(8,128)}, s32[512,8]{0,1:T(8,128)}, u32[]{:S(2)}, u32[]{:S(2)}) collective-permute-start(s32[512,8]{0,1:T(8,128)} %param.18), channel_id=1, source_target_pairs={{0,6},{2,4},{4,2},{6,0},{1,7},{3,5},{5,3},{7,1},{8,14},{10,12},{12... | collective-permute-start | bytes 49160 | tf_op jit(solution)/shard_map/ppermute | solution.py:587
  16.3 360.9 %copy-start.49 = (pred[512]{0:T(512)(128)(4,1)}, pred[512]{0:T(512)(128)(4,1)S(1)}, u32[]{:S(2)}) copy-start(pred[512]{0:T(512)(128)(4,1)S(1)} %get-tuple-element.43) | copy-start | bytes 1540
  17.9 12.7 %all-to-all-start = ((s32[32,1,16]{2,1,0:T(1,128)}), s32[32,1,16]{2,1,0:T(1,128)S(1)}, u32[]{:S(2)}, u32[]{:S(2)}) async-start(s32[32,1,16]{2,1,0:T(1,128)} %bitcast.2), calls=%async_computation | async-start | bytes 32768 | tf_op jit(solution)/shard_map/all_to_all | solution.py:511
  23.9 473.8 %all-gather.6.cloned.1.call-start = ((), (), s32[]{:S(2)}) async-start(), calls=%async_computation.7 | async-start | bytes 7077888 | tf_op jit(solution)/shard_map/all_gather | solution.py:551
  25.4 224.5 %copy-start.19 = (pred[512,512]{0,1:T(8,128)(4,1)}, pred[512,512]{0,1:T(8,128)(4,1)S(1)}, u32[]{:S(2)}) copy-start(pred[512,512]{0,1:T(8,128)(4,1)S(1)} %compare_and_fusion) | copy-start | bytes 786436
  26.4 189.6 %copy-start.25 = (f32[512,32]{0,1:T(8,128)}, f32[512,32]{0,1:T(8,128)S(1)}, u32[]{:S(2)}) copy-start(f32[512,32]{0,1:T(8,128)S(1)} %get-tuple-element.66) | copy-start | bytes 196612
  194.3 68.0 %copy-start.10 = (bf16[512,1536]{1,0:T(8,128)(2,1)}, bf16[512,1536]{1,0:T(8,128)(2,1)S(1)}, u32[]{:S(2)}) copy-start(bf16[512,1536]{1,0:T(8,128)(2,1)S(1)} %gather_fusion.2) | copy-start | bytes 4718596
  196.8 6.8 copy-start.45
  196.8 68.6 %copy-start.41 = (f32[1536]{0:T(1024)}, f32[1536]{0:T(1024)S(1)}, u32[]{:S(2)}) copy-start(f32[1536]{0:T(1024)S(1)} %get-tuple-element.39) | copy-start | bytes 18436
  218.0 74.6 %all-to-all-start.1 = ((bf16[32,16,1536]{2,1,0:T(8,128)(2,1)}), bf16[32,16,1536]{2,1,0:T(8,128)(2,1)S(1)}, u32[]{:S(2)}, u32[]{:S(2)}) async-start(bf16[32,16,1536]{2,1,0:T(8,128)(2,1)} %bitcast.269), calls=%async_computation.1 | async-start | bytes 3145728 | tf_op jit(solution)/shard_map/all_to_all | solution.py:540
  226.1 787.1 %reduce-scatter.5.cloned.1.call-start = ((), (), s32[]{:S(2)}) async-start(), calls=%async_computation.6 | async-start | bytes 7077888 | tf_op jit(solution)/shard_map/reduce_scatter | solution.py:657
  238.1 11.9 %copy-start.35 = (f32[8,3,512]{2,1,0:T(4,128)}, f32[8,3,512]{2,1,0:T(4,128)S(1)}, u32[]{:S(2)}) copy-start(f32[8,3,512]{2,1,0:T(4,128)S(1)} %get-tuple-element.75) | copy-start | bytes 147460
  238.1 11.9 %copy-start.24 = (bf16[512,512]{0,1:T(8,128)(2,1)S(1)}, bf16[512,512]{0,1:T(8,128)(2,1)}, u32[]{:S(2)}) copy-start(bf16[512,512]{0,1:T(8,128)(2,1)} %copy.118) | copy-start | bytes 1572868
  238.1 24.2 %slice-start.1 = ((s8[12976128]{0:T(1024)(128)(4,1)}), s8[4194304]{0:T(1024)(128)(4,1)S(1)}, s32[]{:S(2)}) async-start(s8[12976128]{0:T(1024)(128)(4,1)} %bitcast.319), calls=%async_computation.9 | async-start | bytes 8388608
  250.0 12.3 %copy-start.37 = (f32[8,3,512]{2,1,0:T(4,128)}, f32[8,3,512]{2,1,0:T(4,128)S(1)}, u32[]{:S(2)}) copy-start(f32[8,3,512]{2,1,0:T(4,128)S(1)} %fusion.6) | copy-start | bytes 147460
  250.0 12.3 %slice-start.2 = ((s8[12976128]{0:T(1024)(128)(4,1)}), s8[4194304]{0:T(1024)(128)(4,1)S(1)}, s32[]{:S(2)}) async-start(s8[12976128]{0:T(1024)(128)(4,1)} %bitcast.319), calls=%async_computation.10 | async-start | bytes 8388608
  250.0 12.3 %slice-start.3 = ((s8[12976128]{0:T(1024)(128)(4,1)}), s8[4194304]{0:T(1024)(128)(4,1)S(1)}, s32[]{:S(2)}) async-start(s8[12976128]{0:T(1024)(128)(4,1)} %bitcast.319), calls=%async_computation.11 | async-start | bytes 8388608
  250.0 12.3 %slice-start.4 = ((s8[12976128]{0:T(1024)(128)(4,1)}), s8[393216]{0:T(1024)(128)(4,1)S(1)}, s32[]{:S(2)}) async-start(s8[12976128]{0:T(1024)(128)(4,1)} %bitcast.319), calls=%async_computation.12 | async-start | bytes 786432
  294.8 82.7 %copy-start.8 = (bf16[512,1536]{1,0:T(8,128)(2,1)}, bf16[512,1536]{1,0:T(8,128)(2,1)S(1)}, u32[]{:S(2)}) copy-start(bf16[512,1536]{1,0:T(8,128)(2,1)S(1)} %gather_fusion.4) | copy-start | bytes 4718596
  294.8 78.9 %copy-start.14 = (bf16[512,1536]{1,0:T(8,128)(2,1)S(1)}, bf16[512,1536]{1,0:T(8,128)(2,1)}, u32[]{:S(2)}) copy-start(bf16[512,1536]{1,0:T(8,128)(2,1)} %multiply_convert_fusion.1) | copy-start | bytes 4718596
  295.0 82.5 %collective-permute-start.12 = (bf16[512,1536]{1,0:T(8,128)(2,1)S(1)}, bf16[512,1536]{1,0:T(8,128)(2,1)S(1)}, u32[]{:S(2)}, u32[]{:S(2)}) collective-permute-start(bf16[512,1536]{1,0:T(8,128)(2,1)S(1)} %broadcast_select_fusion.4), channel_id=1, source_target_pairs={{0,2},{2,0},{4,6},{6,4},{1,3},{3,1},{5,7},{7,5},{8,10},{10,8},{12,... | collective-permute-start | bytes 4718600 | tf_op jit(solution)/shard_map/ppermute | solution.py:587
  295.1 82.5 %collective-permute-start.13 = (bf16[512,1536]{1,0:T(8,128)(2,1)S(1)}, bf16[512,1536]{1,0:T(8,128)(2,1)S(1)}, u32[]{:S(2)}, u32[]{:S(2)}) collective-permute-start(bf16[512,1536]{1,0:T(8,128)(2,1)S(1)} %broadcast_select_fusion.4), channel_id=1, source_target_pairs={{0,4},{2,6},{4,0},{6,2},{1,5},{3,7},{5,1},{7,3},{8,12},{10,14},{12... | collective-permute-start | bytes 4718600 | tf_op jit(solution)/shard_map/ppermute | solution.py:587
  297.1 80.5 %collective-permute-start.14 = (bf16[512,1536]{1,0:T(8,128)(2,1)S(1)}, bf16[512,1536]{1,0:T(8,128)(2,1)S(1)}, u32[]{:S(2)}, u32[]{:S(2)}) collective-permute-start(bf16[512,1536]{1,0:T(8,128)(2,1)S(1)} %broadcast_select_fusion.4), channel_id=1, source_target_pairs={{0,6},{2,4},{4,2},{6,0},{1,7},{3,5},{5,3},{7,1},{8,14},{10,12},{12... | collective-permute-start | bytes 4718600 | tf_op jit(solution)/shard_map/ppermute | solution.py:587
  298.6 65.0 %collective-permute-start.6 = (f32[512,8]{0,1:T(8,128)S(1)}, f32[512,8]{0,1:T(8,128)S(1)}, u32[]{:S(2)}, u32[]{:S(2)}) collective-permute-start(f32[512,8]{0,1:T(8,128)S(1)} %copy-done.52), channel_id=1, source_target_pairs={{0,2},{2,0},{4,6},{6,4},{1,3},{3,1},{5,7},{7,5},{8,10},{10,8},{12,... | collective-permute-start | bytes 49160 | tf_op jit(solution)/shard_map/ppermute | solution.py:587
  298.7 68.6 %collective-permute-start.7 = (f32[512,8]{0,1:T(8,128)S(1)}, f32[512,8]{0,1:T(8,128)S(1)}, u32[]{:S(2)}, u32[]{:S(2)}) collective-permute-start(f32[512,8]{0,1:T(8,128)S(1)} %copy-done.52), channel_id=1, source_target_pairs={{0,4},{2,6},{4,0},{6,2},{1,5},{3,7},{5,1},{7,3},{8,12},{10,14},{12... | collective-permute-start | bytes 49160 | tf_op jit(solution)/shard_map/ppermute | solution.py:587
  363.6 5.2 collective-permute-start.8
  373.7 37.3 %collective-permute-start.3 = (bf16[512,1536]{1,0:T(8,128)(2,1)S(1)}, bf16[512,1536]{1,0:T(8,128)(2,1)S(1)}, u32[]{:S(2)}, u32[]{:S(2)}) collective-permute-start(bf16[512,1536]{1,0:T(8,128)(2,1)S(1)} %copy-done.14), channel_id=1, source_target_pairs={{0,2},{2,0},{4,6},{6,4},{1,3},{3,1},{5,7},{7,5},{8,10},{10,8},{12,... | collective-permute-start | bytes 4718600 | tf_op jit(solution)/shard_map/ppermute | solution.py:587
  374.6 68.2 %collective-permute-start.4 = (bf16[512,1536]{1,0:T(8,128)(2,1)S(1)}, bf16[512,1536]{1,0:T(8,128)(2,1)S(1)}, u32[]{:S(2)}, u32[]{:S(2)}) collective-permute-start(bf16[512,1536]{1,0:T(8,128)(2,1)S(1)} %copy-done.14), channel_id=1, source_target_pairs={{0,4},{2,6},{4,0},{6,2},{1,5},{3,7},{5,1},{7,3},{8,12},{10,14},{12... | collective-permute-start | bytes 4718600 | tf_op jit(solution)/shard_map/ppermute | solution.py:587
  377.5 66.0 %collective-permute-start.5 = (bf16[512,1536]{1,0:T(8,128)(2,1)S(1)}, bf16[512,1536]{1,0:T(8,128)(2,1)S(1)}, u32[]{:S(2)}, u32[]{:S(2)}) collective-permute-start(bf16[512,1536]{1,0:T(8,128)(2,1)S(1)} %copy-done.14), channel_id=1, source_target_pairs={{0,6},{2,4},{4,2},{6,0},{1,7},{3,5},{5,3},{7,1},{8,14},{10,12},{12... | collective-permute-start | bytes 4718600 | tf_op jit(solution)/shard_map/ppermute | solution.py:587
  411.1 32.5 %copy-start.27 = (bf16[512,1536]{1,0:T(8,128)(2,1)}, bf16[512,1536]{1,0:T(8,128)(2,1)S(1)}, u32[]{:S(2)}) copy-start(bf16[512,1536]{1,0:T(8,128)(2,1)S(1)} %collective-permute-done.3) | copy-start | bytes 4718596
  571.2 37.3 %collective-permute-start.15 = (bf16[512,1536]{1,0:T(8,128)(2,1)S(1)}, bf16[512,1536]{1,0:T(8,128)(2,1)S(1)}, u32[]{:S(2)}, u32[]{:S(2)}) collective-permute-start(bf16[512,1536]{1,0:T(8,128)(2,1)S(1)} %bitcast.291), channel_id=1, source_target_pairs={{0,2},{2,0},{4,6},{6,4},{1,3},{3,1},{5,7},{7,5},{8,10},{10,8},{12,... | collective-permute-start | bytes 4718600 | tf_op jit(solution)/shard_map/ppermute | solution.py:587
  572.3 67.2 %collective-permute-start.16 = (bf16[512,1536]{1,0:T(8,128)(2,1)S(1)}, bf16[512,1536]{1,0:T(8,128)(2,1)S(1)}, u32[]{:S(2)}, u32[]{:S(2)}) collective-permute-start(bf16[512,1536]{1,0:T(8,128)(2,1)S(1)} %bitcast.290), channel_id=1, source_target_pairs={{0,4},{2,6},{4,0},{6,2},{1,5},{3,7},{5,1},{7,3},{8,12},{10,14},{12... | collective-permute-start | bytes 4718600 | tf_op jit(solution)/shard_map/ppermute | solution.py:587
  574.2 65.2 %collective-permute-start.17 = (bf16[512,1536]{1,0:T(8,128)(2,1)S(1)}, bf16[512,1536]{1,0:T(8,128)(2,1)S(1)}, u32[]{:S(2)}, u32[]{:S(2)}) collective-permute-start(bf16[512,1536]{1,0:T(8,128)(2,1)S(1)} %bitcast.289), channel_id=1, source_target_pairs={{0,6},{2,4},{4,2},{6,0},{1,7},{3,5},{5,3},{7,1},{8,14},{10,12},{12... | collective-permute-start | bytes 4718600 | tf_op jit(solution)/shard_map/ppermute | solution.py:587
  642.0 373.7 %reduce-scatter.3.cloned.1.call-start = ((), (), s32[]{:S(2)}) async-start(), calls=%async_computation.5 | async-start | bytes 14155776 | tf_op jit(solution)/shard_map/reduce_scatter | solution.py:664
  677.4 5.5 copy-start.42
  677.8 64.7 %collective-permute-start.10 = (bf16[512,1536]{1,0:T(8,128)(2,1)S(1)}, bf16[512,1536]{1,0:T(8,128)(2,1)S(1)}, u32[]{:S(2)}, u32[]{:S(2)}) collective-permute-start(bf16[512,1536]{1,0:T(8,128)(2,1)S(1)} %bitcast.287), channel_id=1, source_target_pairs={{0,4},{2,6},{4,0},{6,2},{1,5},{3,7},{5,1},{7,3},{8,12},{10,14},{12... | collective-permute-start | bytes 4718600 | tf_op jit(solution)/shard_map/ppermute | solution.py:587
  678.1 64.3 %collective-permute-start.11 = (bf16[512,1536]{1,0:T(8,128)(2,1)S(1)}, bf16[512,1536]{1,0:T(8,128)(2,1)S(1)}, u32[]{:S(2)}, u32[]{:S(2)}) collective-permute-start(bf16[512,1536]{1,0:T(8,128)(2,1)S(1)} %bitcast.285), channel_id=1, source_target_pairs={{0,6},{2,4},{4,2},{6,0},{1,7},{3,5},{5,3},{7,1},{8,14},{10,12},{12... | collective-permute-start | bytes 4718600 | tf_op jit(solution)/shard_map/ppermute | solution.py:587
  679.1 65.1 %collective-permute-start.9 = (bf16[512,1536]{1,0:T(8,128)(2,1)S(1)}, bf16[512,1536]{1,0:T(8,128)(2,1)S(1)}, u32[]{:S(2)}, u32[]{:S(2)}) collective-permute-start(bf16[512,1536]{1,0:T(8,128)(2,1)S(1)} %bitcast.283), channel_id=1, source_target_pairs={{0,2},{2,0},{4,6},{6,4},{1,3},{3,1},{5,7},{7,5},{8,10},{10,8},{12,... | collective-permute-start | bytes 4718600 | tf_op jit(solution)/shard_map/ppermute | solution.py:587
  685.6 58.6 %copy-start.9 = (bf16[512,1536]{1,0:T(8,128)(2,1)S(1)}, bf16[512,1536]{1,0:T(8,128)(2,1)}, u32[]{:S(2)}) copy-start(bf16[512,1536]{1,0:T(8,128)(2,1)} %copy-done.8) | copy-start | bytes 4718596
  685.6 58.6 %copy-start.50 = (pred[512]{0:T(512)(128)(4,1)S(1)}, pred[512]{0:T(512)(128)(4,1)}, u32[]{:S(2)}) copy-start(pred[512]{0:T(512)(128)(4,1)} %copy-done.49) | copy-start | bytes 1540
  777.7 22.8 %copy-start.22 = (bf16[512,24,32]{0,2,1:T(8,128)(2,1)S(1)}, bf16[512,24,32]{0,2,1:T(8,128)(2,1)}, u32[]{:S(2)}) copy-start(bf16[512,24,32]{0,2,1:T(8,128)(2,1)} %get-tuple-element.56) | copy-start | bytes 2359300
  777.7 22.7 %copy-start.23 = (bf16[512,24,32]{0,2,1:T(8,128)(2,1)S(1)}, bf16[512,24,32]{0,2,1:T(8,128)(2,1)}, u32[]{:S(2)}) copy-start(bf16[512,24,32]{0,2,1:T(8,128)(2,1)} %get-tuple-element.57) | copy-start | bytes 2359300
  800.5 8.7 copy-start.26
  800.5 8.7 copy-start.33
  800.5 9.0 copy-start.31
  800.5 9.0 copy-start.32
  809.4 20.1 %copy-start.34 = (bf16[512,8,64]{0,2,1:T(8,128)(2,1)}, bf16[512,8,64]{0,2,1:T(8,128)(2,1)S(1)}, u32[]{:S(2)}) copy-start(bf16[512,8,64]{0,2,1:T(8,128)(2,1)S(1)} %pad_maximum_fusion.12) | copy-start | bytes 1572868
  817.4 12.2 %copy-start.29 = (bf16[512,24,64]{0,2,1:T(8,128)(2,1)}, bf16[512,24,64]{0,2,1:T(8,128)(2,1)S(1)}, u32[]{:S(2)}) copy-start(bf16[512,24,64]{0,2,1:T(8,128)(2,1)S(1)} %pad_maximum_fusion.7) | copy-start | bytes 4718596
  817.4 12.2 %copy-start.11 = (bf16[512,1536]{1,0:T(8,128)(2,1)S(1)}, bf16[512,1536]{1,0:T(8,128)(2,1)}, u32[]{:S(2)}) copy-start(bf16[512,1536]{1,0:T(8,128)(2,1)} %copy-done.10) | copy-start | bytes 4718596
  817.4 12.2 %copy-start.46 = (f32[1536]{0:T(1024)S(1)}, f32[1536]{0:T(1024)}, u32[]{:S(2)}) copy-start(f32[1536]{0:T(1024)} %copy-done.45) | copy-start | bytes 18436
  817.4 12.2 %copy-start.55 = (f32[512]{0:T(512)S(1)}, f32[512]{0:T(512)}, u32[]{:S(2)}) copy-start(f32[512]{0:T(512)} %add_rsqrt_fusion.1) | copy-start | bytes 6148
  829.5 10.2 copy-start.65
  868.7 133.5 %copy-start.53 = (s32[1024]{0:T(1024)S(1)}, s32[1024]{0:T(1024)}, u32[]{:S(2)}) copy-start(s32[1024]{0:T(1024)} %pad_clamp_fusion) | copy-start | bytes 12292
  1009.7 10.7 %copy-start.1 = (bf16[512,1536]{1,0:T(8,128)(2,1)S(1)}, bf16[512,1536]{1,0:T(8,128)(2,1)}, u32[]{:S(2)}) copy-start(bf16[512,1536]{1,0:T(8,128)(2,1)} %param.14) | copy-start | bytes 4718596
  (32 other events, 100.7 us)
Sparse Core Ops, SparseCore 0:
  11.3 180.9 all-gather.3
  193.9 95.1 all-gather.5
  642.1 66.7 reduce-scatter.4
  711.0 127.6 reduce-scatter.2

commit v3 on v2

--- a/solution.py
+++ b/solution.py
@@ -78,51 +78,67 @@
     return hit.astype(jnp.bfloat16), slot_gate
 
 
+def by_batch(rows, heads):
+    return rows.reshape(-1, TOK_MB, KV_HEADS, heads // KV_HEADS, HEAD)
+
+
 def block_scores(queries, key_rows, segment, position):
-    row_count = queries.shape[0]
-    grouped = queries.reshape(row_count, KV_HEADS, HEADS // KV_HEADS, HEAD)
     scores = jnp.einsum(
-        "qhgd,khd->hgqk", grouped, key_rows, preferred_element_type=jnp.float32
+        "bqhgd,bkhd->bhgqk", queries, key_rows, preferred_element_type=jnp.float32
     ) * HEAD ** (-0.5)
-    allowed = (segment[:, None] == segment[None, :]) & (position[:, None] >= position[None, :])
-    return (jnp.where(allowed, scores, -1e30), grouped)
+    allowed = (segment[:, :, None] == segment[:, None, :]) & (
+        position[:, :, None] >= position[:, None, :]
+    )
+    return jnp.where(allowed[:, None, None], scores, -1e30)
 
 
 def attend_block(queries, key_rows, value_rows, segment, position):
-    row_count = queries.shape[0]
-    masked, grouped = block_scores(queries, key_rows, segment, position)
+    queries = by_batch(queries, HEADS)
+    key_rows = by_batch(key_rows, KV_HEADS)[:, :, :, 0]
+    value_rows = by_batch(value_rows, KV_HEADS)[:, :, :, 0]
+    segment = segment.reshape(-1, TOK_MB)
+    position = position.reshape(-1, TOK_MB)
+    masked = block_scores(queries, key_rows, segment, position)
     row_peak = jnp.max(masked, axis=-1, keepdims=True)
     weights_exp = jnp.exp(masked - row_peak)
     row_total = jnp.sum(weights_exp, axis=-1, keepdims=True)
     probabilities = (weights_exp / row_total).astype(jnp.bfloat16)
     mixed_rows = jnp.einsum(
-        "hgqk,khd->qhgd", probabilities, value_rows, preferred_element_type=jnp.float32
-    )
-    return (mixed_rows.reshape(row_count, HEADS * HEAD), row_peak + jnp.log(row_total))
+        "bhgqk,bkhd->bqhgd", probabilities, value_rows, preferred_element_type=jnp.float32
+    )
+    return (mixed_rows.reshape(-1, HEADS * HEAD), row_peak + jnp.log(row_total))
 
 
 def attend_back(queries, key_rows, value_rows, segment, position, logsum, grad_mixed):
-    row_count = queries.shape[0]
-    masked, grouped = block_scores(queries, key_rows, segment, position)
+    queries = by_batch(queries, HEADS)
+    key_rows = by_batch(key_rows, KV_HEADS)[:, :, :, 0]
+    value_rows = by_batch(value_rows, KV_HEADS)[:, :, :, 0]
+    segment = segment.reshape(-1, TOK_MB)
+    position = position.reshape(-1, TOK_MB)
+    masked = block_scores(queries, key_rows, segment, position)
     exact_probs = jnp.exp(masked - logsum)
     probabilities = exact_probs.astype(jnp.bfloat16)
-    grad_heads = grad_mixed.reshape(row_count, KV_HEADS, HEADS // KV_HEADS, HEAD)
+    grad_heads = by_batch(grad_mixed, HEADS)
     grad_probs = jnp.einsum(
-        "qhgd,khd->hgqk", grad_heads, value_rows, preferred_element_type=jnp.float32
+        "bqhgd,bkhd->bhgqk", grad_heads, value_rows, preferred_element_type=jnp.float32
     )
     grad_values = jnp.einsum(
-        "hgqk,qhgd->khd", probabilities, grad_heads, preferred_element_type=jnp.float32
+        "bhgqk,bqhgd->bkhd", probabilities, grad_heads, preferred_element_type=jnp.float32
     )
     grad_scores = (
         exact_probs * (grad_probs - jnp.sum(grad_probs * exact_probs, axis=-1, keepdims=True))
     ).astype(jnp.bfloat16)
     grad_queries = jnp.einsum(
-        "hgqk,khd->qhgd", grad_scores, key_rows, preferred_element_type=jnp.float32
+        "bhgqk,bkhd->bqhgd", grad_scores, key_rows, preferred_element_type=jnp.float32
     ) * HEAD ** (-0.5)
     grad_keys = jnp.einsum(
-        "hgqk,qhgd->khd", grad_scores, grouped, preferred_element_type=jnp.float32
+        "bhgqk,bqhgd->bkhd", grad_scores, queries, preferred_element_type=jnp.float32
     ) * HEAD ** (-0.5)
-    return (grad_queries.reshape(row_count, HEADS, HEAD), grad_keys, grad_values)
+    return (
+        grad_queries.reshape(-1, HEADS, HEAD),
+        grad_keys.reshape(-1, KV_HEADS, HEAD),
+        grad_values.reshape(-1, KV_HEADS, HEAD),
+    )
 
 
 def norm_back(values, scale, gain, grad_normed):
@@ -214,7 +230,8 @@
 
 
 def opening_kernel(
-    sizes, rows_ref, shard_ref, got_ref, full_ref, own_sem, row_sems, hi_sems, lo_sems, core_sems
+    sizes, rows_ref, grads_ref, shard_ref, got_ref, got_grads_ref, full_ref,
+    own_sem, row_sems, hi_sems, lo_sems, core_sems
 ):
     hi_count, lo_count, _ = sizes
     hi, lo, core = place()
@@ -222,6 +239,7 @@
     own = [
         pltpu.make_async_copy(shard_ref, full_ref.at[hi, lo, core], own_sem.at[0]),
         pltpu.make_async_copy(rows_ref.at[me], got_ref.at[me], own_sem.at[1]),
+        pltpu.make_async_copy(grads_ref.at[me], got_grads_ref.at[me], own_sem.at[2]),
     ]
     for copy in own:
         copy.start()
@@ -243,7 +261,8 @@
             shard_ref, (hi, lo, core), (flip(hi, step), lo, core), hi_sems, step - 1
         )
         along_hi[step].start()
-    send_rows(sizes, rows_ref, got_ref, row_sems.at[0], row_sems.at[1])
+    send_rows(sizes, rows_ref, got_ref, row_sems.at[0, 0], row_sems.at[1, 0])
+    send_rows(sizes, grads_ref, got_grads_ref, row_sems.at[0, 1], row_sems.at[1, 1])
 
     def across(plane, offset, first):
         at = (flip(hi, plane), flip(lo, offset), core)
@@ -285,32 +304,34 @@
             hop(
                 full_ref.at[at[0], at[1], at[2]], at, (hi, lo, 1 - core), core_sems, plane, offset
             ).wait_recv()
-    wait_rows(rows_ref, got_ref, row_sems.at[0], row_sems.at[1])
+    wait_rows(rows_ref, got_ref, row_sems.at[0, 0], row_sems.at[1, 0])
+    wait_rows(grads_ref, got_grads_ref, row_sems.at[0, 1], row_sems.at[1, 1])
     for copy in own:
         copy.wait()
 
 
-def opening(sizes, rows, shard):
+def opening(sizes, rows, grads, shard):
     hi_count, lo_count, _ = sizes
     anywhere = pl.BlockSpec(memory_space=pl.ANY)
     return pl.pallas_call(
         functools.partial(opening_kernel, sizes),
         out_shape=(
             jax.ShapeDtypeStruct(rows.shape, rows.dtype),
+            jax.ShapeDtypeStruct(grads.shape, grads.dtype),
             jax.ShapeDtypeStruct(sizes + shard.shape, shard.dtype),
         ),
-        in_specs=[anywhere] * 2,
-        out_specs=(anywhere, anywhere),
+        in_specs=[anywhere] * 3,
+        out_specs=(anywhere, anywhere, anywhere),
         scratch_shapes=[
-            pltpu.SemaphoreType.DMA((2,)),
-            pltpu.SemaphoreType.DMA((2,)),
+            pltpu.SemaphoreType.DMA((3,)),
+            pltpu.SemaphoreType.DMA((2, 2)),
             pltpu.SemaphoreType.DMA((2, hi_count)),
             pltpu.SemaphoreType.DMA((2, hi_count, lo_count)),
             pltpu.SemaphoreType.DMA((2, hi_count, lo_count)),
         ],
         compiler_params=pltpu.CompilerParams(collective_id=0, has_side_effects=True),
         name="opening",
-    )(rows, shard)
+    )(rows, grads, shard)
 
 
 def add_blocks(target, first, second):
@@ -473,6 +494,41 @@
     )(out_rows, grad_rows, parts)
 
 
+def dispatch_kernel(weighted, choose_ref, rows_ref, *refs):
+    slots = jnp.dot(choose_ref[0, 0], rows_ref[...], preferred_element_type=jnp.float32)
+    if weighted:
+        slots = slots * refs[0][0, 0]
+    refs[-1][0, 0] = slots.astype(jnp.bfloat16)
+
+
+def dispatch(choose, rows, step, slots, weight):
+    _, count, capacity, _ = choose.shape
+    width = rows.shape[1]
+    first = step * MB
+    operands = [choose, rows]
+    in_specs = [
+        pl.BlockSpec((1, 1, capacity, TOK_MB), lambda b, e: (first + b, e, 0, 0)),
+        pl.BlockSpec((TOK_MB, width), lambda b, e: (b, 0)),
+    ]
+    if weight is not None:
+        operands.append(weight)
+        in_specs.append(pl.BlockSpec((1, 1, capacity, 1), lambda b, e: (e, first + b, 0, 0)))
+    aliases = {}
+    if slots is not None:
+        aliases = {len(operands): 0}
+        operands.append(slots)
+        in_specs.append(pl.BlockSpec(memory_space=pl.ANY))
+    return pl.pallas_call(
+        functools.partial(dispatch_kernel, weight is not None),
+        grid=(MB, count),
+        out_shape=jax.ShapeDtypeStruct((count, choose.shape[0], capacity, width), jnp.bfloat16),
+        in_specs=in_specs,
+        out_specs=pl.BlockSpec((1, 1, capacity, width), lambda b, e: (e, first + b, 0, 0)),
+        input_output_aliases=aliases,
+        name="dispatch",
+    )(*operands)
+
+
 def shards(
     tokens,
     cotangent,
@@ -508,6 +564,14 @@
     arrival_match = arrival[:, None] == positions[None, :]
     wanted = jnp.sum(jnp.where(arrival_match, local_row[:, None], 0), axis=0, dtype=jnp.int32)
     by_arrival = jnp.sum(jnp.where(arrival_match, positions[:, None], 0), axis=0, dtype=jnp.int32)
+    def swap(block, step):
+        return lax.ppermute(block, "lo", [(i, i ^ step) for i in range(lo_count)])
+
+    def spread(block):
+        return [block] + [swap(block, step) for step in range(1, lo_count)]
+
+    ids_all = jnp.stack(spread(expert_ids))
+    gates_all = jnp.stack(spread(gate_weights))
     asked_rows = lax.all_to_all(
         wanted.reshape(device_count, peer_rows),
         ALL,
@@ -515,6 +579,7 @@
         concat_axis=0,
         tiled=True,
     ).reshape(tok_dev)
+    asked_rows, ids_all, gates_all = lax.optimization_barrier((asked_rows, ids_all, gates_all))
     asked_match = asked_rows[:, None] == positions[None, :]
     by_asked = jnp.sum(jnp.where(asked_match, positions[:, None], 0), axis=0, dtype=jnp.int32)
     sizes = (hi_count, lo_count, 2)
@@ -534,10 +599,10 @@
     asked_grads = jnp.take(cotangent, asked_rows, axis=0).reshape(
         device_count, peer_rows, model_width
     )
-    got_rows, packed = opening(sizes, asked_tokens, weight_shard)
+    got_rows, got_grad, packed = opening(sizes, asked_tokens, asked_grads, weight_shard)
     packed = packed.reshape(model_width, -1)
-    got_rows, asked_grads = lax.optimization_barrier((got_rows, asked_grads))
-    got_grad = lax.all_to_all(asked_grads, ALL, split_axis=0, concat_axis=0, tiled=True)
+    grad_bf = jnp.take(got_grad.reshape(tok_dev, model_width), arrival, axis=0)
+    grad_blocks = spread(grad_bf)
     rows_in = jnp.take(got_rows.reshape(tok_dev, model_width), arrival, axis=0).astype(jnp.float32)
     qkv_full = packed[:, :qkv_cols]
     out_full = packed[:, qkv_cols : qkv_cols + model_width]
@@ -567,38 +632,36 @@
     value_rows = (
         projected[:, q_dim + kv_dim :].reshape(tok_dev, KV_HEADS, HEAD).astype(jnp.bfloat16)
     )
-    block_rows = min(tok_dev, max(TOK_MB, 512))
     mixed_part, logsum = attend_block(queries, key_rows, value_rows, segment, position)
-    logsums = [logsum]
     mixed_rows = mixed_part.astype(jnp.bfloat16)
     attended = jnp.dot(mixed_rows, out_full, preferred_element_type=jnp.float32)
     residual = rows_in + attended
     scale_two = lax.rsqrt(jnp.mean(residual * residual, axis=1, keepdims=True) + epsilon)
     normed_two = (residual * scale_two * gain_two).astype(jnp.bfloat16)
-    got_grad, normed_two = lax.optimization_barrier((got_grad, normed_two))
-    grad_bf = jnp.take(got_grad.reshape(tok_dev, model_width), arrival, axis=0)
     grad_output = grad_bf.astype(jnp.float32)
     home = lax.axis_index("lo")
-
-    def spread(block):
-        return [block] + [swap(block, step) for step in range(1, lo_count)]
-
-    def swap(block, step):
-        return lax.ppermute(block, "lo", [(i, i ^ step) for i in range(lo_count)])
-
-    ids_all = jnp.stack(spread(expert_ids))
-    gates_all = jnp.stack(spread(gate_weights))
+    row_blocks = spread(normed_two)
+    normed_two, *grad_blocks = lax.optimization_barrier((normed_two, *grad_blocks))
     choose, slot_gate = slot_tables(
         ids_all.reshape(-1, TOK_MB, TOPK),
         gates_all.reshape(-1, TOK_MB, TOPK),
         home + lo_count * jnp.arange(hi_count, dtype=jnp.int32),
         capacity,
     )
-    rows_all = jnp.stack(spread(normed_two)).reshape(lo_count * MB, TOK_MB, model_width)
-    grads_all = jnp.stack(spread(grad_bf)).reshape(lo_count * MB, TOK_MB, model_width)
-    expert_rows = jnp.einsum(
-        "becr,brd->ebcd", choose, rows_all, preferred_element_type=jnp.float32
-    ).astype(jnp.bfloat16).reshape(hi_count, -1, model_width)
+    slot_weight = jnp.transpose(slot_gate, (1, 0, 2))[..., None]
+    grad_expert = None
+    for step in range(lo_count):
+        grad_expert = dispatch(choose, grad_blocks[step], step, grad_expert, slot_weight)
+    grad_expert = grad_expert.reshape(hi_count, -1, model_width)
+    grad_hidden = jnp.einsum(
+        "erd,ekfd->ekrf", grad_expert, weights_out, preferred_element_type=jnp.float32
+    ).astype(jnp.bfloat16)
+    grad_hidden, *others = lax.optimization_barrier((grad_hidden, *row_blocks[1:]))
+    row_blocks = [normed_two] + others
+    expert_rows = None
+    for step in range(lo_count):
+        expert_rows = dispatch(choose, row_blocks[step], step, expert_rows, None)
+    expert_rows = expert_rows.reshape(hi_count, -1, model_width)
     gate_up = jnp.einsum(
         "erd,ekdf->ekrf", expert_rows, weights_in, preferred_element_type=jnp.float32
     )
@@ -606,70 +669,65 @@
     up_part = gate_up[..., shard_cols:]
     sigmoid_gate = jax.nn.sigmoid(gate_part)
     hidden = (gate_part * sigmoid_gate * up_part).astype(jnp.bfloat16)
-    slot_weight = jnp.transpose(slot_gate, (1, 0, 2)).reshape(hi_count, -1, 1)
-    produced = (
-        jnp.einsum("ekrf,ekfd->erd", hidden, weights_out, preferred_element_type=jnp.float32)
-        * slot_weight
-    ).astype(jnp.bfloat16)
-
-    def collect(slot_values):
-        parts = jnp.einsum(
-            "becr,ebcd->brd",
-            choose,
-            slot_values.reshape(hi_count, lo_count * MB, capacity, model_width),
-            preferred_element_type=jnp.float32,
-        ).reshape(lo_count, tok_dev, model_width)
-        total = parts[0]
-        for step in range(1, lo_count):
-            total = total + swap(parts[step].astype(jnp.bfloat16), step).astype(jnp.float32)
-        return total
-
-    output_rows = (residual + collect(produced)).astype(jnp.bfloat16)
-    grad_expert = (
-        jnp.einsum("becr,brd->ebcd", choose, grads_all, preferred_element_type=jnp.float32).reshape(
-            hi_count, -1, model_width
-        )
-        * slot_weight
-    ).astype(jnp.bfloat16)
-    grad_hidden = jnp.einsum(
-        "erd,ekfd->ekrf", grad_expert, weights_out, preferred_element_type=jnp.float32
-    )
-    grad_weights_out = jnp.einsum(
-        "ekrf,erd->ekfd", hidden, grad_expert, preferred_element_type=jnp.float32
-    )
     grad_gate = grad_hidden * up_part * sigmoid_gate * (1.0 + gate_part * (1.0 - sigmoid_gate))
     grad_up = grad_hidden * (gate_part * sigmoid_gate)
     grad_gate_up = jnp.concatenate([grad_gate, grad_up], axis=-1).astype(jnp.bfloat16)
-    grad_weights_in = jnp.einsum(
-        "erd,ekrf->ekdf", expert_rows, grad_gate_up, preferred_element_type=jnp.float32
-    )
     grad_expert_rows = jnp.einsum(
         "ekrf,ekdf->erd", grad_gate_up, weights_in, preferred_element_type=jnp.float32
     ).astype(jnp.bfloat16)
-    grad_normed_two = collect(grad_expert_rows)
-    grad_normed_two, grad_weights_in, grad_weights_out = lax.optimization_barrier(
-        (
-            grad_normed_two,
-            grad_weights_in.astype(jnp.bfloat16),
-            grad_weights_out.astype(jnp.bfloat16),
+
+    def split_back(slot_values):
+        return (
+            jnp.einsum(
+                "becr,ebcd->brd",
+                choose,
+                slot_values.reshape(hi_count, lo_count * MB, capacity, model_width),
+                preferred_element_type=jnp.float32,
+            )
+            .astype(jnp.bfloat16)
+            .reshape(lo_count, tok_dev, model_width)
         )
-    )
+
+    def total_of(parts):
+        total = parts[0].astype(jnp.float32)
+        for part in parts[1:]:
+            total = total + part.astype(jnp.float32)
+        return total
+
+    back = split_back(grad_expert_rows)
+    back_parts = [back[0]] + [swap(back[step], step) for step in range(1, lo_count)]
+    back, hidden, expert_rows, grad_gate_up, grad_expert = lax.optimization_barrier(
+        (back, hidden, expert_rows, grad_gate_up, grad_expert)
+    )
+    grad_weights_out = jnp.einsum(
+        "ekrf,erd->ekfd", hidden, grad_expert, preferred_element_type=jnp.float32
+    ).astype(jnp.bfloat16)
+    grad_weights_in = jnp.einsum(
+        "ekrf,erd->ekfd", grad_gate_up, expert_rows, preferred_element_type=jnp.float32
+    ).astype(jnp.bfloat16)
+    produced = (
+        jnp.einsum("ekrf,ekfd->erd", hidden, weights_out, preferred_element_type=jnp.float32)
+        * slot_weight.reshape(hi_count, -1, 1)
+    ).astype(jnp.bfloat16)
+    ahead = split_back(produced)
+    ahead, grad_weights_in, grad_weights_out, *back_parts = lax.optimization_barrier(
+        (ahead, grad_weights_in, grad_weights_out, *back_parts)
+    )
+    ahead_parts = [ahead[0]] + [swap(ahead[step], step) for step in range(1, lo_count)]
+    grad_normed_two = total_of(back_parts)
     shard_out = lax.psum_scatter(
         grad_weights_out.reshape(hi_count * 2 * shard_cols, model_width),
         ("hi", "core"),
         scatter_dimension=0,
         tiled=True,
     ).astype(jnp.float32)
-    shard_in = (
-        lax.psum_scatter(
-            grad_weights_in.reshape(hi_count * 2 * model_width, 2 * shard_cols),
-            ("hi", "core"),
-            scatter_dimension=0,
-            tiled=True,
-        )
-        .astype(jnp.float32)
-        .reshape(model_width, 2, shard_cols)
-    )
+    shard_in = lax.psum_scatter(
+        grad_weights_in.reshape(hi_count * 2 * 2 * shard_cols, model_width),
+        ("hi", "core"),
+        scatter_dimension=0,
+        tiled=True,
+    )
+    shard_in = shard_in.T.astype(jnp.float32).reshape(model_width, 2, shard_cols)
     grad_gain_two, grad_from_norm = norm_back(residual, scale_two, gain_two, grad_normed_two)
     grad_residual = grad_output + grad_from_norm
     grad_attended = grad_residual.astype(jnp.bfloat16)
@@ -679,19 +737,11 @@
     grad_mixed = jnp.einsum(
         "nd,qd->nq", grad_attended, out_full, preferred_element_type=jnp.float32
     ).astype(jnp.bfloat16)
-    grad_query_parts = []
-    grad_key_parts = []
-    grad_value_parts = []
-    for block_number, block_start in enumerate(range(0, tok_dev, block_rows)):
-        grad_q, grad_k, grad_v = attend_back(
-            queries, key_rows, value_rows, segment, position, logsums[block_number], grad_mixed
-        )
-        grad_query_parts.append(grad_q)
-        grad_key_parts.append(grad_k)
-        grad_value_parts.append(grad_v)
-    grad_queries = rotate(grad_query_parts[0], cosine_table, -sine_table)
-    grad_keys = rotate(grad_key_parts[0], cosine_table, -sine_table)
-    grad_values = grad_value_parts[0]
+    grad_queries, grad_keys, grad_values = attend_back(
+        queries, key_rows, value_rows, segment, position, logsum, grad_mixed
+    )
+    grad_queries = rotate(grad_queries, cosine_table, -sine_table)
+    grad_keys = rotate(grad_keys, cosine_table, -sine_table)
     grad_projected = jnp.concatenate(
         [
             grad_queries.reshape(tok_dev, q_dim),
@@ -700,6 +750,8 @@
         ],
         axis=1,
     ).astype(jnp.bfloat16)
+    grad_projected, *ahead_parts = lax.optimization_barrier((grad_projected, *ahead_parts))
+    output_rows = (residual + total_of(ahead_parts)).astype(jnp.bfloat16)
     grad_qkv_weight = jnp.einsum(
         "nd,nc->dc", normed, grad_projected, preferred_element_type=jnp.float32
     )

time: 1040 us -> 895 us (0.86)
  waiting for transfers between devices: 242 us -> 59.6 us
  Pallas kernels: 277 us -> 421 us
  matrix products: 259 us -> 181 us
    ppermute x18, waiting for transfers between devices: 214 us -> 55.9 us  [swap(): return lax.ppermute(block, 'lo', [(i, i ^ step) for i in range(lo_count)])]
    dot_general x11 -> x9, matrix products: 132 us -> 62.5 us  [the longest x1 21.9 us: shards(): jnp.einsum('ekrf,erd->ekfd', grad_gate_up, expert_rows, preferred_element...]
    pallas_call x0 -> x8, Pallas kernels: none -> 55.4 us  [dispatch(): pl.pallas_call(functools.partial(dispatch_kernel, weight is not None), gr...]
    pallas_call x1, Pallas kernels: 147 us -> 199 us  [opening(): pl.pallas_call(functools.partial(opening_kernel, sizes), out_shape=(jax.S...]
    pallas_call x1, Pallas kernels: 130 us -> 166 us  [closing(): pl.pallas_call(functools.partial(closing_kernel, sizes), out_shape=(jax.S...]
    all_to_all x1 -> x0, waiting for transfers between devices: 24.1 us -> none  [shards(): lax.all_to_all(asked_grads, ALL, split_axis=0, concat_axis=0, tiled=True)]
    optimization_barrier x1 -> x0, local copies, waits for them, and re-layouts: 17.2 us -> none  [shards(): lax.optimization_barrier((grad_normed_two, grad_weights_in.astype(jnp.bfl...]
    convert_element_type x1, other arithmetic: 22.7 us -> 7.02 us  [attend_back(): grad_scores = (exact_probs * (grad_probs - jnp.sum(grad_probs * exact_pro...]
  transfers between devices with their start and end apart: 24 -> 23, of which waited for: 11 -> 8; matrix products, arithmetic and copies ran while one was open for 35% -> 31% of each run, Pallas kernels for 27% -> 47%
where the time goes in v3:
time: 895 us; the launch traced here: 889 us
  Pallas kernels  421 us (47%)
  matrix products  181 us (20%)
  local copies, waits for them, and re-layouts  94.9 us (11%)
  other arithmetic  86.3 us (10%)
  waiting for transfers between devices  59.6 us (7%)
  starting transfers between devices  31.4 us (4%)
  between operations  15.5 us (2%)
    pallas_call x1, Pallas kernels, opening(): pl.pallas_call(functools.partial(opening_kernel, sizes), out_shape=(jax.S...  199 us
    pallas_call x1, Pallas kernels, closing(): pl.pallas_call(functools.partial(closing_kernel, sizes), out_shape=(jax.S...  166 us
    ppermute x18, waiting for transfers between devices, swap(): return lax.ppermute(block, 'lo', [(i, i ^ step) for i in range(lo_count)])  55.9 us
    pallas_call x8, Pallas kernels, dispatch(): pl.pallas_call(functools.partial(dispatch_kernel, weight is not None), gr...  55.4 us
    ppermute x18, starting transfers between devices, swap(): return lax.ppermute(block, 'lo', [(i, i ^ step) for i in range(lo_count)])  25.2 us
    dot_general x1, matrix products, shards(): jnp.einsum('ekrf,erd->ekfd', grad_gate_up, expert_rows, preferred_element...  21.9 us
    dot_general x1, matrix products, shards(): jnp.einsum('ekrf,ekdf->erd', grad_gate_up, weights_in, preferred_element_...  20.8 us
    another operation x7, other arithmetic  20 us
  transfers between devices with their start and end apart: 23, of which 8 were waited for; matrix products, arithmetic and copies ran while one was open for 31% of the time, Pallas kernels for 47%

profile of v3, /device:TPU:12, one launch (start us, length us, event | category | flops | bytes accessed | tf_op | source)
XLA Modules:
  0.0 889.3 jit_solution(1922086363193019613)
XLA Ops:
  8.0 3.7 all_gather_reshape.3
  20.5 6.0 all-to-all-start
  29.3 2.6 all-to-all-done
  37.7 3.1 gather_fusion.1
  40.8 2.9 gather_fusion
  43.8 3.4 broadcast_select_fusion.6
  47.2 198.8 %opening.1 = (bf16[32,16,1536]{2,1,0:T(8,128)(2,1)}, bf16[32,16,1536]{2,1,0:T(8,128)(2,1)}, bf16[4,4,2,48,4224]{4,3,2,1,0:T(8,128)(2,1)}) custom-call(bf16[32,16,1536]{2,1,0:T(8,128)(2,1)} %bitcast.259, bf16[32,16,1536]{2,1,0:T(8,128)(2,1)} %bitcast.258, bf16[48,4224]{1,0:T(8,128)(2,1)} %concatenate.40.shard_ref), custom_call_target="tpu_custom_call" | custom-call | tf_op jit(solution)/shard_map/opening/pallas_call | solution.py:316
  246.0 5.3 gather_fusion.3
  254.7 5.2 collective-permute-start.7
  264.3 6.8 fusion.22
  276.1 3.5 copy.149
  279.6 3.5 add_convert_fusion.2
  283.1 2.9 concatenate.45
  289.5 3.1 concatenate.44
  297.3 3.1 fusion.13
  301.9 3.5 fusion.66
  307.4 5.9 multiply_reduce_fusion.2
  324.6 2.5 collective-permute-done.7.rows_ref
  327.2 6.8 dispatch.12.refs_0_
  334.0 7.0 dispatch.8.refs_1_
  341.0 6.9 dispatch.9.refs_1_
  347.9 7.0 dispatch.10.refs_1_
  355.0 7.0 dispatch.11
  361.9 13.8 %convert_bitcast_fusion = bf16[4,2,1024,256]{3,2,1,0:T(8,128)(2,1)} fusion(bf16[4,1024,1536,1]{2,1,3,0:T(8,128)(2,1)} %bitcast.243, bf16[4,2,256,1536]{3,2,1,0:T(8,128)(2,1)} %bitcast.310), kind=kOutput, calls=%fused_computation.62 | convolution fusion | flops 6444548096 | bytes 23068672 | tf_op jit(solution)/shard_map/erd,ekfd->ekrf/dot_general | solution.py:656
  375.7 18.2 %collective-permute-done.10.rows_ref = bf16[512,1536]{1,0:T(8,128)(2,1)} collective-permute-done((bf16[512,1536]{1,0:T(8,128)(2,1)S(1)}, bf16[512,1536]{1,0:T(8,128)(2,1)}, u32[]{:S(2)}, u32[]{:S(2)}) %collective-permute-start.10) | collective-permute-done | bytes 1572896 | tf_op jit(solution)/shard_map/ppermute | solution.py:568
  394.0 6.9 dispatch.13.refs_0_
  400.9 6.9 dispatch.14.refs_0_
  407.7 6.9 dispatch.15
  414.6 17.9 %convolution_bitcast_fusion = f32[4,2,1024,512]{3,2,1,0:T(8,128)S(1)} fusion(bf16[4,1024,1536,1]{2,1,3,0:T(8,128)(2,1)} %bitcast.239, bf16[4,2,1536,512]{3,2,1,0:T(8,128)(2,1)} %bitcast.308), kind=kOutput, calls=%fused_computation.38 | convolution fusion | flops 12884901888 | bytes 41943040 | tf_op jit(solution)/shard_map/erd,ekdf->ekrf/dot_general | solution.py:665
  432.6 11.3 %fusion.17 = (bf16[4,2,1024,256]{3,2,1,0:T(8,128)(2,1)}, bf16[4,2,1024,256]{3,2,1,0:T(8,128)(2,1)}, bf16[4,2,1024,256]{3,2,1,0:T(8,128)(2,1)}) fusion(bf16[4,2,1024,256]{3,2,1,0:T(8,128)(2,1)} %convert_bitcast_fusion, f32[4,2,1024,512]{3,2,1,0:T(8,128)S(1)} %convolution_bitcast_fusion), kind=kLoop, calls=%fused_computation.41 | loop fusion | flops 33554432 | bytes 33554432 | tf_op jit(solution)/shard_map/convert.19
  443.9 20.8 %bitcast_convert_fusion = bf16[4,1024,1536]{2,1,0:T(8,128)(2,1)} fusion(bf16[4,2,1536,512]{3,2,1,0:T(8,128)(2,1)} %bitcast.309, bf16[4,2,1024,256]{3,2,1,0:T(8,128)(2,1)} %get-tuple-element.90, bf16[4,2,1024,256]{3,2,1,0:T(8,128)(2,1)} %get-tuple-element.89), kind=kOutput, calls=%fused_computation.10 | convolution fusion | flops 12907970560 | bytes 33554432 | tf_op jit(solution)/shard_map/ekrf,ekdf->erd/dot_general | solution.py:675
  464.6 7.5 pad_maximum_fusion
  472.1 8.0 bitcast_convert_fusion.1
  486.6 12.7 %fusion.1 = bf16[4,1024,1536]{2,1,0:T(8,128)(2,1)} fusion(bf16[4,2,1024,256]{3,2,1,0:T(8,128)(2,1)S(1)} %copy-done.22, bf16[4,2,256,1536]{3,2,1,0:T(8,128)(2,1)} %bitcast.311, f32[4,1024]{1,0:T(4,128)S(1)} %bitcast.290), kind=kOutput, calls=%fused_computation.12 | convolution fusion | flops 6455033856 | bytes 23085056 | tf_op jit(solution)/shard_map/ekrf,ekfd->erd/dot_general | solution.py:709
  499.4 10.7 %bitcast_convert_fusion.2 = bf16[8,256,1536]{2,1,0:T(8,128)(2,1)} fusion(bf16[4,8,128,1536]{3,2,1,0:T(8,128)(2,1)} %bitcast.313, s32[8,4,256]{2,1,0:T(4,128)S(1)} %copy.156, pred[8,4,256]{2,1,0:T(4,128)(4,1)S(1)} %bitcast.287), kind=kOutput, calls=%fused_computation.24 | convolution fusion | flops 3226468352 | bytes 18915328 | tf_op jit(solution)/shard_map/becr,ebcd->brd/dot_general | solution.py:681
  510.1 21.9 %convolution_convert_fusion = bf16[4,2,512,1536]{3,2,1,0:T(8,128)(2,1)} fusion(bf16[4,2,1024,512]{3,2,1,0:T(8,128)(2,1)} %pad_maximum_fusion, bf16[4,1024,1536]{2,1,0:T(8,128)(2,1)} %bitcast.240), kind=kOutput, calls=%fused_computation.13 | convolution fusion | flops 12891193344 | bytes 33554432 | tf_op jit(solution)/shard_map/ekrf,erd->ekfd/dot_general | solution.py:705
  532.0 13.8 %fusion.32 = bf16[4,2,256,1536]{3,2,1,0:T(8,128)(2,1)} fusion(bf16[4,2,1024,256]{3,2,1,0:T(8,128)(2,1)} %get-tuple-element.58, bf16[4,1024,1536]{2,1,0:T(8,128)(2,1)} %bitcast.244), kind=kOutput, calls=%fused_computation.60 | convolution fusion | flops 6445596672 | bytes 23068672 | tf_op jit(solution)/shard_map/ekrf,erd->ekfd/dot_general | solution.py:702
  545.8 8.1 collective-permute-done.13
  556.6 4.4 multiply_reduce_fusion
  561.0 3.9 subtract_add_fusion
  566.6 5.0 fusion.58
  572.8 5.9 slice_bitcast_fusion
  578.6 2.8 collective-permute-start.17
  582.1 10.0 %fusion.6 = (f32[2,8,3,256]{3,2,1,0:T(4,128)S(1)}, f32[2,8,256,256,3]{3,2,4,1,0:T(8,128)}) fusion(f32[2,8,3,256]{3,2,1,0:T(4,128)S(1)} %log_add_fusion, f32[2,8,256,256,3]{3,2,4,1,0:T(8,128)} %copy-done.2, pred[2,256,256]{1,2,0:T(8,128)(4,1)S(1)} %copy-done.24, bf16[2,256,8,3,64]{1,0,4,3,2:T(2,128)(2,1)S(1)} %reshape.370, ...), kind=kOutput, calls=%fused_computation.20 | convolution fusion | flops 418369536 | bytes 27492352 | tf_op jit(solution)/shard_map/bqhgd,bkhd->bhgqk/dot_general | solution.py:122
  592.2 7.0 fusion.8
  602.7 3.2 fusion.82
  606.7 4.1 copy.175
  610.8 5.5 reshape.371
  621.4 4.5 convolution_convert_fusion.2
  625.9 23.7 %collective-permute-done.16 = bf16[512,1536]{1,0:T(8,128)(2,1)} collective-permute-done((bf16[512,1536]{1,0:T(8,128)(2,1)}, bf16[512,1536]{1,0:T(8,128)(2,1)}, u32[]{:S(2)}, u32[]{:S(2)}) %collective-permute-start.16) | collective-permute-done | bytes 1572896 | tf_op jit(solution)/shard_map/ppermute | solution.py:568
  649.7 10.1 %fusion.55 = (bf16[1536]{0:T(1024)(128)(2,1)S(1)}, f32[512]{0:T(512)S(1)}, f32[512,1536]{1,0:T(8,128)}) fusion(f32[512]{0:T(512)S(1)} %copy-done.60, bf16[512,1536]{1,0:T(8,128)(2,1)S(1)} %copy-done.11, pred[512]{0:T(512)(128)(4,1)S(1)} %copy-done.58, f32[1536]{0:T(1024)S(1)} %copy-done.51, bf16[512,2560]{0,1:T(8,128)(2,1)S(1)} %pad_maximum_fusion.1, ...), kind=kOutput, calls=%fused_computation.82 | convolution fusion | flops 4032821248 | bytes 15218176 | tf_op jit(solution)/shard_map/nc,dc->nd/dot_general | solution.py:758
  659.9 3.7 add_convert_fusion
  663.5 2.9 gather_fusion.4
  666.5 3.5 fusion.51
  670.0 2.9 gather_fusion.5
  673.2 4.1 broadcast_select_fusion.2
  677.3 6.9 convolution_convert_fusion.1
  684.3 5.4 fusion.2
  689.7 166.3 %closing.1 = (bf16[32,16,1536]{2,1,0:T(8,128)(2,1)}, bf16[32,16,1536]{2,1,0:T(8,128)(2,1)}, f32[48,4224]{1,0:T(8,128)}) custom-call(bf16[32,16,1536]{2,1,0:T(8,128)(2,1)} %bitcast.262, bf16[32,16,1536]{2,1,0:T(8,128)(2,1)} %bitcast.261, bf16[4,4,2,48,4224]{4,3,2,1,0:T(8,128)(2,1)} %bitcast.249), custom_call_target="tpu_custom_call" | custom-call | tf_op jit(solution)/shard_map/closing/pallas_call | solution.py:470
  859.7 2.9 gather_fusion.6
  862.7 2.9 gather_fusion.7
  867.1 3.4 broadcast_select_fusion
  873.0 3.5 reshape.386
  876.5 5.9 copy.214
  (280 shorter events, 83.1 us)
Async XLA Ops:
  7.2 30.5 %copy-start = (bf16[512,1536]{1,0:T(8,128)(2,1)S(1)}, bf16[512,1536]{1,0:T(8,128)(2,1)}, u32[]{:S(2)}) copy-start(bf16[512,1536]{1,0:T(8,128)(2,1)} %param.15) | copy-start | bytes 4718596
  7.2 8.2 copy-start.56
  7.2 10.1 %copy-start.62 = (s32[512]{0:T(512)S(1)}, s32[512]{0:T(512)}, u32[]{:S(2)}) copy-start(s32[512]{0:T(512)} %param.16) | copy-start | bytes 6148
  7.2 19.4 %copy-start.61 = (s32[2,4]{1,0:T(2,128)S(1)}, s32[2,4]{1,0:T(2,128)}, u32[]{:S(2)}) copy-start(s32[2,4]{1,0:T(2,128)} %param.17) | copy-start | bytes 100
  7.2 21.0 %copy-start.63 = (bf16[48]{0:T(256)(128)(2,1)S(1)}, bf16[48]{0:T(256)(128)(2,1)}, u32[]{:S(2)}) copy-start(bf16[48]{0:T(256)(128)(2,1)} %param.20) | copy-start | bytes 292
  7.2 21.1 %copy-start.64 = (bf16[48]{0:T(256)(128)(2,1)S(1)}, bf16[48]{0:T(256)(128)(2,1)}, u32[]{:S(2)}) copy-start(bf16[48]{0:T(256)(128)(2,1)} %param.23) | copy-start | bytes 292
  7.2 21.2 %copy-start.45 = (bf16[48,1536]{1,0:T(8,128)(2,1)S(1)}, bf16[48,1536]{1,0:T(8,128)(2,1)}, u32[]{:S(2)}) copy-start(bf16[48,1536]{1,0:T(8,128)(2,1)} %param.22) | copy-start | bytes 442372
  7.3 21.2 %copy-start.44 = (bf16[48,2560]{1,0:T(8,128)(2,1)S(1)}, bf16[48,2560]{1,0:T(8,128)(2,1)}, u32[]{:S(2)}) copy-start(bf16[48,2560]{1,0:T(8,128)(2,1)} %param.21) | copy-start | bytes 737284
  7.3 354.7 %all-gather.6.cloned.1.call-start = ((), (), s32[]{:S(2)}) async-start(), calls=%async_computation.6 | async-start | bytes 7077888 | tf_op jit(solution)/shard_map/all_gather | solution.py:616
  8.0 406.6 %all-gather.4.cloned.1.call-start = ((), (), s32[]{:S(2)}) async-start(), calls=%async_computation.3 | async-start | bytes 14155776 | tf_op jit(solution)/shard_map/all_gather | solution.py:613
  11.8 21.4 %collective-permute-start = (s32[512,8]{0,1:T(8,128)S(1)}, s32[512,8]{0,1:T(8,128)S(1)}, u32[]{:S(2)}, u32[]{:S(2)}) collective-permute-start(s32[512,8]{0,1:T(8,128)S(1)} %copy-done.55), channel_id=1, source_target_pairs={{0,2},{2,0},{4,6},{6,4},{1,3},{3,1},{5,7},{7,5},{8,10},{10,8},{12,... | collective-permute-start | bytes 49160 | tf_op jit(solution)/shard_map/ppermute | solution.py:568
  13.4 21.3 %collective-permute-start.2 = (s32[512,8]{0,1:T(8,128)S(1)}, s32[512,8]{0,1:T(8,128)S(1)}, u32[]{:S(2)}, u32[]{:S(2)}) collective-permute-start(s32[512,8]{0,1:T(8,128)S(1)} %copy-done.55), channel_id=1, source_target_pairs={{0,6},{2,4},{4,2},{6,0},{1,7},{3,5},{5,3},{7,1},{8,14},{10,12},{12... | collective-permute-start | bytes 49160 | tf_op jit(solution)/shard_map/ppermute | solution.py:568
  13.9 20.8 %collective-permute-start.1 = (s32[512,8]{0,1:T(8,128)S(1)}, s32[512,8]{0,1:T(8,128)S(1)}, u32[]{:S(2)}, u32[]{:S(2)}) collective-permute-start(s32[512,8]{0,1:T(8,128)S(1)} %copy-done.55), channel_id=1, source_target_pairs={{0,4},{2,6},{4,0},{6,2},{1,5},{3,7},{5,1},{7,3},{8,12},{10,14},{12... | collective-permute-start | bytes 49160 | tf_op jit(solution)/shard_map/ppermute | solution.py:568
  15.4 19.9 %collective-permute-start.3 = (f32[512,8]{0,1:T(8,128)S(1)}, f32[512,8]{0,1:T(8,128)S(1)}, u32[]{:S(2)}, u32[]{:S(2)}) collective-permute-start(f32[512,8]{0,1:T(8,128)S(1)} %copy-done.56), channel_id=1, source_target_pairs={{0,2},{2,0},{4,6},{6,4},{1,3},{3,1},{5,7},{7,5},{8,10},{10,8},{12,... | collective-permute-start | bytes 49160 | tf_op jit(solution)/shard_map/ppermute | solution.py:568
  16.9 18.5 %collective-permute-start.5 = (f32[512,8]{0,1:T(8,128)S(1)}, f32[512,8]{0,1:T(8,128)S(1)}, u32[]{:S(2)}, u32[]{:S(2)}) collective-permute-start(f32[512,8]{0,1:T(8,128)S(1)} %copy-done.56), channel_id=1, source_target_pairs={{0,6},{2,4},{4,2},{6,0},{1,7},{3,5},{5,3},{7,1},{8,14},{10,12},{12... | collective-permute-start | bytes 49160 | tf_op jit(solution)/shard_map/ppermute | solution.py:568
  18.9 288.5 %copy-start.57 = (pred[512]{0:T(512)(128)(4,1)}, pred[512]{0:T(512)(128)(4,1)S(1)}, u32[]{:S(2)}) copy-start(pred[512]{0:T(512)(128)(4,1)S(1)} %get-tuple-element.87) | copy-start | bytes 1540
  20.5 11.4 %all-to-all-start = ((s32[32,1,16]{2,1,0:T(1,128)}), s32[32,1,16]{2,1,0:T(1,128)S(1)}, u32[]{:S(2)}, u32[]{:S(2)}) async-start(s32[32,1,16]{2,1,0:T(1,128)} %bitcast.2), calls=%async_computation | async-start | bytes 32768 | tf_op jit(solution)/shard_map/all_to_all | solution.py:575
  26.5 844.0 %reduce-scatter.5.cloned.1.call-start = ((), (), s32[]{:S(2)}) async-start(), calls=%async_computation.5 | async-start | bytes 7077888 | tf_op jit(solution)/shard_map/reduce_scatter | solution.py:718
  27.3 273.2 %copy-start.23 = (pred[2,256,256]{1,2,0:T(8,128)(4,1)}, pred[2,256,256]{1,2,0:T(8,128)(4,1)S(1)}, u32[]{:S(2)}) copy-start(pred[2,256,256]{1,2,0:T(8,128)(4,1)S(1)} %compare_and_fusion) | copy-start | bytes 393220
  28.2 259.1 %copy-start.32 = (f32[512,32]{0,1:T(8,128)}, f32[512,32]{0,1:T(8,128)S(1)}, u32[]{:S(2)}) copy-start(f32[512,32]{0,1:T(8,128)S(1)} %get-tuple-element.110) | copy-start | bytes 196612
  33.2 10.5 %copy-start.52 = (s32[512]{0:T(512)}, s32[512]{0:T(512)S(1)}, u32[]{:S(2)}) copy-start(s32[512]{0:T(512)S(1)} %reshape.355) | copy-start | bytes 6148
  33.2 3.8 collective-permute-start.4
  251.3 8.5 copy-start.12
  251.3 8.5 copy-start.4
  252.7 71.9 %collective-permute-start.8 = (bf16[512,1536]{1,0:T(8,128)(2,1)}, bf16[512,1536]{1,0:T(8,128)(2,1)}, u32[]{:S(2)}, u32[]{:S(2)}) collective-permute-start(bf16[512,1536]{1,0:T(8,128)(2,1)} %broadcast_select_fusion.4.rows_ref), channel_id=1, source_target_pairs={{0,6},{2,4},{4,2},{6,0},{1,7},{3,5},{5,3},{7,1},{8,14},{10,12},{12... | collective-permute-start | bytes 4718600 | tf_op jit(solution)/shard_map/ppermute | solution.py:568
  254.7 72.5 %collective-permute-start.7 = (bf16[512,1536]{1,0:T(8,128)(2,1)}, bf16[512,1536]{1,0:T(8,128)(2,1)}, u32[]{:S(2)}, u32[]{:S(2)}) collective-permute-start(bf16[512,1536]{1,0:T(8,128)(2,1)} %broadcast_select_fusion.4.rows_ref), channel_id=1, source_target_pairs={{0,4},{2,6},{4,0},{6,2},{1,5},{3,7},{5,1},{7,3},{8,12},{10,14},{12... | collective-permute-start | bytes 4718600 | tf_op jit(solution)/shard_map/ppermute | solution.py:568
  259.9 67.3 %collective-permute-start.6 = (bf16[512,1536]{1,0:T(8,128)(2,1)}, bf16[512,1536]{1,0:T(8,128)(2,1)}, u32[]{:S(2)}, u32[]{:S(2)}) collective-permute-start(bf16[512,1536]{1,0:T(8,128)(2,1)} %broadcast_select_fusion.4.rows_ref), channel_id=1, source_target_pairs={{0,2},{2,0},{4,6},{6,4},{1,3},{3,1},{5,7},{7,5},{8,10},{10,8},{12,... | collective-permute-start | bytes 4718600 | tf_op jit(solution)/shard_map/ppermute | solution.py:568
  262.0 45.4 %copy-start.10 = (bf16[512,1536]{1,0:T(8,128)(2,1)}, bf16[512,1536]{1,0:T(8,128)(2,1)S(1)}, u32[]{:S(2)}) copy-start(bf16[512,1536]{1,0:T(8,128)(2,1)S(1)} %gather_fusion.2) | copy-start | bytes 4718596
  263.7 7.4 copy-start.50
  263.7 49.7 %copy-start.46 = (f32[1536]{0:T(1024)}, f32[1536]{0:T(1024)S(1)}, u32[]{:S(2)}) copy-start(f32[1536]{0:T(1024)S(1)} %get-tuple-element.83) | copy-start | bytes 18436
  264.2 6.8 copy-start.59
  288.7 8.5 copy-start.26
  307.4 5.9 copy-start.35
  313.3 5.5 copy-start.40
  313.3 5.9 copy-start.43
  313.3 7.0 copy-start.48
  315.3 11.9 %copy-start.21 = (bf16[512,1536]{1,0:T(8,128)(2,1)}, bf16[512,1536]{1,0:T(8,128)(2,1)S(1)}, u32[]{:S(2)}) copy-start(bf16[512,1536]{1,0:T(8,128)(2,1)S(1)} %multiply_convert_fusion.1.rows_ref) | copy-start | bytes 4718596
  315.3 60.4 %collective-permute-start.11 = (bf16[512,1536]{1,0:T(8,128)(2,1)S(1)}, bf16[512,1536]{1,0:T(8,128)(2,1)S(1)}, u32[]{:S(2)}, u32[]{:S(2)}) collective-permute-start(bf16[512,1536]{1,0:T(8,128)(2,1)S(1)} %multiply_convert_fusion.1.rows_ref), channel_id=1, source_target_pairs={{0,6},{2,4},{4,2},{6,0},{1,7},{3,5},{5,3},{7,1},{8,14},{10,12},{12... | collective-permute-start | bytes 4718600 | tf_op jit(solution)/shard_map/ppermute | solution.py:568
  316.8 77.1 %collective-permute-start.10 = (bf16[512,1536]{1,0:T(8,128)(2,1)S(1)}, bf16[512,1536]{1,0:T(8,128)(2,1)}, u32[]{:S(2)}, u32[]{:S(2)}) collective-permute-start(bf16[512,1536]{1,0:T(8,128)(2,1)S(1)} %multiply_convert_fusion.1.rows_ref), channel_id=1, source_target_pairs={{0,4},{2,6},{4,0},{6,2},{1,5},{3,7},{5,1},{7,3},{8,12},{10,14},{12... | collective-permute-start | bytes 4718600 | tf_op jit(solution)/shard_map/ppermute | solution.py:568
  324.6 69.3 %collective-permute-start.9 = (bf16[512,1536]{1,0:T(8,128)(2,1)S(1)}, bf16[512,1536]{1,0:T(8,128)(2,1)}, u32[]{:S(2)}, u32[]{:S(2)}) collective-permute-start(bf16[512,1536]{1,0:T(8,128)(2,1)S(1)} %multiply_convert_fusion.1.rows_ref), channel_id=1, source_target_pairs={{0,2},{2,0},{4,6},{6,4},{1,3},{3,1},{5,7},{7,5},{8,10},{10,8},{12,... | collective-permute-start | bytes 4718600 | tf_op jit(solution)/shard_map/ppermute | solution.py:568
  375.7 25.2 %copy-start.34 = (bf16[512,1536]{1,0:T(8,128)(2,1)}, bf16[512,1536]{1,0:T(8,128)(2,1)S(1)}, u32[]{:S(2)}) copy-start(bf16[512,1536]{1,0:T(8,128)(2,1)S(1)} %collective-permute-done.11.rows_ref) | copy-start | bytes 4718596
  480.1 6.5 copy-start.22
  482.7 71.2 %collective-permute-start.13 = (bf16[512,1536]{1,0:T(8,128)(2,1)}, bf16[512,1536]{1,0:T(8,128)(2,1)S(1)}, u32[]{:S(2)}, u32[]{:S(2)}) collective-permute-start(bf16[512,1536]{1,0:T(8,128)(2,1)} %bitcast.63), channel_id=1, source_target_pairs={{0,4},{2,6},{4,0},{6,2},{1,5},{3,7},{5,1},{7,3},{8,12},{10,14},{12... | collective-permute-start | bytes 4718600 | tf_op jit(solution)/shard_map/ppermute | solution.py:568
  485.2 68.7 %collective-permute-start.14 = (bf16[512,1536]{1,0:T(8,128)(2,1)}, bf16[512,1536]{1,0:T(8,128)(2,1)}, u32[]{:S(2)}, u32[]{:S(2)}) collective-permute-start(bf16[512,1536]{1,0:T(8,128)(2,1)} %bitcast.64), channel_id=1, source_target_pairs={{0,6},{2,4},{4,2},{6,0},{1,7},{3,5},{5,3},{7,1},{8,14},{10,12},{12... | collective-permute-start | bytes 4718600 | tf_op jit(solution)/shard_map/ppermute | solution.py:568
  486.4 69.2 %collective-permute-start.12 = (bf16[512,1536]{1,0:T(8,128)(2,1)}, bf16[512,1536]{1,0:T(8,128)(2,1)}, u32[]{:S(2)}, u32[]{:S(2)}) collective-permute-start(bf16[512,1536]{1,0:T(8,128)(2,1)} %bitcast.62), channel_id=1, source_target_pairs={{0,2},{2,0},{4,6},{6,4},{1,3},{3,1},{5,7},{7,5},{8,10},{10,8},{12,... | collective-permute-start | bytes 4718600 | tf_op jit(solution)/shard_map/ppermute | solution.py:568
  555.5 317.4 %reduce-scatter.3.cloned.1.call-start = ((), (), s32[]{:S(2)}) async-start(), calls=%async_computation.4 | async-start | bytes 14155776 | tf_op jit(solution)/shard_map/reduce_scatter | solution.py:724
  572.8 9.4 %copy-start.24 = (pred[2,256,256]{1,2,0:T(8,128)(4,1)S(1)}, pred[2,256,256]{1,2,0:T(8,128)(4,1)}, u32[]{:S(2)}) copy-start(pred[2,256,256]{1,2,0:T(8,128)(4,1)} %copy-done.23) | copy-start | bytes 393220
  572.8 9.4 %copy-start.31 = (bf16[2,256,8,64]{1,0,3,2:T(2,128)(2,1)S(1)}, bf16[2,256,8,64]{1,0,3,2:T(2,128)(2,1)}, u32[]{:S(2)}) copy-start(bf16[2,256,8,64]{1,0,3,2:T(2,128)(2,1)} %convert_element_type.160) | copy-start | bytes 1572868
  572.8 19.4 %slice-start = ((s8[12582912]{0:T(1024)(128)(4,1)}), s8[4194304]{0:T(1024)(128)(4,1)S(1)}, s32[]{:S(2)}) async-start(s8[12582912]{0:T(1024)(128)(4,1)} %bitcast.241), calls=%async_computation.7 | async-start | bytes 8388608
  578.6 47.3 %collective-permute-start.17 = (bf16[512,1536]{1,0:T(8,128)(2,1)}, bf16[512,1536]{1,0:T(8,128)(2,1)}, u32[]{:S(2)}, u32[]{:S(2)}) collective-permute-start(bf16[512,1536]{1,0:T(8,128)(2,1)} %get-tuple-element.92), channel_id=1, source_target_pairs={{0,6},{2,4},{4,2},{6,0},{1,7},{3,5},{5,3},{7,1},{8,14},{10,12},{12... | collective-permute-start | bytes 4718600 | tf_op jit(solution)/shard_map/ppermute | solution.py:568
  581.4 68.2 %collective-permute-start.16 = (bf16[512,1536]{1,0:T(8,128)(2,1)}, bf16[512,1536]{1,0:T(8,128)(2,1)}, u32[]{:S(2)}, u32[]{:S(2)}) collective-permute-start(bf16[512,1536]{1,0:T(8,128)(2,1)} %get-tuple-element.93), channel_id=1, source_target_pairs={{0,4},{2,6},{4,0},{6,2},{1,5},{3,7},{5,1},{7,3},{8,12},{10,14},{12... | collective-permute-start | bytes 4718600 | tf_op jit(solution)/shard_map/ppermute | solution.py:568
  581.7 10.5 %slice-start.1 = ((s8[12582912]{0:T(1024)(128)(4,1)}), s8[4194304]{0:T(1024)(128)(4,1)S(1)}, s32[]{:S(2)}) async-start(s8[12582912]{0:T(1024)(128)(4,1)} %bitcast.241), calls=%async_computation.8 | async-start | bytes 8388608
  581.7 10.5 %slice-start.2 = ((s8[12582912]{0:T(1024)(128)(4,1)}), s8[4194304]{0:T(1024)(128)(4,1)S(1)}, s32[]{:S(2)}) async-start(s8[12582912]{0:T(1024)(128)(4,1)} %bitcast.241), calls=%async_computation.9 | async-start | bytes 8388608
  581.7 67.9 %collective-permute-start.15 = (bf16[512,1536]{1,0:T(8,128)(2,1)}, bf16[512,1536]{1,0:T(8,128)(2,1)}, u32[]{:S(2)}, u32[]{:S(2)}) collective-permute-start(bf16[512,1536]{1,0:T(8,128)(2,1)} %get-tuple-element.94), channel_id=1, source_target_pairs={{0,2},{2,0},{4,6},{6,4},{1,3},{3,1},{5,7},{7,5},{8,10},{10,8},{12,... | collective-permute-start | bytes 4718600 | tf_op jit(solution)/shard_map/ppermute | solution.py:568
  592.2 7.0 copy-start.17
  621.4 28.2 %copy-start.25 = (bf16[512,2560]{0,1:T(8,128)(2,1)}, bf16[512,2560]{0,1:T(8,128)(2,1)S(1)}, u32[]{:S(2)}) copy-start(bf16[512,2560]{0,1:T(8,128)(2,1)S(1)} %pad_maximum_fusion.1) | copy-start | bytes 7864324
  621.4 28.2 %copy-start.11 = (bf16[512,1536]{1,0:T(8,128)(2,1)S(1)}, bf16[512,1536]{1,0:T(8,128)(2,1)}, u32[]{:S(2)}) copy-start(bf16[512,1536]{1,0:T(8,128)(2,1)} %copy-done.10) | copy-start | bytes 4718596
  621.4 28.2 %copy-start.51 = (f32[1536]{0:T(1024)S(1)}, f32[1536]{0:T(1024)}, u32[]{:S(2)}) copy-start(f32[1536]{0:T(1024)} %copy-done.50) | copy-start | bytes 18436
  621.4 28.2 %copy-start.60 = (f32[512]{0:T(512)S(1)}, f32[512]{0:T(512)}, u32[]{:S(2)}) copy-start(f32[512]{0:T(512)} %copy-done.59) | copy-start | bytes 6148
  649.7 10.2 %copy-start.9 = (f32[512,1536]{1,0:T(8,128)S(1)}, f32[512,1536]{1,0:T(8,128)}, u32[]{:S(2)}) copy-start(f32[512,1536]{1,0:T(8,128)} %copy-done.7) | copy-start | bytes 9437188
  649.7 10.2 %copy-start.18 = (bf16[512,1536]{1,0:T(8,128)(2,1)S(1)}, bf16[512,1536]{1,0:T(8,128)(2,1)}, u32[]{:S(2)}) copy-start(bf16[512,1536]{1,0:T(8,128)(2,1)} %get-tuple-element.67) | copy-start | bytes 4718596
  673.2 11.1 %slice-start.3 = ((s8[4718592]{0:T(1024)(128)(4,1)}), s8[4194304]{0:T(1024)(128)(4,1)S(1)}, s32[]{:S(2)}) async-start(s8[4718592]{0:T(1024)(128)(4,1)} %bitcast.263), calls=%async_computation.10 | async-start | bytes 8388608
  677.3 7.0 slice-start.4
  876.4 5.9 copy-start.1
  (29 other events, 78.4 us)
Sparse Core Ops, SparseCore 0:
  9.7 89.1 all-gather.5
  101.1 173.5 all-gather.3
  555.7 66.2 reduce-scatter.4
  624.1 209.5 reduce-scatter.2

commit v4 on v3

--- a/solution.py
+++ b/solution.py
@@ -495,10 +495,17 @@
 
 
 def dispatch_kernel(weighted, choose_ref, rows_ref, *refs):
-    slots = jnp.dot(choose_ref[0, 0], rows_ref[...], preferred_element_type=jnp.float32)
-    if weighted:
-        slots = slots * refs[0][0, 0]
-    refs[-1][0, 0] = slots.astype(jnp.bfloat16)
+    count, capacity, rows = choose_ref.shape[1:]
+    chosen = choose_ref[0].reshape(count * capacity, rows)
+    width = rows_ref.shape[1]
+    tile = 256 if width % 256 == 0 else width
+    for start in range(0, width, tile):
+        at = pl.ds(start, tile)
+        slots = jnp.dot(chosen, rows_ref[:, at], preferred_element_type=jnp.float32)
+        slots = slots.reshape(count, capacity, tile)
+        if weighted:
+            slots = slots * refs[0][:, 0]
+        refs[-1][:, 0, :, at] = slots.astype(jnp.bfloat16)
 
 
 def dispatch(choose, rows, step, slots, weight):
@@ -507,12 +514,12 @@
     first = step * MB
     operands = [choose, rows]
     in_specs = [
-        pl.BlockSpec((1, 1, capacity, TOK_MB), lambda b, e: (first + b, e, 0, 0)),
-        pl.BlockSpec((TOK_MB, width), lambda b, e: (b, 0)),
+        pl.BlockSpec((1, count, capacity, TOK_MB), lambda b: (first + b, 0, 0, 0)),
+        pl.BlockSpec((TOK_MB, width), lambda b: (b, 0)),
     ]
     if weight is not None:
         operands.append(weight)
-        in_specs.append(pl.BlockSpec((1, 1, capacity, 1), lambda b, e: (e, first + b, 0, 0)))
+        in_specs.append(pl.BlockSpec((count, 1, capacity, 1), lambda b: (0, first + b, 0, 0)))
     aliases = {}
     if slots is not None:
         aliases = {len(operands): 0}
@@ -520,10 +527,10 @@
         in_specs.append(pl.BlockSpec(memory_space=pl.ANY))
     return pl.pallas_call(
         functools.partial(dispatch_kernel, weight is not None),
-        grid=(MB, count),
+        grid=(MB,),
         out_shape=jax.ShapeDtypeStruct((count, choose.shape[0], capacity, width), jnp.bfloat16),
         in_specs=in_specs,
-        out_specs=pl.BlockSpec((1, 1, capacity, width), lambda b, e: (e, first + b, 0, 0)),
+        out_specs=pl.BlockSpec((count, 1, capacity, width), lambda b: (0, first + b, 0, 0)),
         input_output_aliases=aliases,
         name="dispatch",
     )(*operands)
@@ -600,6 +607,7 @@
         device_count, peer_rows, model_width
     )
     got_rows, got_grad, packed = opening(sizes, asked_tokens, asked_grads, weight_shard)
+    got_rows, packed, expert_in = lax.optimization_barrier((got_rows, packed, expert_in))
     packed = packed.reshape(model_width, -1)
     grad_bf = jnp.take(got_grad.reshape(tok_dev, model_width), arrival, axis=0)
     grad_blocks = spread(grad_bf)
@@ -672,6 +680,16 @@
     grad_gate = grad_hidden * up_part * sigmoid_gate * (1.0 + gate_part * (1.0 - sigmoid_gate))
     grad_up = grad_hidden * (gate_part * sigmoid_gate)
     grad_gate_up = jnp.concatenate([grad_gate, grad_up], axis=-1).astype(jnp.bfloat16)
+    grad_weights_out = jnp.einsum(
+        "ekrf,erd->ekfd", hidden, grad_expert, preferred_element_type=jnp.float32
+    ).astype(jnp.bfloat16)
+    grad_weights_out, grad_gate_up = lax.optimization_barrier((grad_weights_out, grad_gate_up))
+    shard_out = lax.psum_scatter(
+        grad_weights_out.reshape(hi_count * 2 * shard_cols, model_width),
+        ("hi", "core"),
+        scatter_dimension=0,
+        tiled=True,
+    ).astype(jnp.float32)
     grad_expert_rows = jnp.einsum(
         "ekrf,ekdf->erd", grad_gate_up, weights_in, preferred_element_type=jnp.float32
     ).astype(jnp.bfloat16)
@@ -696,31 +714,13 @@
 
     back = split_back(grad_expert_rows)
     back_parts = [back[0]] + [swap(back[step], step) for step in range(1, lo_count)]
-    back, hidden, expert_rows, grad_gate_up, grad_expert = lax.optimization_barrier(
-        (back, hidden, expert_rows, grad_gate_up, grad_expert)
-    )
-    grad_weights_out = jnp.einsum(
-        "ekrf,erd->ekfd", hidden, grad_expert, preferred_element_type=jnp.float32
-    ).astype(jnp.bfloat16)
+    back, hidden, expert_rows, grad_gate_up = lax.optimization_barrier(
+        (back, hidden, expert_rows, grad_gate_up)
+    )
     grad_weights_in = jnp.einsum(
         "ekrf,erd->ekfd", grad_gate_up, expert_rows, preferred_element_type=jnp.float32
     ).astype(jnp.bfloat16)
-    produced = (
-        jnp.einsum("ekrf,ekfd->erd", hidden, weights_out, preferred_element_type=jnp.float32)
-        * slot_weight.reshape(hi_count, -1, 1)
-    ).astype(jnp.bfloat16)
-    ahead = split_back(produced)
-    ahead, grad_weights_in, grad_weights_out, *back_parts = lax.optimization_barrier(
-        (ahead, grad_weights_in, grad_weights_out, *back_parts)
-    )
-    ahead_parts = [ahead[0]] + [swap(ahead[step], step) for step in range(1, lo_count)]
-    grad_normed_two = total_of(back_parts)
-    shard_out = lax.psum_scatter(
-        grad_weights_out.reshape(hi_count * 2 * shard_cols, model_width),
-        ("hi", "core"),
-        scatter_dimension=0,
-        tiled=True,
-    ).astype(jnp.float32)
+    grad_weights_in, hidden = lax.optimization_barrier((grad_weights_in, hidden))
     shard_in = lax.psum_scatter(
         grad_weights_in.reshape(hi_count * 2 * 2 * shard_cols, model_width),
         ("hi", "core"),
@@ -728,6 +728,14 @@
         tiled=True,
     )
     shard_in = shard_in.T.astype(jnp.float32).reshape(model_width, 2, shard_cols)
+    produced = (
+        jnp.einsum("ekrf,ekfd->erd", hidden, weights_out, preferred_element_type=jnp.float32)
+        * slot_weight.reshape(hi_count, -1, 1)
+    ).astype(jnp.bfloat16)
+    ahead = split_back(produced)
+    ahead, *back_parts = lax.optimization_barrier((ahead, *back_parts))
+    ahead_parts = [ahead[0]] + [swap(ahead[step], step) for step in range(1, lo_count)]
+    grad_normed_two = total_of(back_parts)
     grad_gain_two, grad_from_norm = norm_back(residual, scale_two, gain_two, grad_normed_two)
     grad_residual = grad_output + grad_from_norm
     grad_attended = grad_residual.astype(jnp.bfloat16)

time: 895 us -> 826 us (0.923)
  Pallas kernels: 421 us -> 305 us
  waiting for transfers between devices: 59.6 us -> 108 us
    pallas_call x1, Pallas kernels: 199 us -> 149 us  [opening(): pl.pallas_call(functools.partial(opening_kernel, sizes), out_shape=(jax.S...]
    ppermute x18, waiting for transfers between devices: 55.9 us -> 105 us  [swap(): return lax.ppermute(block, 'lo', [(i, i ^ step) for i in range(lo_count)])]
    pallas_call x1, Pallas kernels: 166 us -> 127 us  [closing(): pl.pallas_call(functools.partial(closing_kernel, sizes), out_shape=(jax.S...]
    pallas_call x8, Pallas kernels: 55.4 us -> 29.1 us  [dispatch(): pl.pallas_call(functools.partial(dispatch_kernel, weight is not None), gr...]
  transfers between devices with their start and end apart: 23 -> 23, of which waited for: 8 -> 8; matrix products, arithmetic and copies ran while one was open for 31% -> 36% of each run, Pallas kernels for 47% -> 37%
where the time goes in v4:
time: 826 us; the launch traced here: 821 us
  Pallas kernels  305 us (37%)
  matrix products  183 us (22%)
  waiting for transfers between devices  108 us (13%)
  local copies, waits for them, and re-layouts  93.7 us (11%)
  other arithmetic  88 us (11%)
  starting transfers between devices  27.8 us (3%)
  between operations  15.2 us (2%)
    pallas_call x1, Pallas kernels, opening(): pl.pallas_call(functools.partial(opening_kernel, sizes), out_shape=(jax.S...  149 us
    pallas_call x1, Pallas kernels, closing(): pl.pallas_call(functools.partial(closing_kernel, sizes), out_shape=(jax.S...  127 us
    ppermute x18, waiting for transfers between devices, swap(): return lax.ppermute(block, 'lo', [(i, i ^ step) for i in range(lo_count)])  105 us
    pallas_call x8, Pallas kernels, dispatch(): pl.pallas_call(functools.partial(dispatch_kernel, weight is not None), gr...  29.1 us
    dot_general x1, matrix products, shards(): jnp.einsum('ekrf,erd->ekfd', grad_gate_up, expert_rows, preferred_element...  22.7 us
    ppermute x18, starting transfers between devices, swap(): return lax.ppermute(block, 'lo', [(i, i ^ step) for i in range(lo_count)])  21.1 us
    dot_general x1, matrix products, shards(): jnp.einsum('ekrf,ekdf->erd', grad_gate_up, weights_in, preferred_element_...  20.6 us
    dot_general x2, matrix products, split_back(): jnp.einsum('becr,ebcd->brd', choose, slot_values.reshape(hi_count, lo_cou...  20.1 us
  transfers between devices with their start and end apart: 23, of which 8 were waited for; matrix products, arithmetic and copies ran while one was open for 36% of the time, Pallas kernels for 37%

profile of v4, /device:TPU:12, one launch (start us, length us, event | category | flops | bytes accessed | tf_op | source)
XLA Modules:
  0.0 821.0 jit_solution(16378690481772425115)
XLA Ops:
  17.2 6.0 all-to-all-start
  35.3 2.9 gather_fusion.1
  38.3 2.9 gather_fusion
  41.2 3.4 broadcast_select_fusion.6
  44.6 148.8 %opening.1 = (bf16[32,16,1536]{2,1,0:T(8,128)(2,1)}, bf16[32,16,1536]{2,1,0:T(8,128)(2,1)}, bf16[4,4,2,48,4224]{4,3,2,1,0:T(8,128)(2,1)}) custom-call(bf16[32,16,1536]{2,1,0:T(8,128)(2,1)} %bitcast.254, bf16[32,16,1536]{2,1,0:T(8,128)(2,1)} %bitcast.253, bf16[48,4224]{1,0:T(8,128)(2,1)} %concatenate.40.shard_ref), custom_call_target="tpu_custom_call" | custom-call | tf_op jit(solution)/shard_map/opening/pallas_call | solution.py:316
  193.4 2.3 all_gather_reshape.3
  209.3 6.8 fusion.20
  221.1 3.5 copy.149
  224.7 3.5 add_convert_fusion.2
  228.2 2.9 concatenate.45
  234.6 3.1 concatenate.44
  242.4 3.1 fusion.11
  247.1 3.5 fusion.61
  252.6 5.6 multiply_reduce_fusion.2
  266.4 2.2 fusion.34.choose_ref
  270.1 3.7 collective-permute-done.7.rows_ref
  273.8 3.7 dispatch.12.refs_0_
  277.4 3.6 dispatch.8.refs_1_
  281.0 3.7 dispatch.9.refs_1_
  284.8 3.6 dispatch.10.refs_1_
  288.4 3.8 dispatch.11
  292.2 13.8 %convert_bitcast_fusion = bf16[4,2,1024,256]{3,2,1,0:T(8,128)(2,1)} fusion(bf16[4,1024,1536,1]{2,1,3,0:T(8,128)(2,1)} %bitcast.238, bf16[4,2,256,1536]{3,2,1,0:T(8,128)(2,1)} %bitcast.305), kind=kOutput, calls=%fused_computation.60 | convolution fusion | flops 6444548096 | bytes 23068672 | tf_op jit(solution)/shard_map/erd,ekfd->ekrf/dot_general | solution.py:664
  307.3 33.1 %collective-permute-done.10.rows_ref = bf16[512,1536]{1,0:T(8,128)(2,1)} collective-permute-done((bf16[512,1536]{1,0:T(8,128)(2,1)S(1)}, bf16[512,1536]{1,0:T(8,128)(2,1)}, u32[]{:S(2)}, u32[]{:S(2)}) %collective-permute-start.10) | collective-permute-done | bytes 1572896 | tf_op jit(solution)/shard_map/ppermute | solution.py:575
  340.4 3.6 dispatch.13.refs_0_
  344.0 3.6 dispatch.14.refs_0_
  347.6 3.6 dispatch.15
  351.2 18.3 %convolution_bitcast_fusion = f32[4,2,1024,512]{3,2,1,0:T(8,128)S(1)} fusion(bf16[4,1024,1536,1]{2,1,3,0:T(8,128)(2,1)} %bitcast.234, bf16[4,2,1536,512]{3,2,1,0:T(8,128)(2,1)} %bitcast.303), kind=kOutput, calls=%fused_computation.36 | convolution fusion | flops 12884901888 | bytes 41943040 | tf_op jit(solution)/shard_map/erd,ekdf->ekrf/dot_general | solution.py:673
  369.5 11.2 %fusion.15 = (bf16[4,2,1024,256]{3,2,1,0:T(8,128)(2,1)}, bf16[4,2,1024,256]{3,2,1,0:T(8,128)(2,1)}, bf16[4,2,1024,256]{3,2,1,0:T(8,128)(2,1)}) fusion(bf16[4,2,1024,256]{3,2,1,0:T(8,128)(2,1)} %convert_bitcast_fusion, f32[4,2,1024,512]{3,2,1,0:T(8,128)S(1)} %convolution_bitcast_fusion), kind=kLoop, calls=%fused_computation.39 | loop fusion | flops 33554432 | bytes 33554432 | tf_op jit(solution)/shard_map/convert.19
  380.7 13.8 %convolution_convert_fusion.3 = bf16[4,2,256,1536]{3,2,1,0:T(8,128)(2,1)} fusion(bf16[4,2,1024,256]{3,2,1,0:T(8,128)(2,1)} %get-tuple-element.69, bf16[4,1024,1536,1]{2,1,3,0:T(8,128)(2,1)} %bitcast.239), kind=kOutput, calls=%fused_computation.58 | convolution fusion | flops 6445596672 | bytes 23068672 | tf_op jit(solution)/shard_map/ekrf,erd->ekfd/dot_general | solution.py:683
  394.5 7.4 pad_maximum_fusion
  403.9 22.7 %convolution_convert_fusion = bf16[4,2,512,1536]{3,2,1,0:T(8,128)(2,1)} fusion(bf16[4,2,1024,512]{3,2,1,0:T(8,128)(2,1)} %pad_maximum_fusion, bf16[4,1024,1536]{2,1,0:T(8,128)(2,1)} %bitcast.235), kind=kOutput, calls=%fused_computation.13 | convolution fusion | flops 12891193344 | bytes 33554432 | tf_op jit(solution)/shard_map/ekrf,erd->ekfd/dot_general | solution.py:720
  427.5 20.6 %bitcast_convert_fusion = bf16[4,1024,1536]{2,1,0:T(8,128)(2,1)} fusion(bf16[4,2,1024,512]{3,2,1,0:T(8,128)(2,1)} %pad_maximum_fusion, bf16[4,2,1536,512]{3,2,1,0:T(8,128)(2,1)} %bitcast.304), kind=kOutput, calls=%fused_computation.10 | convolution fusion | flops 12891193344 | bytes 33554432 | tf_op jit(solution)/shard_map/ekrf,ekdf->erd/dot_general | solution.py:693
  448.1 8.2 bitcast_convert_fusion.1
  456.4 2.5 fusion.105
  462.4 12.8 %fusion.1 = bf16[4,1024,1536]{2,1,0:T(8,128)(2,1)} fusion(bf16[4,2,1024,256]{3,2,1,0:T(8,128)(2,1)S(1)} %copy-done.23, bf16[4,2,256,1536]{3,2,1,0:T(8,128)(2,1)} %bitcast.306, f32[4,1024]{1,0:T(4,128)S(1)} %bitcast.285), kind=kOutput, calls=%fused_computation.12 | convolution fusion | flops 6455033856 | bytes 23085056 | tf_op jit(solution)/shard_map/ekrf,ekfd->erd/dot_general | solution.py:732
  475.2 12.0 %bitcast_convert_fusion.2 = bf16[8,256,1536]{2,1,0:T(8,128)(2,1)} fusion(bf16[4,8,128,1536]{3,2,1,0:T(8,128)(2,1)} %bitcast.307, s32[8,4,256]{2,1,0:T(4,128)S(1)} %copy-done.44, pred[8,4,256]{2,1,0:T(4,128)(4,1)S(1)} %bitcast.282), kind=kOutput, calls=%fused_computation.22 | convolution fusion | flops 3226468352 | bytes 18915328 | tf_op jit(solution)/shard_map/becr,ebcd->brd/dot_general | solution.py:699
  487.1 41.9 %collective-permute-done.13 = bf16[512,1536]{1,0:T(8,128)(2,1)S(1)} collective-permute-done((bf16[512,1536]{1,0:T(8,128)(2,1)}, bf16[512,1536]{1,0:T(8,128)(2,1)S(1)}, u32[]{:S(2)}, u32[]{:S(2)}) %collective-permute-start.13) | collective-permute-done | bytes 1572896 | tf_op jit(solution)/shard_map/ppermute | solution.py:575
  530.4 3.1 multiply_reduce_fusion
  533.5 3.3 subtract_add_fusion
  538.6 5.0 fusion.53
  544.8 5.8 slice_bitcast_fusion
  554.0 10.1 %fusion.4 = (f32[2,8,3,256]{3,2,1,0:T(4,128)S(1)}, f32[2,8,256,256,3]{3,2,4,1,0:T(8,128)}) fusion(f32[2,8,3,256]{3,2,1,0:T(4,128)S(1)} %log_add_fusion, f32[2,8,256,256,3]{3,2,4,1,0:T(8,128)} %copy-done.2, pred[2,256,256]{1,2,0:T(8,128)(4,1)S(1)} %copy-done.25, bf16[2,256,8,3,64]{1,0,4,3,2:T(2,128)(2,1)S(1)} %reshape.370, ...), kind=kOutput, calls=%fused_computation.18 | convolution fusion | flops 418369536 | bytes 27492352 | tf_op jit(solution)/shard_map/bqhgd,bkhd->bhgqk/dot_general | solution.py:122
  564.2 7.2 fusion.6
  574.9 3.2 fusion.77
  578.9 4.2 copy.175
  583.0 5.5 reshape.371
  588.6 2.5 subtract_convert_fusion
  593.7 4.5 convolution_convert_fusion.2
  598.2 22.5 %collective-permute-done.16 = bf16[512,1536]{1,0:T(8,128)(2,1)} collective-permute-done((bf16[512,1536]{1,0:T(8,128)(2,1)}, bf16[512,1536]{1,0:T(8,128)(2,1)}, u32[]{:S(2)}, u32[]{:S(2)}) %collective-permute-start.16) | collective-permute-done | bytes 1572896 | tf_op jit(solution)/shard_map/ppermute | solution.py:575
  620.8 10.2 %fusion.50 = (bf16[1536]{0:T(1024)(128)(2,1)S(1)}, f32[512]{0:T(512)S(1)}, f32[512,1536]{1,0:T(8,128)}) fusion(f32[512]{0:T(512)S(1)} %copy-done.65, bf16[512,1536]{1,0:T(8,128)(2,1)S(1)} %copy-done.12, pred[512]{0:T(512)(128)(4,1)S(1)} %copy-done.63, f32[1536]{0:T(1024)S(1)} %copy-done.57, bf16[512,2560]{0,1:T(8,128)(2,1)S(1)} %pad_maximum_fusion.1, ...), kind=kOutput, calls=%fused_computation.80 | convolution fusion | flops 4032821248 | bytes 15218176 | tf_op jit(solution)/shard_map/nc,dc->nd/dot_general | solution.py:766
  630.9 3.5 add_convert_fusion
  634.5 2.9 gather_fusion.4
  637.4 3.5 fusion.46
  641.0 2.9 gather_fusion.5
  644.2 4.0 broadcast_select_fusion.2
  648.2 6.9 convolution_convert_fusion.1
  655.2 5.4 fusion.2
  660.5 127.5 %closing.1 = (bf16[32,16,1536]{2,1,0:T(8,128)(2,1)}, bf16[32,16,1536]{2,1,0:T(8,128)(2,1)}, f32[48,4224]{1,0:T(8,128)}) custom-call(bf16[32,16,1536]{2,1,0:T(8,128)(2,1)} %bitcast.257, bf16[32,16,1536]{2,1,0:T(8,128)(2,1)} %bitcast.256, bf16[4,4,2,48,4224]{4,3,2,1,0:T(8,128)(2,1)} %bitcast.244), custom_call_target="tpu_custom_call" | custom-call | tf_op jit(solution)/shard_map/closing/pallas_call | solution.py:470
  791.7 2.9 gather_fusion.6
  794.6 2.9 gather_fusion.7
  799.1 3.4 broadcast_select_fusion
  802.5 2.5 convert_element_type.199
  804.9 3.4 reshape.386
  808.4 5.9 copy.213
  (288 shorter events, 89.4 us)
Async XLA Ops:
  7.2 28.1 %copy-start = (bf16[512,1536]{1,0:T(8,128)(2,1)S(1)}, bf16[512,1536]{1,0:T(8,128)(2,1)}, u32[]{:S(2)}) copy-start(bf16[512,1536]{1,0:T(8,128)(2,1)} %param.15) | copy-start | bytes 4718596
  7.2 285.0 %all-gather.6.cloned.1.call-start = ((), (), s32[]{:S(2)}) async-start(), calls=%async_computation.6 | async-start | bytes 7077888 | tf_op jit(solution)/shard_map/all_gather | solution.py:624
  7.9 22.0 %collective-permute-start = (s32[512,8]{0,1:T(8,128)}, s32[512,8]{0,1:T(8,128)S(1)}, u32[]{:S(2)}, u32[]{:S(2)}) collective-permute-start(s32[512,8]{0,1:T(8,128)} %param.18), channel_id=1, source_target_pairs={{0,2},{2,0},{4,6},{6,4},{1,3},{3,1},{5,7},{7,5},{8,10},{10,8},{12,... | collective-permute-start | bytes 49160 | tf_op jit(solution)/shard_map/ppermute | solution.py:575
  9.5 22.0 %collective-permute-start.2 = (s32[512,8]{0,1:T(8,128)}, s32[512,8]{0,1:T(8,128)S(1)}, u32[]{:S(2)}, u32[]{:S(2)}) collective-permute-start(s32[512,8]{0,1:T(8,128)} %param.18), channel_id=1, source_target_pairs={{0,6},{2,4},{4,2},{6,0},{1,7},{3,5},{5,3},{7,1},{8,14},{10,12},{12... | collective-permute-start | bytes 49160 | tf_op jit(solution)/shard_map/ppermute | solution.py:575
  10.0 21.5 %collective-permute-start.1 = (s32[512,8]{0,1:T(8,128)}, s32[512,8]{0,1:T(8,128)S(1)}, u32[]{:S(2)}, u32[]{:S(2)}) collective-permute-start(s32[512,8]{0,1:T(8,128)} %param.18), channel_id=1, source_target_pairs={{0,4},{2,6},{4,0},{6,2},{1,5},{3,7},{5,1},{7,3},{8,12},{10,14},{12... | collective-permute-start | bytes 49160 | tf_op jit(solution)/shard_map/ppermute | solution.py:575
  11.5 21.3 %collective-permute-start.3 = (f32[512,8]{0,1:T(8,128)}, f32[512,8]{0,1:T(8,128)S(1)}, u32[]{:S(2)}, u32[]{:S(2)}) collective-permute-start(f32[512,8]{0,1:T(8,128)} %param.19), channel_id=1, source_target_pairs={{0,2},{2,0},{4,6},{6,4},{1,3},{3,1},{5,7},{7,5},{8,10},{10,8},{12,... | collective-permute-start | bytes 49160 | tf_op jit(solution)/shard_map/ppermute | solution.py:575
  13.0 19.8 %collective-permute-start.5 = (f32[512,8]{0,1:T(8,128)}, f32[512,8]{0,1:T(8,128)S(1)}, u32[]{:S(2)}, u32[]{:S(2)}) collective-permute-start(f32[512,8]{0,1:T(8,128)} %param.19), channel_id=1, source_target_pairs={{0,6},{2,4},{4,2},{6,0},{1,7},{3,5},{5,3},{7,1},{8,14},{10,12},{12... | collective-permute-start | bytes 49160 | tf_op jit(solution)/shard_map/ppermute | solution.py:575
  15.7 236.8 %copy-start.62 = (pred[512]{0:T(512)(128)(4,1)}, pred[512]{0:T(512)(128)(4,1)S(1)}, u32[]{:S(2)}) copy-start(pred[512]{0:T(512)(128)(4,1)S(1)} %get-tuple-element.95) | copy-start | bytes 1540
  17.2 11.4 %all-to-all-start = ((s32[32,1,16]{2,1,0:T(1,128)}), s32[32,1,16]{2,1,0:T(1,128)S(1)}, u32[]{:S(2)}, u32[]{:S(2)}) async-start(s32[32,1,16]{2,1,0:T(1,128)} %bitcast.2), calls=%async_computation | async-start | bytes 32768 | tf_op jit(solution)/shard_map/all_to_all | solution.py:582
  23.3 327.9 %all-gather.4.cloned.1.call-start = ((), (), s32[]{:S(2)}) async-start(), calls=%async_computation.3 | async-start | bytes 14155776 | tf_op jit(solution)/shard_map/all_gather | solution.py:621
  29.9 11.3 %copy-start.58 = (s32[512]{0:T(512)}, s32[512]{0:T(512)S(1)}, u32[]{:S(2)}) copy-start(s32[512]{0:T(512)S(1)} %reshape.355) | copy-start | bytes 6148
  29.9 4.0 collective-permute-start.4
  44.6 148.8 %copy-start.36 = (bf16[1536,2,256]{2,1,0:T(2,128)(2,1)S(1)}, bf16[1536,2,256]{2,1,0:T(2,128)(2,1)}, u32[]{:S(2)}) copy-start(bf16[1536,2,256]{2,1,0:T(2,128)(2,1)} %param.24) | copy-start | bytes 4718596
  195.7 606.7 %reduce-scatter.5.cloned.1.call-start = ((), (), s32[]{:S(2)}) async-start(), calls=%async_computation.5 | async-start | bytes 7077888 | tf_op jit(solution)/shard_map/reduce_scatter | solution.py:687
  197.0 48.5 %copy-start.24 = (pred[2,256,256]{1,2,0:T(8,128)(4,1)}, pred[2,256,256]{1,2,0:T(8,128)(4,1)S(1)}, u32[]{:S(2)}) copy-start(pred[2,256,256]{1,2,0:T(8,128)(4,1)S(1)} %compare_and_fusion) | copy-start | bytes 393220
  197.9 34.5 %copy-start.33 = (f32[512,32]{0,1:T(8,128)}, f32[512,32]{0,1:T(8,128)S(1)}, u32[]{:S(2)}) copy-start(f32[512,32]{0,1:T(8,128)S(1)} %get-tuple-element.118) | copy-start | bytes 196612
  200.1 4.9 copy-start.13
  201.5 67.2 %collective-permute-start.8 = (bf16[512,1536]{1,0:T(8,128)(2,1)}, bf16[512,1536]{1,0:T(8,128)(2,1)}, u32[]{:S(2)}, u32[]{:S(2)}) collective-permute-start(bf16[512,1536]{1,0:T(8,128)(2,1)} %broadcast_select_fusion.4.rows_ref), channel_id=1, source_target_pairs={{0,6},{2,4},{4,2},{6,0},{1,7},{3,5},{5,3},{7,1},{8,14},{10,12},{12... | collective-permute-start | bytes 4718600 | tf_op jit(solution)/shard_map/ppermute | solution.py:575
  203.5 70.2 %collective-permute-start.7 = (bf16[512,1536]{1,0:T(8,128)(2,1)}, bf16[512,1536]{1,0:T(8,128)(2,1)}, u32[]{:S(2)}, u32[]{:S(2)}) collective-permute-start(bf16[512,1536]{1,0:T(8,128)(2,1)} %broadcast_select_fusion.4.rows_ref), channel_id=1, source_target_pairs={{0,4},{2,6},{4,0},{6,2},{1,5},{3,7},{5,1},{7,3},{8,12},{10,14},{12... | collective-permute-start | bytes 4718600 | tf_op jit(solution)/shard_map/ppermute | solution.py:575
  203.5 70.2 %collective-permute-start.6 = (bf16[512,1536]{1,0:T(8,128)(2,1)}, bf16[512,1536]{1,0:T(8,128)(2,1)}, u32[]{:S(2)}, u32[]{:S(2)}) collective-permute-start(bf16[512,1536]{1,0:T(8,128)(2,1)} %broadcast_select_fusion.4.rows_ref), channel_id=1, source_target_pairs={{0,2},{2,0},{4,6},{6,4},{1,3},{3,1},{5,7},{7,5},{8,10},{10,8},{12,... | collective-permute-start | bytes 4718600 | tf_op jit(solution)/shard_map/ppermute | solution.py:575
  207.1 45.4 %copy-start.11 = (bf16[512,1536]{1,0:T(8,128)(2,1)}, bf16[512,1536]{1,0:T(8,128)(2,1)S(1)}, u32[]{:S(2)}) copy-start(bf16[512,1536]{1,0:T(8,128)(2,1)S(1)} %gather_fusion.2) | copy-start | bytes 4718596
  208.8 7.4 copy-start.56
  208.8 49.5 %copy-start.48 = (f32[1536]{0:T(1024)}, f32[1536]{0:T(1024)S(1)}, u32[]{:S(2)}) copy-start(f32[1536]{0:T(1024)S(1)} %get-tuple-element.91) | copy-start | bytes 18436
  209.3 6.8 copy-start.64
  233.8 8.5 %copy-start.27 = (bf16[8,4,2,8,256]{4,3,1,0,2:T(8,128)(2,1)}, bf16[8,4,2,8,256]{4,3,1,0,2:T(8,128)(2,1)S(1)}, u32[]{:S(2)}) copy-start(bf16[8,4,2,8,256]{4,3,1,0,2:T(8,128)(2,1)S(1)} %copy.257) | copy-start | bytes 786436
  252.5 5.7 copy-start.37
  258.2 6.2 copy-start.54
  260.2 13.6 %copy-start.22 = (bf16[512,1536]{1,0:T(8,128)(2,1)}, bf16[512,1536]{1,0:T(8,128)(2,1)S(1)}, u32[]{:S(2)}) copy-start(bf16[512,1536]{1,0:T(8,128)(2,1)S(1)} %multiply_convert_fusion.1.rows_ref) | copy-start | bytes 4718596
  260.2 47.1 %collective-permute-start.11 = (bf16[512,1536]{1,0:T(8,128)(2,1)S(1)}, bf16[512,1536]{1,0:T(8,128)(2,1)S(1)}, u32[]{:S(2)}, u32[]{:S(2)}) collective-permute-start(bf16[512,1536]{1,0:T(8,128)(2,1)S(1)} %multiply_convert_fusion.1.rows_ref), channel_id=1, source_target_pairs={{0,6},{2,4},{4,2},{6,0},{1,7},{3,5},{5,3},{7,1},{8,14},{10,12},{12... | collective-permute-start | bytes 4718600 | tf_op jit(solution)/shard_map/ppermute | solution.py:575
  262.3 78.2 %collective-permute-start.10 = (bf16[512,1536]{1,0:T(8,128)(2,1)S(1)}, bf16[512,1536]{1,0:T(8,128)(2,1)}, u32[]{:S(2)}, u32[]{:S(2)}) collective-permute-start(bf16[512,1536]{1,0:T(8,128)(2,1)S(1)} %multiply_convert_fusion.1.rows_ref), channel_id=1, source_target_pairs={{0,4},{2,6},{4,0},{6,2},{1,5},{3,7},{5,1},{7,3},{8,12},{10,14},{12... | collective-permute-start | bytes 4718600 | tf_op jit(solution)/shard_map/ppermute | solution.py:575
  262.5 14.9 %copy-start.50 = (pred[8,256,4]{1,2,0:T(4,128)(4,1)}, pred[8,256,4]{1,2,0:T(4,128)(4,1)S(1)}, u32[]{:S(2)}) copy-start(pred[8,256,4]{1,2,0:T(4,128)(4,1)S(1)} %compare_reduce_fusion) | copy-start | bytes 24580
  262.7 14.7 %copy-start.43 = (s32[8,4,256]{2,1,0:T(4,128)}, s32[8,4,256]{2,1,0:T(4,128)S(1)}, u32[]{:S(2)}) copy-start(s32[8,4,256]{2,1,0:T(4,128)S(1)} %copy.156) | copy-start | bytes 98308
  268.6 71.8 %collective-permute-start.9 = (bf16[512,1536]{1,0:T(8,128)(2,1)S(1)}, bf16[512,1536]{1,0:T(8,128)(2,1)}, u32[]{:S(2)}, u32[]{:S(2)}) collective-permute-start(bf16[512,1536]{1,0:T(8,128)(2,1)S(1)} %multiply_convert_fusion.1.rows_ref), channel_id=1, source_target_pairs={{0,2},{2,0},{4,6},{6,4},{1,3},{3,1},{5,7},{7,5},{8,10},{10,8},{12,... | collective-permute-start | bytes 4718600 | tf_op jit(solution)/shard_map/ppermute | solution.py:575
  307.3 36.7 %copy-start.35 = (bf16[512,1536]{1,0:T(8,128)(2,1)}, bf16[512,1536]{1,0:T(8,128)(2,1)S(1)}, u32[]{:S(2)}) copy-start(bf16[512,1536]{1,0:T(8,128)(2,1)S(1)} %collective-permute-done.11.rows_ref) | copy-start | bytes 4718596
  401.9 403.0 %reduce-scatter.3.cloned.1.call-start = ((), (), s32[]{:S(2)}) async-start(), calls=%async_computation.4 | async-start | bytes 14155776 | tf_op jit(solution)/shard_map/reduce_scatter | solution.py:724
  427.4 20.7 %copy-start.44 = (s32[8,4,256]{2,1,0:T(4,128)S(1)}, s32[8,4,256]{2,1,0:T(4,128)}, u32[]{:S(2)}) copy-start(s32[8,4,256]{2,1,0:T(4,128)} %copy-done.43) | copy-start | bytes 98308
  427.4 20.7 %copy-start.51 = (pred[8,256,4]{1,2,0:T(4,128)(4,1)S(1)}, pred[8,256,4]{1,2,0:T(4,128)(4,1)}, u32[]{:S(2)}) copy-start(pred[8,256,4]{1,2,0:T(4,128)(4,1)} %copy-done.50) | copy-start | bytes 24580
  456.3 6.0 copy-start.23
  456.3 6.0 copy-start.53
  458.9 70.2 %collective-permute-start.13 = (bf16[512,1536]{1,0:T(8,128)(2,1)}, bf16[512,1536]{1,0:T(8,128)(2,1)S(1)}, u32[]{:S(2)}, u32[]{:S(2)}) collective-permute-start(bf16[512,1536]{1,0:T(8,128)(2,1)} %bitcast.63), channel_id=1, source_target_pairs={{0,4},{2,6},{4,0},{6,2},{1,5},{3,7},{5,1},{7,3},{8,12},{10,14},{12... | collective-permute-start | bytes 4718600 | tf_op jit(solution)/shard_map/ppermute | solution.py:575
  459.5 69.6 %collective-permute-start.14 = (bf16[512,1536]{1,0:T(8,128)(2,1)}, bf16[512,1536]{1,0:T(8,128)(2,1)S(1)}, u32[]{:S(2)}, u32[]{:S(2)}) collective-permute-start(bf16[512,1536]{1,0:T(8,128)(2,1)} %bitcast.64), channel_id=1, source_target_pairs={{0,6},{2,4},{4,2},{6,0},{1,7},{3,5},{5,3},{7,1},{8,14},{10,12},{12... | collective-permute-start | bytes 4718600 | tf_op jit(solution)/shard_map/ppermute | solution.py:575
  461.6 68.8 %collective-permute-start.12 = (bf16[512,1536]{1,0:T(8,128)(2,1)}, bf16[512,1536]{1,0:T(8,128)(2,1)}, u32[]{:S(2)}, u32[]{:S(2)}) collective-permute-start(bf16[512,1536]{1,0:T(8,128)(2,1)} %bitcast.62), channel_id=1, source_target_pairs={{0,2},{2,0},{4,6},{6,4},{1,3},{3,1},{5,7},{7,5},{8,10},{10,8},{12,... | collective-permute-start | bytes 4718600 | tf_op jit(solution)/shard_map/ppermute | solution.py:575
  475.1 55.3 %copy-start.9 = (f32[512,1536]{1,0:T(8,128)S(1)}, f32[512,1536]{1,0:T(8,128)}, u32[]{:S(2)}) copy-start(f32[512,1536]{1,0:T(8,128)} %copy-done.8) | copy-start | bytes 9437188
  475.1 55.3 %copy-start.49 = (f32[1536]{0:T(1024)S(1)}, f32[1536]{0:T(1024)}, u32[]{:S(2)}) copy-start(f32[1536]{0:T(1024)} %copy-done.48) | copy-start | bytes 18436
  475.2 55.3 %copy-start.55 = (f32[512]{0:T(512)S(1)}, f32[512]{0:T(512)}, u32[]{:S(2)}) copy-start(f32[512]{0:T(512)} %copy-done.54) | copy-start | bytes 6148
  544.7 9.3 %copy-start.25 = (pred[2,256,256]{1,2,0:T(8,128)(4,1)S(1)}, pred[2,256,256]{1,2,0:T(8,128)(4,1)}, u32[]{:S(2)}) copy-start(pred[2,256,256]{1,2,0:T(8,128)(4,1)} %copy-done.24) | copy-start | bytes 393220
  544.7 9.3 %copy-start.32 = (bf16[2,256,8,64]{1,0,3,2:T(2,128)(2,1)S(1)}, bf16[2,256,8,64]{1,0,3,2:T(2,128)(2,1)}, u32[]{:S(2)}) copy-start(bf16[2,256,8,64]{1,0,3,2:T(2,128)(2,1)} %convert_element_type.160) | copy-start | bytes 1572868
  544.8 19.4 %slice-start = ((s8[12582912]{0:T(1024)(128)(4,1)}), s8[4194304]{0:T(1024)(128)(4,1)S(1)}, s32[]{:S(2)}) async-start(s8[12582912]{0:T(1024)(128)(4,1)} %bitcast.236), calls=%async_computation.7 | async-start | bytes 8388608
  550.5 47.6 %collective-permute-start.17 = (bf16[512,1536]{1,0:T(8,128)(2,1)}, bf16[512,1536]{1,0:T(8,128)(2,1)}, u32[]{:S(2)}, u32[]{:S(2)}) collective-permute-start(bf16[512,1536]{1,0:T(8,128)(2,1)} %get-tuple-element.100), channel_id=1, source_target_pairs={{0,6},{2,4},{4,2},{6,0},{1,7},{3,5},{5,3},{7,1},{8,14},{10,12},{12... | collective-permute-start | bytes 4718600 | tf_op jit(solution)/shard_map/ppermute | solution.py:575
  552.0 68.7 %collective-permute-start.16 = (bf16[512,1536]{1,0:T(8,128)(2,1)}, bf16[512,1536]{1,0:T(8,128)(2,1)}, u32[]{:S(2)}, u32[]{:S(2)}) collective-permute-start(bf16[512,1536]{1,0:T(8,128)(2,1)} %get-tuple-element.101), channel_id=1, source_target_pairs={{0,4},{2,6},{4,0},{6,2},{1,5},{3,7},{5,1},{7,3},{8,12},{10,14},{12... | collective-permute-start | bytes 4718600 | tf_op jit(solution)/shard_map/ppermute | solution.py:575
  552.8 11.4 %slice-start.1 = ((s8[12582912]{0:T(1024)(128)(4,1)}), s8[4194304]{0:T(1024)(128)(4,1)S(1)}, s32[]{:S(2)}) async-start(s8[12582912]{0:T(1024)(128)(4,1)} %bitcast.236), calls=%async_computation.8 | async-start | bytes 8388608
  552.8 11.4 %slice-start.2 = ((s8[12582912]{0:T(1024)(128)(4,1)}), s8[4194304]{0:T(1024)(128)(4,1)S(1)}, s32[]{:S(2)}) async-start(s8[12582912]{0:T(1024)(128)(4,1)} %bitcast.236), calls=%async_computation.9 | async-start | bytes 8388608
  552.8 67.9 %collective-permute-start.15 = (bf16[512,1536]{1,0:T(8,128)(2,1)}, bf16[512,1536]{1,0:T(8,128)(2,1)}, u32[]{:S(2)}, u32[]{:S(2)}) collective-permute-start(bf16[512,1536]{1,0:T(8,128)(2,1)} %get-tuple-element.102), channel_id=1, source_target_pairs={{0,2},{2,0},{4,6},{6,4},{1,3},{3,1},{5,7},{7,5},{8,10},{10,8},{12,... | collective-permute-start | bytes 4718600 | tf_op jit(solution)/shard_map/ppermute | solution.py:575
  564.2 7.2 copy-start.18
  593.7 27.1 %copy-start.26 = (bf16[512,2560]{0,1:T(8,128)(2,1)}, bf16[512,2560]{0,1:T(8,128)(2,1)S(1)}, u32[]{:S(2)}) copy-start(bf16[512,2560]{0,1:T(8,128)(2,1)S(1)} %pad_maximum_fusion.1) | copy-start | bytes 7864324
  593.7 27.1 %copy-start.12 = (bf16[512,1536]{1,0:T(8,128)(2,1)S(1)}, bf16[512,1536]{1,0:T(8,128)(2,1)}, u32[]{:S(2)}) copy-start(bf16[512,1536]{1,0:T(8,128)(2,1)} %copy-done.11) | copy-start | bytes 4718596
  593.7 27.1 %copy-start.57 = (f32[1536]{0:T(1024)S(1)}, f32[1536]{0:T(1024)}, u32[]{:S(2)}) copy-start(f32[1536]{0:T(1024)} %copy-done.56) | copy-start | bytes 18436
  593.7 27.1 %copy-start.65 = (f32[512]{0:T(512)S(1)}, f32[512]{0:T(512)}, u32[]{:S(2)}) copy-start(f32[512]{0:T(512)} %copy-done.64) | copy-start | bytes 6148
  620.7 10.2 %copy-start.10 = (f32[512,1536]{1,0:T(8,128)S(1)}, f32[512,1536]{1,0:T(8,128)}, u32[]{:S(2)}) copy-start(f32[512,1536]{1,0:T(8,128)} %copy-done.8) | copy-start | bytes 9437188
  620.8 10.2 %copy-start.19 = (bf16[512,1536]{1,0:T(8,128)(2,1)S(1)}, bf16[512,1536]{1,0:T(8,128)(2,1)}, u32[]{:S(2)}) copy-start(bf16[512,1536]{1,0:T(8,128)(2,1)} %get-tuple-element.75) | copy-start | bytes 4718596
  644.2 10.9 %slice-start.3 = ((s8[4718592]{0:T(1024)(128)(4,1)}), s8[4194304]{0:T(1024)(128)(4,1)S(1)}, s32[]{:S(2)}) async-start(s8[4718592]{0:T(1024)(128)(4,1)} %bitcast.258), calls=%async_computation.10 | async-start | bytes 8388608
  648.2 6.9 slice-start.4
  660.5 131.1 %copy-start.61 = (s32[1024]{0:T(1024)S(1)}, s32[1024]{0:T(1024)}, u32[]{:S(2)}) copy-start(s32[1024]{0:T(1024)} %get-tuple-element.136) | copy-start | bytes 12292
  808.4 5.9 copy-start.1
  (33 other events, 94.5 us)
Sparse Core Ops, SparseCore 0:
  9.6 89.9 all-gather.5
  195.9 112.7 all-gather.3
  402.0 65.7 reduce-scatter.4
  470.0 127.5 reduce-scatter.2

commit v5 on v4

--- a/solution.py
+++ b/solution.py
@@ -139,6 +139,22 @@
         grad_keys.reshape(-1, KV_HEADS, HEAD),
         grad_values.reshape(-1, KV_HEADS, HEAD),
     )
+
+
+def pick(rows, index):
+    return jnp.take(rows, index, axis=0, mode="clip")
+
+
+def hold(value, *after):
+    anywhere = pl.BlockSpec(memory_space=pl.ANY)
+    return pl.pallas_call(
+        lambda *refs: None,
+        out_shape=jax.ShapeDtypeStruct(value.shape, value.dtype),
+        in_specs=[anywhere] * (1 + len(after)),
+        out_specs=anywhere,
+        input_output_aliases={0: 0},
+        name="hold",
+    )(value, *after)
 
 
 def norm_back(values, scale, gain, grad_normed):
@@ -508,18 +524,17 @@
         refs[-1][:, 0, :, at] = slots.astype(jnp.bfloat16)
 
 
-def dispatch(choose, rows, step, slots, weight):
+def dispatch(choose, rows, first, stride, slots, weight):
     _, count, capacity, _ = choose.shape
     width = rows.shape[1]
-    first = step * MB
     operands = [choose, rows]
     in_specs = [
-        pl.BlockSpec((1, count, capacity, TOK_MB), lambda b: (first + b, 0, 0, 0)),
+        pl.BlockSpec((1, count, capacity, TOK_MB), lambda b: (first + b * stride, 0, 0, 0)),
         pl.BlockSpec((TOK_MB, width), lambda b: (b, 0)),
     ]
     if weight is not None:
         operands.append(weight)
-        in_specs.append(pl.BlockSpec((count, 1, capacity, 1), lambda b: (0, first + b, 0, 0)))
+        in_specs.append(pl.BlockSpec((count, 1, capacity, 1), lambda b: (0, first + b * stride, 0, 0)))
     aliases = {}
     if slots is not None:
         aliases = {len(operands): 0}
@@ -527,10 +542,10 @@
         in_specs.append(pl.BlockSpec(memory_space=pl.ANY))
     return pl.pallas_call(
         functools.partial(dispatch_kernel, weight is not None),
-        grid=(MB,),
+        grid=(rows.shape[0] // TOK_MB,),
         out_shape=jax.ShapeDtypeStruct((count, choose.shape[0], capacity, width), jnp.bfloat16),
         in_specs=in_specs,
-        out_specs=pl.BlockSpec((count, 1, capacity, width), lambda b: (0, first + b, 0, 0)),
+        out_specs=pl.BlockSpec((count, 1, capacity, width), lambda b: (0, first + b * stride, 0, 0)),
         input_output_aliases=aliases,
         name="dispatch",
     )(*operands)
@@ -575,10 +590,21 @@
         return lax.ppermute(block, "lo", [(i, i ^ step) for i in range(lo_count)])
 
     def spread(block):
-        return [block] + [swap(block, step) for step in range(1, lo_count)]
-
-    ids_all = jnp.stack(spread(expert_ids))
-    gates_all = jnp.stack(spread(gate_weights))
+        if lo_count != 4:
+            return [[block]] + [[swap(block, step)] for step in range(1, lo_count)]
+        half = block.shape[0] // 2
+        one, two = swap(block, 1), swap(block, 2)
+        return [[block], [one], [two], [swap(one[:half], 2), swap(two[half:], 1)]]
+
+    if lo_count == 4:
+        order = [(0, 0), (0, 1), (1, 0), (3, 0), (2, 1), (3, 1), (1, 1), (2, 0)]
+    else:
+        order = [(step, batch) for step in range(lo_count) for batch in range(MB)]
+    routing = jnp.concatenate([expert_ids.astype(jnp.float32), gate_weights], axis=1)
+    routing_all = [routing] + [swap(routing, step) for step in range(1, lo_count)]
+    routing_all = jnp.stack(
+        [routing_all[step][batch * TOK_MB : (batch + 1) * TOK_MB] for step, batch in order]
+    )
     asked_rows = lax.all_to_all(
         wanted.reshape(device_count, peer_rows),
         ALL,
@@ -586,7 +612,7 @@
         concat_axis=0,
         tiled=True,
     ).reshape(tok_dev)
-    asked_rows, ids_all, gates_all = lax.optimization_barrier((asked_rows, ids_all, gates_all))
+    asked_rows, routing_all = lax.optimization_barrier((asked_rows, routing_all))
     asked_match = asked_rows[:, None] == positions[None, :]
     by_asked = jnp.sum(jnp.where(asked_match, positions[:, None], 0), axis=0, dtype=jnp.int32)
     sizes = (hi_count, lo_count, 2)
@@ -602,16 +628,17 @@
         ],
         axis=1,
     )
-    asked_tokens = jnp.take(tokens, asked_rows, axis=0).reshape(device_count, peer_rows, model_width)
-    asked_grads = jnp.take(cotangent, asked_rows, axis=0).reshape(
+    asked_tokens = pick(tokens, asked_rows).reshape(device_count, peer_rows, model_width)
+    asked_grads = pick(cotangent, asked_rows).reshape(
         device_count, peer_rows, model_width
     )
     got_rows, got_grad, packed = opening(sizes, asked_tokens, asked_grads, weight_shard)
     got_rows, packed, expert_in = lax.optimization_barrier((got_rows, packed, expert_in))
     packed = packed.reshape(model_width, -1)
-    grad_bf = jnp.take(got_grad.reshape(tok_dev, model_width), arrival, axis=0)
+    grad_bf = pick(got_grad.reshape(tok_dev, model_width), arrival)
+    got_rows = hold(got_rows, grad_bf)
     grad_blocks = spread(grad_bf)
-    rows_in = jnp.take(got_rows.reshape(tok_dev, model_width), arrival, axis=0).astype(jnp.float32)
+    rows_in = pick(got_rows.reshape(tok_dev, model_width), arrival).astype(jnp.float32)
     qkv_full = packed[:, :qkv_cols]
     out_full = packed[:, qkv_cols : qkv_cols + model_width]
     gain_pair = packed[:, qkv_cols + model_width :].astype(jnp.float32)
@@ -642,6 +669,8 @@
     )
     mixed_part, logsum = attend_block(queries, key_rows, value_rows, segment, position)
     mixed_rows = mixed_part.astype(jnp.bfloat16)
+    if lo_count == 4:
+        mixed_rows = hold(mixed_rows, grad_blocks[1][0], grad_blocks[2][0])
     attended = jnp.dot(mixed_rows, out_full, preferred_element_type=jnp.float32)
     residual = rows_in + attended
     scale_two = lax.rsqrt(jnp.mean(residual * residual, axis=1, keepdims=True) + epsilon)
@@ -649,26 +678,36 @@
     grad_output = grad_bf.astype(jnp.float32)
     home = lax.axis_index("lo")
     row_blocks = spread(normed_two)
-    normed_two, *grad_blocks = lax.optimization_barrier((normed_two, *grad_blocks))
+    normed_two, grad_blocks = lax.optimization_barrier((normed_two, grad_blocks))
     choose, slot_gate = slot_tables(
-        ids_all.reshape(-1, TOK_MB, TOPK),
-        gates_all.reshape(-1, TOK_MB, TOPK),
+        routing_all[..., :TOPK].astype(jnp.int32),
+        routing_all[..., TOPK:],
         home + lo_count * jnp.arange(hi_count, dtype=jnp.int32),
         capacity,
     )
     slot_weight = jnp.transpose(slot_gate, (1, 0, 2))[..., None]
-    grad_expert = None
-    for step in range(lo_count):
-        grad_expert = dispatch(choose, grad_blocks[step], step, grad_expert, slot_weight)
+    place_of = {name: number for number, name in enumerate(order)}
+
+    def fill(blocks, slots, weight):
+        for step, pieces in blocks:
+            batch = 0
+            for piece in pieces:
+                first = place_of[step, batch]
+                stride = place_of[step, MB - 1] - place_of[step, 0]
+                slots = dispatch(choose, piece, first, stride, slots, weight)
+                batch += piece.shape[0] // TOK_MB
+        return slots
+
+    grad_expert = fill(list(enumerate(grad_blocks)), None, slot_weight)
     grad_expert = grad_expert.reshape(hi_count, -1, model_width)
     grad_hidden = jnp.einsum(
         "erd,ekfd->ekrf", grad_expert, weights_out, preferred_element_type=jnp.float32
     ).astype(jnp.bfloat16)
-    grad_hidden, *others = lax.optimization_barrier((grad_hidden, *row_blocks[1:]))
-    row_blocks = [normed_two] + others
-    expert_rows = None
-    for step in range(lo_count):
-        expert_rows = dispatch(choose, row_blocks[step], step, expert_rows, None)
+    expert_rows = fill([(0, [normed_two])], None, None)
+    grad_hidden, expert_rows, others = lax.optimization_barrier(
+        (grad_hidden, expert_rows, row_blocks[1:])
+    )
+    expert_rows = fill(list(enumerate(others, 1)), expert_rows, None)
     expert_rows = expert_rows.reshape(hi_count, -1, model_width)
     gate_up = jnp.einsum(
         "erd,ekdf->ekrf", expert_rows, weights_in, preferred_element_type=jnp.float32
@@ -695,28 +734,44 @@
     ).astype(jnp.bfloat16)
 
     def split_back(slot_values):
-        return (
-            jnp.einsum(
-                "becr,ebcd->brd",
-                choose,
-                slot_values.reshape(hi_count, lo_count * MB, capacity, model_width),
-                preferred_element_type=jnp.float32,
-            )
-            .astype(jnp.bfloat16)
-            .reshape(lo_count, tok_dev, model_width)
+        return jnp.einsum(
+            "becr,ebcd->brd",
+            choose,
+            slot_values.reshape(hi_count, lo_count * MB, capacity, model_width),
+            preferred_element_type=jnp.float32,
+        ).astype(jnp.bfloat16)
+
+    def wide(value):
+        return value.astype(jnp.float32)
+
+    def bring_back(parts):
+        if lo_count != 4:
+            parts = parts.reshape(lo_count, tok_dev, model_width)
+            return [parts[0]] + [swap(parts[step], step) for step in range(1, lo_count)]
+        one = swap(parts[2:4], 1)
+        two = swap(parts[4:6], 2)
+        for_one = (wide(parts[6]) + wide(two[1])).astype(jnp.bfloat16)
+        for_two = (wide(parts[7]) + wide(one[1])).astype(jnp.bfloat16)
+        return [parts[:2], one, two, swap(for_two, 2), swap(for_one, 1)]
+
+    def total_of(terms):
+        if lo_count != 4:
+            total = wide(terms[0])
+            for term in terms[1:]:
+                total = total + wide(term)
+            return total
+        own, one, two, last_two, last_one = terms
+        return jnp.concatenate(
+            [
+                wide(own[0]) + wide(one[0]) + wide(last_two),
+                wide(own[1]) + wide(two[0]) + wide(last_one),
+            ],
+            axis=0,
         )
 
-    def total_of(parts):
-        total = parts[0].astype(jnp.float32)
-        for part in parts[1:]:
-            total = total + part.astype(jnp.float32)
-        return total
-
     back = split_back(grad_expert_rows)
-    back_parts = [back[0]] + [swap(back[step], step) for step in range(1, lo_count)]
-    back, hidden, expert_rows, grad_gate_up = lax.optimization_barrier(
-        (back, hidden, expert_rows, grad_gate_up)
-    )
+    back_parts = bring_back(back)
+    grad_gate_up = hold(grad_gate_up, *back_parts[1:3])
     grad_weights_in = jnp.einsum(
         "ekrf,erd->ekfd", grad_gate_up, expert_rows, preferred_element_type=jnp.float32
     ).astype(jnp.bfloat16)
@@ -733,8 +788,8 @@
         * slot_weight.reshape(hi_count, -1, 1)
     ).astype(jnp.bfloat16)
     ahead = split_back(produced)
-    ahead, *back_parts = lax.optimization_barrier((ahead, *back_parts))
-    ahead_parts = [ahead[0]] + [swap(ahead[step], step) for step in range(1, lo_count)]
+    ahead, back_parts = lax.optimization_barrier((ahead, back_parts))
+    ahead_parts = bring_back(ahead)
     grad_normed_two = total_of(back_parts)
     grad_gain_two, grad_from_norm = norm_back(residual, scale_two, gain_two, grad_normed_two)
     grad_residual = grad_output + grad_from_norm
@@ -758,8 +813,8 @@
         ],
         axis=1,
     ).astype(jnp.bfloat16)
-    grad_projected, *ahead_parts = lax.optimization_barrier((grad_projected, *ahead_parts))
-    output_rows = (residual + total_of(ahead_parts)).astype(jnp.bfloat16)
+    if lo_count == 4:
+        normed = hold(normed, *ahead_parts[1:3])
     grad_qkv_weight = jnp.einsum(
         "nd,nc->dc", normed, grad_projected, preferred_element_type=jnp.float32
     )
@@ -777,18 +832,22 @@
         ],
         axis=1,
     ).reshape(sizes + (shard_rows, -1))
+    parts, shard_in, shard_out, ahead_parts = lax.optimization_barrier(
+        (parts, shard_in, shard_out, ahead_parts)
+    )
+    output_rows = (residual + total_of(ahead_parts)).astype(jnp.bfloat16)
     home_out, home_grad, sums = closing(
         sizes,
-        jnp.take(output_rows, by_arrival, axis=0).reshape(device_count, peer_rows, model_width),
-        jnp.take(grad_input, by_arrival, axis=0).reshape(device_count, peer_rows, model_width),
+        pick(output_rows, by_arrival).reshape(device_count, peer_rows, model_width),
+        pick(grad_input, by_arrival).reshape(device_count, peer_rows, model_width),
         parts,
     )
     shard_qkv = sums[:, :qkv_cols]
     shard_attn_out = sums[:, qkv_cols : qkv_cols + model_width]
     shard_gain_one = sums[:, qkv_cols + model_width]
     shard_gain_two = sums[:, qkv_cols + model_width + 1]
-    output = jnp.take(home_out.reshape(tok_dev, model_width), by_asked, axis=0)
-    input_grad = jnp.take(home_grad.reshape(tok_dev, model_width), by_asked, axis=0)
+    output = pick(home_out.reshape(tok_dev, model_width), by_asked)
+    input_grad = pick(home_grad.reshape(tok_dev, model_width), by_asked)
     return (
         output,
         input_grad,

time: 826 us -> 821 us (level)
  waiting for transfers between devices: 108 us -> 75.1 us
  local copies, waits for them, and re-layouts: 93.7 us -> 117 us
  other arithmetic: 88 us -> 76.6 us
  Pallas kernels: 305 us -> 315 us
    ppermute x18 -> x19, waiting for transfers between devices: 105 us -> 73.9 us  [swap(): return lax.ppermute(block, 'lo', [(i, i ^ step) for i in range(lo_count)])]
    select_n x8 -> x0, other arithmetic: 12.2 us -> none  [the longest x1 4.04 us: shards(): jnp.take(grad_input, by_arrival, axis=0)]
    slice x2 -> x7, local copies, waits for them, and re-layouts: 2.74 us -> 12.3 us  [the longest x4 6.4 us: spread(): return [[block], [one], [two], [swap(one[:half], 2), swap(two[half:], 1)]]]
    unnamed x153 -> x160, local copies, waits for them, and re-layouts: 10.8 us -> 18.6 us
    pallas_call x8 -> x10, Pallas kernels: 29.1 us -> 33.9 us  [dispatch(): pl.pallas_call(functools.partial(dispatch_kernel, weight is not None), gr...]
    another operation x9 -> x7, other arithmetic: 22.6 us -> 18.1 us
    ppermute x18 -> x19, starting transfers between devices: 21.1 us -> 25.6 us  [swap(): return lax.ppermute(block, 'lo', [(i, i ^ step) for i in range(lo_count)])]
  transfers between devices with their start and end apart: 23 -> 24, of which waited for: 8 -> 6; matrix products, arithmetic and copies ran while one was open for 36% -> 36% of each run, Pallas kernels for 37% -> 23%
where the time goes in v5:
time: 821 us; the launch traced here: 816 us
  Pallas kernels  315 us (38%)
  matrix products  185 us (23%)
  local copies, waits for them, and re-layouts  117 us (14%)
  other arithmetic  76.6 us (9%)
  waiting for transfers between devices  75.1 us (9%)
  starting transfers between devices  32.2 us (4%)
  between operations  15.2 us (2%)
    pallas_call x1, Pallas kernels, opening(): pl.pallas_call(functools.partial(opening_kernel, sizes), out_shape=(jax.S...  153 us
    pallas_call x1, Pallas kernels, closing(): pl.pallas_call(functools.partial(closing_kernel, sizes), out_shape=(jax.S...  128 us
    ppermute x19, waiting for transfers between devices, swap(): return lax.ppermute(block, 'lo', [(i, i ^ step) for i in range(lo_count)])  73.9 us
    pallas_call x10, Pallas kernels, dispatch(): pl.pallas_call(functools.partial(dispatch_kernel, weight is not None), gr...  33.9 us
    gather x8, local copies, waits for them, and re-layouts, pick(): return jnp.take(rows, index, axis=0, mode='clip')  25.6 us
    ppermute x19, starting transfers between devices, swap(): return lax.ppermute(block, 'lo', [(i, i ^ step) for i in range(lo_count)])  25.6 us
    dot_general x1, matrix products, shards(): jnp.einsum('ekrf,erd->ekfd', grad_gate_up, expert_rows, preferred_element...  22.1 us
    dot_general x1, matrix products, shards(): jnp.einsum('ekrf,ekdf->erd', grad_gate_up, weights_in, preferred_element_...  20.4 us
  transfers between devices with their start and end apart: 24, of which 6 were waited for; matrix products, arithmetic and copies ran while one was open for 36% of the time, Pallas kernels for 23%

profile of v5, /device:TPU:12, one launch (start us, length us, event | category | flops | bytes accessed | tf_op | source)
XLA Modules:
  0.0 816.2 jit_solution(17323688645495191597)
XLA Ops:
  16.6 6.0 all-to-all-start
  30.0 2.9 gather_fusion.1
  32.9 2.9 gather_fusion
  35.9 153.5 %opening.1 = (bf16[32,16,1536]{2,1,0:T(8,128)(2,1)}, bf16[32,16,1536]{2,1,0:T(8,128)(2,1)}, bf16[4,4,2,48,4224]{4,3,2,1,0:T(8,128)(2,1)}) custom-call(bf16[32,16,1536]{2,1,0:T(8,128)(2,1)} %bitcast.273, bf16[32,16,1536]{2,1,0:T(8,128)(2,1)} %bitcast.272, bf16[48,4224]{1,0:T(8,128)(2,1)} %concatenate.50.shard_ref), custom_call_target="tpu_custom_call" | custom-call | tf_op jit(solution)/shard_map/opening/pallas_call | solution.py:332
  189.4 2.3 all_gather_reshape.3
  196.0 4.3 collective-permute-start.4
  204.8 5.7 gather_fusion.3
  212.3 7.2 fusion.19
  227.2 3.5 copy.162
  230.8 3.6 add_convert_fusion.5
  234.4 2.9 concatenate.55
  237.3 2.6 copy.159
  242.1 3.1 concatenate.54
  249.9 3.1 fusion.10
  254.3 3.4 fusion.61
  260.9 2.6 copy.168.refs_0_
  263.5 5.4 multiply_reduce_fusion.2
  283.2 2.3 fusion.33.choose_ref
  285.5 38.5 %collective-permute-done.6.rows_ref = bf16[256,1536]{1,0:T(8,128)(2,1)} collective-permute-done((bf16[256,1536]{1,0:T(8,128)(2,1)}, bf16[256,1536]{1,0:T(8,128)(2,1)}, u32[]{:S(2)}, u32[]{:S(2)}) %collective-permute-start.6) | collective-permute-done | bytes 786464 | tf_op jit(solution)/shard_map/ppermute | solution.py:590
  324.0 3.5 dispatch.15.refs_0_
  327.6 3.7 dispatch.10.refs_1_
  331.2 3.7 dispatch.11.refs_1_
  334.9 3.6 dispatch.12.refs_1_
  338.6 3.0 dispatch.13.refs_1_
  341.6 3.0 dispatch.14
  348.8 13.7 %convert_bitcast_fusion = bf16[4,2,1024,256]{3,2,1,0:T(8,128)(2,1)} fusion(bf16[4,1024,1536,1]{2,1,3,0:T(8,128)(2,1)} %bitcast.257, bf16[4,2,256,1536]{3,2,1,0:T(8,128)(2,1)} %bitcast.314), kind=kOutput, calls=%fused_computation.59 | convolution fusion | flops 6444548096 | bytes 23068672 | tf_op jit(solution)/shard_map/erd,ekfd->ekrf/dot_general | solution.py:703
  365.5 3.8 dispatch.16.refs_0_
  369.3 3.6 dispatch.17.refs_0_
  372.9 3.0 dispatch.18.refs_0_
  375.8 3.0 dispatch.19
  378.8 18.3 %convolution_bitcast_fusion = f32[4,2,1024,512]{3,2,1,0:T(8,128)S(1)} fusion(bf16[4,1024,1536,1]{2,1,3,0:T(8,128)(2,1)} %bitcast.255, bf16[4,2,1536,512]{3,2,1,0:T(8,128)(2,1)} %bitcast.312), kind=kOutput, calls=%fused_computation.35 | convolution fusion | flops 12884901888 | bytes 41943040 | tf_op jit(solution)/shard_map/erd,ekdf->ekrf/dot_general | solution.py:712
  397.2 11.1 %fusion.14 = (bf16[4,2,1024,256]{3,2,1,0:T(8,128)(2,1)}, bf16[4,2,1024,256]{3,2,1,0:T(8,128)(2,1)}, bf16[4,2,1024,256]{3,2,1,0:T(8,128)(2,1)}) fusion(bf16[4,2,1024,256]{3,2,1,0:T(8,128)(2,1)} %convert_bitcast_fusion, f32[4,2,1024,512]{3,2,1,0:T(8,128)S(1)} %convolution_bitcast_fusion), kind=kLoop, calls=%fused_computation.38 | loop fusion | flops 33554432 | bytes 33554432 | tf_op jit(solution)/shard_map/convert.19
  408.3 13.8 %convolution_convert_fusion.3 = bf16[4,2,256,1536]{3,2,1,0:T(8,128)(2,1)} fusion(bf16[4,2,1024,256]{3,2,1,0:T(8,128)(2,1)} %get-tuple-element.70, bf16[4,1024,1536,1]{2,1,3,0:T(8,128)(2,1)} %bitcast.258), kind=kOutput, calls=%fused_computation.57 | convolution fusion | flops 6445596672 | bytes 23068672 | tf_op jit(solution)/shard_map/ekrf,erd->ekfd/dot_general | solution.py:722
  422.1 7.4 pad_maximum_fusion.refs_0_
  429.6 20.4 %bitcast_convert_fusion = bf16[4,1024,1536]{2,1,0:T(8,128)(2,1)} fusion(bf16[4,2,1024,512]{3,2,1,0:T(8,128)(2,1)} %pad_maximum_fusion.refs_0_, bf16[4,2,1536,512]{3,2,1,0:T(8,128)(2,1)} %bitcast.313), kind=kOutput, calls=%fused_computation.12 | convolution fusion | flops 12891193344 | bytes 33554432 | tf_op jit(solution)/shard_map/ekrf,ekdf->erd/dot_general | solution.py:732
  450.0 8.2 %bitcast_convert_fusion.2 = bf16[8,256,1536]{2,1,0:T(8,128)(2,1)S(1)} fusion(bf16[4,8,128,1536]{3,2,1,0:T(8,128)(2,1)} %bitcast.317, s32[8,4,256]{2,1,0:T(4,128)S(1)} %copy-done.48, pred[8,4,256]{2,1,0:T(4,128)(4,1)S(1)} %bitcast.298), kind=kOutput, calls=%fused_computation.21 | convolution fusion | flops 3226468352 | bytes 18915328 | tf_op jit(solution)/shard_map/becr,ebcd->brd/dot_general | solution.py:737
  458.5 2.3 copy-done.19
  463.8 31.3 %collective-permute-done.12.refs_2_ = bf16[2,256,1536]{2,1,0:T(8,128)(2,1)S(1)} collective-permute-done((bf16[2,256,1536]{2,1,0:T(8,128)(2,1)S(1)}, bf16[2,256,1536]{2,1,0:T(8,128)(2,1)S(1)}, u32[]{:S(2)}, u32[]{:S(2)}) %collective-permute-start.12) | collective-permute-done | bytes 1572896 | tf_op jit(solution)/shard_map/ppermute | solution.py:590
  496.2 22.1 %convolution_convert_fusion = bf16[4,2,512,1536]{3,2,1,0:T(8,128)(2,1)} fusion(bf16[4,2,1024,512]{3,2,1,0:T(8,128)(2,1)} %hold.6, bf16[4,1024,1536,1]{2,1,3,0:T(8,128)(2,1)} %bitcast.256), kind=kOutput, calls=%fused_computation.13 | convolution fusion | flops 12891193344 | bytes 33554432 | tf_op jit(solution)/shard_map/ekrf,erd->ekfd/dot_general | solution.py:775
  524.6 12.7 %fusion.1 = bf16[4,1024,1536]{2,1,0:T(8,128)(2,1)} fusion(bf16[4,2,1024,256]{3,2,1,0:T(8,128)(2,1)S(1)} %copy-done.26, bf16[4,2,256,1536]{3,2,1,0:T(8,128)(2,1)} %bitcast.315, f32[4,1024]{1,0:T(4,128)S(1)} %bitcast.302), kind=kOutput, calls=%fused_computation.11 | convolution fusion | flops 6455033856 | bytes 23085056 | tf_op jit(solution)/shard_map/ekrf,ekfd->erd/dot_general | solution.py:787
  537.3 10.8 %bitcast_convert_fusion.1 = bf16[8,256,1536]{2,1,0:T(8,128)(2,1)} fusion(bf16[4,8,128,1536]{3,2,1,0:T(8,128)(2,1)} %bitcast.316, s32[8,4,256]{2,1,0:T(4,128)S(1)} %copy-done.48, pred[8,4,256]{2,1,0:T(4,128)(4,1)S(1)} %bitcast.299), kind=kOutput, calls=%fused_computation.20 | convolution fusion | flops 3226468352 | bytes 18915328 | tf_op jit(solution)/shard_map/becr,ebcd->brd/dot_general | solution.py:737
  554.6 5.0 fusion.53
  560.8 6.4 fusion.77
  568.6 5.3 fusion.113
  575.8 7.2 fusion.3
  583.0 6.9 fusion.5
  592.7 4.1 copy.190
  596.7 5.8 reshape.381
  602.5 5.0 fusion.71
  611.3 9.8 %fusion.49 = (f32[512]{0:T(512)S(1)}, bf16[1536]{0:T(1024)(128)(2,1)S(1)}, f32[512,1536]{1,0:T(8,128)}) fusion(bf16[512,1536]{1,0:T(8,128)(2,1)S(1)} %copy-done.12, f32[1536]{0:T(1024)S(1)} %copy-done.56, f32[512]{0:T(512)S(1)} %copy-done.66, bf16[1536,4224]{1,0:T(8,128)(2,1)} %bitcast.308, bf16[512,512]{0,1:T(8,128)(2,1)S(1)} %bitcast.292, ...), kind=kOutput, calls=%fused_computation.79 | convolution fusion | flops 4039899136 | bytes 15217664 | tf_op jit(solution)/shard_map/nc,dc->nd/dot_general | solution.py:821
  621.4 3.9 fusion.45
  625.3 3.2 gather_fusion.5
  628.5 6.4 convolution_convert_fusion.2
  634.9 3.2 fusion.85
  640.7 6.1 convolution_convert_fusion.1
  646.9 5.4 fusion.2
  652.2 2.5 convert_element_type.285
  654.7 3.5 reshape.396
  658.2 5.9 copy.227
  664.1 2.6 bitcast_add_fusion.1
  667.6 2.9 gather_fusion.4
  670.6 127.9 %closing.1 = (bf16[32,16,1536]{2,1,0:T(8,128)(2,1)}, bf16[32,16,1536]{2,1,0:T(8,128)(2,1)}, f32[48,4224]{1,0:T(8,128)}) custom-call(bf16[32,16,1536]{2,1,0:T(8,128)(2,1)} %bitcast.275, bf16[32,16,1536]{2,1,0:T(8,128)(2,1)} %bitcast.274, bf16[4,4,2,48,4224]{4,3,2,1,0:T(8,128)(2,1)} %bitcast.265), custom_call_target="tpu_custom_call" | custom-call | tf_op jit(solution)/shard_map/closing/pallas_call | solution.py:486
  803.6 2.9 gather_fusion.6
  806.5 2.9 gather_fusion.7
  (306 shorter events, 104.5 us)
Async XLA Ops:
  7.2 22.8 %copy-start = (bf16[512,1536]{1,0:T(8,128)(2,1)S(1)}, bf16[512,1536]{1,0:T(8,128)(2,1)}, u32[]{:S(2)}) copy-start(bf16[512,1536]{1,0:T(8,128)(2,1)} %param.13) | copy-start | bytes 4718596
  7.2 341.6 %all-gather.6.cloned.1.call-start = ((), (), s32[]{:S(2)}) async-start(), calls=%async_computation.6 | async-start | bytes 7077888 | tf_op jit(solution)/shard_map/all_gather | solution.py:651
  9.4 19.9 %collective-permute-start = (f32[512,16]{0,1:T(8,128)S(1)}, f32[512,16]{0,1:T(8,128)S(1)}, u32[]{:S(2)}, u32[]{:S(2)}) collective-permute-start(f32[512,16]{0,1:T(8,128)S(1)} %pad_maximum_fusion.7), channel_id=1, source_target_pairs={{0,2},{2,0},{4,6},{6,4},{1,3},{3,1},{5,7},{7,5},{8,10},{10,8},{12,... | collective-permute-start | bytes 98312 | tf_op jit(solution)/shard_map/ppermute | solution.py:590
  10.9 18.4 %collective-permute-start.1 = (f32[512,16]{0,1:T(8,128)S(1)}, f32[512,16]{0,1:T(8,128)S(1)}, u32[]{:S(2)}, u32[]{:S(2)}) collective-permute-start(f32[512,16]{0,1:T(8,128)S(1)} %pad_maximum_fusion.7), channel_id=1, source_target_pairs={{0,6},{2,4},{4,2},{6,0},{1,7},{3,5},{5,3},{7,1},{8,14},{10,12},{12... | collective-permute-start | bytes 98312 | tf_op jit(solution)/shard_map/ppermute | solution.py:590
  11.3 18.0 %collective-permute-start.2 = (f32[512,16]{0,1:T(8,128)S(1)}, f32[512,16]{0,1:T(8,128)S(1)}, u32[]{:S(2)}, u32[]{:S(2)}) collective-permute-start(f32[512,16]{0,1:T(8,128)S(1)} %pad_maximum_fusion.7), channel_id=1, source_target_pairs={{0,4},{2,6},{4,0},{6,2},{1,5},{3,7},{5,1},{7,3},{8,12},{10,14},{12... | collective-permute-start | bytes 98312 | tf_op jit(solution)/shard_map/ppermute | solution.py:590
  16.6 11.3 %all-to-all-start = ((s32[32,1,16]{2,1,0:T(1,128)}), s32[32,1,16]{2,1,0:T(1,128)S(1)}, u32[]{:S(2)}, u32[]{:S(2)}) async-start(s32[32,1,16]{2,1,0:T(1,128)} %bitcast.2), calls=%async_computation | async-start | bytes 32768 | tf_op jit(solution)/shard_map/all_to_all | solution.py:608
  22.6 356.2 %all-gather.4.cloned.1.call-start = ((), (), s32[]{:S(2)}) async-start(), calls=%async_computation.3 | async-start | bytes 14155776 | tf_op jit(solution)/shard_map/all_gather | solution.py:648
  35.9 153.5 %copy-start.38 = (bf16[1536,2,256]{2,1,0:T(2,128)(2,1)S(1)}, bf16[1536,2,256]{2,1,0:T(2,128)(2,1)}, u32[]{:S(2)}) copy-start(bf16[1536,2,256]{2,1,0:T(2,128)(2,1)} %param.22) | copy-start | bytes 4718596
  189.4 4.5 copy-start.4
  191.7 460.5 %reduce-scatter.5.cloned.1.call-start = ((), (), s32[]{:S(2)}) async-start(), calls=%async_computation.5 | async-start | bytes 7077888 | tf_op jit(solution)/shard_map/reduce_scatter | solution.py:726
  192.9 60.1 %copy-start.28 = (pred[2,256,256]{1,2,0:T(8,128)(4,1)}, pred[2,256,256]{1,2,0:T(8,128)(4,1)S(1)}, u32[]{:S(2)}) copy-start(pred[2,256,256]{1,2,0:T(8,128)(4,1)S(1)} %compare_and_fusion) | copy-start | bytes 393220
  193.9 46.1 %copy-start.36 = (f32[512,32]{0,1:T(8,128)}, f32[512,32]{0,1:T(8,128)S(1)}, u32[]{:S(2)}) copy-start(f32[512,32]{0,1:T(8,128)S(1)} %get-tuple-element.129) | copy-start | bytes 196612
  196.0 8.8 %copy-start.13 = (bf16[512,1536]{1,0:T(8,128)(2,1)}, bf16[512,1536]{1,0:T(8,128)(2,1)S(1)}, u32[]{:S(2)}) copy-start(bf16[512,1536]{1,0:T(8,128)(2,1)S(1)} %gather_fusion.2) | copy-start | bytes 4718596
  196.0 67.5 %collective-permute-start.4 = (bf16[512,1536]{1,0:T(8,128)(2,1)S(1)}, bf16[512,1536]{1,0:T(8,128)(2,1)}, u32[]{:S(2)}, u32[]{:S(2)}) collective-permute-start(bf16[512,1536]{1,0:T(8,128)(2,1)S(1)} %gather_fusion.2), channel_id=1, source_target_pairs={{0,4},{2,6},{4,0},{6,2},{1,5},{3,7},{5,1},{7,3},{8,12},{10,14},{12... | collective-permute-start | bytes 4718600 | tf_op jit(solution)/shard_map/ppermute | solution.py:590
  200.4 63.1 %collective-permute-start.3 = (bf16[512,1536]{1,0:T(8,128)(2,1)S(1)}, bf16[512,1536]{1,0:T(8,128)(2,1)}, u32[]{:S(2)}, u32[]{:S(2)}) collective-permute-start(bf16[512,1536]{1,0:T(8,128)(2,1)S(1)} %gather_fusion.2), channel_id=1, source_target_pairs={{0,2},{2,0},{4,6},{6,4},{1,3},{3,1},{5,7},{7,5},{8,10},{10,8},{12,... | collective-permute-start | bytes 4718600 | tf_op jit(solution)/shard_map/ppermute | solution.py:590
  210.5 53.0 %copy-start.11 = (bf16[512,1536]{1,0:T(8,128)(2,1)}, bf16[512,1536]{1,0:T(8,128)(2,1)S(1)}, u32[]{:S(2)}) copy-start(bf16[512,1536]{1,0:T(8,128)(2,1)S(1)} %gather_fusion.3) | copy-start | bytes 4718596
  211.4 8.0 copy-start.55
  211.4 57.5 %copy-start.53 = (f32[1536]{0:T(1024)}, f32[1536]{0:T(1024)S(1)}, u32[]{:S(2)}) copy-start(f32[1536]{0:T(1024)S(1)} %get-tuple-element.96) | copy-start | bytes 18436
  211.8 7.6 copy-start.65
  212.3 7.2 copy-start.21
  241.4 8.5 %copy-start.30 = (bf16[8,4,2,8,256]{4,3,1,0,2:T(8,128)(2,1)}, bf16[8,4,2,8,256]{4,3,1,0,2:T(8,128)(2,1)S(1)}, u32[]{:S(2)}) copy-start(bf16[8,4,2,8,256]{4,3,1,0,2:T(8,128)(2,1)S(1)} %copy.271) | copy-start | bytes 786436
  249.9 4.5 copy-start.2
  249.9 4.5 copy-start.42
  249.9 4.5 copy-start.34
  253.0 4.8 copy-start.49
  268.9 4.6 copy-start.61
  270.8 14.7 %copy-start.25 = (bf16[512,1536]{1,0:T(8,128)(2,1)}, bf16[512,1536]{1,0:T(8,128)(2,1)S(1)}, u32[]{:S(2)}) copy-start(bf16[512,1536]{1,0:T(8,128)(2,1)S(1)} %multiply_convert_fusion.1.rows_ref) | copy-start | bytes 4718596
  270.8 73.8 %collective-permute-start.8 = (bf16[512,1536]{1,0:T(8,128)(2,1)S(1)}, bf16[512,1536]{1,0:T(8,128)(2,1)S(1)}, u32[]{:S(2)}, u32[]{:S(2)}) collective-permute-start(bf16[512,1536]{1,0:T(8,128)(2,1)S(1)} %multiply_convert_fusion.1.rows_ref), channel_id=1, source_target_pairs={{0,4},{2,6},{4,0},{6,2},{1,5},{3,7},{5,1},{7,3},{8,12},{10,14},{12... | collective-permute-start | bytes 4718600 | tf_op jit(solution)/shard_map/ppermute | solution.py:590
  270.9 75.0 %collective-permute-start.7 = (bf16[512,1536]{1,0:T(8,128)(2,1)S(1)}, bf16[512,1536]{1,0:T(8,128)(2,1)}, u32[]{:S(2)}, u32[]{:S(2)}) collective-permute-start(bf16[512,1536]{1,0:T(8,128)(2,1)S(1)} %multiply_convert_fusion.1.rows_ref), channel_id=1, source_target_pairs={{0,2},{2,0},{4,6},{6,4},{1,3},{3,1},{5,7},{7,5},{8,10},{10,8},{12,... | collective-permute-start | bytes 4718600 | tf_op jit(solution)/shard_map/ppermute | solution.py:590
  271.4 14.1 %copy-start.57 = (pred[8,256,4]{1,2,0:T(4,128)(4,1)}, pred[8,256,4]{1,2,0:T(4,128)(4,1)S(1)}, u32[]{:S(2)}) copy-start(pred[8,256,4]{1,2,0:T(4,128)(4,1)S(1)} %compare_reduce_fusion) | copy-start | bytes 24580
  273.5 50.5 %collective-permute-start.6 = (bf16[256,1536]{1,0:T(8,128)(2,1)}, bf16[256,1536]{1,0:T(8,128)(2,1)}, u32[]{:S(2)}, u32[]{:S(2)}) collective-permute-start(bf16[256,1536]{1,0:T(8,128)(2,1)} %slice.281), channel_id=1, source_target_pairs={{0,2},{2,0},{4,6},{6,4},{1,3},{3,1},{5,7},{7,5},{8,10},{10,8},{12,... | collective-permute-start | bytes 2359304 | tf_op jit(solution)/shard_map/ppermute | solution.py:590
  277.4 46.7 %collective-permute-start.5 = (bf16[256,1536]{1,0:T(8,128)(2,1)}, bf16[256,1536]{1,0:T(8,128)(2,1)}, u32[]{:S(2)}, u32[]{:S(2)}) collective-permute-start(bf16[256,1536]{1,0:T(8,128)(2,1)} %slice.280), channel_id=1, source_target_pairs={{0,4},{2,6},{4,0},{6,2},{1,5},{3,7},{5,1},{7,3},{8,12},{10,14},{12... | collective-permute-start | bytes 2359304 | tf_op jit(solution)/shard_map/ppermute | solution.py:590
  279.5 48.1 %copy-start.47 = (s32[8,4,256]{2,1,0:T(4,128)}, s32[8,4,256]{2,1,0:T(4,128)S(1)}, u32[]{:S(2)}) copy-start(s32[8,4,256]{2,1,0:T(4,128)S(1)} %copy.170) | copy-start | bytes 98308
  344.6 17.9 %copy-start.27 = (bf16[512,1536]{1,0:T(8,128)(2,1)}, bf16[512,1536]{1,0:T(8,128)(2,1)S(1)}, u32[]{:S(2)}) copy-start(bf16[512,1536]{1,0:T(8,128)(2,1)S(1)} %collective-permute-done.8.rows_ref) | copy-start | bytes 4718596
  345.6 18.7 %collective-permute-start.10 = (bf16[256,1536]{1,0:T(8,128)(2,1)}, bf16[256,1536]{1,0:T(8,128)(2,1)}, u32[]{:S(2)}, u32[]{:S(2)}) collective-permute-start(bf16[256,1536]{1,0:T(8,128)(2,1)} %slice.283), channel_id=1, source_target_pairs={{0,2},{2,0},{4,6},{6,4},{1,3},{3,1},{5,7},{7,5},{8,10},{10,8},{12,... | collective-permute-start | bytes 2359304 | tf_op jit(solution)/shard_map/ppermute | solution.py:590
  347.1 18.3 %collective-permute-start.9 = (bf16[256,1536]{1,0:T(8,128)(2,1)S(1)}, bf16[256,1536]{1,0:T(8,128)(2,1)S(1)}, u32[]{:S(2)}, u32[]{:S(2)}) collective-permute-start(bf16[256,1536]{1,0:T(8,128)(2,1)S(1)} %slice.282), channel_id=1, source_target_pairs={{0,4},{2,6},{4,0},{6,2},{1,5},{3,7},{5,1},{7,3},{8,12},{10,14},{12... | collective-permute-start | bytes 2359304 | tf_op jit(solution)/shard_map/ppermute | solution.py:590
  365.4 3.8 copy-start.41
  429.5 20.5 %copy-start.48 = (s32[8,4,256]{2,1,0:T(4,128)S(1)}, s32[8,4,256]{2,1,0:T(4,128)}, u32[]{:S(2)}) copy-start(s32[8,4,256]{2,1,0:T(4,128)} %copy-done.47) | copy-start | bytes 98308
  429.5 20.4 %copy-start.58 = (pred[8,256,4]{1,2,0:T(4,128)(4,1)S(1)}, pred[8,256,4]{1,2,0:T(4,128)(4,1)}, u32[]{:S(2)}) copy-start(pred[8,256,4]{1,2,0:T(4,128)(4,1)} %copy-done.57) | copy-start | bytes 24580
  429.5 225.2 %reduce-scatter.3.cloned.1.call-start = ((), (), s32[]{:S(2)}) async-start(), calls=%async_computation.4 | async-start | bytes 14155776 | tf_op jit(solution)/shard_map/reduce_scatter | solution.py:779
  460.7 34.4 %collective-permute-start.12 = (bf16[2,256,1536]{2,1,0:T(8,128)(2,1)S(1)}, bf16[2,256,1536]{2,1,0:T(8,128)(2,1)S(1)}, u32[]{:S(2)}, u32[]{:S(2)}) collective-permute-start(bf16[2,256,1536]{2,1,0:T(8,128)(2,1)S(1)} %get-tuple-element.111), channel_id=1, source_target_pairs={{0,4},{2,6},{4,0},{6,2},{1,5},{3,7},{5,1},{7,3},{8,12},{10,14},{12... | collective-permute-start | bytes 4718600 | tf_op jit(solution)/shard_map/ppermute | solution.py:590
  462.3 33.9 %collective-permute-start.11 = (bf16[2,256,1536]{2,1,0:T(8,128)(2,1)S(1)}, bf16[2,256,1536]{2,1,0:T(8,128)(2,1)}, u32[]{:S(2)}, u32[]{:S(2)}) collective-permute-start(bf16[2,256,1536]{2,1,0:T(8,128)(2,1)S(1)} %get-tuple-element.112), channel_id=1, source_target_pairs={{0,2},{2,0},{4,6},{6,4},{1,3},{3,1},{5,7},{7,5},{8,10},{10,8},{12,... | collective-permute-start | bytes 4718600 | tf_op jit(solution)/shard_map/ppermute | solution.py:590
  518.4 6.2 copy-start.26
  518.4 6.2 copy-start.60
  522.1 26.0 %collective-permute-start.14 = (bf16[256,1536]{1,0:T(8,128)(2,1)S(1)}, bf16[256,1536]{1,0:T(8,128)(2,1)S(1)}, u32[]{:S(2)}, u32[]{:S(2)}) collective-permute-start(bf16[256,1536]{1,0:T(8,128)(2,1)S(1)} %get-tuple-element.108), channel_id=1, source_target_pairs={{0,2},{2,0},{4,6},{6,4},{1,3},{3,1},{5,7},{7,5},{8,10},{10,8},{12,... | collective-permute-start | bytes 2359304 | tf_op jit(solution)/shard_map/ppermute | solution.py:590
  523.5 24.6 %collective-permute-start.13 = (bf16[256,1536]{1,0:T(8,128)(2,1)S(1)}, bf16[256,1536]{1,0:T(8,128)(2,1)S(1)}, u32[]{:S(2)}, u32[]{:S(2)}) collective-permute-start(bf16[256,1536]{1,0:T(8,128)(2,1)S(1)} %get-tuple-element.109), channel_id=1, source_target_pairs={{0,4},{2,6},{4,0},{6,2},{1,5},{3,7},{5,1},{7,3},{8,12},{10,14},{12... | collective-permute-start | bytes 2359304 | tf_op jit(solution)/shard_map/ppermute | solution.py:590
  560.7 15.0 %slice-start = ((s8[12582912]{0:T(1024)(128)(4,1)}), s8[4194304]{0:T(1024)(128)(4,1)S(1)}, s32[]{:S(2)}) async-start(s8[12582912]{0:T(1024)(128)(4,1)} %bitcast.259), calls=%async_computation.7 | async-start | bytes 8388608
  560.7 15.0 %slice-start.1 = ((s8[12582912]{0:T(1024)(128)(4,1)}), s8[4194304]{0:T(1024)(128)(4,1)S(1)}, s32[]{:S(2)}) async-start(s8[12582912]{0:T(1024)(128)(4,1)} %bitcast.259), calls=%async_computation.8 | async-start | bytes 8388608
  567.7 8.0 slice-start.2
  568.6 7.1 copy-start.35
  574.0 60.9 %collective-permute-start.16 = (bf16[2,256,1536]{2,1,0:T(8,128)(2,1)}, bf16[2,256,1536]{2,1,0:T(8,128)(2,1)}, u32[]{:S(2)}, u32[]{:S(2)}) collective-permute-start(bf16[2,256,1536]{2,1,0:T(8,128)(2,1)} %get-tuple-element.106), channel_id=1, source_target_pairs={{0,4},{2,6},{4,0},{6,2},{1,5},{3,7},{5,1},{7,3},{8,12},{10,14},{12... | collective-permute-start | bytes 4718600 | tf_op jit(solution)/shard_map/ppermute | solution.py:590
  574.7 60.2 %collective-permute-start.15 = (bf16[2,256,1536]{2,1,0:T(8,128)(2,1)}, bf16[2,256,1536]{2,1,0:T(8,128)(2,1)}, u32[]{:S(2)}, u32[]{:S(2)}) collective-permute-start(bf16[2,256,1536]{2,1,0:T(8,128)(2,1)} %get-tuple-element.107), channel_id=1, source_target_pairs={{0,2},{2,0},{4,6},{6,4},{1,3},{3,1},{5,7},{7,5},{8,10},{10,8},{12,... | collective-permute-start | bytes 4718600 | tf_op jit(solution)/shard_map/ppermute | solution.py:590
  583.0 6.9 copy-start.31
  583.0 6.9 copy-start.33
  596.7 5.8 copy-start.18
  602.5 5.1 copy-start.37
  602.5 5.1 copy-start.44
  610.2 10.8 %copy-start.39 = (bf16[512,24,64]{0,2,1:T(8,128)(2,1)}, bf16[512,24,64]{0,2,1:T(8,128)(2,1)S(1)}, u32[]{:S(2)}) copy-start(bf16[512,24,64]{0,2,1:T(8,128)(2,1)S(1)} %pad_maximum_fusion.3) | copy-start | bytes 4718596
  638.1 26.0 %collective-permute-start.18 = (bf16[256,1536]{1,0:T(8,128)(2,1)}, bf16[256,1536]{1,0:T(8,128)(2,1)}, u32[]{:S(2)}, u32[]{:S(2)}) collective-permute-start(bf16[256,1536]{1,0:T(8,128)(2,1)} %get-tuple-element.103), channel_id=1, source_target_pairs={{0,2},{2,0},{4,6},{6,4},{1,3},{3,1},{5,7},{7,5},{8,10},{10,8},{12,... | collective-permute-start | bytes 2359304 | tf_op jit(solution)/shard_map/ppermute | solution.py:590
  639.3 24.8 %collective-permute-start.17 = (bf16[256,1536]{1,0:T(8,128)(2,1)S(1)}, bf16[256,1536]{1,0:T(8,128)(2,1)}, u32[]{:S(2)}, u32[]{:S(2)}) collective-permute-start(bf16[256,1536]{1,0:T(8,128)(2,1)S(1)} %get-tuple-element.104), channel_id=1, source_target_pairs={{0,4},{2,6},{4,0},{6,2},{1,5},{3,7},{5,1},{7,3},{8,12},{10,14},{12... | collective-permute-start | bytes 2359304 | tf_op jit(solution)/shard_map/ppermute | solution.py:590
  640.2 6.6 slice-start.3
  640.7 6.1 slice-start.4
  658.2 5.9 copy-start.22
  798.4 5.1 copy-start.6
  (35 other events, 64.0 us)
Sparse Core Ops, SparseCore 0:
  9.6 94.1 all-gather.5
  191.8 116.5 all-gather.3
  429.6 66.0 reduce-scatter.4
  518.5 125.3 reduce-scatter.2

commit v6 on v5

--- a/solution.py
+++ b/solution.py
@@ -551,6 +551,44 @@
     )(*operands)
 
 
+def middle_kernel(rows_ref, weight_ref, grad_ref, hidden_ref, grad_out_ref):
+    half = grad_ref.shape[3]
+    for part in range(weight_ref.shape[1]):
+        gate_up = jnp.dot(rows_ref[0], weight_ref[0, part], preferred_element_type=jnp.float32)
+        gate, up = gate_up[:, :half], gate_up[:, half:]
+        sigmoid_gate = jax.nn.sigmoid(gate)
+        active = gate * sigmoid_gate
+        grad_hidden = grad_ref[0, part].astype(jnp.float32)
+        hidden_ref[0, part] = (active * up).astype(jnp.bfloat16)
+        slope = sigmoid_gate * (1.0 + gate * (1.0 - sigmoid_gate))
+        grad_out_ref[0, part, :, :half] = (grad_hidden * up * slope).astype(jnp.bfloat16)
+        grad_out_ref[0, part, :, half:] = (grad_hidden * active).astype(jnp.bfloat16)
+
+
+def middle(expert_rows, weights_in, grad_hidden):
+    count, row_count, width = expert_rows.shape
+    parts, both = weights_in.shape[1], weights_in.shape[3]
+    tile = 512 if row_count % 512 == 0 else row_count
+    return pl.pallas_call(
+        middle_kernel,
+        grid=(count, row_count // tile),
+        out_shape=(
+            jax.ShapeDtypeStruct((count, parts, row_count, both // 2), jnp.bfloat16),
+            jax.ShapeDtypeStruct((count, parts, row_count, both), jnp.bfloat16),
+        ),
+        in_specs=[
+            pl.BlockSpec((1, tile, width), lambda e, t: (e, t, 0)),
+            pl.BlockSpec((1, parts, width, both), lambda e, t: (e, 0, 0, 0)),
+            pl.BlockSpec((1, parts, tile, both // 2), lambda e, t: (e, 0, t, 0)),
+        ],
+        out_specs=(
+            pl.BlockSpec((1, parts, tile, both // 2), lambda e, t: (e, 0, t, 0)),
+            pl.BlockSpec((1, parts, tile, both), lambda e, t: (e, 0, t, 0)),
+        ),
+        name="middle",
+    )(expert_rows, weights_in, grad_hidden)
+
+
 def shards(
     tokens,
     cotangent,
@@ -656,6 +694,8 @@
     normed = (rows_in * scale_one * gain_one).astype(jnp.bfloat16)
     projected = jnp.dot(normed, qkv_full, preferred_element_type=jnp.float32)
     cosine_table, sine_table = rope_tables(position)
+    if lo_count == 4:
+        segment = hold(segment, grad_blocks[1][0], grad_blocks[2][0])
     queries = rotate(
         projected[:, :q_dim].reshape(tok_dev, HEADS, HEAD), cosine_table, sine_table
     ).astype(jnp.bfloat16)
@@ -669,14 +709,14 @@
     )
     mixed_part, logsum = attend_block(queries, key_rows, value_rows, segment, position)
     mixed_rows = mixed_part.astype(jnp.bfloat16)
-    if lo_count == 4:
-        mixed_rows = hold(mixed_rows, grad_blocks[1][0], grad_blocks[2][0])
     attended = jnp.dot(mixed_rows, out_full, preferred_element_type=jnp.float32)
     residual = rows_in + attended
     scale_two = lax.rsqrt(jnp.mean(residual * residual, axis=1, keepdims=True) + epsilon)
     normed_two = (residual * scale_two * gain_two).astype(jnp.bfloat16)
     grad_output = grad_bf.astype(jnp.float32)
     home = lax.axis_index("lo")
+    if lo_count == 4:
+        normed_two = hold(normed_two, *grad_blocks[3])
     row_blocks = spread(normed_two)
     normed_two, grad_blocks = lax.optimization_barrier((normed_two, grad_blocks))
     choose, slot_gate = slot_tables(
@@ -709,16 +749,7 @@
     )
     expert_rows = fill(list(enumerate(others, 1)), expert_rows, None)
     expert_rows = expert_rows.reshape(hi_count, -1, model_width)
-    gate_up = jnp.einsum(
-        "erd,ekdf->ekrf", expert_rows, weights_in, preferred_element_type=jnp.float32
-    )
-    gate_part = gate_up[..., :shard_cols]
-    up_part = gate_up[..., shard_cols:]
-    sigmoid_gate = jax.nn.sigmoid(gate_part)
-    hidden = (gate_part * sigmoid_gate * up_part).astype(jnp.bfloat16)
-    grad_gate = grad_hidden * up_part * sigmoid_gate * (1.0 + gate_part * (1.0 - sigmoid_gate))
-    grad_up = grad_hidden * (gate_part * sigmoid_gate)
-    grad_gate_up = jnp.concatenate([grad_gate, grad_up], axis=-1).astype(jnp.bfloat16)
+    hidden, grad_gate_up = middle(expert_rows, weights_in, grad_hidden)
     grad_weights_out = jnp.einsum(
         "ekrf,erd->ekfd", hidden, grad_expert, preferred_element_type=jnp.float32
     ).astype(jnp.bfloat16)
@@ -771,11 +802,15 @@
 
     back = split_back(grad_expert_rows)
     back_parts = bring_back(back)
-    grad_gate_up = hold(grad_gate_up, *back_parts[1:3])
+    produced = (
+        jnp.einsum("ekrf,ekfd->erd", hidden, weights_out, preferred_element_type=jnp.float32)
+        * slot_weight.reshape(hi_count, -1, 1)
+    ).astype(jnp.bfloat16)
+    ahead = split_back(produced)
+    grad_gate_up = hold(grad_gate_up, ahead, *back_parts[1:3])
     grad_weights_in = jnp.einsum(
         "ekrf,erd->ekfd", grad_gate_up, expert_rows, preferred_element_type=jnp.float32
     ).astype(jnp.bfloat16)
-    grad_weights_in, hidden = lax.optimization_barrier((grad_weights_in, hidden))
     shard_in = lax.psum_scatter(
         grad_weights_in.reshape(hi_count * 2 * 2 * shard_cols, model_width),
         ("hi", "core"),
@@ -783,11 +818,6 @@
         tiled=True,
     )
     shard_in = shard_in.T.astype(jnp.float32).reshape(model_width, 2, shard_cols)
-    produced = (
-        jnp.einsum("ekrf,ekfd->erd", hidden, weights_out, preferred_element_type=jnp.float32)
-        * slot_weight.reshape(hi_count, -1, 1)
-    ).astype(jnp.bfloat16)
-    ahead = split_back(produced)
     ahead, back_parts = lax.optimization_barrier((ahead, back_parts))
     ahead_parts = bring_back(ahead)
     grad_normed_two = total_of(back_parts)
@@ -832,9 +862,7 @@
         ],
         axis=1,
     ).reshape(sizes + (shard_rows, -1))
-    parts, shard_in, shard_out, ahead_parts = lax.optimization_barrier(
-        (parts, shard_in, shard_out, ahead_parts)
-    )
+    parts, shard_out, ahead_parts = lax.optimization_barrier((parts, shard_out, ahead_parts))
     output_rows = (residual + total_of(ahead_parts)).astype(jnp.bfloat16)
     home_out, home_grad, sums = closing(
         sizes,

time: 821 us -> 779 us (0.949)
  Pallas kernels: 315 us -> 337 us
  waiting for transfers between devices: 75.1 us -> 53.8 us
  matrix products: 185 us -> 165 us
  other arithmetic: 76.6 us -> 59.4 us
    pallas_call x0 -> x1, Pallas kernels: none -> 23.5 us  [middle(): pl.pallas_call(middle_kernel, grid=(count, row_count // tile), out_shape=...]
    ppermute x19, waiting for transfers between devices: 73.9 us -> 52.6 us  [swap(): return lax.ppermute(block, 'lo', [(i, i ^ step) for i in range(lo_count)])]
    dot_general x1 -> x0, matrix products: 18.3 us -> none  [shards(): jnp.einsum('erd,ekdf->ekrf', expert_rows, weights_in, preferred_element_t...]
    another operation x7 -> x6, other arithmetic: 18.1 us -> 6.93 us
    unnamed x160 -> x153, local copies, waits for them, and re-layouts: 18.6 us -> 20.3 us
  transfers between devices with their start and end apart: 24 -> 24, of which waited for: 6 -> 11; matrix products, arithmetic and copies ran while one was open for 36% -> 39% of each run, Pallas kernels for 23% -> 41%
where the time goes in v6:
time: 779 us; the launch traced here: 774 us
  Pallas kernels  337 us (43%)
  matrix products  165 us (21%)
  local copies, waits for them, and re-layouts  114 us (15%)
  other arithmetic  59.4 us (8%)
  waiting for transfers between devices  53.8 us (7%)
  starting transfers between devices  29.1 us (4%)
  between operations  15.2 us (2%)
    pallas_call x1, Pallas kernels, opening(): pl.pallas_call(functools.partial(opening_kernel, sizes), out_shape=(jax.S...  154 us
    pallas_call x1, Pallas kernels, closing(): pl.pallas_call(functools.partial(closing_kernel, sizes), out_shape=(jax.S...  127 us
    ppermute x19, waiting for transfers between devices, swap(): return lax.ppermute(block, 'lo', [(i, i ^ step) for i in range(lo_count)])  52.6 us
    pallas_call x10, Pallas kernels, dispatch(): pl.pallas_call(functools.partial(dispatch_kernel, weight is not None), gr...  33.6 us
    gather x8, local copies, waits for them, and re-layouts, pick(): return jnp.take(rows, index, axis=0, mode='clip')  25.4 us
    pallas_call x1, Pallas kernels, middle(): pl.pallas_call(middle_kernel, grid=(count, row_count // tile), out_shape=...  23.5 us
    ppermute x19, starting transfers between devices, swap(): return lax.ppermute(block, 'lo', [(i, i ^ step) for i in range(lo_count)])  22.8 us
    dot_general x1, matrix products, shards(): jnp.einsum('ekrf,erd->ekfd', grad_gate_up, expert_rows, preferred_element...  22.4 us
  transfers between devices with their start and end apart: 24, of which 11 were waited for; matrix products, arithmetic and copies ran while one was open for 39% of the time, Pallas kernels for 41%

profile of v6, /device:TPU:12, one launch (start us, length us, event | category | flops | bytes accessed | tf_op | source)
XLA Modules:
  0.0 773.6 jit_solution(16064124927367728991)
XLA Ops:
  16.6 6.0 all-to-all-start
  29.8 2.9 gather_fusion
  32.8 2.9 gather_fusion.1
  35.7 153.6 %opening.1 = (bf16[32,16,1536]{2,1,0:T(8,128)(2,1)}, bf16[32,16,1536]{2,1,0:T(8,128)(2,1)}, bf16[4,4,2,48,4224]{4,3,2,1,0:T(8,128)(2,1)}) custom-call(bf16[32,16,1536]{2,1,0:T(8,128)(2,1)} %bitcast.270, bf16[32,16,1536]{2,1,0:T(8,128)(2,1)} %bitcast.271, bf16[48,4224]{1,0:T(8,128)(2,1)} %concatenate.46.shard_ref), custom_call_target="tpu_custom_call" | custom-call | tf_op jit(solution)/shard_map/opening/pallas_call | solution.py:332
  196.1 3.5 collective-permute-start.3
  199.6 3.1 collective-permute-start.4
  202.7 5.5 gather_fusion.3
  214.2 7.2 fusion.14
  225.2 3.5 copy.151
  228.7 3.6 add_convert_fusion.5
  232.3 2.9 concatenate.50
  235.2 3.1 concatenate.51
  238.3 2.5 copy.148
  252.3 2.9 fusion.24
  255.2 3.1 fusion.10
  259.9 3.4 fusion.56
  269.5 5.3 multiply_reduce_fusion.2
  277.9 8.4 %collective-permute-done.5.refs_1_.rows_ref = bf16[256,1536]{1,0:T(8,128)(2,1)S(1)} collective-permute-done((bf16[256,1536]{1,0:T(8,128)(2,1)S(1)}, bf16[256,1536]{1,0:T(8,128)(2,1)S(1)}, u32[]{:S(2)}, u32[]{:S(2)}) %collective-permute-start.5) | collective-permute-done | bytes 786464 | tf_op jit(solution)/shard_map/ppermute | solution.py:628
  296.3 3.5 dispatch.15.refs_0_
  299.8 3.6 dispatch.10.refs_1_
  303.5 3.6 dispatch.11.refs_1_
  307.1 3.7 dispatch.12.refs_1_
  310.8 3.0 dispatch.13.refs_1_
  313.8 3.0 dispatch.14
  316.8 7.0 collective-permute-done.8.rows_ref
  328.1 13.7 %convert_bitcast_fusion.grad_ref = bf16[4,2,1024,256]{3,2,1,0:T(8,128)(2,1)} fusion(bf16[4,1024,1536,1]{2,1,3,0:T(8,128)(2,1)} %bitcast.254, bf16[4,2,256,1536]{3,2,1,0:T(8,128)(2,1)} %bitcast.315), kind=kOutput, calls=%fused_computation.48 | convolution fusion | flops 6444548096 | bytes 23068672 | tf_op jit(solution)/shard_map/erd,ekfd->ekrf/dot_general | solution.py:743
  343.0 2.5 collective-permute-done.9.rows_ref
  345.5 3.6 dispatch.16.refs_0_
  349.1 3.5 dispatch.17.refs_0_
  352.6 3.0 dispatch.18.refs_0_
  355.6 2.9 dispatch.19
  358.6 23.5 %middle.1 = (bf16[4,2,1024,256]{3,2,1,0:T(8,128)(2,1)}, bf16[4,2,1024,512]{3,2,1,0:T(8,128)(2,1)}) custom-call(bf16[4,1024,1536]{2,1,0:T(8,128)(2,1)} %bitcast.252, bf16[4,2,1536,512]{3,2,1,0:T(8,128)(2,1)} %bitcast.263, bf16[4,2,1024,256]{3,2,1,0:T(8,128)(2,1)} %convert_bitcast_fusion.grad_ref), custom_call_target="tpu_custom_call" | custom-call | tf_op jit(solution)/shard_map/middle/pallas_call | solution.py:572
  382.1 14.0 %convolution_convert_fusion.3 = bf16[4,2,256,1536]{3,2,1,0:T(8,128)(2,1)} fusion(bf16[4,2,1024,256]{3,2,1,0:T(8,128)(2,1)} %get-tuple-element.68, bf16[4,1024,1536,1]{2,1,3,0:T(8,128)(2,1)} %bitcast.255), kind=kOutput, calls=%fused_computation.46 | convolution fusion | flops 6445596672 | bytes 23068672 | tf_op jit(solution)/shard_map/ekrf,erd->ekfd/dot_general | solution.py:753
  396.2 20.2 %bitcast_convert_fusion = bf16[4,1024,1536]{2,1,0:T(8,128)(2,1)} fusion(bf16[4,2,1024,512]{3,2,1,0:T(8,128)(2,1)} %get-tuple-element.70.refs_0_, bf16[4,2,1536,512]{3,2,1,0:T(8,128)(2,1)} %bitcast.264), kind=kOutput, calls=%fused_computation.10 | convolution fusion | flops 12891193344 | bytes 33554432 | tf_op jit(solution)/shard_map/ekrf,ekdf->erd/dot_general | solution.py:763
  416.4 8.2 %bitcast_convert_fusion.1 = bf16[8,256,1536]{2,1,0:T(8,128)(2,1)S(1)} fusion(bf16[4,8,128,1536]{3,2,1,0:T(8,128)(2,1)} %bitcast.318, s32[8,4,256]{2,1,0:T(4,128)S(1)} %copy.158, pred[8,4,256]{2,1,0:T(4,128)(4,1)S(1)} %bitcast.298), kind=kOutput, calls=%fused_computation.20 | convolution fusion | flops 3226468352 | bytes 18915328 | tf_op jit(solution)/shard_map/becr,ebcd->brd/dot_general | solution.py:768
  430.1 12.6 %fusion.1 = bf16[4,1024,1536]{2,1,0:T(8,128)(2,1)} fusion(bf16[4,2,1024,256]{3,2,1,0:T(8,128)(2,1)S(1)} %copy-done.62, bf16[4,2,256,1536]{3,2,1,0:T(8,128)(2,1)} %bitcast.316, f32[4,1024]{1,0:T(4,128)S(1)} %bitcast.302), kind=kOutput, calls=%fused_computation.12 | convolution fusion | flops 6455033856 | bytes 23085056 | tf_op jit(solution)/shard_map/ekrf,ekfd->erd/dot_general | solution.py:806
  442.7 10.8 %bitcast_convert_fusion.2.refs_1_ = bf16[8,256,1536]{2,1,0:T(8,128)(2,1)} fusion(bf16[4,8,128,1536]{3,2,1,0:T(8,128)(2,1)} %bitcast.317, s32[8,4,256]{2,1,0:T(4,128)S(1)} %copy.158, pred[8,4,256]{2,1,0:T(4,128)(4,1)S(1)} %bitcast.299), kind=kOutput, calls=%fused_computation.21 | convolution fusion | flops 3226468352 | bytes 18915328 | tf_op jit(solution)/shard_map/becr,ebcd->brd/dot_general | solution.py:768
  453.5 9.5 %collective-permute-done.11.refs_2_ = bf16[2,256,1536]{2,1,0:T(8,128)(2,1)S(1)} collective-permute-done((bf16[2,256,1536]{2,1,0:T(8,128)(2,1)}, bf16[2,256,1536]{2,1,0:T(8,128)(2,1)S(1)}, u32[]{:S(2)}, u32[]{:S(2)}) %collective-permute-start.11) | collective-permute-done | bytes 1572896 | tf_op jit(solution)/shard_map/ppermute | solution.py:628
  464.1 22.4 %convolution_convert_fusion = bf16[4,2,512,1536]{3,2,1,0:T(8,128)(2,1)} fusion(bf16[4,2,1024,512]{3,2,1,0:T(8,128)(2,1)} %hold.9, bf16[4,1024,1536,1]{2,1,3,0:T(8,128)(2,1)} %bitcast.253), kind=kOutput, calls=%fused_computation.13 | convolution fusion | flops 12891193344 | bytes 33554432 | tf_op jit(solution)/shard_map/ekrf,erd->ekfd/dot_general | solution.py:811
  491.8 14.2 %collective-permute-done.13 = bf16[256,1536]{1,0:T(8,128)(2,1)S(1)} collective-permute-done((bf16[256,1536]{1,0:T(8,128)(2,1)S(1)}, bf16[256,1536]{1,0:T(8,128)(2,1)S(1)}, u32[]{:S(2)}, u32[]{:S(2)}) %collective-permute-start.13) | collective-permute-done | bytes 786464 | tf_op jit(solution)/shard_map/ppermute | solution.py:628
  512.5 5.0 fusion.48
  518.6 7.1 fusion.3
  525.8 7.0 fusion.5
  535.4 4.2 copy.174
  539.6 5.6 reshape.356
  545.2 5.0 fusion.66
  550.4 6.7 fusion.72
  557.8 2.5 fusion.108
  564.2 6.3 fusion.44
  570.9 3.9 fusion.40
  574.8 3.2 gather_fusion.5
  578.0 6.4 convolution_convert_fusion.2
  584.4 8.4 %collective-permute-done.15.refs_1_ = bf16[2,256,1536]{2,1,0:T(8,128)(2,1)} collective-permute-done((bf16[2,256,1536]{2,1,0:T(8,128)(2,1)}, bf16[2,256,1536]{2,1,0:T(8,128)(2,1)}, u32[]{:S(2)}, u32[]{:S(2)}) %collective-permute-start.15) | collective-permute-done | bytes 1572896 | tf_op jit(solution)/shard_map/ppermute | solution.py:628
  592.8 3.1 fusion.80
  599.1 6.1 convolution_convert_fusion.1
  605.2 5.4 fusion.2
  610.6 2.6 convert_element_type.275
  613.3 2.6 bitcast_add_fusion.1
  616.8 2.9 gather_fusion.4
  619.8 126.7 %closing.1 = (bf16[32,16,1536]{2,1,0:T(8,128)(2,1)}, bf16[32,16,1536]{2,1,0:T(8,128)(2,1)}, f32[48,4224]{1,0:T(8,128)}) custom-call(bf16[32,16,1536]{2,1,0:T(8,128)(2,1)} %bitcast.273, bf16[32,16,1536]{2,1,0:T(8,128)(2,1)} %bitcast.272, bf16[4,4,2,48,4224]{4,3,2,1,0:T(8,128)(2,1)} %bitcast.260), custom_call_target="tpu_custom_call" | custom-call | tf_op jit(solution)/shard_map/closing/pallas_call | solution.py:486
  750.1 2.9 gather_fusion.7
  753.1 2.9 gather_fusion.6
  757.5 3.4 reshape.371
  760.9 5.9 copy.208
  (300 shorter events, 107.0 us)
Async XLA Ops:
  7.2 22.7 %copy-start = (bf16[512,1536]{1,0:T(8,128)(2,1)S(1)}, bf16[512,1536]{1,0:T(8,128)(2,1)}, u32[]{:S(2)}) copy-start(bf16[512,1536]{1,0:T(8,128)(2,1)} %param.12) | copy-start | bytes 4718596
  7.2 320.9 %all-gather.6.cloned.1.call-start = ((), (), s32[]{:S(2)}) async-start(), calls=%async_computation.6 | async-start | bytes 7077888 | tf_op jit(solution)/shard_map/all_gather | solution.py:689
  9.4 19.9 %collective-permute-start = (f32[512,16]{0,1:T(8,128)S(1)}, f32[512,16]{0,1:T(8,128)S(1)}, u32[]{:S(2)}, u32[]{:S(2)}) collective-permute-start(f32[512,16]{0,1:T(8,128)S(1)} %pad_maximum_fusion.6), channel_id=1, source_target_pairs={{0,2},{2,0},{4,6},{6,4},{1,3},{3,1},{5,7},{7,5},{8,10},{10,8},{12,... | collective-permute-start | bytes 98312 | tf_op jit(solution)/shard_map/ppermute | solution.py:628
  10.9 18.4 %collective-permute-start.1 = (f32[512,16]{0,1:T(8,128)S(1)}, f32[512,16]{0,1:T(8,128)S(1)}, u32[]{:S(2)}, u32[]{:S(2)}) collective-permute-start(f32[512,16]{0,1:T(8,128)S(1)} %pad_maximum_fusion.6), channel_id=1, source_target_pairs={{0,6},{2,4},{4,2},{6,0},{1,7},{3,5},{5,3},{7,1},{8,14},{10,12},{12... | collective-permute-start | bytes 98312 | tf_op jit(solution)/shard_map/ppermute | solution.py:628
  11.3 18.0 %collective-permute-start.2 = (f32[512,16]{0,1:T(8,128)S(1)}, f32[512,16]{0,1:T(8,128)S(1)}, u32[]{:S(2)}, u32[]{:S(2)}) collective-permute-start(f32[512,16]{0,1:T(8,128)S(1)} %pad_maximum_fusion.6), channel_id=1, source_target_pairs={{0,4},{2,6},{4,0},{6,2},{1,5},{3,7},{5,1},{7,3},{8,12},{10,14},{12... | collective-permute-start | bytes 98312 | tf_op jit(solution)/shard_map/ppermute | solution.py:628
  16.6 11.3 %all-to-all-start = ((s32[32,1,16]{2,1,0:T(1,128)}), s32[32,1,16]{2,1,0:T(1,128)S(1)}, u32[]{:S(2)}, u32[]{:S(2)}) async-start(s32[32,1,16]{2,1,0:T(1,128)} %bitcast.2), calls=%async_computation | async-start | bytes 32768 | tf_op jit(solution)/shard_map/all_to_all | solution.py:646
  22.6 335.9 %all-gather.4.cloned.1.call-start = ((), (), s32[]{:S(2)}) async-start(), calls=%async_computation.3 | async-start | bytes 14155776 | tf_op jit(solution)/shard_map/all_gather | solution.py:686
  35.7 153.7 %copy-start.37 = (bf16[1536,2,256]{2,1,0:T(2,128)(2,1)S(1)}, bf16[1536,2,256]{2,1,0:T(2,128)(2,1)}, u32[]{:S(2)}) copy-start(bf16[1536,2,256]{2,1,0:T(2,128)(2,1)} %param.22) | copy-start | bytes 4718596
  189.3 4.6 copy-start.4
  191.7 418.9 %reduce-scatter.3.cloned.1.call-start = ((), (), s32[]{:S(2)}) async-start(), calls=%async_computation.4 | async-start | bytes 7077888 | tf_op jit(solution)/shard_map/reduce_scatter | solution.py:757
  193.9 46.9 %copy-start.35 = (f32[512,32]{0,1:T(8,128)}, f32[512,32]{0,1:T(8,128)S(1)}, u32[]{:S(2)}) copy-start(f32[512,32]{0,1:T(8,128)S(1)} %get-tuple-element.124) | copy-start | bytes 196612
  196.1 6.6 copy-start.13
  196.1 53.6 %collective-permute-start.3 = (bf16[512,1536]{1,0:T(8,128)(2,1)S(1)}, bf16[512,1536]{1,0:T(8,128)(2,1)}, u32[]{:S(2)}, u32[]{:S(2)}) collective-permute-start(bf16[512,1536]{1,0:T(8,128)(2,1)S(1)} %gather_fusion.2), channel_id=1, source_target_pairs={{0,2},{2,0},{4,6},{6,4},{1,3},{3,1},{5,7},{7,5},{8,10},{10,8},{12,... | collective-permute-start | bytes 4718600 | tf_op jit(solution)/shard_map/ppermute | solution.py:628
  199.6 50.1 %collective-permute-start.4 = (bf16[512,1536]{1,0:T(8,128)(2,1)S(1)}, bf16[512,1536]{1,0:T(8,128)(2,1)}, u32[]{:S(2)}, u32[]{:S(2)}) collective-permute-start(bf16[512,1536]{1,0:T(8,128)(2,1)S(1)} %gather_fusion.2), channel_id=1, source_target_pairs={{0,4},{2,6},{4,0},{6,2},{1,5},{3,7},{5,1},{7,3},{8,12},{10,14},{12... | collective-permute-start | bytes 4718600 | tf_op jit(solution)/shard_map/ppermute | solution.py:628
  208.1 61.4 %copy-start.11 = (bf16[512,1536]{1,0:T(8,128)(2,1)}, bf16[512,1536]{1,0:T(8,128)(2,1)S(1)}, u32[]{:S(2)}) copy-start(bf16[512,1536]{1,0:T(8,128)(2,1)S(1)} %gather_fusion.3) | copy-start | bytes 4718596
  213.3 8.0 %copy-start.51 = (f32[1536]{0:T(1024)}, f32[1536]{0:T(1024)S(1)}, u32[]{:S(2)}) copy-start(f32[1536]{0:T(1024)S(1)} %get-tuple-element.95) | copy-start | bytes 18436
  213.3 61.5 %copy-start.49 = (f32[1536]{0:T(1024)}, f32[1536]{0:T(1024)S(1)}, u32[]{:S(2)}) copy-start(f32[1536]{0:T(1024)S(1)} %get-tuple-element.94) | copy-start | bytes 18436
  213.7 7.6 copy-start.57
  214.2 7.2 copy-start.21
  242.3 9.6 %copy-start.31 = (bf16[8,4,2,8,256]{4,3,1,0,2:T(8,128)(2,1)}, bf16[8,4,2,8,256]{4,3,1,0,2:T(8,128)(2,1)S(1)}, u32[]{:S(2)}) copy-start(bf16[8,4,2,8,256]{4,3,1,0,2:T(8,128)(2,1)S(1)} %copy.252) | copy-start | bytes 786436
  251.9 6.4 copy-start.27
  255.2 4.6 copy-start.2
  255.2 4.7 copy-start.42
  255.2 4.7 copy-start.34
  258.3 5.1 copy-start.47
  265.4 9.4 %copy-start.38 = (bf16[192,8,2,256]{3,1,2,0:T(8,128)(2,1)}, bf16[192,8,2,256]{3,1,2,0:T(8,128)(2,1)S(1)}, u32[]{:S(2)}) copy-start(bf16[192,8,2,256]{3,1,2,0:T(8,128)(2,1)S(1)} %copy.216) | copy-start | bytes 4718596
  267.1 19.1 %collective-permute-start.5 = (bf16[256,1536]{1,0:T(8,128)(2,1)S(1)}, bf16[256,1536]{1,0:T(8,128)(2,1)S(1)}, u32[]{:S(2)}, u32[]{:S(2)}) collective-permute-start(bf16[256,1536]{1,0:T(8,128)(2,1)S(1)} %slice.272), channel_id=1, source_target_pairs={{0,4},{2,6},{4,0},{6,2},{1,5},{3,7},{5,1},{7,3},{8,12},{10,14},{12... | collective-permute-start | bytes 2359304 | tf_op jit(solution)/shard_map/ppermute | solution.py:628
  268.4 19.2 %collective-permute-start.6 = (bf16[256,1536]{1,0:T(8,128)(2,1)S(1)}, bf16[256,1536]{1,0:T(8,128)(2,1)S(1)}, u32[]{:S(2)}, u32[]{:S(2)}) collective-permute-start(bf16[256,1536]{1,0:T(8,128)(2,1)S(1)} %slice.273), channel_id=1, source_target_pairs={{0,2},{2,0},{4,6},{6,4},{1,3},{3,1},{5,7},{7,5},{8,10},{10,8},{12,... | collective-permute-start | bytes 2359304 | tf_op jit(solution)/shard_map/ppermute | solution.py:628
  274.8 13.7 %copy-start.53 = (f32[512]{0:T(512)}, f32[512]{0:T(512)S(1)}, u32[]{:S(2)}) copy-start(f32[512]{0:T(512)S(1)} %add_rsqrt_fusion) | copy-start | bytes 6148
  288.5 35.4 %collective-permute-start.8 = (bf16[512,1536]{1,0:T(8,128)(2,1)}, bf16[512,1536]{1,0:T(8,128)(2,1)S(1)}, u32[]{:S(2)}, u32[]{:S(2)}) collective-permute-start(bf16[512,1536]{1,0:T(8,128)(2,1)} %hold.7.rows_ref), channel_id=1, source_target_pairs={{0,4},{2,6},{4,0},{6,2},{1,5},{3,7},{5,1},{7,3},{8,12},{10,14},{12... | collective-permute-start | bytes 4718600 | tf_op jit(solution)/shard_map/ppermute | solution.py:628
  290.2 36.5 %collective-permute-start.7 = (bf16[512,1536]{1,0:T(8,128)(2,1)}, bf16[512,1536]{1,0:T(8,128)(2,1)S(1)}, u32[]{:S(2)}, u32[]{:S(2)}) collective-permute-start(bf16[512,1536]{1,0:T(8,128)(2,1)} %hold.7.rows_ref), channel_id=1, source_target_pairs={{0,2},{2,0},{4,6},{6,4},{1,3},{3,1},{5,7},{7,5},{8,10},{10,8},{12,... | collective-permute-start | bytes 4718600 | tf_op jit(solution)/shard_map/ppermute | solution.py:628
  323.9 18.0 %copy-start.25 = (bf16[512,1536]{1,0:T(8,128)(2,1)}, bf16[512,1536]{1,0:T(8,128)(2,1)S(1)}, u32[]{:S(2)}) copy-start(bf16[512,1536]{1,0:T(8,128)(2,1)S(1)} %collective-permute-done.8.rows_ref) | copy-start | bytes 4718596
  324.9 18.2 %collective-permute-start.10 = (bf16[256,1536]{1,0:T(8,128)(2,1)}, bf16[256,1536]{1,0:T(8,128)(2,1)}, u32[]{:S(2)}, u32[]{:S(2)}) collective-permute-start(bf16[256,1536]{1,0:T(8,128)(2,1)} %slice.275), channel_id=1, source_target_pairs={{0,2},{2,0},{4,6},{6,4},{1,3},{3,1},{5,7},{7,5},{8,10},{10,8},{12,... | collective-permute-start | bytes 2359304 | tf_op jit(solution)/shard_map/ppermute | solution.py:628
  326.6 15.2 %copy-start.26 = (bf16[512,1536]{1,0:T(8,128)(2,1)}, bf16[512,1536]{1,0:T(8,128)(2,1)S(1)}, u32[]{:S(2)}) copy-start(bf16[512,1536]{1,0:T(8,128)(2,1)S(1)} %collective-permute-done.7.rows_ref) | copy-start | bytes 4718596
  327.6 17.9 %collective-permute-start.9 = (bf16[256,1536]{1,0:T(8,128)(2,1)}, bf16[256,1536]{1,0:T(8,128)(2,1)}, u32[]{:S(2)}, u32[]{:S(2)}) collective-permute-start(bf16[256,1536]{1,0:T(8,128)(2,1)} %slice.274), channel_id=1, source_target_pairs={{0,4},{2,6},{4,0},{6,2},{1,5},{3,7},{5,1},{7,3},{8,12},{10,14},{12... | collective-permute-start | bytes 2359304 | tf_op jit(solution)/shard_map/ppermute | solution.py:628
  396.1 361.4 %reduce-scatter.5.cloned.1.call-start = ((), (), s32[]{:S(2)}) async-start(), calls=%async_computation.5 | async-start | bytes 14155776 | tf_op jit(solution)/shard_map/reduce_scatter | solution.py:814
  424.6 4.6 copy-start.20
  424.6 5.5 copy-start.62
  429.2 33.7 %collective-permute-start.11 = (bf16[2,256,1536]{2,1,0:T(8,128)(2,1)}, bf16[2,256,1536]{2,1,0:T(8,128)(2,1)S(1)}, u32[]{:S(2)}, u32[]{:S(2)}) collective-permute-start(bf16[2,256,1536]{2,1,0:T(8,128)(2,1)} %get-tuple-element.106), channel_id=1, source_target_pairs={{0,2},{2,0},{4,6},{6,4},{1,3},{3,1},{5,7},{7,5},{8,10},{10,8},{12,... | collective-permute-start | bytes 4718600 | tf_op jit(solution)/shard_map/ppermute | solution.py:628
  429.4 33.6 %collective-permute-start.12 = (bf16[2,256,1536]{2,1,0:T(8,128)(2,1)}, bf16[2,256,1536]{2,1,0:T(8,128)(2,1)}, u32[]{:S(2)}, u32[]{:S(2)}) collective-permute-start(bf16[2,256,1536]{2,1,0:T(8,128)(2,1)} %get-tuple-element.105), channel_id=1, source_target_pairs={{0,4},{2,6},{4,0},{6,2},{1,5},{3,7},{5,1},{7,3},{8,12},{10,14},{12... | collective-permute-start | bytes 4718600 | tf_op jit(solution)/shard_map/ppermute | solution.py:628
  487.9 3.9 copy-start.48
  489.9 16.1 %collective-permute-start.13 = (bf16[256,1536]{1,0:T(8,128)(2,1)S(1)}, bf16[256,1536]{1,0:T(8,128)(2,1)S(1)}, u32[]{:S(2)}, u32[]{:S(2)}) collective-permute-start(bf16[256,1536]{1,0:T(8,128)(2,1)S(1)} %get-tuple-element.104), channel_id=1, source_target_pairs={{0,4},{2,6},{4,0},{6,2},{1,5},{3,7},{5,1},{7,3},{8,12},{10,14},{12... | collective-permute-start | bytes 2359304 | tf_op jit(solution)/shard_map/ppermute | solution.py:628
  490.1 16.0 %collective-permute-start.14 = (bf16[256,1536]{1,0:T(8,128)(2,1)S(1)}, bf16[256,1536]{1,0:T(8,128)(2,1)S(1)}, u32[]{:S(2)}, u32[]{:S(2)}) collective-permute-start(bf16[256,1536]{1,0:T(8,128)(2,1)S(1)} %get-tuple-element.103), channel_id=1, source_target_pairs={{0,2},{2,0},{4,6},{6,4},{1,3},{3,1},{5,7},{7,5},{8,10},{10,8},{12,... | collective-permute-start | bytes 2359304 | tf_op jit(solution)/shard_map/ppermute | solution.py:628
  525.7 7.0 copy-start.32
  525.8 7.0 copy-start.33
  539.6 5.6 copy-start.19
  545.2 18.2 %slice-start.4 = ((s8[12976128]{0:T(1024)(128)(4,1)}), s8[4194304]{0:T(1024)(128)(4,1)S(1)}, s32[]{:S(2)}) async-start(s8[12976128]{0:T(1024)(128)(4,1)} %bitcast.309), calls=%async_computation.11 | async-start | bytes 8388608
  550.2 7.5 slice-start
  550.4 7.4 slice-start.1
  550.4 13.1 %slice-start.5 = ((s8[12976128]{0:T(1024)(128)(4,1)}), s8[4194304]{0:T(1024)(128)(4,1)S(1)}, s32[]{:S(2)}) async-start(s8[12976128]{0:T(1024)(128)(4,1)} %bitcast.309), calls=%async_computation.12 | async-start | bytes 8388608
  550.4 13.1 %slice-start.6 = ((s8[12976128]{0:T(1024)(128)(4,1)}), s8[4194304]{0:T(1024)(128)(4,1)S(1)}, s32[]{:S(2)}) async-start(s8[12976128]{0:T(1024)(128)(4,1)} %bitcast.309), calls=%async_computation.13 | async-start | bytes 8388608
  557.7 5.7 copy-start.45
  557.8 4.6 copy-start.36
  557.8 4.6 copy-start.44
  557.8 4.8 copy-start.16
  557.8 5.7 slice-start.7
  560.3 32.5 %collective-permute-start.15 = (bf16[2,256,1536]{2,1,0:T(8,128)(2,1)}, bf16[2,256,1536]{2,1,0:T(8,128)(2,1)}, u32[]{:S(2)}, u32[]{:S(2)}) collective-permute-start(bf16[2,256,1536]{2,1,0:T(8,128)(2,1)} %get-tuple-element.102), channel_id=1, source_target_pairs={{0,2},{2,0},{4,6},{6,4},{1,3},{3,1},{5,7},{7,5},{8,10},{10,8},{12,... | collective-permute-start | bytes 4718600 | tf_op jit(solution)/shard_map/ppermute | solution.py:628
  560.9 31.9 %collective-permute-start.16 = (bf16[2,256,1536]{2,1,0:T(8,128)(2,1)}, bf16[2,256,1536]{2,1,0:T(8,128)(2,1)}, u32[]{:S(2)}, u32[]{:S(2)}) collective-permute-start(bf16[2,256,1536]{2,1,0:T(8,128)(2,1)} %get-tuple-element.101), channel_id=1, source_target_pairs={{0,4},{2,6},{4,0},{6,2},{1,5},{3,7},{5,1},{7,3},{8,12},{10,14},{12... | collective-permute-start | bytes 4718600 | tf_op jit(solution)/shard_map/ppermute | solution.py:628
  563.4 7.2 copy-start.40
  595.9 17.3 %collective-permute-start.17 = (bf16[256,1536]{1,0:T(8,128)(2,1)}, bf16[256,1536]{1,0:T(8,128)(2,1)}, u32[]{:S(2)}, u32[]{:S(2)}) collective-permute-start(bf16[256,1536]{1,0:T(8,128)(2,1)} %get-tuple-element.99), channel_id=1, source_target_pairs={{0,4},{2,6},{4,0},{6,2},{1,5},{3,7},{5,1},{7,3},{8,12},{10,14},{12... | collective-permute-start | bytes 2359304 | tf_op jit(solution)/shard_map/ppermute | solution.py:628
  597.3 15.9 %collective-permute-start.18 = (bf16[256,1536]{1,0:T(8,128)(2,1)S(1)}, bf16[256,1536]{1,0:T(8,128)(2,1)}, u32[]{:S(2)}, u32[]{:S(2)}) collective-permute-start(bf16[256,1536]{1,0:T(8,128)(2,1)S(1)} %get-tuple-element.98), channel_id=1, source_target_pairs={{0,2},{2,0},{4,6},{6,4},{1,3},{3,1},{5,7},{7,5},{8,10},{10,8},{12,... | collective-permute-start | bytes 2359304 | tf_op jit(solution)/shard_map/ppermute | solution.py:628
  599.0 6.1 slice-start.2
  599.1 6.1 slice-start.3
  760.9 5.9 copy-start.1
  (31 other events, 62.4 us)
Sparse Core Ops, SparseCore 0:
  9.6 94.3 all-gather.5
  191.8 116.6 all-gather.3
  396.2 65.0 reduce-scatter.2
  486.6 124.6 reduce-scatter.4

commit v7 on v6

--- a/solution.py
+++ b/solution.py
@@ -41,21 +41,6 @@
     frequency = theta_base ** (-(2.0 / HEAD) * jnp.arange(half_width, dtype=jnp.float32))
     angles = position.astype(jnp.float32)[:, None] * frequency[None, :]
     return (jnp.cos(angles), jnp.sin(angles))
-
-
-def rotate(values, cosine_table, sine_table):
-    half_width = HEAD // 2
-    front_half = values[..., :half_width]
-    behind = values[..., half_width:]
-    cosine_part = cosine_table[:, None, :]
-    sine_part = sine_table[:, None, :]
-    return jnp.concatenate(
-        [
-            front_half * cosine_part - behind * sine_part,
-            behind * cosine_part + front_half * sine_part,
-        ],
-        axis=-1,
-    )
 
 
 def slot_tables(ids, gates, experts, capacity):
@@ -78,67 +63,165 @@
     return hit.astype(jnp.bfloat16), slot_gate
 
 
-def by_batch(rows, heads):
-    return rows.reshape(-1, TOK_MB, KV_HEADS, heads // KV_HEADS, HEAD)
-
-
-def block_scores(queries, key_rows, segment, position):
-    scores = jnp.einsum(
-        "bqhgd,bkhd->bhgqk", queries, key_rows, preferred_element_type=jnp.float32
-    ) * HEAD ** (-0.5)
-    allowed = (segment[:, :, None] == segment[:, None, :]) & (
-        position[:, :, None] >= position[:, None, :]
-    )
-    return jnp.where(allowed[:, None, None], scores, -1e30)
-
-
-def attend_block(queries, key_rows, value_rows, segment, position):
-    queries = by_batch(queries, HEADS)
-    key_rows = by_batch(key_rows, KV_HEADS)[:, :, :, 0]
-    value_rows = by_batch(value_rows, KV_HEADS)[:, :, :, 0]
-    segment = segment.reshape(-1, TOK_MB)
-    position = position.reshape(-1, TOK_MB)
-    masked = block_scores(queries, key_rows, segment, position)
-    row_peak = jnp.max(masked, axis=-1, keepdims=True)
-    weights_exp = jnp.exp(masked - row_peak)
-    row_total = jnp.sum(weights_exp, axis=-1, keepdims=True)
-    probabilities = (weights_exp / row_total).astype(jnp.bfloat16)
-    mixed_rows = jnp.einsum(
-        "bhgqk,bkhd->bqhgd", probabilities, value_rows, preferred_element_type=jnp.float32
-    )
-    return (mixed_rows.reshape(-1, HEADS * HEAD), row_peak + jnp.log(row_total))
-
-
-def attend_back(queries, key_rows, value_rows, segment, position, logsum, grad_mixed):
-    queries = by_batch(queries, HEADS)
-    key_rows = by_batch(key_rows, KV_HEADS)[:, :, :, 0]
-    value_rows = by_batch(value_rows, KV_HEADS)[:, :, :, 0]
-    segment = segment.reshape(-1, TOK_MB)
-    position = position.reshape(-1, TOK_MB)
-    masked = block_scores(queries, key_rows, segment, position)
-    exact_probs = jnp.exp(masked - logsum)
-    probabilities = exact_probs.astype(jnp.bfloat16)
-    grad_heads = by_batch(grad_mixed, HEADS)
-    grad_probs = jnp.einsum(
-        "bqhgd,bkhd->bhgqk", grad_heads, value_rows, preferred_element_type=jnp.float32
-    )
-    grad_values = jnp.einsum(
-        "bhgqk,bqhgd->bkhd", probabilities, grad_heads, preferred_element_type=jnp.float32
-    )
-    grad_scores = (
-        exact_probs * (grad_probs - jnp.sum(grad_probs * exact_probs, axis=-1, keepdims=True))
-    ).astype(jnp.bfloat16)
-    grad_queries = jnp.einsum(
-        "bhgqk,bkhd->bqhgd", grad_scores, key_rows, preferred_element_type=jnp.float32
-    ) * HEAD ** (-0.5)
-    grad_keys = jnp.einsum(
-        "bhgqk,bqhgd->bkhd", grad_scores, queries, preferred_element_type=jnp.float32
-    ) * HEAD ** (-0.5)
-    return (
-        grad_queries.reshape(-1, HEADS, HEAD),
-        grad_keys.reshape(-1, KV_HEADS, HEAD),
-        grad_values.reshape(-1, KV_HEADS, HEAD),
-    )
+def partner(values):
+    half = HEAD // 2
+    lane = lax.broadcasted_iota(jnp.int32, values.shape, 1) % HEAD
+    return jnp.where(
+        lane < half, pltpu.roll(values, 2 * HEAD - half, 1), pltpu.roll(values, half, 1)
+    )
+
+
+def allowed_keys(seg_col_ref, seg_row_ref, first, count):
+    keys = first + count
+    rows = lax.broadcasted_iota(jnp.int32, (count, keys), 0) + first
+    columns = lax.broadcasted_iota(jnp.int32, (count, keys), 1)
+    same = seg_col_ref[0, first : first + count, :] == seg_row_ref[0, :, :keys]
+    return same & (rows >= columns)
+
+
+def soft_weights(queries, keys, allowed):
+    scores = lax.dot_general(
+        queries, keys, (((1,), (1,)), ((), ())), preferred_element_type=jnp.float32
+    )
+    scores = jnp.where(allowed, scores, -1e30)
+    weights = jnp.exp(scores - jnp.max(scores, axis=-1, keepdims=True))
+    return weights * (1.0 / jnp.sum(weights, axis=-1, keepdims=True))
+
+
+def attend_kernel(
+    q_ref, k_ref, v_ref, cos_ref, sin_ref, seg_col_ref, seg_row_ref,
+    q_out, k_out, v_out, mixed_ref
+):
+    cosine, sine = cos_ref[...], sin_ref[...]
+    pair = 2 * HEAD
+    group = HEADS // KV_HEADS
+    for start in range(0, q_ref.shape[1], pair):
+        values = q_ref[:, start : start + pair]
+        turned = (values * cosine + partner(values) * sine).astype(jnp.bfloat16)
+        q_out[:, start : start + pair] = turned * jnp.bfloat16(HEAD**-0.5)
+    values = k_ref[...]
+    k_out[...] = (values * cosine + partner(values) * sine).astype(jnp.bfloat16)
+    v_out[...] = v_ref[...].astype(jnp.bfloat16)
+    block = TOK_MB // 2
+    for first in range(0, TOK_MB, block):
+        rows, keys = slice(first, first + block), slice(0, first + block)
+        allowed = allowed_keys(seg_col_ref, seg_row_ref, first, block)
+        for one in range(2):
+            lanes = slice(one * HEAD, (one + 1) * HEAD)
+            key_rows, value_rows = k_out[keys, lanes], v_out[keys, lanes]
+            for head in range(one * group, (one + 1) * group):
+                at = slice(head * HEAD, (head + 1) * HEAD)
+                weights = soft_weights(q_out[rows, at], key_rows, allowed).astype(jnp.bfloat16)
+                mixed_ref[rows, at] = jnp.dot(
+                    weights, value_rows, preferred_element_type=jnp.float32
+                ).astype(jnp.bfloat16)
+
+
+def attend_back_kernel(
+    q_ref, k_ref, v_ref, grad_ref, cos_ref, sin_ref, seg_col_ref, seg_row_ref,
+    dq_ref, dk_ref, dv_ref, dq_sum, dk_sum, dv_sum
+):
+    cosine, sine = cos_ref[...], sin_ref[...]
+    pair = 2 * HEAD
+    group = HEADS // KV_HEADS
+    block = TOK_MB // 2
+    over_rows = (((0,), (0,)), ((), ()))
+    over_lanes = (((1,), (1,)), ((), ()))
+    for first in range(TOK_MB - block, -1, -block):
+        rows, keys = slice(first, first + block), slice(0, first + block)
+        allowed = allowed_keys(seg_col_ref, seg_row_ref, first, block)
+        for one in range(2):
+            lanes = slice(one * HEAD, (one + 1) * HEAD)
+            key_rows, value_rows = k_ref[keys, lanes], v_ref[keys, lanes]
+            grad_keys = grad_values = 0.0
+            for head in range(one * group, (one + 1) * group):
+                at = slice(head * HEAD, (head + 1) * HEAD)
+                queries, grads = q_ref[rows, at], grad_ref[rows, at]
+                weights = soft_weights(queries, key_rows, allowed)
+                grad_weights = lax.dot_general(
+                    grads, value_rows, over_lanes, preferred_element_type=jnp.float32
+                )
+                grad_values += lax.dot_general(
+                    weights.astype(jnp.bfloat16), grads, over_rows,
+                    preferred_element_type=jnp.float32,
+                )
+                inner = jnp.sum(grad_weights * weights, axis=-1, keepdims=True)
+                grad_scores = (weights * (grad_weights - inner)).astype(jnp.bfloat16)
+                dq_sum[rows, at] = jnp.dot(
+                    grad_scores, key_rows, preferred_element_type=jnp.float32
+                ) * HEAD ** (-0.5)
+                grad_keys += lax.dot_general(
+                    grad_scores, queries, over_rows, preferred_element_type=jnp.float32
+                )
+            if first == TOK_MB - block:
+                dk_sum[keys, lanes] = grad_keys
+                dv_sum[keys, lanes] = grad_values
+            else:
+                dk_sum[keys, lanes] = dk_sum[keys, lanes] + grad_keys
+                dv_sum[keys, lanes] = dv_sum[keys, lanes] + grad_values
+    for start in range(0, q_ref.shape[1], pair):
+        values = dq_sum[:, start : start + pair]
+        dq_ref[:, start : start + pair] = (
+            values * cosine - partner(values) * sine
+        ).astype(jnp.bfloat16)
+    values = dk_sum[...]
+    dk_ref[...] = (values * cosine - partner(values) * sine).astype(jnp.bfloat16)
+    dv_ref[...] = dv_sum[...].astype(jnp.bfloat16)
+
+
+def attend_blocks(row_count):
+    pair = 2 * HEAD
+    wide = pair * (HEADS // KV_HEADS)
+    narrow = pl.BlockSpec((TOK_MB, pair), lambda b, g: (b, g))
+    broad = pl.BlockSpec((TOK_MB, wide), lambda b, g: (b, g))
+    sides = [
+        pl.BlockSpec((TOK_MB, pair), lambda b, g: (b, 0)),
+        pl.BlockSpec((TOK_MB, pair), lambda b, g: (b, 0)),
+        pl.BlockSpec((1, TOK_MB, 1), lambda b, g: (b, 0, 0)),
+        pl.BlockSpec((1, 1, TOK_MB), lambda b, g: (b, 0, 0)),
+    ]
+    return (row_count // TOK_MB, KV_HEADS // 2), narrow, broad, sides
+
+
+def attend(projected, sides):
+    row_count = projected.shape[0]
+    grid, narrow, broad, side_specs = attend_blocks(row_count)
+    q_dim, kv_dim, pair = HEADS * HEAD, KV_HEADS * HEAD, 2 * HEAD
+    key_start, value_start = q_dim // pair, (q_dim + kv_dim) // pair
+    q_shape = jax.ShapeDtypeStruct((row_count, q_dim), jnp.bfloat16)
+    kv_shape = jax.ShapeDtypeStruct((row_count, kv_dim), jnp.bfloat16)
+    return pl.pallas_call(
+        attend_kernel,
+        grid=grid,
+        out_shape=(q_shape, kv_shape, kv_shape, q_shape),
+        in_specs=[
+            broad,
+            pl.BlockSpec((TOK_MB, pair), lambda b, g: (b, key_start + g)),
+            pl.BlockSpec((TOK_MB, pair), lambda b, g: (b, value_start + g)),
+        ]
+        + side_specs,
+        out_specs=(broad, narrow, narrow, broad),
+        name="attend",
+    )(projected, projected, projected, *sides)
+
+
+def attend_back(queries, key_rows, value_rows, grad_mixed, sides):
+    row_count = queries.shape[0]
+    grid, narrow, broad, side_specs = attend_blocks(row_count)
+    shapes = [jax.ShapeDtypeStruct(x.shape, jnp.bfloat16) for x in (queries, key_rows, value_rows)]
+    return pl.pallas_call(
+        attend_back_kernel,
+        grid=grid,
+        out_shape=tuple(shapes),
+        in_specs=[broad, narrow, narrow, broad] + side_specs,
+        out_specs=(broad, narrow, narrow),
+        scratch_shapes=[
+            pltpu.VMEM((TOK_MB, 2 * HEAD * (HEADS // KV_HEADS)), jnp.float32),
+            pltpu.VMEM((TOK_MB, 2 * HEAD), jnp.float32),
+            pltpu.VMEM((TOK_MB, 2 * HEAD), jnp.float32),
+        ],
+        name="attend_back",
+    )(queries, key_rows, value_rows, grad_mixed, *sides)
 
 
 def pick(rows, index):
@@ -609,8 +692,6 @@
     tok_dev = permutation.shape[0]
     model_width = tokens.shape[1]
     peer_rows = tok_dev // device_count
-    q_dim = HEADS * HEAD
-    kv_dim = KV_HEADS * HEAD
     positions = jnp.arange(tok_dev, dtype=jnp.int32)
     expert_count = expert_in.shape[2] * device_count // FF_E
     capacity = TOK_MB * TOPK // expert_count
@@ -696,19 +777,13 @@
     cosine_table, sine_table = rope_tables(position)
     if lo_count == 4:
         segment = hold(segment, grad_blocks[1][0], grad_blocks[2][0])
-    queries = rotate(
-        projected[:, :q_dim].reshape(tok_dev, HEADS, HEAD), cosine_table, sine_table
-    ).astype(jnp.bfloat16)
-    key_rows = rotate(
-        projected[:, q_dim : q_dim + kv_dim].reshape(tok_dev, KV_HEADS, HEAD),
-        cosine_table,
-        sine_table,
-    ).astype(jnp.bfloat16)
-    value_rows = (
-        projected[:, q_dim + kv_dim :].reshape(tok_dev, KV_HEADS, HEAD).astype(jnp.bfloat16)
-    )
-    mixed_part, logsum = attend_block(queries, key_rows, value_rows, segment, position)
-    mixed_rows = mixed_part.astype(jnp.bfloat16)
+    sides = (
+        jnp.tile(cosine_table, (1, 4)),
+        jnp.concatenate([-sine_table, sine_table] * 2, axis=1),
+        segment.reshape(-1, TOK_MB, 1),
+        segment.reshape(-1, 1, TOK_MB),
+    )
+    queries, key_rows, value_rows, mixed_rows = attend(projected, sides)
     attended = jnp.dot(mixed_rows, out_full, preferred_element_type=jnp.float32)
     residual = rows_in + attended
     scale_two = lax.rsqrt(jnp.mean(residual * residual, axis=1, keepdims=True) + epsilon)
@@ -830,19 +905,9 @@
     grad_mixed = jnp.einsum(
         "nd,qd->nq", grad_attended, out_full, preferred_element_type=jnp.float32
     ).astype(jnp.bfloat16)
-    grad_queries, grad_keys, grad_values = attend_back(
-        queries, key_rows, value_rows, segment, position, logsum, grad_mixed
-    )
-    grad_queries = rotate(grad_queries, cosine_table, -sine_table)
-    grad_keys = rotate(grad_keys, cosine_table, -sine_table)
     grad_projected = jnp.concatenate(
-        [
-            grad_queries.reshape(tok_dev, q_dim),
-            grad_keys.reshape(tok_dev, kv_dim),
-            grad_values.reshape(tok_dev, kv_dim),
-        ],
-        axis=1,
-    ).astype(jnp.bfloat16)
+        attend_back(queries, key_rows, value_rows, grad_mixed, sides), axis=1
+    )
     if lo_count == 4:
         normed = hold(normed, *ahead_parts[1:3])
     grad_qkv_weight = jnp.einsum(

time: 779 us -> 778 us (level)
  Pallas kernels: 337 us -> 409 us
  local copies, waits for them, and re-layouts: 114 us -> 79.7 us
  matrix products: 165 us -> 148 us
  other arithmetic: 59.4 us -> 42.9 us
    pallas_call x0 -> x2, Pallas kernels: none -> 70.3 us  [the longest x1 41.4 us: attend_back(): pl.pallas_call(attend_back_kernel, grid=grid, out_shape=tuple(shapes), in...]
    dot_general x6 -> x0, matrix products: 26.3 us -> none  [the longest x1 7.1 us: attend_back(): jnp.einsum('bqhgd,bkhd->bhgqk', grad_heads, value_rows, preferred_element...]
    slice x7 -> x1, local copies, waits for them, and re-layouts: 12.1 us -> 0.22 us  [the longest x2 5.37 us: shards(): projected[:, :q_dim].reshape(tok_dev, HEADS, HEAD)]
    concatenate x5 -> x1, local copies, waits for them, and re-layouts: 8.15 us -> 0.04 us  [shards(): jnp.concatenate(attend_back(queries, key_rows, value_rows, grad_mixed, si...]
    unnamed x153 -> x110, local copies, waits for them, and re-layouts: 20.3 us -> 16 us
  transfers between devices with their start and end apart: 24 -> 24, of which waited for: 11 -> 10; matrix products, arithmetic and copies ran while one was open for 39% -> 30% of each run, Pallas kernels for 41% -> 50%
where the time goes in v7:
time: 778 us; the launch traced here: 772 us
  Pallas kernels  409 us (53%)
  matrix products  148 us (19%)
  local copies, waits for them, and re-layouts  79.7 us (10%)
  waiting for transfers between devices  47.5 us (6%)
  other arithmetic  42.9 us (6%)
  starting transfers between devices  29.5 us (4%)
  between operations  15 us (2%)
    pallas_call x1, Pallas kernels, opening(): pl.pallas_call(functools.partial(opening_kernel, sizes), out_shape=(jax.S...  154 us
    pallas_call x1, Pallas kernels, closing(): pl.pallas_call(functools.partial(closing_kernel, sizes), out_shape=(jax.S...  128 us
    ppermute x19, waiting for transfers between devices, swap(): return lax.ppermute(block, 'lo', [(i, i ^ step) for i in range(lo_count)])  46.3 us
    pallas_call x1, Pallas kernels, attend_back(): pl.pallas_call(attend_back_kernel, grid=grid, out_shape=tuple(shapes), in...  41.4 us
    pallas_call x10, Pallas kernels, dispatch(): pl.pallas_call(functools.partial(dispatch_kernel, weight is not None), gr...  33.9 us
    pallas_call x1, Pallas kernels, attend(): pl.pallas_call(attend_kernel, grid=grid, out_shape=(q_shape, kv_shape, kv...  28.9 us
    gather x8, local copies, waits for them, and re-layouts, pick(): return jnp.take(rows, index, axis=0, mode='clip')  25.8 us
    pallas_call x1, Pallas kernels, middle(): pl.pallas_call(middle_kernel, grid=(count, row_count // tile), out_shape=...  23.6 us
  transfers between devices with their start and end apart: 24, of which 10 were waited for; matrix products, arithmetic and copies ran while one was open for 30% of the time, Pallas kernels for 50%

profile of v7, /device:TPU:12, one launch (start us, length us, event | category | flops | bytes accessed | tf_op | source)
XLA Modules:
  0.0 771.8 jit_solution(3979025611469956445)
XLA Ops:
  16.6 6.0 all-to-all-start
  25.6 1.9 concatenate.22.shard_ref
  30.0 2.9 gather_fusion
  32.9 2.9 gather_fusion.1
  35.9 153.5 %opening.1 = (bf16[32,16,1536]{2,1,0:T(8,128)(2,1)}, bf16[32,16,1536]{2,1,0:T(8,128)(2,1)}, bf16[4,4,2,48,4224]{4,3,2,1,0:T(8,128)(2,1)}) custom-call(bf16[32,16,1536]{2,1,0:T(8,128)(2,1)} %bitcast.165, bf16[32,16,1536]{2,1,0:T(8,128)(2,1)} %bitcast.166, bf16[48,4224]{1,0:T(8,128)(2,1)} %concatenate.22.shard_ref), custom_call_target="tpu_custom_call" | custom-call | tf_op jit(solution)/shard_map/opening/pallas_call | solution.py:415
  189.4 2.3 all_gather_reshape.3
  195.9 2.3 gather_fusion.2
  198.2 3.4 collective-permute-start.3
  201.6 3.1 collective-permute-start.4
  204.7 5.7 gather_fusion.3
  215.2 9.8 %fusion.9.q_ref.k_ref.v_ref = f32[512,2560]{1,0:T(8,128)} fusion(bf16[512,1536]{1,0:T(8,128)(2,1)S(1)} %fusion.25.refs_0_, bf16[1536,4224]{1,0:T(8,128)(2,1)} %bitcast.185), kind=kOutput, calls=%fused_computation.25 | convolution fusion | flops 4026531840 | bytes 14680064 | tf_op jit(solution)/shard_map/dot_general | solution.py:776
  225.0 11.6 %collective-permute-done.3.refs_1_.rows_ref = bf16[512,1536]{1,0:T(8,128)(2,1)} collective-permute-done((bf16[512,1536]{1,0:T(8,128)(2,1)S(1)}, bf16[512,1536]{1,0:T(8,128)(2,1)}, u32[]{:S(2)}, u32[]{:S(2)}) %collective-permute-start.3) | collective-permute-done | bytes 1572896 | tf_op jit(solution)/shard_map/ppermute | solution.py:709
  236.6 2.8 collective-permute-done.4.refs_2_.rows_ref
  241.0 2.1 slice.220
  243.1 1.7 collective-permute-start.5
  244.8 2.1 slice.221
  247.3 28.9 %attend.1 = (bf16[512,1536]{1,0:T(8,128)(2,1)}, bf16[512,512]{1,0:T(8,128)(2,1)}, bf16[512,512]{1,0:T(8,128)(2,1)}, bf16[512,1536]{1,0:T(8,128)(2,1)}) custom-call(f32[512,2560]{1,0:T(8,128)} %fusion.9.q_ref.k_ref.v_ref, f32[512,2560]{1,0:T(8,128)} %fusion.9.q_ref.k_ref.v_ref, f32[512,2560]{1,0:T(8,128)} %fusion.9.q_ref.k_ref.v_ref, ...), custom_call_target="tpu_custom_call" | custom-call | tf_op jit(solution)/shard_map/attend/pallas_call | solution.py:193
  276.2 5.1 multiply_reduce_fusion.2
  289.8 2.0 copy.147.refs_0_
  291.8 2.3 fusion.18.choose_ref
  294.1 3.7 dispatch.15.refs_0_
  297.8 3.6 dispatch.10.refs_1_
  301.4 3.6 dispatch.11.refs_1_
  305.1 3.8 dispatch.12.refs_1_
  308.8 3.0 dispatch.13.refs_1_
  311.9 3.0 dispatch.14
  314.9 6.9 collective-permute-done.8.rows_ref
  325.7 13.7 %convert_bitcast_fusion.grad_ref = bf16[4,2,1024,256]{3,2,1,0:T(8,128)(2,1)} fusion(bf16[4,1024,1536,1]{2,1,3,0:T(8,128)(2,1)} %bitcast.153, bf16[4,2,256,1536]{3,2,1,0:T(8,128)(2,1)} %bitcast.192), kind=kOutput, calls=%fused_computation.33 | convolution fusion | flops 6444548096 | bytes 23068672 | tf_op jit(solution)/shard_map/erd,ekfd->ekrf/dot_general | solution.py:818
  340.6 1.8 collective-permute-done.9.rows_ref
  342.4 3.6 dispatch.16.refs_0_
  346.0 3.6 dispatch.17.refs_0_
  349.6 3.0 dispatch.18.refs_0_
  352.6 2.9 dispatch.19
  355.5 23.6 %middle.1 = (bf16[4,2,1024,256]{3,2,1,0:T(8,128)(2,1)}, bf16[4,2,1024,512]{3,2,1,0:T(8,128)(2,1)}) custom-call(bf16[4,1024,1536]{2,1,0:T(8,128)(2,1)} %bitcast.151, bf16[4,2,1536,512]{3,2,1,0:T(8,128)(2,1)} %bitcast.160, bf16[4,2,1024,256]{3,2,1,0:T(8,128)(2,1)} %convert_bitcast_fusion.grad_ref), custom_call_target="tpu_custom_call" | custom-call | tf_op jit(solution)/shard_map/middle/pallas_call | solution.py:655
  379.1 13.8 %convolution_convert_fusion.3 = bf16[4,2,256,1536]{3,2,1,0:T(8,128)(2,1)} fusion(bf16[4,2,1024,256]{3,2,1,0:T(8,128)(2,1)} %get-tuple-element.76, bf16[4,1024,1536,1]{2,1,3,0:T(8,128)(2,1)} %bitcast.154), kind=kOutput, calls=%fused_computation.32 | convolution fusion | flops 6445596672 | bytes 23068672 | tf_op jit(solution)/shard_map/ekrf,erd->ekfd/dot_general | solution.py:828
  393.0 20.7 %bitcast_convert_fusion = bf16[4,1024,1536]{2,1,0:T(8,128)(2,1)} fusion(bf16[4,2,1024,512]{3,2,1,0:T(8,128)(2,1)} %get-tuple-element.78.refs_0_, bf16[4,2,1536,512]{3,2,1,0:T(8,128)(2,1)} %bitcast.161), kind=kOutput, calls=%fused_computation.10 | convolution fusion | flops 12891193344 | bytes 33554432 | tf_op jit(solution)/shard_map/ekrf,ekdf->erd/dot_general | solution.py:838
  413.7 8.2 %bitcast_convert_fusion.1 = bf16[8,256,1536]{2,1,0:T(8,128)(2,1)S(1)} fusion(bf16[4,8,128,1536]{3,2,1,0:T(8,128)(2,1)} %bitcast.195, s32[8,4,256]{2,1,0:T(4,128)S(1)} %copy.141, pred[8,4,256]{2,1,0:T(4,128)(4,1)S(1)} %bitcast.175), kind=kOutput, calls=%fused_computation.15 | convolution fusion | flops 3226468352 | bytes 18915328 | tf_op jit(solution)/shard_map/becr,ebcd->brd/dot_general | solution.py:843
  421.9 2.4 fusion.66
  424.3 2.7 copy-done.14
  428.7 12.6 %fusion.1 = bf16[4,1024,1536]{2,1,0:T(8,128)(2,1)} fusion(bf16[4,2,1024,256]{3,2,1,0:T(8,128)(2,1)S(1)} %copy-done.46, bf16[4,2,256,1536]{3,2,1,0:T(8,128)(2,1)} %bitcast.193, f32[4,1024]{1,0:T(4,128)S(1)} %bitcast.179), kind=kOutput, calls=%fused_computation.12 | convolution fusion | flops 6455033856 | bytes 23085056 | tf_op jit(solution)/shard_map/ekrf,ekfd->erd/dot_general | solution.py:881
  441.3 10.9 %bitcast_convert_fusion.2.refs_1_ = bf16[8,256,1536]{2,1,0:T(8,128)(2,1)} fusion(bf16[4,8,128,1536]{3,2,1,0:T(8,128)(2,1)} %bitcast.194, s32[8,4,256]{2,1,0:T(4,128)S(1)} %copy.141, pred[8,4,256]{2,1,0:T(4,128)(4,1)S(1)} %bitcast.176), kind=kOutput, calls=%fused_computation.16 | convolution fusion | flops 3226468352 | bytes 18915328 | tf_op jit(solution)/shard_map/becr,ebcd->brd/dot_general | solution.py:843
  452.2 7.9 %collective-permute-done.11.refs_2_ = bf16[2,256,1536]{2,1,0:T(8,128)(2,1)S(1)} collective-permute-done((bf16[2,256,1536]{2,1,0:T(8,128)(2,1)}, bf16[2,256,1536]{2,1,0:T(8,128)(2,1)S(1)}, u32[]{:S(2)}, u32[]{:S(2)}) %collective-permute-start.11) | collective-permute-done | bytes 1572896 | tf_op jit(solution)/shard_map/ppermute | solution.py:709
  462.4 22.2 %convolution_convert_fusion = bf16[4,2,512,1536]{3,2,1,0:T(8,128)(2,1)} fusion(bf16[4,2,1024,512]{3,2,1,0:T(8,128)(2,1)} %hold.9, bf16[4,1024,1536,1]{2,1,3,0:T(8,128)(2,1)} %bitcast.152), kind=kOutput, calls=%fused_computation.13 | convolution fusion | flops 12891193344 | bytes 33554432 | tf_op jit(solution)/shard_map/ekrf,erd->ekfd/dot_general | solution.py:886
  486.5 1.8 fusion.46
  491.4 12.2 %collective-permute-done.13 = bf16[256,1536]{1,0:T(8,128)(2,1)S(1)} collective-permute-done((bf16[256,1536]{1,0:T(8,128)(2,1)S(1)}, bf16[256,1536]{1,0:T(8,128)(2,1)S(1)}, u32[]{:S(2)}, u32[]{:S(2)}) %collective-permute-start.13) | collective-permute-done | bytes 786464 | tf_op jit(solution)/shard_map/ppermute | solution.py:709
  504.7 4.7 fusion.65
  515.4 7.3 fusion.38.grad_ref
  522.7 41.4 %attend_back.1 = (bf16[512,1536]{1,0:T(8,128)(2,1)}, bf16[512,512]{1,0:T(8,128)(2,1)}, bf16[512,512]{1,0:T(8,128)(2,1)}) custom-call(bf16[512,1536]{1,0:T(8,128)(2,1)} %get-tuple-element.80.q_ref, bf16[512,512]{1,0:T(8,128)(2,1)} %get-tuple-element.81.k_ref, bf16[512,512]{1,0:T(8,128)(2,1)} %get-tuple-element.82.v_ref, bf16[512,1536]{1,0:T(8,128)(2,1)} %fusion.38.grad_ref, ...), custom_call_target="tpu_custom_call" | custom-call | tf_op jit(solution)/shard_map/attend_back/pallas_call | solution.py:212
  566.5 10.5 %fusion.34 = (f32[512]{0:T(512)S(1)}, bf16[1536]{0:T(1024)(128)(2,1)S(1)}, f32[512,1536]{1,0:T(8,128)}) fusion(bf16[512,1536]{1,0:T(8,128)(2,1)S(1)} %copy-done.10, f32[1536]{0:T(1024)S(1)} %copy-done.36, f32[512]{0:T(512)S(1)} %copy-done.42, bf16[512,2560]{1,0:T(8,128)(2,1)S(1)} %constant_dynamic-update-slice_fusion.8, bf16[1536,4224]{1,0:T(8,128)(2,1)} %bitcast.188), kind=kOutput, calls=%fused_computation.53 | convolution fusion | flops 4032034816 | bytes 15217664 | tf_op jit(solution)/shard_map/nc,dc->nd/dot_general | solution.py:916
  577.3 4.0 fusion.30
  581.3 3.2 gather_fusion.5
  584.6 6.2 convolution_convert_fusion.2
  590.8 3.1 fusion.48
  594.9 6.7 convolution_convert_fusion.1
  601.6 5.6 fusion.2
  607.3 2.6 convert_element_type.240
  609.9 2.6 bitcast_add_fusion.1
  613.5 2.9 gather_fusion.4
  616.4 127.9 %closing.1 = (bf16[32,16,1536]{2,1,0:T(8,128)(2,1)}, bf16[32,16,1536]{2,1,0:T(8,128)(2,1)}, f32[48,4224]{1,0:T(8,128)}) custom-call(bf16[32,16,1536]{2,1,0:T(8,128)(2,1)} %bitcast.168, bf16[32,16,1536]{2,1,0:T(8,128)(2,1)} %bitcast.167, bf16[4,4,2,48,4224]{4,3,2,1,0:T(8,128)(2,1)} %bitcast.159), custom_call_target="tpu_custom_call" | custom-call | tf_op jit(solution)/shard_map/closing/pallas_call | solution.py:569
  744.4 2.0 slice.185
  748.0 2.9 gather_fusion.7
  751.0 2.9 gather_fusion.6
  755.4 3.5 reshape.262
  758.9 5.9 copy.170
  (227 shorter events, 63.1 us)
Async XLA Ops:
  7.2 22.8 %copy-start = (bf16[512,1536]{1,0:T(8,128)(2,1)S(1)}, bf16[512,1536]{1,0:T(8,128)(2,1)}, u32[]{:S(2)}) copy-start(bf16[512,1536]{1,0:T(8,128)(2,1)} %param.12) | copy-start | bytes 4718596
  7.2 318.5 %all-gather.6.cloned.1.call-start = ((), (), s32[]{:S(2)}) async-start(), calls=%async_computation.6 | async-start | bytes 7077888 | tf_op jit(solution)/shard_map/all_gather | solution.py:770
  9.4 19.9 %collective-permute-start = (f32[512,16]{0,1:T(8,128)S(1)}, f32[512,16]{0,1:T(8,128)S(1)}, u32[]{:S(2)}, u32[]{:S(2)}) collective-permute-start(f32[512,16]{0,1:T(8,128)S(1)} %pad_maximum_fusion.2), channel_id=1, source_target_pairs={{0,2},{2,0},{4,6},{6,4},{1,3},{3,1},{5,7},{7,5},{8,10},{10,8},{12,... | collective-permute-start | bytes 98312 | tf_op jit(solution)/shard_map/ppermute | solution.py:709
  10.9 18.4 %collective-permute-start.1 = (f32[512,16]{0,1:T(8,128)S(1)}, f32[512,16]{0,1:T(8,128)S(1)}, u32[]{:S(2)}, u32[]{:S(2)}) collective-permute-start(f32[512,16]{0,1:T(8,128)S(1)} %pad_maximum_fusion.2), channel_id=1, source_target_pairs={{0,6},{2,4},{4,2},{6,0},{1,7},{3,5},{5,3},{7,1},{8,14},{10,12},{12... | collective-permute-start | bytes 98312 | tf_op jit(solution)/shard_map/ppermute | solution.py:709
  11.3 18.0 %collective-permute-start.2 = (f32[512,16]{0,1:T(8,128)S(1)}, f32[512,16]{0,1:T(8,128)S(1)}, u32[]{:S(2)}, u32[]{:S(2)}) collective-permute-start(f32[512,16]{0,1:T(8,128)S(1)} %pad_maximum_fusion.2), channel_id=1, source_target_pairs={{0,4},{2,6},{4,0},{6,2},{1,5},{3,7},{5,1},{7,3},{8,12},{10,14},{12... | collective-permute-start | bytes 98312 | tf_op jit(solution)/shard_map/ppermute | solution.py:709
  16.6 11.3 %all-to-all-start = ((s32[32,1,16]{2,1,0:T(1,128)}), s32[32,1,16]{2,1,0:T(1,128)S(1)}, u32[]{:S(2)}, u32[]{:S(2)}) async-start(s32[32,1,16]{2,1,0:T(1,128)} %bitcast.2), calls=%async_computation | async-start | bytes 32768 | tf_op jit(solution)/shard_map/all_to_all | solution.py:727
  22.6 332.9 %all-gather.4.cloned.1.call-start = ((), (), s32[]{:S(2)}) async-start(), calls=%async_computation.3 | async-start | bytes 14155776 | tf_op jit(solution)/shard_map/all_gather | solution.py:767
  30.0 2.9 copy-start.2
  35.9 153.6 %copy-start.27 = (bf16[1536,2,256]{2,1,0:T(2,128)(2,1)S(1)}, bf16[1536,2,256]{2,1,0:T(2,128)(2,1)}, u32[]{:S(2)}) copy-start(bf16[1536,2,256]{2,1,0:T(2,128)(2,1)} %param.22) | copy-start | bytes 4718596
  189.4 2.4 copy-start.45
  189.4 6.4 copy-start.3
  191.8 415.5 %reduce-scatter.3.cloned.1.call-start = ((), (), s32[]{:S(2)}) async-start(), calls=%async_computation.4 | async-start | bytes 7077888 | tf_op jit(solution)/shard_map/reduce_scatter | solution.py:832
  198.2 6.5 copy-start.11
  198.2 38.4 %collective-permute-start.3 = (bf16[512,1536]{1,0:T(8,128)(2,1)S(1)}, bf16[512,1536]{1,0:T(8,128)(2,1)}, u32[]{:S(2)}, u32[]{:S(2)}) collective-permute-start(bf16[512,1536]{1,0:T(8,128)(2,1)S(1)} %gather_fusion.2), channel_id=1, source_target_pairs={{0,2},{2,0},{4,6},{6,4},{1,3},{3,1},{5,7},{7,5},{8,10},{10,8},{12,... | collective-permute-start | bytes 4718600 | tf_op jit(solution)/shard_map/ppermute | solution.py:709
  201.6 37.8 %collective-permute-start.4 = (bf16[512,1536]{1,0:T(8,128)(2,1)S(1)}, bf16[512,1536]{1,0:T(8,128)(2,1)}, u32[]{:S(2)}, u32[]{:S(2)}) collective-permute-start(bf16[512,1536]{1,0:T(8,128)(2,1)S(1)} %gather_fusion.2), channel_id=1, source_target_pairs={{0,4},{2,6},{4,0},{6,2},{1,5},{3,7},{5,1},{7,3},{8,12},{10,14},{12... | collective-permute-start | bytes 4718600 | tf_op jit(solution)/shard_map/ppermute | solution.py:709
  210.4 65.8 %copy-start.9 = (bf16[512,1536]{1,0:T(8,128)(2,1)}, bf16[512,1536]{1,0:T(8,128)(2,1)S(1)}, u32[]{:S(2)}) copy-start(bf16[512,1536]{1,0:T(8,128)(2,1)S(1)} %gather_fusion.3) | copy-start | bytes 4718596
  213.8 67.6 %copy-start.33 = (f32[1536]{0:T(1024)}, f32[1536]{0:T(1024)S(1)}, u32[]{:S(2)}) copy-start(f32[1536]{0:T(1024)S(1)} %get-tuple-element.108) | copy-start | bytes 18436
  215.2 9.8 %copy-start.15 = (bf16[512,1536]{1,0:T(8,128)(2,1)}, bf16[512,1536]{1,0:T(8,128)(2,1)S(1)}, u32[]{:S(2)}) copy-start(bf16[512,1536]{1,0:T(8,128)(2,1)S(1)} %fusion.25.refs_0_) | copy-start | bytes 4718596
  243.1 41.4 %collective-permute-start.5 = (bf16[256,1536]{1,0:T(8,128)(2,1)}, bf16[256,1536]{1,0:T(8,128)(2,1)S(1)}, u32[]{:S(2)}, u32[]{:S(2)}) collective-permute-start(bf16[256,1536]{1,0:T(8,128)(2,1)} %slice.220), channel_id=1, source_target_pairs={{0,4},{2,6},{4,0},{6,2},{1,5},{3,7},{5,1},{7,3},{8,12},{10,14},{12... | collective-permute-start | bytes 2359304 | tf_op jit(solution)/shard_map/ppermute | solution.py:709
  246.9 37.6 %collective-permute-start.6 = (bf16[256,1536]{1,0:T(8,128)(2,1)}, bf16[256,1536]{1,0:T(8,128)(2,1)S(1)}, u32[]{:S(2)}, u32[]{:S(2)}) collective-permute-start(bf16[256,1536]{1,0:T(8,128)(2,1)} %slice.221), channel_id=1, source_target_pairs={{0,2},{2,0},{4,6},{6,4},{1,3},{3,1},{5,7},{7,5},{8,10},{10,8},{12,... | collective-permute-start | bytes 2359304 | tf_op jit(solution)/shard_map/ppermute | solution.py:709
  281.3 1.7 copy-start.6
  281.3 3.2 copy-start.37
  284.5 3.8 copy-start.32
  286.3 35.4 %collective-permute-start.8 = (bf16[512,1536]{1,0:T(8,128)(2,1)}, bf16[512,1536]{1,0:T(8,128)(2,1)S(1)}, u32[]{:S(2)}, u32[]{:S(2)}) collective-permute-start(bf16[512,1536]{1,0:T(8,128)(2,1)} %hold.7.rows_ref), channel_id=1, source_target_pairs={{0,4},{2,6},{4,0},{6,2},{1,5},{3,7},{5,1},{7,3},{8,12},{10,14},{12... | collective-permute-start | bytes 4718600 | tf_op jit(solution)/shard_map/ppermute | solution.py:709
  286.7 37.5 %collective-permute-start.7 = (bf16[512,1536]{1,0:T(8,128)(2,1)}, bf16[512,1536]{1,0:T(8,128)(2,1)S(1)}, u32[]{:S(2)}, u32[]{:S(2)}) collective-permute-start(bf16[512,1536]{1,0:T(8,128)(2,1)} %hold.7.rows_ref), channel_id=1, source_target_pairs={{0,2},{2,0},{4,6},{6,4},{1,3},{3,1},{5,7},{7,5},{8,10},{10,8},{12,... | collective-permute-start | bytes 4718600 | tf_op jit(solution)/shard_map/ppermute | solution.py:709
  321.8 17.7 %copy-start.23 = (bf16[512,1536]{1,0:T(8,128)(2,1)}, bf16[512,1536]{1,0:T(8,128)(2,1)S(1)}, u32[]{:S(2)}) copy-start(bf16[512,1536]{1,0:T(8,128)(2,1)S(1)} %collective-permute-done.8.rows_ref) | copy-start | bytes 4718596
  322.8 17.8 %collective-permute-start.10 = (bf16[256,1536]{1,0:T(8,128)(2,1)}, bf16[256,1536]{1,0:T(8,128)(2,1)}, u32[]{:S(2)}, u32[]{:S(2)}) collective-permute-start(bf16[256,1536]{1,0:T(8,128)(2,1)} %slice.223), channel_id=1, source_target_pairs={{0,2},{2,0},{4,6},{6,4},{1,3},{3,1},{5,7},{7,5},{8,10},{10,8},{12,... | collective-permute-start | bytes 2359304 | tf_op jit(solution)/shard_map/ppermute | solution.py:709
  324.1 15.3 %copy-start.24 = (bf16[512,1536]{1,0:T(8,128)(2,1)}, bf16[512,1536]{1,0:T(8,128)(2,1)S(1)}, u32[]{:S(2)}) copy-start(bf16[512,1536]{1,0:T(8,128)(2,1)S(1)} %collective-permute-done.7.rows_ref) | copy-start | bytes 4718596
  325.2 17.3 %collective-permute-start.9 = (bf16[256,1536]{1,0:T(8,128)(2,1)}, bf16[256,1536]{1,0:T(8,128)(2,1)}, u32[]{:S(2)}, u32[]{:S(2)}) collective-permute-start(bf16[256,1536]{1,0:T(8,128)(2,1)} %slice.222), channel_id=1, source_target_pairs={{0,4},{2,6},{4,0},{6,2},{1,5},{3,7},{5,1},{7,3},{8,12},{10,14},{12... | collective-permute-start | bytes 2359304 | tf_op jit(solution)/shard_map/ppermute | solution.py:709
  393.0 362.5 %reduce-scatter.5.cloned.1.call-start = ((), (), s32[]{:S(2)}) async-start(), calls=%async_computation.5 | async-start | bytes 14155776 | tf_op jit(solution)/shard_map/reduce_scatter | solution.py:889
  421.9 5.1 copy-start.14
  421.9 6.8 copy-start.46
  427.0 33.1 %collective-permute-start.11 = (bf16[2,256,1536]{2,1,0:T(8,128)(2,1)}, bf16[2,256,1536]{2,1,0:T(8,128)(2,1)S(1)}, u32[]{:S(2)}, u32[]{:S(2)}) collective-permute-start(bf16[2,256,1536]{2,1,0:T(8,128)(2,1)} %get-tuple-element.120), channel_id=1, source_target_pairs={{0,2},{2,0},{4,6},{6,4},{1,3},{3,1},{5,7},{7,5},{8,10},{10,8},{12,... | collective-permute-start | bytes 4718600 | tf_op jit(solution)/shard_map/ppermute | solution.py:709
  427.9 33.1 %collective-permute-start.12 = (bf16[2,256,1536]{2,1,0:T(8,128)(2,1)}, bf16[2,256,1536]{2,1,0:T(8,128)(2,1)S(1)}, u32[]{:S(2)}, u32[]{:S(2)}) collective-permute-start(bf16[2,256,1536]{2,1,0:T(8,128)(2,1)} %get-tuple-element.119), channel_id=1, source_target_pairs={{0,4},{2,6},{4,0},{6,2},{1,5},{3,7},{5,1},{7,3},{8,12},{10,14},{12... | collective-permute-start | bytes 4718600 | tf_op jit(solution)/shard_map/ppermute | solution.py:709
  484.6 1.4 copy-start.19
  484.6 1.9 copy-start.21
  486.5 4.1 copy-start.44
  486.5 4.7 copy-start.40
  488.2 15.4 %collective-permute-start.13 = (bf16[256,1536]{1,0:T(8,128)(2,1)S(1)}, bf16[256,1536]{1,0:T(8,128)(2,1)S(1)}, u32[]{:S(2)}, u32[]{:S(2)}) collective-permute-start(bf16[256,1536]{1,0:T(8,128)(2,1)S(1)} %get-tuple-element.118), channel_id=1, source_target_pairs={{0,4},{2,6},{4,0},{6,2},{1,5},{3,7},{5,1},{7,3},{8,12},{10,14},{12... | collective-permute-start | bytes 2359304 | tf_op jit(solution)/shard_map/ppermute | solution.py:709
  489.5 15.2 %collective-permute-start.14 = (bf16[256,1536]{1,0:T(8,128)(2,1)S(1)}, bf16[256,1536]{1,0:T(8,128)(2,1)S(1)}, u32[]{:S(2)}, u32[]{:S(2)}) collective-permute-start(bf16[256,1536]{1,0:T(8,128)(2,1)S(1)} %get-tuple-element.117), channel_id=1, source_target_pairs={{0,2},{2,0},{4,6},{6,4},{1,3},{3,1},{5,7},{7,5},{8,10},{10,8},{12,... | collective-permute-start | bytes 2359304 | tf_op jit(solution)/shard_map/ppermute | solution.py:709
  504.7 7.0 copy-start.17
  504.7 7.0 copy-start.22
  509.4 81.4 %collective-permute-start.15 = (bf16[2,256,1536]{2,1,0:T(8,128)(2,1)}, bf16[2,256,1536]{2,1,0:T(8,128)(2,1)}, u32[]{:S(2)}, u32[]{:S(2)}) collective-permute-start(bf16[2,256,1536]{2,1,0:T(8,128)(2,1)} %get-tuple-element.116), channel_id=1, source_target_pairs={{0,2},{2,0},{4,6},{6,4},{1,3},{3,1},{5,7},{7,5},{8,10},{10,8},{12,... | collective-permute-start | bytes 4718600 | tf_op jit(solution)/shard_map/ppermute | solution.py:709
  511.0 1.9 copy-start.7
  511.0 1.9 copy-start.34
  511.0 1.9 copy-start.38
  511.0 79.8 %collective-permute-start.16 = (bf16[2,256,1536]{2,1,0:T(8,128)(2,1)}, bf16[2,256,1536]{2,1,0:T(8,128)(2,1)}, u32[]{:S(2)}, u32[]{:S(2)}) collective-permute-start(bf16[2,256,1536]{2,1,0:T(8,128)(2,1)} %get-tuple-element.115), channel_id=1, source_target_pairs={{0,4},{2,6},{4,0},{6,2},{1,5},{3,7},{5,1},{7,3},{8,12},{10,14},{12... | collective-permute-start | bytes 4718600 | tf_op jit(solution)/shard_map/ppermute | solution.py:709
  515.4 7.3 copy-start.13
  564.1 1.7 copy-start.30
  564.2 1.8 copy-start.29
  564.2 2.3 copy-start.10
  564.2 2.3 copy-start.36
  564.2 2.3 copy-start.42
  566.5 10.5 %copy-start.28 = (bf16[512,2560]{1,0:T(8,128)(2,1)}, bf16[512,2560]{1,0:T(8,128)(2,1)S(1)}, u32[]{:S(2)}) copy-start(bf16[512,2560]{1,0:T(8,128)(2,1)S(1)} %constant_dynamic-update-slice_fusion.8) | copy-start | bytes 7864324
  581.3 3.2 copy-start.47
  593.9 16.0 %collective-permute-start.17 = (bf16[256,1536]{1,0:T(8,128)(2,1)}, bf16[256,1536]{1,0:T(8,128)(2,1)}, u32[]{:S(2)}, u32[]{:S(2)}) collective-permute-start(bf16[256,1536]{1,0:T(8,128)(2,1)} %get-tuple-element.113), channel_id=1, source_target_pairs={{0,4},{2,6},{4,0},{6,2},{1,5},{3,7},{5,1},{7,3},{8,12},{10,14},{12... | collective-permute-start | bytes 2359304 | tf_op jit(solution)/shard_map/ppermute | solution.py:709
  594.6 15.3 %collective-permute-start.18 = (bf16[256,1536]{1,0:T(8,128)(2,1)S(1)}, bf16[256,1536]{1,0:T(8,128)(2,1)}, u32[]{:S(2)}, u32[]{:S(2)}) collective-permute-start(bf16[256,1536]{1,0:T(8,128)(2,1)S(1)} %get-tuple-element.112), channel_id=1, source_target_pairs={{0,2},{2,0},{4,6},{6,4},{1,3},{3,1},{5,7},{7,5},{8,10},{10,8},{12,... | collective-permute-start | bytes 2359304 | tf_op jit(solution)/shard_map/ppermute | solution.py:709
  594.9 6.7 slice-start
  594.9 6.7 slice-start.1
  607.3 2.6 copy-start.16
  609.9 2.8 copy-start.8
  744.4 3.7 copy-start.5
  748.0 2.9 copy-start.4
  758.9 5.9 copy-start.1
  (10 other events, 8.7 us)
Sparse Core Ops, SparseCore 0:
  9.6 94.1 all-gather.5
  191.9 116.5 all-gather.3
  393.1 65.4 reduce-scatter.2
  484.7 125.1 reduce-scatter.4

commit v8 on v7

--- a/solution.py
+++ b/solution.py
@@ -77,6 +77,19 @@
     columns = lax.broadcasted_iota(jnp.int32, (count, keys), 1)
     same = seg_col_ref[0, first : first + count, :] == seg_row_ref[0, :, :keys]
     return same & (rows >= columns)
+
+
+def stacked(ref, rows, one, group):
+    starts = range(one * group * HEAD, (one + 1) * group * HEAD, HEAD)
+    return jnp.concatenate([ref[rows, start : start + HEAD] for start in starts], axis=0)
+
+
+def unstack(ref, rows, one, values):
+    count = rows.stop - rows.start
+    group = values.shape[0] // count
+    for head in range(group):
+        start = (one * group + head) * HEAD
+        ref[rows, start : start + HEAD] = values[head * count : (head + 1) * count]
 
 
 def soft_weights(queries, keys, allowed):
@@ -106,15 +119,14 @@
     for first in range(0, TOK_MB, block):
         rows, keys = slice(first, first + block), slice(0, first + block)
         allowed = allowed_keys(seg_col_ref, seg_row_ref, first, block)
+        allowed = jnp.concatenate([allowed] * group, axis=0)
         for one in range(2):
             lanes = slice(one * HEAD, (one + 1) * HEAD)
-            key_rows, value_rows = k_out[keys, lanes], v_out[keys, lanes]
-            for head in range(one * group, (one + 1) * group):
-                at = slice(head * HEAD, (head + 1) * HEAD)
-                weights = soft_weights(q_out[rows, at], key_rows, allowed).astype(jnp.bfloat16)
-                mixed_ref[rows, at] = jnp.dot(
-                    weights, value_rows, preferred_element_type=jnp.float32
-                ).astype(jnp.bfloat16)
+            weights = soft_weights(
+                stacked(q_out, rows, one, group), k_out[keys, lanes], allowed
+            ).astype(jnp.bfloat16)
+            mixed = jnp.dot(weights, v_out[keys, lanes], preferred_element_type=jnp.float32)
+            unstack(mixed_ref, rows, one, mixed.astype(jnp.bfloat16))
 
 
 def attend_back_kernel(
@@ -130,29 +142,26 @@
     for first in range(TOK_MB - block, -1, -block):
         rows, keys = slice(first, first + block), slice(0, first + block)
         allowed = allowed_keys(seg_col_ref, seg_row_ref, first, block)
+        allowed = jnp.concatenate([allowed] * group, axis=0)
         for one in range(2):
             lanes = slice(one * HEAD, (one + 1) * HEAD)
             key_rows, value_rows = k_ref[keys, lanes], v_ref[keys, lanes]
-            grad_keys = grad_values = 0.0
-            for head in range(one * group, (one + 1) * group):
-                at = slice(head * HEAD, (head + 1) * HEAD)
-                queries, grads = q_ref[rows, at], grad_ref[rows, at]
-                weights = soft_weights(queries, key_rows, allowed)
-                grad_weights = lax.dot_general(
-                    grads, value_rows, over_lanes, preferred_element_type=jnp.float32
-                )
-                grad_values += lax.dot_general(
-                    weights.astype(jnp.bfloat16), grads, over_rows,
-                    preferred_element_type=jnp.float32,
-                )
-                inner = jnp.sum(grad_weights * weights, axis=-1, keepdims=True)
-                grad_scores = (weights * (grad_weights - inner)).astype(jnp.bfloat16)
-                dq_sum[rows, at] = jnp.dot(
-                    grad_scores, key_rows, preferred_element_type=jnp.float32
-                ) * HEAD ** (-0.5)
-                grad_keys += lax.dot_general(
-                    grad_scores, queries, over_rows, preferred_element_type=jnp.float32
-                )
+            queries = stacked(q_ref, rows, one, group)
+            grads = stacked(grad_ref, rows, one, group)
+            weights = soft_weights(queries, key_rows, allowed)
+            grad_weights = lax.dot_general(
+                grads, value_rows, over_lanes, preferred_element_type=jnp.float32
+            )
+            grad_values = lax.dot_general(
+                weights.astype(jnp.bfloat16), grads, over_rows, preferred_element_type=jnp.float32
+            )
+            inner = jnp.sum(grad_weights * weights, axis=-1, keepdims=True)
+            grad_scores = (weights * (grad_weights - inner)).astype(jnp.bfloat16)
+            grad_queries = jnp.dot(grad_scores, key_rows, preferred_element_type=jnp.float32)
+            unstack(dq_sum, rows, one, grad_queries * HEAD ** (-0.5))
+            grad_keys = lax.dot_general(
+                grad_scores, queries, over_rows, preferred_element_type=jnp.float32
+            )
             if first == TOK_MB - block:
                 dk_sum[keys, lanes] = grad_keys
                 dv_sum[keys, lanes] = grad_values
@@ -775,8 +784,6 @@
     normed = (rows_in * scale_one * gain_one).astype(jnp.bfloat16)
     projected = jnp.dot(normed, qkv_full, preferred_element_type=jnp.float32)
     cosine_table, sine_table = rope_tables(position)
-    if lo_count == 4:
-        segment = hold(segment, grad_blocks[1][0], grad_blocks[2][0])
     sides = (
         jnp.tile(cosine_table, (1, 4)),
         jnp.concatenate([-sine_table, sine_table] * 2, axis=1),
@@ -784,6 +791,8 @@
         segment.reshape(-1, 1, TOK_MB),
     )
     queries, key_rows, value_rows, mixed_rows = attend(projected, sides)
+    if lo_count == 4:
+        mixed_rows = hold(mixed_rows, grad_blocks[1][0], grad_blocks[2][0])
     attended = jnp.dot(mixed_rows, out_full, preferred_element_type=jnp.float32)
     residual = rows_in + attended
     scale_two = lax.rsqrt(jnp.mean(residual * residual, axis=1, keepdims=True) + epsilon)

time: 778 us -> 752 us (0.967)
  Pallas kernels: 409 us -> 389 us
    pallas_call x1, Pallas kernels: 41.4 us -> 31.4 us  [attend_back(): pl.pallas_call(attend_back_kernel, grid=grid, out_shape=tuple(shapes), in...]
    pallas_call x1, Pallas kernels: 28.9 us -> 18.9 us  [attend(): pl.pallas_call(attend_kernel, grid=grid, out_shape=(q_shape, kv_shape, kv...]
    unnamed x110 -> x107, local copies, waits for them, and re-layouts: 16 us -> 15.7 us
  transfers between devices with their start and end apart: 24 -> 24, of which waited for: 10 -> 9; matrix products, arithmetic and copies ran while one was open for 30% -> 31% of each run, Pallas kernels for 50% -> 49%
where the time goes in v8:
time: 752 us; the launch traced here: 746 us
  Pallas kernels  389 us (52%)
  matrix products  148 us (20%)
  local copies, waits for them, and re-layouts  76.6 us (10%)
  waiting for transfers between devices  45.3 us (6%)
  other arithmetic  44.2 us (6%)
  starting transfers between devices  28.3 us (4%)
  between operations  15 us (2%)
    pallas_call x1, Pallas kernels, opening(): pl.pallas_call(functools.partial(opening_kernel, sizes), out_shape=(jax.S...  154 us
    pallas_call x1, Pallas kernels, closing(): pl.pallas_call(functools.partial(closing_kernel, sizes), out_shape=(jax.S...  128 us
    ppermute x19, waiting for transfers between devices, swap(): return lax.ppermute(block, 'lo', [(i, i ^ step) for i in range(lo_count)])  44.1 us
    pallas_call x10, Pallas kernels, dispatch(): pl.pallas_call(functools.partial(dispatch_kernel, weight is not None), gr...  33.8 us
    pallas_call x1, Pallas kernels, attend_back(): pl.pallas_call(attend_back_kernel, grid=grid, out_shape=tuple(shapes), in...  31.4 us
    gather x8, local copies, waits for them, and re-layouts, pick(): return jnp.take(rows, index, axis=0, mode='clip')  25.5 us
    pallas_call x1, Pallas kernels, middle(): pl.pallas_call(middle_kernel, grid=(count, row_count // tile), out_shape=...  23.6 us
    dot_general x1, matrix products, shards(): jnp.einsum('ekrf,erd->ekfd', grad_gate_up, expert_rows, preferred_element...  22.2 us
  transfers between devices with their start and end apart: 24, of which 9 were waited for; matrix products, arithmetic and copies ran while one was open for 31% of the time, Pallas kernels for 49%

profile of v8, /device:TPU:12, one launch (start us, length us, event | category | flops | bytes accessed | tf_op | source)
XLA Modules:
  0.0 745.9 jit_solution(8294348598820478276)
XLA Ops:
  16.6 6.0 all-to-all-start
  25.6 1.9 concatenate.22.shard_ref
  30.0 2.9 gather_fusion
  32.9 2.9 gather_fusion.1
  35.8 153.5 %opening.1 = (bf16[32,16,1536]{2,1,0:T(8,128)(2,1)}, bf16[32,16,1536]{2,1,0:T(8,128)(2,1)}, bf16[4,4,2,48,4224]{4,3,2,1,0:T(8,128)(2,1)}) custom-call(bf16[32,16,1536]{2,1,0:T(8,128)(2,1)} %bitcast.162, bf16[32,16,1536]{2,1,0:T(8,128)(2,1)} %bitcast.163, bf16[48,4224]{1,0:T(8,128)(2,1)} %concatenate.22.shard_ref), custom_call_target="tpu_custom_call" | custom-call | tf_op jit(solution)/shard_map/opening/pallas_call | solution.py:424
  189.4 2.3 all_gather_reshape.3
  196.7 2.3 gather_fusion.2
  199.0 3.5 collective-permute-start.3
  202.5 3.1 collective-permute-start.4
  205.6 5.3 gather_fusion.3
  216.9 9.2 %fusion.9.q_ref.k_ref.v_ref = f32[512,2560]{1,0:T(8,128)} fusion(bf16[512,1536]{1,0:T(8,128)(2,1)S(1)} %fusion.25.refs_0_, bf16[1536,4224]{1,0:T(8,128)(2,1)} %bitcast.180), kind=kOutput, calls=%fused_computation.25 | convolution fusion | flops 4026531840 | bytes 14680064 | tf_op jit(solution)/shard_map/dot_general | solution.py:785
  226.1 18.9 %attend.1 = (bf16[512,1536]{1,0:T(8,128)(2,1)}, bf16[512,512]{1,0:T(8,128)(2,1)}, bf16[512,512]{1,0:T(8,128)(2,1)}, bf16[512,1536]{1,0:T(8,128)(2,1)}) custom-call(f32[512,2560]{1,0:T(8,128)} %fusion.9.q_ref.k_ref.v_ref, f32[512,2560]{1,0:T(8,128)} %fusion.9.q_ref.k_ref.v_ref, f32[512,2560]{1,0:T(8,128)} %fusion.9.q_ref.k_ref.v_ref, ...), custom_call_target="tpu_custom_call" | custom-call | tf_op jit(solution)/shard_map/attend/pallas_call | solution.py:202
  245.0 2.1 slice.220
  249.8 5.1 multiply_reduce_fusion.2
  258.1 8.6 %collective-permute-done.5.refs_1_.rows_ref = bf16[256,1536]{1,0:T(8,128)(2,1)} collective-permute-done((bf16[256,1536]{1,0:T(8,128)(2,1)}, bf16[256,1536]{1,0:T(8,128)(2,1)}, u32[]{:S(2)}, u32[]{:S(2)}) %collective-permute-start.5) | collective-permute-done | bytes 786464 | tf_op jit(solution)/shard_map/ppermute | solution.py:718
  272.1 2.0 copy.173.refs_0_
  274.1 2.3 fusion.18.choose_ref
  276.4 3.7 dispatch.15.refs_0_
  280.1 3.6 dispatch.10.refs_1_
  283.8 3.6 dispatch.11.refs_1_
  287.4 3.7 dispatch.12.refs_1_
  291.1 3.0 dispatch.13.refs_1_
  294.1 3.0 dispatch.14
  297.1 7.0 collective-permute-done.8.rows_ref
  305.2 1.7 collective-permute-start.10
  308.2 13.7 %convert_bitcast_fusion.grad_ref = bf16[4,2,1024,256]{3,2,1,0:T(8,128)(2,1)} fusion(bf16[4,1024,1536,1]{2,1,3,0:T(8,128)(2,1)} %bitcast.150, bf16[4,2,256,1536]{3,2,1,0:T(8,128)(2,1)} %bitcast.187), kind=kOutput, calls=%fused_computation.33 | convolution fusion | flops 6444548096 | bytes 23068672 | tf_op jit(solution)/shard_map/erd,ekfd->ekrf/dot_general | solution.py:827
  323.4 2.5 collective-permute-done.9.rows_ref
  325.9 3.6 dispatch.16.refs_0_
  329.5 3.6 dispatch.17.refs_0_
  333.1 3.0 dispatch.18.refs_0_
  336.0 2.9 dispatch.19
  339.0 23.6 %middle.1 = (bf16[4,2,1024,256]{3,2,1,0:T(8,128)(2,1)}, bf16[4,2,1024,512]{3,2,1,0:T(8,128)(2,1)}) custom-call(bf16[4,1024,1536]{2,1,0:T(8,128)(2,1)} %bitcast.148, bf16[4,2,1536,512]{3,2,1,0:T(8,128)(2,1)} %bitcast.157, bf16[4,2,1024,256]{3,2,1,0:T(8,128)(2,1)} %convert_bitcast_fusion.grad_ref), custom_call_target="tpu_custom_call" | custom-call | tf_op jit(solution)/shard_map/middle/pallas_call | solution.py:664
  362.5 13.9 %convolution_convert_fusion.3 = bf16[4,2,256,1536]{3,2,1,0:T(8,128)(2,1)} fusion(bf16[4,2,1024,256]{3,2,1,0:T(8,128)(2,1)} %get-tuple-element.76, bf16[4,1024,1536,1]{2,1,3,0:T(8,128)(2,1)} %bitcast.151), kind=kOutput, calls=%fused_computation.32 | convolution fusion | flops 6445596672 | bytes 23068672 | tf_op jit(solution)/shard_map/ekrf,erd->ekfd/dot_general | solution.py:837
  376.5 21.0 %bitcast_convert_fusion = bf16[4,1024,1536]{2,1,0:T(8,128)(2,1)} fusion(bf16[4,2,1024,512]{3,2,1,0:T(8,128)(2,1)} %get-tuple-element.78.refs_0_, bf16[4,2,1536,512]{3,2,1,0:T(8,128)(2,1)} %bitcast.158), kind=kOutput, calls=%fused_computation.10 | convolution fusion | flops 12891193344 | bytes 33554432 | tf_op jit(solution)/shard_map/ekrf,ekdf->erd/dot_general | solution.py:847
  397.5 8.1 %bitcast_convert_fusion.1 = bf16[8,256,1536]{2,1,0:T(8,128)(2,1)S(1)} fusion(bf16[4,8,128,1536]{3,2,1,0:T(8,128)(2,1)} %bitcast.190, s32[8,4,256]{2,1,0:T(4,128)S(1)} %copy.167, pred[8,4,256]{2,1,0:T(4,128)(4,1)S(1)} %bitcast.172), kind=kOutput, calls=%fused_computation.15 | convolution fusion | flops 3226468352 | bytes 18915328 | tf_op jit(solution)/shard_map/becr,ebcd->brd/dot_general | solution.py:852
  405.7 2.4 fusion.66
  408.0 2.7 copy-done.14
  411.6 12.6 %fusion.1 = bf16[4,1024,1536]{2,1,0:T(8,128)(2,1)} fusion(bf16[4,2,1024,256]{3,2,1,0:T(8,128)(2,1)S(1)} %copy-done.46, bf16[4,2,256,1536]{3,2,1,0:T(8,128)(2,1)} %bitcast.188, f32[4,1024]{1,0:T(4,128)S(1)} %bitcast.176), kind=kOutput, calls=%fused_computation.12 | convolution fusion | flops 6455033856 | bytes 23085056 | tf_op jit(solution)/shard_map/ekrf,ekfd->erd/dot_general | solution.py:890
  424.2 10.9 %bitcast_convert_fusion.2.refs_1_ = bf16[8,256,1536]{2,1,0:T(8,128)(2,1)} fusion(bf16[4,8,128,1536]{3,2,1,0:T(8,128)(2,1)} %bitcast.189, s32[8,4,256]{2,1,0:T(4,128)S(1)} %copy.167, pred[8,4,256]{2,1,0:T(4,128)(4,1)S(1)} %bitcast.173), kind=kOutput, calls=%fused_computation.16 | convolution fusion | flops 3226468352 | bytes 18915328 | tf_op jit(solution)/shard_map/becr,ebcd->brd/dot_general | solution.py:852
  435.1 9.2 %collective-permute-done.11.refs_2_ = bf16[2,256,1536]{2,1,0:T(8,128)(2,1)S(1)} collective-permute-done((bf16[2,256,1536]{2,1,0:T(8,128)(2,1)}, bf16[2,256,1536]{2,1,0:T(8,128)(2,1)S(1)}, u32[]{:S(2)}, u32[]{:S(2)}) %collective-permute-start.11) | collective-permute-done | bytes 1572896 | tf_op jit(solution)/shard_map/ppermute | solution.py:718
  446.6 22.2 %convolution_convert_fusion = bf16[4,2,512,1536]{3,2,1,0:T(8,128)(2,1)} fusion(bf16[4,2,1024,512]{3,2,1,0:T(8,128)(2,1)} %hold.9, bf16[4,1024,1536,1]{2,1,3,0:T(8,128)(2,1)} %bitcast.149), kind=kOutput, calls=%fused_computation.13 | convolution fusion | flops 12891193344 | bytes 33554432 | tf_op jit(solution)/shard_map/ekrf,erd->ekfd/dot_general | solution.py:895
  470.7 1.8 fusion.46
  474.2 14.0 %collective-permute-done.13 = bf16[256,1536]{1,0:T(8,128)(2,1)S(1)} collective-permute-done((bf16[256,1536]{1,0:T(8,128)(2,1)S(1)}, bf16[256,1536]{1,0:T(8,128)(2,1)S(1)}, u32[]{:S(2)}, u32[]{:S(2)}) %collective-permute-start.13) | collective-permute-done | bytes 786464 | tf_op jit(solution)/shard_map/ppermute | solution.py:718
  488.5 4.7 fusion.65
  498.5 7.3 fusion.38.grad_ref
  505.7 31.4 %attend_back.1 = (bf16[512,1536]{1,0:T(8,128)(2,1)}, bf16[512,512]{1,0:T(8,128)(2,1)}, bf16[512,512]{1,0:T(8,128)(2,1)}) custom-call(bf16[512,1536]{1,0:T(8,128)(2,1)} %get-tuple-element.80.q_ref, bf16[512,512]{1,0:T(8,128)(2,1)} %get-tuple-element.81.k_ref, bf16[512,512]{1,0:T(8,128)(2,1)} %get-tuple-element.82.v_ref, bf16[512,1536]{1,0:T(8,128)(2,1)} %fusion.38.grad_ref, ...), custom_call_target="tpu_custom_call" | custom-call | tf_op jit(solution)/shard_map/attend_back/pallas_call | solution.py:221
  537.2 1.7 constant_dynamic-update-slice_fusion.10
  539.3 10.4 %fusion.34 = (f32[512]{0:T(512)S(1)}, bf16[1536]{0:T(1024)(128)(2,1)S(1)}, f32[512,1536]{1,0:T(8,128)}) fusion(bf16[512,1536]{1,0:T(8,128)(2,1)S(1)} %copy-done.10, f32[1536]{0:T(1024)S(1)} %copy-done.36, f32[512]{0:T(512)S(1)} %copy-done.42, bf16[512,2560]{1,0:T(8,128)(2,1)S(1)} %constant_dynamic-update-slice_fusion.8, bf16[1536,4224]{1,0:T(8,128)(2,1)} %bitcast.183), kind=kOutput, calls=%fused_computation.53 | convolution fusion | flops 4032034816 | bytes 15217664 | tf_op jit(solution)/shard_map/nc,dc->nd/dot_general | solution.py:925
  550.1 3.9 fusion.30
  554.0 3.2 gather_fusion.5
  557.2 6.3 convolution_convert_fusion.2
  563.5 3.1 fusion.48
  569.3 6.8 convolution_convert_fusion.1
  576.1 5.6 fusion.2
  581.7 2.6 convert_element_type.240
  584.3 2.6 bitcast_add_fusion.1
  588.0 2.9 gather_fusion.4
  590.9 127.5 %closing.1 = (bf16[32,16,1536]{2,1,0:T(8,128)(2,1)}, bf16[32,16,1536]{2,1,0:T(8,128)(2,1)}, f32[48,4224]{1,0:T(8,128)}) custom-call(bf16[32,16,1536]{2,1,0:T(8,128)(2,1)} %bitcast.165, bf16[32,16,1536]{2,1,0:T(8,128)(2,1)} %bitcast.164, bf16[4,4,2,48,4224]{4,3,2,1,0:T(8,128)(2,1)} %bitcast.156), custom_call_target="tpu_custom_call" | custom-call | tf_op jit(solution)/shard_map/closing/pallas_call | solution.py:578
  718.5 2.0 slice.185
  720.5 1.7 slice.186
  722.2 2.9 gather_fusion.7
  725.1 2.9 gather_fusion.6
  729.5 3.4 reshape.303
  733.0 5.9 copy.195
  (225 shorter events, 59.1 us)
Async XLA Ops:
  7.2 22.8 %copy-start = (bf16[512,1536]{1,0:T(8,128)(2,1)S(1)}, bf16[512,1536]{1,0:T(8,128)(2,1)}, u32[]{:S(2)}) copy-start(bf16[512,1536]{1,0:T(8,128)(2,1)} %param.12) | copy-start | bytes 4718596
  7.2 301.0 %all-gather.6.cloned.1.call-start = ((), (), s32[]{:S(2)}) async-start(), calls=%async_computation.6 | async-start | bytes 7077888 | tf_op jit(solution)/shard_map/all_gather | solution.py:779
  9.4 19.9 %collective-permute-start = (f32[512,16]{0,1:T(8,128)S(1)}, f32[512,16]{0,1:T(8,128)S(1)}, u32[]{:S(2)}, u32[]{:S(2)}) collective-permute-start(f32[512,16]{0,1:T(8,128)S(1)} %pad_maximum_fusion.2), channel_id=1, source_target_pairs={{0,2},{2,0},{4,6},{6,4},{1,3},{3,1},{5,7},{7,5},{8,10},{10,8},{12,... | collective-permute-start | bytes 98312 | tf_op jit(solution)/shard_map/ppermute | solution.py:718
  10.9 18.4 %collective-permute-start.1 = (f32[512,16]{0,1:T(8,128)S(1)}, f32[512,16]{0,1:T(8,128)S(1)}, u32[]{:S(2)}, u32[]{:S(2)}) collective-permute-start(f32[512,16]{0,1:T(8,128)S(1)} %pad_maximum_fusion.2), channel_id=1, source_target_pairs={{0,6},{2,4},{4,2},{6,0},{1,7},{3,5},{5,3},{7,1},{8,14},{10,12},{12... | collective-permute-start | bytes 98312 | tf_op jit(solution)/shard_map/ppermute | solution.py:718
  11.3 18.0 %collective-permute-start.2 = (f32[512,16]{0,1:T(8,128)S(1)}, f32[512,16]{0,1:T(8,128)S(1)}, u32[]{:S(2)}, u32[]{:S(2)}) collective-permute-start(f32[512,16]{0,1:T(8,128)S(1)} %pad_maximum_fusion.2), channel_id=1, source_target_pairs={{0,4},{2,6},{4,0},{6,2},{1,5},{3,7},{5,1},{7,3},{8,12},{10,14},{12... | collective-permute-start | bytes 98312 | tf_op jit(solution)/shard_map/ppermute | solution.py:718
  16.6 11.3 %all-to-all-start = ((s32[32,1,16]{2,1,0:T(1,128)}), s32[32,1,16]{2,1,0:T(1,128)S(1)}, u32[]{:S(2)}, u32[]{:S(2)}) async-start(s32[32,1,16]{2,1,0:T(1,128)} %bitcast.2), calls=%async_computation | async-start | bytes 32768 | tf_op jit(solution)/shard_map/all_to_all | solution.py:736
  22.6 316.3 %all-gather.4.cloned.1.call-start = ((), (), s32[]{:S(2)}) async-start(), calls=%async_computation.3 | async-start | bytes 14155776 | tf_op jit(solution)/shard_map/all_gather | solution.py:776
  30.0 2.9 copy-start.2
  35.8 153.6 %copy-start.26 = (bf16[1536,2,256]{2,1,0:T(2,128)(2,1)S(1)}, bf16[1536,2,256]{2,1,0:T(2,128)(2,1)}, u32[]{:S(2)}) copy-start(bf16[1536,2,256]{2,1,0:T(2,128)(2,1)} %param.22) | copy-start | bytes 4718596
  189.4 2.4 copy-start.45
  191.7 5.0 copy-start.3
  191.7 390.0 %reduce-scatter.3.cloned.1.call-start = ((), (), s32[]{:S(2)}) async-start(), calls=%async_computation.4 | async-start | bytes 7077888 | tf_op jit(solution)/shard_map/reduce_scatter | solution.py:841
  199.0 6.5 copy-start.11
  199.0 46.0 %collective-permute-start.3 = (bf16[512,1536]{1,0:T(8,128)(2,1)S(1)}, bf16[512,1536]{1,0:T(8,128)(2,1)}, u32[]{:S(2)}, u32[]{:S(2)}) collective-permute-start(bf16[512,1536]{1,0:T(8,128)(2,1)S(1)} %gather_fusion.2), channel_id=1, source_target_pairs={{0,2},{2,0},{4,6},{6,4},{1,3},{3,1},{5,7},{7,5},{8,10},{10,8},{12,... | collective-permute-start | bytes 4718600 | tf_op jit(solution)/shard_map/ppermute | solution.py:718
  202.5 44.7 %collective-permute-start.4 = (bf16[512,1536]{1,0:T(8,128)(2,1)S(1)}, bf16[512,1536]{1,0:T(8,128)(2,1)}, u32[]{:S(2)}, u32[]{:S(2)}) collective-permute-start(bf16[512,1536]{1,0:T(8,128)(2,1)S(1)} %gather_fusion.2), channel_id=1, source_target_pairs={{0,4},{2,6},{4,0},{6,2},{1,5},{3,7},{5,1},{7,3},{8,12},{10,14},{12... | collective-permute-start | bytes 4718600 | tf_op jit(solution)/shard_map/ppermute | solution.py:718
  210.9 38.8 %copy-start.9 = (bf16[512,1536]{1,0:T(8,128)(2,1)}, bf16[512,1536]{1,0:T(8,128)(2,1)S(1)}, u32[]{:S(2)}) copy-start(bf16[512,1536]{1,0:T(8,128)(2,1)S(1)} %gather_fusion.3) | copy-start | bytes 4718596
  214.3 40.6 %copy-start.33 = (f32[1536]{0:T(1024)}, f32[1536]{0:T(1024)S(1)}, u32[]{:S(2)}) copy-start(f32[1536]{0:T(1024)S(1)} %get-tuple-element.108) | copy-start | bytes 18436
  247.1 19.6 %collective-permute-start.5 = (bf16[256,1536]{1,0:T(8,128)(2,1)}, bf16[256,1536]{1,0:T(8,128)(2,1)}, u32[]{:S(2)}, u32[]{:S(2)}) collective-permute-start(bf16[256,1536]{1,0:T(8,128)(2,1)} %slice.220), channel_id=1, source_target_pairs={{0,4},{2,6},{4,0},{6,2},{1,5},{3,7},{5,1},{7,3},{8,12},{10,14},{12... | collective-permute-start | bytes 2359304 | tf_op jit(solution)/shard_map/ppermute | solution.py:718
  248.4 19.4 %collective-permute-start.6 = (bf16[256,1536]{1,0:T(8,128)(2,1)S(1)}, bf16[256,1536]{1,0:T(8,128)(2,1)S(1)}, u32[]{:S(2)}, u32[]{:S(2)}) collective-permute-start(bf16[256,1536]{1,0:T(8,128)(2,1)S(1)} %slice.221), channel_id=1, source_target_pairs={{0,2},{2,0},{4,6},{6,4},{1,3},{3,1},{5,7},{7,5},{8,10},{10,8},{12,... | collective-permute-start | bytes 2359304 | tf_op jit(solution)/shard_map/ppermute | solution.py:718
  254.9 1.7 copy-start.6
  254.9 12.8 %copy-start.37 = (f32[512]{0:T(512)}, f32[512]{0:T(512)S(1)}, u32[]{:S(2)}) copy-start(f32[512]{0:T(512)S(1)} %add_rsqrt_fusion) | copy-start | bytes 6148
  258.1 12.5 %copy-start.32 = (f32[8,256,16]{1,2,0:T(8,128)S(1)}, f32[8,256,16]{1,2,0:T(8,128)}, u32[]{:S(2)}) copy-start(f32[8,256,16]{1,2,0:T(8,128)} %copy-done.31) | copy-start | bytes 393220
  268.6 35.5 %collective-permute-start.8 = (bf16[512,1536]{1,0:T(8,128)(2,1)}, bf16[512,1536]{1,0:T(8,128)(2,1)S(1)}, u32[]{:S(2)}, u32[]{:S(2)}) collective-permute-start(bf16[512,1536]{1,0:T(8,128)(2,1)} %hold.7.rows_ref), channel_id=1, source_target_pairs={{0,4},{2,6},{4,0},{6,2},{1,5},{3,7},{5,1},{7,3},{8,12},{10,14},{12... | collective-permute-start | bytes 4718600 | tf_op jit(solution)/shard_map/ppermute | solution.py:718
  270.2 36.6 %collective-permute-start.7 = (bf16[512,1536]{1,0:T(8,128)(2,1)}, bf16[512,1536]{1,0:T(8,128)(2,1)S(1)}, u32[]{:S(2)}, u32[]{:S(2)}) collective-permute-start(bf16[512,1536]{1,0:T(8,128)(2,1)} %hold.7.rows_ref), channel_id=1, source_target_pairs={{0,2},{2,0},{4,6},{6,4},{1,3},{3,1},{5,7},{7,5},{8,10},{10,8},{12,... | collective-permute-start | bytes 4718600 | tf_op jit(solution)/shard_map/ppermute | solution.py:718
  304.2 17.7 %copy-start.23 = (bf16[512,1536]{1,0:T(8,128)(2,1)}, bf16[512,1536]{1,0:T(8,128)(2,1)S(1)}, u32[]{:S(2)}) copy-start(bf16[512,1536]{1,0:T(8,128)(2,1)S(1)} %collective-permute-done.8.rows_ref) | copy-start | bytes 4718596
  305.2 18.2 %collective-permute-start.10 = (bf16[256,1536]{1,0:T(8,128)(2,1)}, bf16[256,1536]{1,0:T(8,128)(2,1)}, u32[]{:S(2)}, u32[]{:S(2)}) collective-permute-start(bf16[256,1536]{1,0:T(8,128)(2,1)} %slice.223), channel_id=1, source_target_pairs={{0,2},{2,0},{4,6},{6,4},{1,3},{3,1},{5,7},{7,5},{8,10},{10,8},{12,... | collective-permute-start | bytes 2359304 | tf_op jit(solution)/shard_map/ppermute | solution.py:718
  306.9 15.0 %copy-start.24 = (bf16[512,1536]{1,0:T(8,128)(2,1)}, bf16[512,1536]{1,0:T(8,128)(2,1)S(1)}, u32[]{:S(2)}) copy-start(bf16[512,1536]{1,0:T(8,128)(2,1)S(1)} %collective-permute-done.7.rows_ref) | copy-start | bytes 4718596
  307.9 18.0 %collective-permute-start.9 = (bf16[256,1536]{1,0:T(8,128)(2,1)}, bf16[256,1536]{1,0:T(8,128)(2,1)}, u32[]{:S(2)}, u32[]{:S(2)}) collective-permute-start(bf16[256,1536]{1,0:T(8,128)(2,1)} %slice.222), channel_id=1, source_target_pairs={{0,4},{2,6},{4,0},{6,2},{1,5},{3,7},{5,1},{7,3},{8,12},{10,14},{12... | collective-permute-start | bytes 2359304 | tf_op jit(solution)/shard_map/ppermute | solution.py:718
  376.4 353.1 %reduce-scatter.5.cloned.1.call-start = ((), (), s32[]{:S(2)}) async-start(), calls=%async_computation.5 | async-start | bytes 14155776 | tf_op jit(solution)/shard_map/reduce_scatter | solution.py:898
  405.7 5.1 copy-start.14
  405.7 5.9 copy-start.46
  410.7 33.6 %collective-permute-start.11 = (bf16[2,256,1536]{2,1,0:T(8,128)(2,1)}, bf16[2,256,1536]{2,1,0:T(8,128)(2,1)S(1)}, u32[]{:S(2)}, u32[]{:S(2)}) collective-permute-start(bf16[2,256,1536]{2,1,0:T(8,128)(2,1)} %get-tuple-element.120), channel_id=1, source_target_pairs={{0,2},{2,0},{4,6},{6,4},{1,3},{3,1},{5,7},{7,5},{8,10},{10,8},{12,... | collective-permute-start | bytes 4718600 | tf_op jit(solution)/shard_map/ppermute | solution.py:718
  410.7 33.6 %collective-permute-start.12 = (bf16[2,256,1536]{2,1,0:T(8,128)(2,1)}, bf16[2,256,1536]{2,1,0:T(8,128)(2,1)S(1)}, u32[]{:S(2)}, u32[]{:S(2)}) collective-permute-start(bf16[2,256,1536]{2,1,0:T(8,128)(2,1)} %get-tuple-element.119), channel_id=1, source_target_pairs={{0,4},{2,6},{4,0},{6,2},{1,5},{3,7},{5,1},{7,3},{8,12},{10,14},{12... | collective-permute-start | bytes 4718600 | tf_op jit(solution)/shard_map/ppermute | solution.py:718
  468.8 1.4 copy-start.19
  468.8 1.9 copy-start.21
  470.7 2.8 copy-start.44
  470.7 3.4 copy-start.40
  472.4 15.8 %collective-permute-start.13 = (bf16[256,1536]{1,0:T(8,128)(2,1)S(1)}, bf16[256,1536]{1,0:T(8,128)(2,1)S(1)}, u32[]{:S(2)}, u32[]{:S(2)}) collective-permute-start(bf16[256,1536]{1,0:T(8,128)(2,1)S(1)} %get-tuple-element.118), channel_id=1, source_target_pairs={{0,4},{2,6},{4,0},{6,2},{1,5},{3,7},{5,1},{7,3},{8,12},{10,14},{12... | collective-permute-start | bytes 2359304 | tf_op jit(solution)/shard_map/ppermute | solution.py:718
  472.8 15.7 %collective-permute-start.14 = (bf16[256,1536]{1,0:T(8,128)(2,1)S(1)}, bf16[256,1536]{1,0:T(8,128)(2,1)S(1)}, u32[]{:S(2)}, u32[]{:S(2)}) collective-permute-start(bf16[256,1536]{1,0:T(8,128)(2,1)S(1)} %get-tuple-element.117), channel_id=1, source_target_pairs={{0,2},{2,0},{4,6},{6,4},{1,3},{3,1},{5,7},{7,5},{8,10},{10,8},{12,... | collective-permute-start | bytes 2359304 | tf_op jit(solution)/shard_map/ppermute | solution.py:718
  488.5 6.9 copy-start.17
  488.5 6.9 copy-start.22
  493.2 70.2 %collective-permute-start.15 = (bf16[2,256,1536]{2,1,0:T(8,128)(2,1)}, bf16[2,256,1536]{2,1,0:T(8,128)(2,1)}, u32[]{:S(2)}, u32[]{:S(2)}) collective-permute-start(bf16[2,256,1536]{2,1,0:T(8,128)(2,1)} %get-tuple-element.116), channel_id=1, source_target_pairs={{0,2},{2,0},{4,6},{6,4},{1,3},{3,1},{5,7},{7,5},{8,10},{10,8},{12,... | collective-permute-start | bytes 4718600 | tf_op jit(solution)/shard_map/ppermute | solution.py:718
  493.8 2.1 copy-start.7
  493.8 2.1 copy-start.34
  493.8 2.2 copy-start.38
  493.8 69.7 %collective-permute-start.16 = (bf16[2,256,1536]{2,1,0:T(8,128)(2,1)}, bf16[2,256,1536]{2,1,0:T(8,128)(2,1)}, u32[]{:S(2)}, u32[]{:S(2)}) collective-permute-start(bf16[2,256,1536]{2,1,0:T(8,128)(2,1)} %get-tuple-element.115), channel_id=1, source_target_pairs={{0,4},{2,6},{4,0},{6,2},{1,5},{3,7},{5,1},{7,3},{8,12},{10,14},{12... | collective-permute-start | bytes 4718600 | tf_op jit(solution)/shard_map/ppermute | solution.py:718
  495.9 1.4 copy-start.12
  498.4 7.3 copy-start.13
  537.1 1.7 copy-start.30
  537.1 1.8 copy-start.29
  537.1 2.2 copy-start.10
  537.1 2.2 copy-start.36
  537.1 2.2 copy-start.42
  539.3 10.4 %copy-start.28 = (bf16[512,2560]{1,0:T(8,128)(2,1)}, bf16[512,2560]{1,0:T(8,128)(2,1)S(1)}, u32[]{:S(2)}) copy-start(bf16[512,2560]{1,0:T(8,128)(2,1)S(1)} %constant_dynamic-update-slice_fusion.8) | copy-start | bytes 7864324
  553.9 3.2 copy-start.27
  566.6 17.7 %collective-permute-start.17 = (bf16[256,1536]{1,0:T(8,128)(2,1)}, bf16[256,1536]{1,0:T(8,128)(2,1)}, u32[]{:S(2)}, u32[]{:S(2)}) collective-permute-start(bf16[256,1536]{1,0:T(8,128)(2,1)} %get-tuple-element.113), channel_id=1, source_target_pairs={{0,4},{2,6},{4,0},{6,2},{1,5},{3,7},{5,1},{7,3},{8,12},{10,14},{12... | collective-permute-start | bytes 2359304 | tf_op jit(solution)/shard_map/ppermute | solution.py:718
  567.9 16.4 %collective-permute-start.18 = (bf16[256,1536]{1,0:T(8,128)(2,1)S(1)}, bf16[256,1536]{1,0:T(8,128)(2,1)}, u32[]{:S(2)}, u32[]{:S(2)}) collective-permute-start(bf16[256,1536]{1,0:T(8,128)(2,1)S(1)} %get-tuple-element.112), channel_id=1, source_target_pairs={{0,2},{2,0},{4,6},{6,4},{1,3},{3,1},{5,7},{7,5},{8,10},{10,8},{12,... | collective-permute-start | bytes 2359304 | tf_op jit(solution)/shard_map/ppermute | solution.py:718
  569.3 6.8 slice-start
  569.3 6.8 slice-start.1
  581.7 2.6 copy-start.16
  584.3 2.9 copy-start.8
  718.5 3.7 copy-start.5
  722.2 2.9 copy-start.4
  733.0 5.9 copy-start.1
  (9 other events, 7.5 us)
Sparse Core Ops, SparseCore 0:
  9.6 94.1 all-gather.5
  191.8 116.5 all-gather.3
  376.5 65.0 reduce-scatter.2
  468.9 124.5 reduce-scatter.4

commit v9 on v8

--- a/solution.py
+++ b/solution.py
@@ -71,12 +71,16 @@
     )
 
 
+OVER_ROWS = (((0,), (0,)), ((), ()))
+OVER_LANES = (((1,), (1,)), ((), ()))
+
+
 def allowed_keys(seg_col_ref, seg_row_ref, first, count):
     keys = first + count
-    rows = lax.broadcasted_iota(jnp.int32, (count, keys), 0) + first
-    columns = lax.broadcasted_iota(jnp.int32, (count, keys), 1)
-    same = seg_col_ref[0, first : first + count, :] == seg_row_ref[0, :, :keys]
-    return same & (rows >= columns)
+    key_at = lax.broadcasted_iota(jnp.int32, (keys, count), 0)
+    row_at = lax.broadcasted_iota(jnp.int32, (keys, count), 1) + first
+    same = seg_col_ref[0, :keys, :] == seg_row_ref[0, :, first : first + count]
+    return same & (row_at >= key_at)
 
 
 def stacked(ref, rows, one, group):
@@ -93,12 +97,10 @@
 
 
 def soft_weights(queries, keys, allowed):
-    scores = lax.dot_general(
-        queries, keys, (((1,), (1,)), ((), ())), preferred_element_type=jnp.float32
-    )
+    scores = lax.dot_general(keys, queries, OVER_LANES, preferred_element_type=jnp.float32)
     scores = jnp.where(allowed, scores, -1e30)
-    weights = jnp.exp(scores - jnp.max(scores, axis=-1, keepdims=True))
-    return weights * (1.0 / jnp.sum(weights, axis=-1, keepdims=True))
+    weights = jnp.exp(scores - jnp.max(scores, axis=0, keepdims=True))
+    return weights * (1.0 / jnp.sum(weights, axis=0, keepdims=True))
 
 
 def attend_kernel(
@@ -119,13 +121,15 @@
     for first in range(0, TOK_MB, block):
         rows, keys = slice(first, first + block), slice(0, first + block)
         allowed = allowed_keys(seg_col_ref, seg_row_ref, first, block)
-        allowed = jnp.concatenate([allowed] * group, axis=0)
+        allowed = jnp.concatenate([allowed] * group, axis=1)
         for one in range(2):
             lanes = slice(one * HEAD, (one + 1) * HEAD)
             weights = soft_weights(
                 stacked(q_out, rows, one, group), k_out[keys, lanes], allowed
             ).astype(jnp.bfloat16)
-            mixed = jnp.dot(weights, v_out[keys, lanes], preferred_element_type=jnp.float32)
+            mixed = lax.dot_general(
+                weights, v_out[keys, lanes], OVER_ROWS, preferred_element_type=jnp.float32
+            )
             unstack(mixed_ref, rows, one, mixed.astype(jnp.bfloat16))
 
 
@@ -137,12 +141,10 @@
     pair = 2 * HEAD
     group = HEADS // KV_HEADS
     block = TOK_MB // 2
-    over_rows = (((0,), (0,)), ((), ()))
-    over_lanes = (((1,), (1,)), ((), ()))
     for first in range(TOK_MB - block, -1, -block):
         rows, keys = slice(first, first + block), slice(0, first + block)
         allowed = allowed_keys(seg_col_ref, seg_row_ref, first, block)
-        allowed = jnp.concatenate([allowed] * group, axis=0)
+        allowed = jnp.concatenate([allowed] * group, axis=1)
         for one in range(2):
             lanes = slice(one * HEAD, (one + 1) * HEAD)
             key_rows, value_rows = k_ref[keys, lanes], v_ref[keys, lanes]
@@ -150,18 +152,18 @@
             grads = stacked(grad_ref, rows, one, group)
             weights = soft_weights(queries, key_rows, allowed)
             grad_weights = lax.dot_general(
-                grads, value_rows, over_lanes, preferred_element_type=jnp.float32
+                value_rows, grads, OVER_LANES, preferred_element_type=jnp.float32
             )
-            grad_values = lax.dot_general(
-                weights.astype(jnp.bfloat16), grads, over_rows, preferred_element_type=jnp.float32
+            grad_values = jnp.dot(
+                weights.astype(jnp.bfloat16), grads, preferred_element_type=jnp.float32
             )
-            inner = jnp.sum(grad_weights * weights, axis=-1, keepdims=True)
+            inner = jnp.sum(grad_weights * weights, axis=0, keepdims=True)
             grad_scores = (weights * (grad_weights - inner)).astype(jnp.bfloat16)
-            grad_queries = jnp.dot(grad_scores, key_rows, preferred_element_type=jnp.float32)
+            grad_queries = lax.dot_general(
+                grad_scores, key_rows, OVER_ROWS, preferred_element_type=jnp.float32
+            )
             unstack(dq_sum, rows, one, grad_queries * HEAD ** (-0.5))
-            grad_keys = lax.dot_general(
-                grad_scores, queries, over_rows, preferred_element_type=jnp.float32
-            )
+            grad_keys = jnp.dot(grad_scores, queries, preferred_element_type=jnp.float32)
             if first == TOK_MB - block:
                 dk_sum[keys, lanes] = grad_keys
                 dv_sum[keys, lanes] = grad_values
@@ -862,12 +864,13 @@
     def bring_back(parts):
         if lo_count != 4:
             parts = parts.reshape(lo_count, tok_dev, model_width)
-            return [parts[0]] + [swap(parts[step], step) for step in range(1, lo_count)]
+            swapped = [swap(parts[step], step) for step in range(1, lo_count)]
+            return [parts[0]] + swapped, ()
         one = swap(parts[2:4], 1)
         two = swap(parts[4:6], 2)
         for_one = (wide(parts[6]) + wide(two[1])).astype(jnp.bfloat16)
         for_two = (wide(parts[7]) + wide(one[1])).astype(jnp.bfloat16)
-        return [parts[:2], one, two, swap(for_two, 2), swap(for_one, 1)]
+        return [parts[:2], one, two, swap(for_two, 2), swap(for_one, 1)], (for_one, for_two)
 
     def total_of(terms):
         if lo_count != 4:
@@ -885,13 +888,13 @@
         )
 
     back = split_back(grad_expert_rows)
-    back_parts = bring_back(back)
+    back_parts, passed_on = bring_back(back)
     produced = (
         jnp.einsum("ekrf,ekfd->erd", hidden, weights_out, preferred_element_type=jnp.float32)
         * slot_weight.reshape(hi_count, -1, 1)
     ).astype(jnp.bfloat16)
     ahead = split_back(produced)
-    grad_gate_up = hold(grad_gate_up, ahead, *back_parts[1:3])
+    grad_gate_up = hold(grad_gate_up, ahead, *passed_on)
     grad_weights_in = jnp.einsum(
         "ekrf,erd->ekfd", grad_gate_up, expert_rows, preferred_element_type=jnp.float32
     ).astype(jnp.bfloat16)
@@ -901,9 +904,10 @@
         scatter_dimension=0,
         tiled=True,
     )
-    shard_in = shard_in.T.astype(jnp.float32).reshape(model_width, 2, shard_cols)
+    shard_in = shard_in.astype(jnp.float32).reshape(2, shard_cols, model_width)
+    shard_in = jnp.transpose(shard_in, (2, 0, 1))
     ahead, back_parts = lax.optimization_barrier((ahead, back_parts))
-    ahead_parts = bring_back(ahead)
+    ahead_parts, _ = bring_back(ahead)
     grad_normed_two = total_of(back_parts)
     grad_gain_two, grad_from_norm = norm_back(residual, scale_two, gain_two, grad_normed_two)
     grad_residual = grad_output + grad_from_norm

time: 752 us -> 727 us (0.967)
  Pallas kernels: 389 us -> 373 us
    pallas_call x1, Pallas kernels: 31.4 us -> 20.2 us  [attend_back(): pl.pallas_call(attend_back_kernel, grid=grid, out_shape=tuple(shapes), in...]
    unnamed x107 -> x99, local copies, waits for them, and re-layouts: 15.7 us -> 9.89 us
  transfers between devices with their start and end apart: 24 -> 24, of which waited for: 9 -> 10; matrix products, arithmetic and copies ran while one was open for 31% -> 32% of each run, Pallas kernels for 49% -> 48%
where the time goes in v9:
time: 727 us; the launch traced here: 721 us
  Pallas kernels  373 us (51%)
  matrix products  148 us (20%)
  local copies, waits for them, and re-layouts  70 us (10%)
  waiting for transfers between devices  43.8 us (6%)
  other arithmetic  43 us (6%)
  starting transfers between devices  28.7 us (4%)
  between operations  14.9 us (2%)
    pallas_call x1, Pallas kernels, opening(): pl.pallas_call(functools.partial(opening_kernel, sizes), out_shape=(jax.S...  153 us
    pallas_call x1, Pallas kernels, closing(): pl.pallas_call(functools.partial(closing_kernel, sizes), out_shape=(jax.S...  127 us
    ppermute x19, waiting for transfers between devices, swap(): return lax.ppermute(block, 'lo', [(i, i ^ step) for i in range(lo_count)])  42.6 us
    pallas_call x10, Pallas kernels, dispatch(): pl.pallas_call(functools.partial(dispatch_kernel, weight is not None), gr...  33.9 us
    gather x8, local copies, waits for them, and re-layouts, pick(): return jnp.take(rows, index, axis=0, mode='clip')  25.5 us
    pallas_call x1, Pallas kernels, middle(): pl.pallas_call(middle_kernel, grid=(count, row_count // tile), out_shape=...  23.5 us
    ppermute x19, starting transfers between devices, swap(): return lax.ppermute(block, 'lo', [(i, i ^ step) for i in range(lo_count)])  22.6 us
    dot_general x1, matrix products, shards(): jnp.einsum('ekrf,erd->ekfd', grad_gate_up, expert_rows, preferred_element...  22.1 us
  transfers between devices with their start and end apart: 24, of which 10 were waited for; matrix products, arithmetic and copies ran while one was open for 32% of the time, Pallas kernels for 48%

profile of v9, /device:TPU:12, one launch (start us, length us, event | category | flops | bytes accessed | tf_op | source)
XLA Modules:
  0.0 721.3 jit_solution(18081489464498124387)
XLA Ops:
  16.6 6.0 all-to-all-start
  25.6 1.9 concatenate.22.shard_ref
  30.0 2.9 gather_fusion
  32.9 2.9 gather_fusion.1
  35.9 153.5 %opening.1 = (bf16[32,16,1536]{2,1,0:T(8,128)(2,1)}, bf16[32,16,1536]{2,1,0:T(8,128)(2,1)}, bf16[4,4,2,48,4224]{4,3,2,1,0:T(8,128)(2,1)}) custom-call(bf16[32,16,1536]{2,1,0:T(8,128)(2,1)} %bitcast.161, bf16[32,16,1536]{2,1,0:T(8,128)(2,1)} %bitcast.162, bf16[48,4224]{1,0:T(8,128)(2,1)} %concatenate.22.shard_ref), custom_call_target="tpu_custom_call" | custom-call | tf_op jit(solution)/shard_map/opening/pallas_call | solution.py:426
  189.4 2.3 all_gather_reshape.3
  196.8 2.3 gather_fusion.2
  199.1 3.5 collective-permute-start.3
  202.5 3.1 collective-permute-start.4
  205.6 5.3 gather_fusion.3
  216.9 9.2 %fusion.9.q_ref.k_ref.v_ref = f32[512,2560]{1,0:T(8,128)} fusion(bf16[512,1536]{1,0:T(8,128)(2,1)S(1)} %fusion.25.refs_0_, bf16[1536,4224]{1,0:T(8,128)(2,1)} %bitcast.181), kind=kOutput, calls=%fused_computation.25 | convolution fusion | flops 4026531840 | bytes 14680064 | tf_op jit(solution)/shard_map/dot_general | solution.py:787
  226.1 14.7 %attend.1 = (bf16[512,1536]{1,0:T(8,128)(2,1)}, bf16[512,512]{1,0:T(8,128)(2,1)}, bf16[512,512]{1,0:T(8,128)(2,1)}, bf16[512,1536]{1,0:T(8,128)(2,1)}) custom-call(f32[512,2560]{1,0:T(8,128)} %fusion.9.q_ref.k_ref.v_ref, f32[512,2560]{1,0:T(8,128)} %fusion.9.q_ref.k_ref.v_ref, f32[512,2560]{1,0:T(8,128)} %fusion.9.q_ref.k_ref.v_ref, ...), custom_call_target="tpu_custom_call" | custom-call | tf_op jit(solution)/shard_map/attend/pallas_call | solution.py:204
  240.8 2.1 slice.220
  245.7 5.2 multiply_reduce_fusion.2
  251.0 1.6 copy-done.6
  254.1 8.4 %collective-permute-done.5.refs_1_.rows_ref = bf16[256,1536]{1,0:T(8,128)(2,1)} collective-permute-done((bf16[256,1536]{1,0:T(8,128)(2,1)}, bf16[256,1536]{1,0:T(8,128)(2,1)}, u32[]{:S(2)}, u32[]{:S(2)}) %collective-permute-start.5) | collective-permute-done | bytes 786464 | tf_op jit(solution)/shard_map/ppermute | solution.py:720
  264.4 1.6 collective-permute-start.8
  267.9 2.0 copy.173.refs_0_
  269.9 2.3 fusion.18.choose_ref
  272.2 3.5 dispatch.15.refs_0_
  275.7 3.8 dispatch.10.refs_1_
  279.6 3.7 dispatch.11.refs_1_
  283.3 3.7 dispatch.12.refs_1_
  286.9 3.0 dispatch.13.refs_1_
  290.0 3.0 dispatch.14
  293.0 7.1 collective-permute-done.8.rows_ref
  303.8 13.9 %convert_bitcast_fusion.grad_ref = bf16[4,2,1024,256]{3,2,1,0:T(8,128)(2,1)} fusion(bf16[4,1024,1536,1]{2,1,3,0:T(8,128)(2,1)} %bitcast.150, bf16[4,2,256,1536]{3,2,1,0:T(8,128)(2,1)} %bitcast.188), kind=kOutput, calls=%fused_computation.33 | convolution fusion | flops 6444548096 | bytes 23068672 | tf_op jit(solution)/shard_map/erd,ekfd->ekrf/dot_general | solution.py:829
  319.2 2.1 collective-permute-done.9.rows_ref
  321.4 3.6 dispatch.16.refs_0_
  325.0 3.6 dispatch.17.refs_0_
  328.5 2.9 dispatch.18.refs_0_
  331.5 3.0 dispatch.19
  334.4 23.5 %middle.1 = (bf16[4,2,1024,256]{3,2,1,0:T(8,128)(2,1)}, bf16[4,2,1024,512]{3,2,1,0:T(8,128)(2,1)}) custom-call(bf16[4,1024,1536]{2,1,0:T(8,128)(2,1)} %bitcast.148, bf16[4,2,1536,512]{3,2,1,0:T(8,128)(2,1)} %bitcast.157, bf16[4,2,1024,256]{3,2,1,0:T(8,128)(2,1)} %convert_bitcast_fusion.grad_ref), custom_call_target="tpu_custom_call" | custom-call | tf_op jit(solution)/shard_map/middle/pallas_call | solution.py:666
  358.0 13.9 %convolution_convert_fusion.3 = bf16[4,2,256,1536]{3,2,1,0:T(8,128)(2,1)} fusion(bf16[4,2,1024,256]{3,2,1,0:T(8,128)(2,1)} %get-tuple-element.76, bf16[4,1024,1536,1]{2,1,3,0:T(8,128)(2,1)} %bitcast.151), kind=kOutput, calls=%fused_computation.32 | convolution fusion | flops 6445596672 | bytes 23068672 | tf_op jit(solution)/shard_map/ekrf,erd->ekfd/dot_general | solution.py:839
  371.9 21.0 %bitcast_convert_fusion = bf16[4,1024,1536]{2,1,0:T(8,128)(2,1)} fusion(bf16[4,2,1024,512]{3,2,1,0:T(8,128)(2,1)} %get-tuple-element.78.refs_0_, bf16[4,2,1536,512]{3,2,1,0:T(8,128)(2,1)} %bitcast.158), kind=kOutput, calls=%fused_computation.10 | convolution fusion | flops 12891193344 | bytes 33554432 | tf_op jit(solution)/shard_map/ekrf,ekdf->erd/dot_general | solution.py:849
  393.0 8.1 %bitcast_convert_fusion.1 = bf16[8,256,1536]{2,1,0:T(8,128)(2,1)S(1)} fusion(bf16[4,8,128,1536]{3,2,1,0:T(8,128)(2,1)} %bitcast.191, s32[8,4,256]{2,1,0:T(4,128)S(1)} %copy.167, pred[8,4,256]{2,1,0:T(4,128)(4,1)S(1)} %bitcast.173), kind=kOutput, calls=%fused_computation.15 | convolution fusion | flops 3226468352 | bytes 18915328 | tf_op jit(solution)/shard_map/becr,ebcd->brd/dot_general | solution.py:854
  401.1 2.2 fusion.66
  404.5 12.6 %fusion.1 = bf16[4,1024,1536]{2,1,0:T(8,128)(2,1)} fusion(bf16[4,2,1024,256]{3,2,1,0:T(8,128)(2,1)S(1)} %copy-done.42, bf16[4,2,256,1536]{3,2,1,0:T(8,128)(2,1)} %bitcast.189, f32[4,1024]{1,0:T(4,128)S(1)} %bitcast.177), kind=kOutput, calls=%fused_computation.12 | convolution fusion | flops 6455033856 | bytes 23085056 | tf_op jit(solution)/shard_map/ekrf,ekfd->erd/dot_general | solution.py:893
  417.2 10.9 %bitcast_convert_fusion.2.refs_1_ = bf16[8,256,1536]{2,1,0:T(8,128)(2,1)} fusion(bf16[4,8,128,1536]{3,2,1,0:T(8,128)(2,1)} %bitcast.190, s32[8,4,256]{2,1,0:T(4,128)S(1)} %copy.167, pred[8,4,256]{2,1,0:T(4,128)(4,1)S(1)} %bitcast.174), kind=kOutput, calls=%fused_computation.16 | convolution fusion | flops 3226468352 | bytes 18915328 | tf_op jit(solution)/shard_map/becr,ebcd->brd/dot_general | solution.py:854
  428.1 8.8 %collective-permute-done.11 = bf16[2,256,1536]{2,1,0:T(8,128)(2,1)} collective-permute-done((bf16[2,256,1536]{2,1,0:T(8,128)(2,1)}, bf16[2,256,1536]{2,1,0:T(8,128)(2,1)}, u32[]{:S(2)}, u32[]{:S(2)}) %collective-permute-start.11) | collective-permute-done | bytes 1572896 | tf_op jit(solution)/shard_map/ppermute | solution.py:720
  437.1 2.9 fusion.46
  440.0 22.1 %convolution_convert_fusion = bf16[4,2,512,1536]{3,2,1,0:T(8,128)(2,1)} fusion(bf16[4,2,1024,512]{3,2,1,0:T(8,128)(2,1)} %hold.9, bf16[4,1024,1536,1]{2,1,3,0:T(8,128)(2,1)} %bitcast.149), kind=kOutput, calls=%fused_computation.13 | convolution fusion | flops 12891193344 | bytes 33554432 | tf_op jit(solution)/shard_map/ekrf,erd->ekfd/dot_general | solution.py:898
  465.8 13.2 %collective-permute-done.13 = bf16[256,1536]{1,0:T(8,128)(2,1)S(1)} collective-permute-done((bf16[256,1536]{1,0:T(8,128)(2,1)S(1)}, bf16[256,1536]{1,0:T(8,128)(2,1)S(1)}, u32[]{:S(2)}, u32[]{:S(2)}) %collective-permute-start.13) | collective-permute-done | bytes 786464 | tf_op jit(solution)/shard_map/ppermute | solution.py:720
  479.2 4.8 fusion.65
  486.5 1.9 bitcast_add_fusion.3
  491.0 7.3 %fusion.38.grad_ref = bf16[512,1536]{1,0:T(8,128)(2,1)} fusion(bf16[1536,4224]{1,0:T(8,128)(2,1)} %bitcast.183, f32[512,1536]{1,0:T(8,128)S(1)} %subtract_add_fusion), kind=kOutput, calls=%fused_computation.62 | convolution fusion | flops 2417491968 | bytes 9437184 | tf_op jit(solution)/shard_map/nd,qd->nq/dot_general | solution.py:918
  498.3 20.2 %attend_back.1 = (bf16[512,1536]{1,0:T(8,128)(2,1)}, bf16[512,512]{1,0:T(8,128)(2,1)}, bf16[512,512]{1,0:T(8,128)(2,1)}) custom-call(bf16[512,1536]{1,0:T(8,128)(2,1)} %get-tuple-element.80.q_ref, bf16[512,512]{1,0:T(8,128)(2,1)} %get-tuple-element.81.k_ref, bf16[512,512]{1,0:T(8,128)(2,1)} %get-tuple-element.82.v_ref, bf16[512,1536]{1,0:T(8,128)(2,1)} %fusion.38.grad_ref, ...), custom_call_target="tpu_custom_call" | custom-call | tf_op jit(solution)/shard_map/attend_back/pallas_call | solution.py:223
  518.5 1.7 constant_dynamic-update-slice_fusion.10
  520.7 10.4 %fusion.34 = (f32[512]{0:T(512)S(1)}, bf16[1536]{0:T(1024)(128)(2,1)S(1)}, f32[512,1536]{1,0:T(8,128)}) fusion(bf16[512,1536]{1,0:T(8,128)(2,1)S(1)} %copy-done.10, f32[1536]{0:T(1024)S(1)} %copy-done.32, f32[512]{0:T(512)S(1)} %copy-done.38, bf16[512,2560]{1,0:T(8,128)(2,1)S(1)} %constant_dynamic-update-slice_fusion.8, bf16[1536,4224]{1,0:T(8,128)(2,1)} %bitcast.184), kind=kOutput, calls=%fused_computation.53 | convolution fusion | flops 4032034816 | bytes 15217664 | tf_op jit(solution)/shard_map/nc,dc->nd/dot_general | solution.py:929
  531.4 3.9 fusion.30
  535.3 3.3 gather_fusion.5
  538.6 6.5 convolution_convert_fusion.2
  545.1 3.1 fusion.48
  550.1 6.7 convolution_convert_fusion.1
  556.9 5.3 fusion.2
  562.2 2.6 convert_element_type.235
  564.8 2.6 bitcast_add_fusion.1
  568.4 2.9 gather_fusion.4
  571.3 126.9 %closing.1 = (bf16[32,16,1536]{2,1,0:T(8,128)(2,1)}, bf16[32,16,1536]{2,1,0:T(8,128)(2,1)}, f32[48,4224]{1,0:T(8,128)}) custom-call(bf16[32,16,1536]{2,1,0:T(8,128)(2,1)} %bitcast.164, bf16[32,16,1536]{2,1,0:T(8,128)(2,1)} %bitcast.163, bf16[4,4,2,48,4224]{4,3,2,1,0:T(8,128)(2,1)} %bitcast.156), custom_call_target="tpu_custom_call" | custom-call | tf_op jit(solution)/shard_map/closing/pallas_call | solution.py:580
  698.2 2.0 slice.185
  700.2 1.7 slice.186
  701.9 2.9 gather_fusion.7
  704.8 2.9 gather_fusion.6
  709.3 5.1 copy.195
  (216 shorter events, 54.5 us)
Async XLA Ops:
  7.2 22.8 %copy-start = (bf16[512,1536]{1,0:T(8,128)(2,1)S(1)}, bf16[512,1536]{1,0:T(8,128)(2,1)}, u32[]{:S(2)}) copy-start(bf16[512,1536]{1,0:T(8,128)(2,1)} %param.12) | copy-start | bytes 4718596
  7.2 296.7 %all-gather.6.cloned.1.call-start = ((), (), s32[]{:S(2)}) async-start(), calls=%async_computation.6 | async-start | bytes 7077888 | tf_op jit(solution)/shard_map/all_gather | solution.py:781
  9.4 19.9 %collective-permute-start = (f32[512,16]{0,1:T(8,128)S(1)}, f32[512,16]{0,1:T(8,128)S(1)}, u32[]{:S(2)}, u32[]{:S(2)}) collective-permute-start(f32[512,16]{0,1:T(8,128)S(1)} %pad_maximum_fusion.2), channel_id=1, source_target_pairs={{0,2},{2,0},{4,6},{6,4},{1,3},{3,1},{5,7},{7,5},{8,10},{10,8},{12,... | collective-permute-start | bytes 98312 | tf_op jit(solution)/shard_map/ppermute | solution.py:720
  10.9 18.4 %collective-permute-start.1 = (f32[512,16]{0,1:T(8,128)S(1)}, f32[512,16]{0,1:T(8,128)S(1)}, u32[]{:S(2)}, u32[]{:S(2)}) collective-permute-start(f32[512,16]{0,1:T(8,128)S(1)} %pad_maximum_fusion.2), channel_id=1, source_target_pairs={{0,6},{2,4},{4,2},{6,0},{1,7},{3,5},{5,3},{7,1},{8,14},{10,12},{12... | collective-permute-start | bytes 98312 | tf_op jit(solution)/shard_map/ppermute | solution.py:720
  11.3 18.0 %collective-permute-start.2 = (f32[512,16]{0,1:T(8,128)S(1)}, f32[512,16]{0,1:T(8,128)S(1)}, u32[]{:S(2)}, u32[]{:S(2)}) collective-permute-start(f32[512,16]{0,1:T(8,128)S(1)} %pad_maximum_fusion.2), channel_id=1, source_target_pairs={{0,4},{2,6},{4,0},{6,2},{1,5},{3,7},{5,1},{7,3},{8,12},{10,14},{12... | collective-permute-start | bytes 98312 | tf_op jit(solution)/shard_map/ppermute | solution.py:720
  16.6 11.3 %all-to-all-start = ((s32[32,1,16]{2,1,0:T(1,128)}), s32[32,1,16]{2,1,0:T(1,128)S(1)}, u32[]{:S(2)}, u32[]{:S(2)}) async-start(s32[32,1,16]{2,1,0:T(1,128)} %bitcast.2), calls=%async_computation | async-start | bytes 32768 | tf_op jit(solution)/shard_map/all_to_all | solution.py:738
  22.6 311.8 %all-gather.4.cloned.1.call-start = ((), (), s32[]{:S(2)}) async-start(), calls=%async_computation.3 | async-start | bytes 14155776 | tf_op jit(solution)/shard_map/all_gather | solution.py:778
  30.0 2.9 copy-start.2
  35.9 153.5 %copy-start.22 = (bf16[1536,2,256]{2,1,0:T(2,128)(2,1)S(1)}, bf16[1536,2,256]{2,1,0:T(2,128)(2,1)}, u32[]{:S(2)}) copy-start(bf16[1536,2,256]{2,1,0:T(2,128)(2,1)} %param.22) | copy-start | bytes 4718596
  189.4 2.4 copy-start.41
  191.7 5.1 copy-start.3
  191.7 370.5 %reduce-scatter.3.cloned.1.call-start = ((), (), s32[]{:S(2)}) async-start(), calls=%async_computation.4 | async-start | bytes 7077888 | tf_op jit(solution)/shard_map/reduce_scatter | solution.py:843
  199.1 6.6 copy-start.11
  199.1 41.7 %collective-permute-start.3 = (bf16[512,1536]{1,0:T(8,128)(2,1)S(1)}, bf16[512,1536]{1,0:T(8,128)(2,1)}, u32[]{:S(2)}, u32[]{:S(2)}) collective-permute-start(bf16[512,1536]{1,0:T(8,128)(2,1)S(1)} %gather_fusion.2), channel_id=1, source_target_pairs={{0,2},{2,0},{4,6},{6,4},{1,3},{3,1},{5,7},{7,5},{8,10},{10,8},{12,... | collective-permute-start | bytes 4718600 | tf_op jit(solution)/shard_map/ppermute | solution.py:720
  202.5 40.4 %collective-permute-start.4 = (bf16[512,1536]{1,0:T(8,128)(2,1)S(1)}, bf16[512,1536]{1,0:T(8,128)(2,1)}, u32[]{:S(2)}, u32[]{:S(2)}) collective-permute-start(bf16[512,1536]{1,0:T(8,128)(2,1)S(1)} %gather_fusion.2), channel_id=1, source_target_pairs={{0,4},{2,6},{4,0},{6,2},{1,5},{3,7},{5,1},{7,3},{8,12},{10,14},{12... | collective-permute-start | bytes 4718600 | tf_op jit(solution)/shard_map/ppermute | solution.py:720
  211.0 34.7 %copy-start.9 = (bf16[512,1536]{1,0:T(8,128)(2,1)}, bf16[512,1536]{1,0:T(8,128)(2,1)S(1)}, u32[]{:S(2)}) copy-start(bf16[512,1536]{1,0:T(8,128)(2,1)S(1)} %gather_fusion.3) | copy-start | bytes 4718596
  214.4 36.6 %copy-start.29 = (f32[1536]{0:T(1024)}, f32[1536]{0:T(1024)S(1)}, u32[]{:S(2)}) copy-start(f32[1536]{0:T(1024)S(1)} %get-tuple-element.108) | copy-start | bytes 18436
  215.7 1.2 copy-start.14
  242.9 19.6 %collective-permute-start.5 = (bf16[256,1536]{1,0:T(8,128)(2,1)}, bf16[256,1536]{1,0:T(8,128)(2,1)}, u32[]{:S(2)}, u32[]{:S(2)}) collective-permute-start(bf16[256,1536]{1,0:T(8,128)(2,1)} %slice.220), channel_id=1, source_target_pairs={{0,4},{2,6},{4,0},{6,2},{1,5},{3,7},{5,1},{7,3},{8,12},{10,14},{12... | collective-permute-start | bytes 2359304 | tf_op jit(solution)/shard_map/ppermute | solution.py:720
  244.1 19.4 %collective-permute-start.6 = (bf16[256,1536]{1,0:T(8,128)(2,1)S(1)}, bf16[256,1536]{1,0:T(8,128)(2,1)S(1)}, u32[]{:S(2)}, u32[]{:S(2)}) collective-permute-start(bf16[256,1536]{1,0:T(8,128)(2,1)S(1)} %slice.221), channel_id=1, source_target_pairs={{0,2},{2,0},{4,6},{6,4},{1,3},{3,1},{5,7},{7,5},{8,10},{10,8},{12,... | collective-permute-start | bytes 2359304 | tf_op jit(solution)/shard_map/ppermute | solution.py:720
  250.9 1.7 copy-start.6
  251.0 12.6 %copy-start.33 = (f32[512]{0:T(512)}, f32[512]{0:T(512)S(1)}, u32[]{:S(2)}) copy-start(f32[512]{0:T(512)S(1)} %add_rsqrt_fusion) | copy-start | bytes 6148
  254.1 12.3 %copy-start.28 = (f32[8,256,16]{1,2,0:T(8,128)S(1)}, f32[8,256,16]{1,2,0:T(8,128)}, u32[]{:S(2)}) copy-start(f32[8,256,16]{1,2,0:T(8,128)} %copy-done.27) | copy-start | bytes 393220
  263.5 0.9 copy-start.21
  264.4 35.6 %collective-permute-start.8 = (bf16[512,1536]{1,0:T(8,128)(2,1)}, bf16[512,1536]{1,0:T(8,128)(2,1)S(1)}, u32[]{:S(2)}, u32[]{:S(2)}) collective-permute-start(bf16[512,1536]{1,0:T(8,128)(2,1)} %hold.7.rows_ref), channel_id=1, source_target_pairs={{0,4},{2,6},{4,0},{6,2},{1,5},{3,7},{5,1},{7,3},{8,12},{10,14},{12... | collective-permute-start | bytes 4718600 | tf_op jit(solution)/shard_map/ppermute | solution.py:720
  266.1 36.5 %collective-permute-start.7 = (bf16[512,1536]{1,0:T(8,128)(2,1)}, bf16[512,1536]{1,0:T(8,128)(2,1)S(1)}, u32[]{:S(2)}, u32[]{:S(2)}) collective-permute-start(bf16[512,1536]{1,0:T(8,128)(2,1)} %hold.7.rows_ref), channel_id=1, source_target_pairs={{0,2},{2,0},{4,6},{6,4},{1,3},{3,1},{5,7},{7,5},{8,10},{10,8},{12,... | collective-permute-start | bytes 4718600 | tf_op jit(solution)/shard_map/ppermute | solution.py:720
  300.1 17.6 %copy-start.17 = (bf16[512,1536]{1,0:T(8,128)(2,1)}, bf16[512,1536]{1,0:T(8,128)(2,1)S(1)}, u32[]{:S(2)}) copy-start(bf16[512,1536]{1,0:T(8,128)(2,1)S(1)} %collective-permute-done.8.rows_ref) | copy-start | bytes 4718596
  301.1 18.1 %collective-permute-start.10 = (bf16[256,1536]{1,0:T(8,128)(2,1)}, bf16[256,1536]{1,0:T(8,128)(2,1)}, u32[]{:S(2)}, u32[]{:S(2)}) collective-permute-start(bf16[256,1536]{1,0:T(8,128)(2,1)} %slice.223), channel_id=1, source_target_pairs={{0,2},{2,0},{4,6},{6,4},{1,3},{3,1},{5,7},{7,5},{8,10},{10,8},{12,... | collective-permute-start | bytes 2359304 | tf_op jit(solution)/shard_map/ppermute | solution.py:720
  302.5 15.2 %copy-start.18 = (bf16[512,1536]{1,0:T(8,128)(2,1)}, bf16[512,1536]{1,0:T(8,128)(2,1)S(1)}, u32[]{:S(2)}) copy-start(bf16[512,1536]{1,0:T(8,128)(2,1)S(1)} %collective-permute-done.7.rows_ref) | copy-start | bytes 4718596
  303.5 17.8 %collective-permute-start.9 = (bf16[256,1536]{1,0:T(8,128)(2,1)}, bf16[256,1536]{1,0:T(8,128)(2,1)}, u32[]{:S(2)}, u32[]{:S(2)}) collective-permute-start(bf16[256,1536]{1,0:T(8,128)(2,1)} %slice.222), channel_id=1, source_target_pairs={{0,4},{2,6},{4,0},{6,2},{1,5},{3,7},{5,1},{7,3},{8,12},{10,14},{12... | collective-permute-start | bytes 2359304 | tf_op jit(solution)/shard_map/ppermute | solution.py:720
  371.9 337.4 %reduce-scatter.5.cloned.1.call-start = ((), (), s32[]{:S(2)}) async-start(), calls=%async_computation.5 | async-start | bytes 14155776 | tf_op jit(solution)/shard_map/reduce_scatter | solution.py:901
  401.1 3.4 copy-start.42
  403.4 33.5 %collective-permute-start.11 = (bf16[2,256,1536]{2,1,0:T(8,128)(2,1)}, bf16[2,256,1536]{2,1,0:T(8,128)(2,1)}, u32[]{:S(2)}, u32[]{:S(2)}) collective-permute-start(bf16[2,256,1536]{2,1,0:T(8,128)(2,1)} %get-tuple-element.120), channel_id=1, source_target_pairs={{0,2},{2,0},{4,6},{6,4},{1,3},{3,1},{5,7},{7,5},{8,10},{10,8},{12,... | collective-permute-start | bytes 4718600 | tf_op jit(solution)/shard_map/ppermute | solution.py:720
  403.7 33.4 %collective-permute-start.12 = (bf16[2,256,1536]{2,1,0:T(8,128)(2,1)S(1)}, bf16[2,256,1536]{2,1,0:T(8,128)(2,1)}, u32[]{:S(2)}, u32[]{:S(2)}) collective-permute-start(bf16[2,256,1536]{2,1,0:T(8,128)(2,1)S(1)} %get-tuple-element.119), channel_id=1, source_target_pairs={{0,4},{2,6},{4,0},{6,2},{1,5},{3,7},{5,1},{7,3},{8,12},{10,14},{12... | collective-permute-start | bytes 4718600 | tf_op jit(solution)/shard_map/ppermute | solution.py:720
  462.2 1.1 copy-start.20
  462.2 1.5 copy-start.19
  462.2 2.8 copy-start.40
  462.2 3.4 copy-start.36
  463.3 15.7 %collective-permute-start.13 = (bf16[256,1536]{1,0:T(8,128)(2,1)S(1)}, bf16[256,1536]{1,0:T(8,128)(2,1)S(1)}, u32[]{:S(2)}, u32[]{:S(2)}) collective-permute-start(bf16[256,1536]{1,0:T(8,128)(2,1)S(1)} %copy-done.20), channel_id=1, source_target_pairs={{0,4},{2,6},{4,0},{6,2},{1,5},{3,7},{5,1},{7,3},{8,12},{10,14},{12... | collective-permute-start | bytes 2359304 | tf_op jit(solution)/shard_map/ppermute | solution.py:720
  463.6 15.6 %collective-permute-start.14 = (bf16[256,1536]{1,0:T(8,128)(2,1)S(1)}, bf16[256,1536]{1,0:T(8,128)(2,1)S(1)}, u32[]{:S(2)}, u32[]{:S(2)}) collective-permute-start(bf16[256,1536]{1,0:T(8,128)(2,1)S(1)} %copy-done.19), channel_id=1, source_target_pairs={{0,2},{2,0},{4,6},{6,4},{1,3},{3,1},{5,7},{7,5},{8,10},{10,8},{12,... | collective-permute-start | bytes 2359304 | tf_op jit(solution)/shard_map/ppermute | solution.py:720
  479.2 7.3 %copy-start.16 = (bf16[2,256,1536]{2,1,0:T(8,128)(2,1)S(1)}, bf16[2,256,1536]{2,1,0:T(8,128)(2,1)}, u32[]{:S(2)}) copy-start(bf16[2,256,1536]{2,1,0:T(8,128)(2,1)} %get-tuple-element.83) | copy-start | bytes 4718596
  483.9 61.2 %collective-permute-start.15 = (bf16[2,256,1536]{2,1,0:T(8,128)(2,1)}, bf16[2,256,1536]{2,1,0:T(8,128)(2,1)}, u32[]{:S(2)}, u32[]{:S(2)}) collective-permute-start(bf16[2,256,1536]{2,1,0:T(8,128)(2,1)} %get-tuple-element.116), channel_id=1, source_target_pairs={{0,2},{2,0},{4,6},{6,4},{1,3},{3,1},{5,7},{7,5},{8,10},{10,8},{12,... | collective-permute-start | bytes 4718600 | tf_op jit(solution)/shard_map/ppermute | solution.py:720
  485.0 3.4 copy-start.7
  485.0 3.4 copy-start.30
  485.0 3.4 copy-start.34
  485.0 60.1 %collective-permute-start.16 = (bf16[2,256,1536]{2,1,0:T(8,128)(2,1)}, bf16[2,256,1536]{2,1,0:T(8,128)(2,1)}, u32[]{:S(2)}, u32[]{:S(2)}) collective-permute-start(bf16[2,256,1536]{2,1,0:T(8,128)(2,1)} %get-tuple-element.115), channel_id=1, source_target_pairs={{0,4},{2,6},{4,0},{6,2},{1,5},{3,7},{5,1},{7,3},{8,12},{10,14},{12... | collective-permute-start | bytes 4718600 | tf_op jit(solution)/shard_map/ppermute | solution.py:720
  488.4 1.4 copy-start.12
  491.0 7.3 %copy-start.13 = (f32[512,1536]{1,0:T(8,128)}, f32[512,1536]{1,0:T(8,128)S(1)}, u32[]{:S(2)}) copy-start(f32[512,1536]{1,0:T(8,128)S(1)} %subtract_add_fusion) | copy-start | bytes 9437188
  518.5 1.7 copy-start.26
  518.5 1.8 copy-start.25
  518.5 2.2 copy-start.10
  518.5 2.2 copy-start.32
  518.5 2.2 copy-start.38
  520.7 10.4 %copy-start.24 = (bf16[512,2560]{1,0:T(8,128)(2,1)}, bf16[512,2560]{1,0:T(8,128)(2,1)S(1)}, u32[]{:S(2)}) copy-start(bf16[512,2560]{1,0:T(8,128)(2,1)S(1)} %constant_dynamic-update-slice_fusion.8) | copy-start | bytes 7864324
  535.3 3.3 copy-start.23
  548.2 16.5 %collective-permute-start.17 = (bf16[256,1536]{1,0:T(8,128)(2,1)}, bf16[256,1536]{1,0:T(8,128)(2,1)}, u32[]{:S(2)}, u32[]{:S(2)}) collective-permute-start(bf16[256,1536]{1,0:T(8,128)(2,1)} %get-tuple-element.113), channel_id=1, source_target_pairs={{0,4},{2,6},{4,0},{6,2},{1,5},{3,7},{5,1},{7,3},{8,12},{10,14},{12... | collective-permute-start | bytes 2359304 | tf_op jit(solution)/shard_map/ppermute | solution.py:720
  548.9 15.8 %collective-permute-start.18 = (bf16[256,1536]{1,0:T(8,128)(2,1)S(1)}, bf16[256,1536]{1,0:T(8,128)(2,1)}, u32[]{:S(2)}, u32[]{:S(2)}) collective-permute-start(bf16[256,1536]{1,0:T(8,128)(2,1)S(1)} %get-tuple-element.112), channel_id=1, source_target_pairs={{0,2},{2,0},{4,6},{6,4},{1,3},{3,1},{5,7},{7,5},{8,10},{10,8},{12,... | collective-permute-start | bytes 2359304 | tf_op jit(solution)/shard_map/ppermute | solution.py:720
  550.1 6.8 slice-start
  550.1 6.8 slice-start.1
  562.2 2.6 copy-start.15
  564.8 2.8 copy-start.8
  698.2 3.7 copy-start.5
  701.9 2.9 copy-start.4
  704.8 9.5 %copy-start.1 = (bf16[512,1536]{1,0:T(8,128)(2,1)S(1)}, bf16[512,1536]{1,0:T(8,128)(2,1)}, u32[]{:S(2)}) copy-start(bf16[512,1536]{1,0:T(8,128)(2,1)} %param.12) | copy-start | bytes 4718596
  (5 other events, 3.1 us)
Sparse Core Ops, SparseCore 0:
  9.6 94.1 all-gather.5
  191.8 116.5 all-gather.3
  372.0 65.1 reduce-scatter.2
  462.3 142.0 reduce-scatter.4

commit v10 on v9

--- a/solution.py
+++ b/solution.py
@@ -762,6 +762,17 @@
     asked_grads = pick(cotangent, asked_rows).reshape(
         device_count, peer_rows, model_width
     )
+    segment, position = layout_rows(lengths)
+    cosine_table, sine_table = rope_tables(position)
+    sides = (
+        jnp.tile(cosine_table, (1, 4)),
+        jnp.concatenate([-sine_table, sine_table] * 2, axis=1),
+        segment.reshape(-1, TOK_MB, 1),
+        segment.reshape(-1, 1, TOK_MB),
+    )
+    asked_tokens = hold(asked_tokens, *sides)
+    shard_cols = expert_in.shape[2]
+    expert_in = expert_in.reshape(model_width, 2 * shard_cols)
     got_rows, got_grad, packed = opening(sizes, asked_tokens, asked_grads, weight_shard)
     got_rows, packed, expert_in = lax.optimization_barrier((got_rows, packed, expert_in))
     packed = packed.reshape(model_width, -1)
@@ -774,24 +785,15 @@
     gain_pair = packed[:, qkv_cols + model_width :].astype(jnp.float32)
     gain_one = gain_pair[:, 0]
     gain_two = gain_pair[:, 1]
-    shard_cols = expert_in.shape[2]
     weights_in = lax.all_gather(
-        expert_in.reshape(model_width, 2 * shard_cols), ("hi", "core"), axis=0
+        expert_in, ("hi", "core"), axis=0
     ).reshape(hi_count, 2, model_width, 2 * shard_cols)
     weights_out = lax.all_gather(expert_out, ("hi", "core"), axis=0).reshape(
         hi_count, 2, shard_cols, model_width
     )
-    segment, position = layout_rows(lengths)
     scale_one = lax.rsqrt(jnp.mean(rows_in * rows_in, axis=1, keepdims=True) + epsilon)
     normed = (rows_in * scale_one * gain_one).astype(jnp.bfloat16)
     projected = jnp.dot(normed, qkv_full, preferred_element_type=jnp.float32)
-    cosine_table, sine_table = rope_tables(position)
-    sides = (
-        jnp.tile(cosine_table, (1, 4)),
-        jnp.concatenate([-sine_table, sine_table] * 2, axis=1),
-        segment.reshape(-1, TOK_MB, 1),
-        segment.reshape(-1, 1, TOK_MB),
-    )
     queries, key_rows, value_rows, mixed_rows = attend(projected, sides)
     if lo_count == 4:
         mixed_rows = hold(mixed_rows, grad_blocks[1][0], grad_blocks[2][0])
@@ -865,12 +867,12 @@
         if lo_count != 4:
             parts = parts.reshape(lo_count, tok_dev, model_width)
             swapped = [swap(parts[step], step) for step in range(1, lo_count)]
-            return [parts[0]] + swapped, ()
+            return [parts[0]] + swapped
         one = swap(parts[2:4], 1)
         two = swap(parts[4:6], 2)
         for_one = (wide(parts[6]) + wide(two[1])).astype(jnp.bfloat16)
         for_two = (wide(parts[7]) + wide(one[1])).astype(jnp.bfloat16)
-        return [parts[:2], one, two, swap(for_two, 2), swap(for_one, 1)], (for_one, for_two)
+        return [parts[:2], one, two, swap(for_two, 2), swap(for_one, 1)]
 
     def total_of(terms):
         if lo_count != 4:
@@ -888,13 +890,12 @@
         )
 
     back = split_back(grad_expert_rows)
-    back_parts, passed_on = bring_back(back)
+    back_parts = bring_back(back)
     produced = (
         jnp.einsum("ekrf,ekfd->erd", hidden, weights_out, preferred_element_type=jnp.float32)
         * slot_weight.reshape(hi_count, -1, 1)
     ).astype(jnp.bfloat16)
     ahead = split_back(produced)
-    grad_gate_up = hold(grad_gate_up, ahead, *passed_on)
     grad_weights_in = jnp.einsum(
         "ekrf,erd->ekfd", grad_gate_up, expert_rows, preferred_element_type=jnp.float32
     ).astype(jnp.bfloat16)
@@ -907,7 +908,7 @@
     shard_in = shard_in.astype(jnp.float32).reshape(2, shard_cols, model_width)
     shard_in = jnp.transpose(shard_in, (2, 0, 1))
     ahead, back_parts = lax.optimization_barrier((ahead, back_parts))
-    ahead_parts, _ = bring_back(ahead)
+    ahead_parts = bring_back(ahead)
     grad_normed_two = total_of(back_parts)
     grad_gain_two, grad_from_norm = norm_back(residual, scale_two, gain_two, grad_normed_two)
     grad_residual = grad_output + grad_from_norm

time: 727 us -> 717 us (0.986)
  Pallas kernels: 373 us -> 363 us
    pallas_call x1, Pallas kernels: 153 us -> 143 us  [opening(): pl.pallas_call(functools.partial(opening_kernel, sizes), out_shape=(jax.S...]
    unnamed x99 -> x120, local copies, waits for them, and re-layouts: 9.89 us -> 16.6 us
  transfers between devices with their start and end apart: 24 -> 24, of which waited for: 10 -> 8; matrix products, arithmetic and copies ran while one was open for 32% -> 33% of each run, Pallas kernels for 48% -> 48%
where the time goes in v10:
time: 717 us; the launch traced here: 711 us
  Pallas kernels  363 us (51%)
  matrix products  145 us (20%)
  local copies, waits for them, and re-layouts  72.5 us (10%)
  waiting for transfers between devices  45.4 us (6%)
  other arithmetic  44.7 us (6%)
  starting transfers between devices  25.7 us (4%)
  between operations  15 us (2%)
    pallas_call x1, Pallas kernels, opening(): pl.pallas_call(functools.partial(opening_kernel, sizes), out_shape=(jax.S...  143 us
    pallas_call x1, Pallas kernels, closing(): pl.pallas_call(functools.partial(closing_kernel, sizes), out_shape=(jax.S...  128 us
    ppermute x19, waiting for transfers between devices, swap(): return lax.ppermute(block, 'lo', [(i, i ^ step) for i in range(lo_count)])  44.7 us
    pallas_call x10, Pallas kernels, dispatch(): pl.pallas_call(functools.partial(dispatch_kernel, weight is not None), gr...  33.9 us
    gather x8, local copies, waits for them, and re-layouts, pick(): return jnp.take(rows, index, axis=0, mode='clip')  25.2 us
    pallas_call x1, Pallas kernels, middle(): pl.pallas_call(middle_kernel, grid=(count, row_count // tile), out_shape=...  23.6 us
    dot_general x1, matrix products, shards(): jnp.einsum('ekrf,erd->ekfd', grad_gate_up, expert_rows, preferred_element...  22.9 us
    dot_general x1, matrix products, shards(): jnp.einsum('ekrf,ekdf->erd', grad_gate_up, weights_in, preferred_element_...  20.5 us
  transfers between devices with their start and end apart: 24, of which 8 were waited for; matrix products, arithmetic and copies ran while one was open for 33% of the time, Pallas kernels for 48%

profile of v10, /device:TPU:12, one launch (start us, length us, event | category | flops | bytes accessed | tf_op | source)
XLA Modules:
  0.0 711.2 jit_solution(1510799303763798651)
XLA Ops:
  17.3 6.0 all-to-all-start
  26.5 1.7 fusion.54
  36.2 1.8 concatenate.23.shard_ref
  45.0 2.9 gather_fusion
  48.0 2.9 gather_fusion.1
  50.9 142.5 %opening.1 = (bf16[32,16,1536]{2,1,0:T(8,128)(2,1)}, bf16[32,16,1536]{2,1,0:T(8,128)(2,1)}, bf16[4,4,2,48,4224]{4,3,2,1,0:T(8,128)(2,1)}) custom-call(bf16[32,16,1536]{2,1,0:T(8,128)(2,1)} %hold.5.rows_ref, bf16[32,16,1536]{2,1,0:T(8,128)(2,1)} %bitcast.165, bf16[48,4224]{1,0:T(8,128)(2,1)} %concatenate.23.shard_ref), custom_call_target="tpu_custom_call" | custom-call | tf_op jit(solution)/shard_map/opening/pallas_call | solution.py:426
  194.8 2.1 gather_fusion.2
  197.1 2.5 collective-permute-start.4
  199.6 5.4 gather_fusion.3
  211.0 9.2 %fusion.9.q_ref.k_ref.v_ref = f32[512,2560]{1,0:T(8,128)} fusion(bf16[512,1536]{1,0:T(8,128)(2,1)S(1)} %fusion.25.refs_0_, bf16[1536,4224]{1,0:T(8,128)(2,1)} %bitcast.185), kind=kOutput, calls=%fused_computation.25 | convolution fusion | flops 4026531840 | bytes 14680064 | tf_op jit(solution)/shard_map/dot_general | solution.py:796
  220.2 14.7 %attend.1 = (bf16[512,1536]{1,0:T(8,128)(2,1)}, bf16[512,512]{1,0:T(8,128)(2,1)}, bf16[512,512]{1,0:T(8,128)(2,1)}, bf16[512,1536]{1,0:T(8,128)(2,1)}) custom-call(f32[512,2560]{1,0:T(8,128)} %fusion.9.q_ref.k_ref.v_ref, f32[512,2560]{1,0:T(8,128)} %fusion.9.q_ref.k_ref.v_ref, f32[512,2560]{1,0:T(8,128)} %fusion.9.q_ref.k_ref.v_ref, ...), custom_call_target="tpu_custom_call" | custom-call | tf_op jit(solution)/shard_map/attend/pallas_call | solution.py:204
  234.9 2.1 slice.220
  238.2 1.6 collective-permute-start.6
  239.7 5.1 multiply_reduce_fusion.2
  244.9 1.6 copy-done.6
  248.0 8.5 %collective-permute-done.5.refs_1_.rows_ref = bf16[256,1536]{1,0:T(8,128)(2,1)} collective-permute-done((bf16[256,1536]{1,0:T(8,128)(2,1)}, bf16[256,1536]{1,0:T(8,128)(2,1)}, u32[]{:S(2)}, u32[]{:S(2)}) %collective-permute-start.5) | collective-permute-done | bytes 786464 | tf_op jit(solution)/shard_map/ppermute | solution.py:720
  258.5 1.6 collective-permute-start.8
  262.6 2.0 copy.181.refs_0_
  264.7 2.3 fusion.18.choose_ref
  266.9 3.5 dispatch.15.refs_0_
  270.5 3.9 dispatch.10.refs_1_
  274.3 3.7 dispatch.11.refs_1_
  278.0 3.7 dispatch.12.refs_1_
  281.7 3.0 dispatch.13.refs_1_
  284.7 3.1 dispatch.14
  287.8 6.4 collective-permute-done.8.rows_ref
  298.2 13.7 %convert_bitcast_fusion.grad_ref = bf16[4,2,1024,256]{3,2,1,0:T(8,128)(2,1)} fusion(bf16[4,1024,1536,1]{2,1,3,0:T(8,128)(2,1)} %bitcast.152, bf16[4,2,256,1536]{3,2,1,0:T(8,128)(2,1)} %bitcast.192), kind=kOutput, calls=%fused_computation.33 | convolution fusion | flops 6444548096 | bytes 23068672 | tf_op jit(solution)/shard_map/erd,ekfd->ekrf/dot_general | solution.py:831
  311.9 1.6 collective-permute-done.10.rows_ref
  313.4 1.6 collective-permute-done.9.rows_ref
  315.0 3.5 dispatch.16.refs_0_
  318.6 3.6 dispatch.17.refs_0_
  322.2 2.9 dispatch.18.refs_0_
  325.2 2.9 dispatch.19
  328.1 23.6 %middle.1 = (bf16[4,2,1024,256]{3,2,1,0:T(8,128)(2,1)}, bf16[4,2,1024,512]{3,2,1,0:T(8,128)(2,1)}) custom-call(bf16[4,1024,1536]{2,1,0:T(8,128)(2,1)} %bitcast.150, bf16[4,2,1536,512]{3,2,1,0:T(8,128)(2,1)} %bitcast.160, bf16[4,2,1024,256]{3,2,1,0:T(8,128)(2,1)} %convert_bitcast_fusion.grad_ref), custom_call_target="tpu_custom_call" | custom-call | tf_op jit(solution)/shard_map/middle/pallas_call | solution.py:666
  351.7 13.8 %convolution_convert_fusion.3 = bf16[4,2,256,1536]{3,2,1,0:T(8,128)(2,1)} fusion(bf16[4,2,1024,256]{3,2,1,0:T(8,128)(2,1)} %get-tuple-element.76, bf16[4,1024,1536,1]{2,1,3,0:T(8,128)(2,1)} %bitcast.153), kind=kOutput, calls=%fused_computation.32 | convolution fusion | flops 6445596672 | bytes 23068672 | tf_op jit(solution)/shard_map/ekrf,erd->ekfd/dot_general | solution.py:841
  365.5 22.9 %convolution_convert_fusion = bf16[4,2,512,1536]{3,2,1,0:T(8,128)(2,1)} fusion(bf16[4,2,1024,512]{3,2,1,0:T(8,128)(2,1)} %get-tuple-element.78, bf16[4,1024,1536,1]{2,1,3,0:T(8,128)(2,1)} %bitcast.151), kind=kOutput, calls=%fused_computation.13 | convolution fusion | flops 12891193344 | bytes 33554432 | tf_op jit(solution)/shard_map/ekrf,erd->ekfd/dot_general | solution.py:899
  389.3 20.5 %bitcast_convert_fusion = bf16[4,1024,1536]{2,1,0:T(8,128)(2,1)} fusion(bf16[4,2,1024,512]{3,2,1,0:T(8,128)(2,1)} %get-tuple-element.78, bf16[4,2,1536,512]{3,2,1,0:T(8,128)(2,1)} %bitcast.161), kind=kOutput, calls=%fused_computation.10 | convolution fusion | flops 12891193344 | bytes 33554432 | tf_op jit(solution)/shard_map/ekrf,ekdf->erd/dot_general | solution.py:851
  409.9 8.2 %bitcast_convert_fusion.1 = bf16[8,256,1536]{2,1,0:T(8,128)(2,1)S(1)} fusion(bf16[4,8,128,1536]{3,2,1,0:T(8,128)(2,1)} %bitcast.195, s32[8,4,256]{2,1,0:T(4,128)S(1)} %copy-done.31, pred[8,4,256]{2,1,0:T(4,128)(4,1)S(1)} %bitcast.177), kind=kOutput, calls=%fused_computation.15 | convolution fusion | flops 3226468352 | bytes 18915328 | tf_op jit(solution)/shard_map/becr,ebcd->brd/dot_general | solution.py:856
  422.0 12.6 %fusion.1 = bf16[4,1024,1536]{2,1,0:T(8,128)(2,1)} fusion(bf16[4,2,1024,256]{3,2,1,0:T(8,128)(2,1)S(1)} %copy-done.52, bf16[4,2,256,1536]{3,2,1,0:T(8,128)(2,1)} %bitcast.193, f32[4,1024]{1,0:T(4,128)S(1)} %bitcast.181), kind=kOutput, calls=%fused_computation.12 | convolution fusion | flops 6455033856 | bytes 23085056 | tf_op jit(solution)/shard_map/ekrf,ekfd->erd/dot_general | solution.py:895
  434.6 17.8 %collective-permute-done.11 = bf16[2,256,1536]{2,1,0:T(8,128)(2,1)S(1)} collective-permute-done((bf16[2,256,1536]{2,1,0:T(8,128)(2,1)S(1)}, bf16[2,256,1536]{2,1,0:T(8,128)(2,1)S(1)}, u32[]{:S(2)}, u32[]{:S(2)}) %collective-permute-start.11) | collective-permute-done | bytes 1572896 | tf_op jit(solution)/shard_map/ppermute | solution.py:720
  452.4 2.2 collective-permute-done.12
  456.9 8.0 %bitcast_convert_fusion.2 = bf16[8,256,1536]{2,1,0:T(8,128)(2,1)S(1)} fusion(bf16[4,8,128,1536]{3,2,1,0:T(8,128)(2,1)} %bitcast.194, s32[8,4,256]{2,1,0:T(4,128)S(1)} %copy-done.31, pred[8,4,256]{2,1,0:T(4,128)(4,1)S(1)} %bitcast.178), kind=kOutput, calls=%fused_computation.16 | convolution fusion | flops 3226468352 | bytes 18915328 | tf_op jit(solution)/shard_map/becr,ebcd->brd/dot_general | solution.py:856
  465.0 5.4 collective-permute-done.13
  470.4 2.5 fusion.65
  474.7 1.9 bitcast_add_fusion.3
  479.1 7.3 %fusion.38.grad_ref = bf16[512,1536]{1,0:T(8,128)(2,1)} fusion(bf16[1536,4224]{1,0:T(8,128)(2,1)} %bitcast.187, f32[512,1536]{1,0:T(8,128)S(1)} %subtract_add_fusion), kind=kOutput, calls=%fused_computation.62 | convolution fusion | flops 2417491968 | bytes 9437184 | tf_op jit(solution)/shard_map/nd,qd->nq/dot_general | solution.py:919
  486.4 20.4 %attend_back.1 = (bf16[512,1536]{1,0:T(8,128)(2,1)}, bf16[512,512]{1,0:T(8,128)(2,1)}, bf16[512,512]{1,0:T(8,128)(2,1)}) custom-call(bf16[512,1536]{1,0:T(8,128)(2,1)} %get-tuple-element.80.q_ref, bf16[512,512]{1,0:T(8,128)(2,1)} %get-tuple-element.81.k_ref, bf16[512,512]{1,0:T(8,128)(2,1)} %get-tuple-element.82.v_ref, bf16[512,1536]{1,0:T(8,128)(2,1)} %fusion.38.grad_ref, ...), custom_call_target="tpu_custom_call" | custom-call | tf_op jit(solution)/shard_map/attend_back/pallas_call | solution.py:223
  506.9 1.7 constant_dynamic-update-slice_fusion.10
  509.1 10.5 %fusion.34 = (f32[512]{0:T(512)S(1)}, bf16[1536]{0:T(1024)(128)(2,1)S(1)}, f32[512,1536]{1,0:T(8,128)}) fusion(bf16[512,1536]{1,0:T(8,128)(2,1)S(1)} %copy-done.10, f32[1536]{0:T(1024)S(1)} %copy-done.38, f32[512]{0:T(512)S(1)} %copy-done.49, bf16[512,2560]{1,0:T(8,128)(2,1)S(1)} %constant_dynamic-update-slice_fusion.8, bf16[1536,4224]{1,0:T(8,128)(2,1)} %bitcast.188), kind=kOutput, calls=%fused_computation.53 | convolution fusion | flops 4032034816 | bytes 15217664 | tf_op jit(solution)/shard_map/nc,dc->nd/dot_general | solution.py:930
  520.0 4.0 fusion.30
  524.0 3.0 gather_fusion.5
  527.0 6.2 convolution_convert_fusion.2
  533.2 3.2 fusion.48
  538.7 6.6 convolution_convert_fusion.1
  545.3 5.6 fusion.2
  551.0 2.6 convert_element_type.237
  553.6 2.6 bitcast_add_fusion.1
  557.2 2.9 gather_fusion.4
  560.1 128.0 %closing.1 = (bf16[32,16,1536]{2,1,0:T(8,128)(2,1)}, bf16[32,16,1536]{2,1,0:T(8,128)(2,1)}, f32[48,4224]{1,0:T(8,128)}) custom-call(bf16[32,16,1536]{2,1,0:T(8,128)(2,1)} %bitcast.167, bf16[32,16,1536]{2,1,0:T(8,128)(2,1)} %bitcast.166, bf16[4,4,2,48,4224]{4,3,2,1,0:T(8,128)(2,1)} %bitcast.158), custom_call_target="tpu_custom_call" | custom-call | tf_op jit(solution)/shard_map/closing/pallas_call | solution.py:580
  688.1 2.0 slice.185
  690.0 1.7 slice.186
  691.7 2.9 gather_fusion.7
  694.7 2.9 gather_fusion.6
  699.1 5.1 copy.203
  (236 shorter events, 63.8 us)
Async XLA Ops:
  7.2 37.8 %copy-start = (bf16[512,1536]{1,0:T(8,128)(2,1)S(1)}, bf16[512,1536]{1,0:T(8,128)(2,1)}, u32[]{:S(2)}) copy-start(bf16[512,1536]{1,0:T(8,128)(2,1)} %param.12) | copy-start | bytes 4718596
  7.2 23.5 %copy-start.34 = (f32[512,8]{0,1:T(8,128)S(1)}, f32[512,8]{0,1:T(8,128)}, u32[]{:S(2)}) copy-start(f32[512,8]{0,1:T(8,128)} %param.17) | copy-start | bytes 49156
  7.2 27.5 %copy-start.21 = (bf16[1536,2,256]{2,1,0:T(2,128)(2,1)S(1)}, bf16[1536,2,256]{2,1,0:T(2,128)(2,1)}, u32[]{:S(2)}) copy-start(bf16[1536,2,256]{2,1,0:T(2,128)(2,1)} %param.22) | copy-start | bytes 4718596
  7.2 291.0 %all-gather.5.cloned.1.call-start = ((), (), s32[]{:S(2)}) async-start(), calls=%async_computation.5 | async-start | bytes 7077888 | tf_op jit(solution)/shard_map/all_gather | solution.py:791
  10.0 29.3 %collective-permute-start = (f32[512,16]{0,1:T(8,128)}, f32[512,16]{0,1:T(8,128)S(1)}, u32[]{:S(2)}, u32[]{:S(2)}) collective-permute-start(f32[512,16]{0,1:T(8,128)} %pad_maximum_fusion.2), channel_id=1, source_target_pairs={{0,2},{2,0},{4,6},{6,4},{1,3},{3,1},{5,7},{7,5},{8,10},{10,8},{12,... | collective-permute-start | bytes 98312 | tf_op jit(solution)/shard_map/ppermute | solution.py:720
  11.5 28.4 %collective-permute-start.1 = (f32[512,16]{0,1:T(8,128)}, f32[512,16]{0,1:T(8,128)}, u32[]{:S(2)}, u32[]{:S(2)}) collective-permute-start(f32[512,16]{0,1:T(8,128)} %pad_maximum_fusion.2), channel_id=1, source_target_pairs={{0,6},{2,4},{4,2},{6,0},{1,7},{3,5},{5,3},{7,1},{8,14},{10,12},{12... | collective-permute-start | bytes 98312 | tf_op jit(solution)/shard_map/ppermute | solution.py:720
  12.0 29.2 %collective-permute-start.2 = (f32[512,16]{0,1:T(8,128)}, f32[512,16]{0,1:T(8,128)S(1)}, u32[]{:S(2)}, u32[]{:S(2)}) collective-permute-start(f32[512,16]{0,1:T(8,128)} %pad_maximum_fusion.2), channel_id=1, source_target_pairs={{0,4},{2,6},{4,0},{6,2},{1,5},{3,7},{5,1},{7,3},{8,12},{10,14},{12... | collective-permute-start | bytes 98312 | tf_op jit(solution)/shard_map/ppermute | solution.py:720
  15.7 8.4 %copy-start.47 = (s32[512]{0:T(512)}, s32[512]{0:T(512)S(1)}, u32[]{:S(2)}) copy-start(s32[512]{0:T(512)S(1)} %multiply_add_fusion) | copy-start | bytes 6148
  17.3 20.7 %all-to-all-start = ((s32[32,1,16]{2,1,0:T(1,128)}), s32[32,1,16]{2,1,0:T(1,128)S(1)}, u32[]{:S(2)}, u32[]{:S(2)}) async-start(s32[32,1,16]{2,1,0:T(1,128)} %bitcast.2), calls=%async_computation | async-start | bytes 32768 | tf_op jit(solution)/shard_map/all_to_all | solution.py:738
  23.3 304.8 %all-gather.7.cloned.1.call-start = ((), (), s32[]{:S(2)}) async-start(), calls=%async_computation.6 | async-start | bytes 14155776 | tf_op jit(solution)/shard_map/all_gather | solution.py:788
  33.2 3.0 copy-start.32
  39.3 5.7 copy-start.45
  45.0 3.0 copy-start.2
  193.4 357.5 %reduce-scatter.3.cloned.1.call-start = ((), (), s32[]{:S(2)}) async-start(), calls=%async_computation.3 | async-start | bytes 7077888 | tf_op jit(solution)/shard_map/reduce_scatter | solution.py:845
  197.0 2.6 copy-start.11
  197.0 37.9 %collective-permute-start.3 = (bf16[512,1536]{1,0:T(8,128)(2,1)S(1)}, bf16[512,1536]{1,0:T(8,128)(2,1)}, u32[]{:S(2)}, u32[]{:S(2)}) collective-permute-start(bf16[512,1536]{1,0:T(8,128)(2,1)S(1)} %gather_fusion.2), channel_id=1, source_target_pairs={{0,2},{2,0},{4,6},{6,4},{1,3},{3,1},{5,7},{7,5},{8,10},{10,8},{12,... | collective-permute-start | bytes 4718600 | tf_op jit(solution)/shard_map/ppermute | solution.py:720
  197.1 39.9 %collective-permute-start.4 = (bf16[512,1536]{1,0:T(8,128)(2,1)S(1)}, bf16[512,1536]{1,0:T(8,128)(2,1)}, u32[]{:S(2)}, u32[]{:S(2)}) collective-permute-start(bf16[512,1536]{1,0:T(8,128)(2,1)S(1)} %gather_fusion.2), channel_id=1, source_target_pairs={{0,4},{2,6},{4,0},{6,2},{1,5},{3,7},{5,1},{7,3},{8,12},{10,14},{12... | collective-permute-start | bytes 4718600 | tf_op jit(solution)/shard_map/ppermute | solution.py:720
  205.0 34.8 %copy-start.9 = (bf16[512,1536]{1,0:T(8,128)(2,1)}, bf16[512,1536]{1,0:T(8,128)(2,1)S(1)}, u32[]{:S(2)}) copy-start(bf16[512,1536]{1,0:T(8,128)(2,1)S(1)} %gather_fusion.3) | copy-start | bytes 4718596
  208.4 36.5 %copy-start.35 = (f32[1536]{0:T(1024)}, f32[1536]{0:T(1024)S(1)}, u32[]{:S(2)}) copy-start(f32[1536]{0:T(1024)S(1)} %get-tuple-element.108) | copy-start | bytes 18436
  237.0 19.6 %collective-permute-start.5 = (bf16[256,1536]{1,0:T(8,128)(2,1)}, bf16[256,1536]{1,0:T(8,128)(2,1)}, u32[]{:S(2)}, u32[]{:S(2)}) collective-permute-start(bf16[256,1536]{1,0:T(8,128)(2,1)} %slice.220), channel_id=1, source_target_pairs={{0,4},{2,6},{4,0},{6,2},{1,5},{3,7},{5,1},{7,3},{8,12},{10,14},{12... | collective-permute-start | bytes 2359304 | tf_op jit(solution)/shard_map/ppermute | solution.py:720
  238.2 19.4 %collective-permute-start.6 = (bf16[256,1536]{1,0:T(8,128)(2,1)S(1)}, bf16[256,1536]{1,0:T(8,128)(2,1)S(1)}, u32[]{:S(2)}, u32[]{:S(2)}) collective-permute-start(bf16[256,1536]{1,0:T(8,128)(2,1)S(1)} %slice.221), channel_id=1, source_target_pairs={{0,2},{2,0},{4,6},{6,4},{1,3},{3,1},{5,7},{7,5},{8,10},{10,8},{12,... | collective-permute-start | bytes 2359304 | tf_op jit(solution)/shard_map/ppermute | solution.py:720
  244.9 12.7 %copy-start.43 = (f32[512]{0:T(512)}, f32[512]{0:T(512)S(1)}, u32[]{:S(2)}) copy-start(f32[512]{0:T(512)S(1)} %add_rsqrt_fusion) | copy-start | bytes 6148
  248.0 12.5 %copy-start.33 = (f32[8,256,16]{1,2,0:T(8,128)S(1)}, f32[8,256,16]{1,2,0:T(8,128)}, u32[]{:S(2)}) copy-start(f32[8,256,16]{1,2,0:T(8,128)} %constant_dynamic-update-slice_fusion) | copy-start | bytes 393220
  258.5 35.7 %collective-permute-start.8 = (bf16[512,1536]{1,0:T(8,128)(2,1)}, bf16[512,1536]{1,0:T(8,128)(2,1)S(1)}, u32[]{:S(2)}, u32[]{:S(2)}) collective-permute-start(bf16[512,1536]{1,0:T(8,128)(2,1)} %hold.8.rows_ref), channel_id=1, source_target_pairs={{0,4},{2,6},{4,0},{6,2},{1,5},{3,7},{5,1},{7,3},{8,12},{10,14},{12... | collective-permute-start | bytes 4718600 | tf_op jit(solution)/shard_map/ppermute | solution.py:720
  260.2 36.2 %collective-permute-start.7 = (bf16[512,1536]{1,0:T(8,128)(2,1)}, bf16[512,1536]{1,0:T(8,128)(2,1)S(1)}, u32[]{:S(2)}, u32[]{:S(2)}) collective-permute-start(bf16[512,1536]{1,0:T(8,128)(2,1)} %hold.8.rows_ref), channel_id=1, source_target_pairs={{0,2},{2,0},{4,6},{6,4},{1,3},{3,1},{5,7},{7,5},{8,10},{10,8},{12,... | collective-permute-start | bytes 4718600 | tf_op jit(solution)/shard_map/ppermute | solution.py:720
  260.7 9.8 %copy-start.39 = (pred[8,256,4]{1,2,0:T(4,128)(4,1)}, pred[8,256,4]{1,2,0:T(4,128)(4,1)S(1)}, u32[]{:S(2)}) copy-start(pred[8,256,4]{1,2,0:T(4,128)(4,1)S(1)} %compare_reduce_fusion) | copy-start | bytes 24580
  260.9 9.5 %copy-start.30 = (s32[8,4,256]{2,1,0:T(4,128)}, s32[8,4,256]{2,1,0:T(4,128)S(1)}, u32[]{:S(2)}) copy-start(s32[8,4,256]{2,1,0:T(4,128)S(1)} %copy.175) | copy-start | bytes 98308
  294.2 17.6 %copy-start.18 = (bf16[512,1536]{1,0:T(8,128)(2,1)}, bf16[512,1536]{1,0:T(8,128)(2,1)S(1)}, u32[]{:S(2)}) copy-start(bf16[512,1536]{1,0:T(8,128)(2,1)S(1)} %collective-permute-done.8.rows_ref) | copy-start | bytes 4718596
  295.2 18.2 %collective-permute-start.10 = (bf16[256,1536]{1,0:T(8,128)(2,1)}, bf16[256,1536]{1,0:T(8,128)(2,1)}, u32[]{:S(2)}, u32[]{:S(2)}) collective-permute-start(bf16[256,1536]{1,0:T(8,128)(2,1)} %slice.223), channel_id=1, source_target_pairs={{0,2},{2,0},{4,6},{6,4},{1,3},{3,1},{5,7},{7,5},{8,10},{10,8},{12,... | collective-permute-start | bytes 2359304 | tf_op jit(solution)/shard_map/ppermute | solution.py:720
  296.3 15.5 %copy-start.19 = (bf16[512,1536]{1,0:T(8,128)(2,1)}, bf16[512,1536]{1,0:T(8,128)(2,1)S(1)}, u32[]{:S(2)}) copy-start(bf16[512,1536]{1,0:T(8,128)(2,1)S(1)} %collective-permute-done.7.rows_ref) | copy-start | bytes 4718596
  297.3 17.7 %collective-permute-start.9 = (bf16[256,1536]{1,0:T(8,128)(2,1)}, bf16[256,1536]{1,0:T(8,128)(2,1)}, u32[]{:S(2)}, u32[]{:S(2)}) collective-permute-start(bf16[256,1536]{1,0:T(8,128)(2,1)} %slice.222), channel_id=1, source_target_pairs={{0,4},{2,6},{4,0},{6,2},{1,5},{3,7},{5,1},{7,3},{8,12},{10,14},{12... | collective-permute-start | bytes 2359304 | tf_op jit(solution)/shard_map/ppermute | solution.py:720
  365.5 333.6 %reduce-scatter.5.cloned.1.call-start = ((), (), s32[]{:S(2)}) async-start(), calls=%async_computation.4 | async-start | bytes 14155776 | tf_op jit(solution)/shard_map/reduce_scatter | solution.py:902
  389.3 20.5 %copy-start.31 = (s32[8,4,256]{2,1,0:T(4,128)S(1)}, s32[8,4,256]{2,1,0:T(4,128)}, u32[]{:S(2)}) copy-start(s32[8,4,256]{2,1,0:T(4,128)} %copy-done.30) | copy-start | bytes 98308
  389.3 20.5 %copy-start.40 = (pred[8,256,4]{1,2,0:T(4,128)(4,1)S(1)}, pred[8,256,4]{1,2,0:T(4,128)(4,1)}, u32[]{:S(2)}) copy-start(pred[8,256,4]{1,2,0:T(4,128)(4,1)} %copy-done.39) | copy-start | bytes 24580
  418.1 4.0 copy-start.42
  418.1 4.0 copy-start.52
  419.5 32.9 %collective-permute-start.11 = (bf16[2,256,1536]{2,1,0:T(8,128)(2,1)S(1)}, bf16[2,256,1536]{2,1,0:T(8,128)(2,1)S(1)}, u32[]{:S(2)}, u32[]{:S(2)}) collective-permute-start(bf16[2,256,1536]{2,1,0:T(8,128)(2,1)S(1)} %get-tuple-element.120), channel_id=1, source_target_pairs={{0,2},{2,0},{4,6},{6,4},{1,3},{3,1},{5,7},{7,5},{8,10},{10,8},{12,... | collective-permute-start | bytes 4718600 | tf_op jit(solution)/shard_map/ppermute | solution.py:720
  420.6 34.0 %collective-permute-start.12 = (bf16[2,256,1536]{2,1,0:T(8,128)(2,1)S(1)}, bf16[2,256,1536]{2,1,0:T(8,128)(2,1)S(1)}, u32[]{:S(2)}, u32[]{:S(2)}) collective-permute-start(bf16[2,256,1536]{2,1,0:T(8,128)(2,1)S(1)} %get-tuple-element.119), channel_id=1, source_target_pairs={{0,4},{2,6},{4,0},{6,2},{1,5},{3,7},{5,1},{7,3},{8,12},{10,14},{12... | collective-permute-start | bytes 4718600 | tf_op jit(solution)/shard_map/ppermute | solution.py:720
  452.4 4.6 copy-start.23
  454.6 2.3 copy-start.25
  455.0 15.4 %collective-permute-start.13 = (bf16[256,1536]{1,0:T(8,128)(2,1)S(1)}, bf16[256,1536]{1,0:T(8,128)(2,1)}, u32[]{:S(2)}, u32[]{:S(2)}) collective-permute-start(bf16[256,1536]{1,0:T(8,128)(2,1)S(1)} %get-tuple-element.118), channel_id=1, source_target_pairs={{0,4},{2,6},{4,0},{6,2},{1,5},{3,7},{5,1},{7,3},{8,12},{10,14},{12... | collective-permute-start | bytes 2359304 | tf_op jit(solution)/shard_map/ppermute | solution.py:720
  455.5 14.9 %collective-permute-start.14 = (bf16[256,1536]{1,0:T(8,128)(2,1)S(1)}, bf16[256,1536]{1,0:T(8,128)(2,1)}, u32[]{:S(2)}, u32[]{:S(2)}) collective-permute-start(bf16[256,1536]{1,0:T(8,128)(2,1)S(1)} %get-tuple-element.117), channel_id=1, source_target_pairs={{0,2},{2,0},{4,6},{6,4},{1,3},{3,1},{5,7},{7,5},{8,10},{10,8},{12,... | collective-permute-start | bytes 2359304 | tf_op jit(solution)/shard_map/ppermute | solution.py:720
  465.0 7.9 %copy-start.14 = (bf16[8,256,1536]{2,1,0:T(8,128)(2,1)}, bf16[8,256,1536]{2,1,0:T(8,128)(2,1)S(1)}, u32[]{:S(2)}) copy-start(bf16[8,256,1536]{2,1,0:T(8,128)(2,1)S(1)} %bitcast_convert_fusion.2) | copy-start | bytes 18874372
  470.4 4.2 copy-start.17
  470.4 4.2 copy-start.24
  470.4 4.2 copy-start.26
  472.9 60.3 %collective-permute-start.15 = (bf16[2,256,1536]{2,1,0:T(8,128)(2,1)}, bf16[2,256,1536]{2,1,0:T(8,128)(2,1)}, u32[]{:S(2)}, u32[]{:S(2)}) collective-permute-start(bf16[2,256,1536]{2,1,0:T(8,128)(2,1)} %get-tuple-element.116), channel_id=1, source_target_pairs={{0,2},{2,0},{4,6},{6,4},{1,3},{3,1},{5,7},{7,5},{8,10},{10,8},{12,... | collective-permute-start | bytes 4718600 | tf_op jit(solution)/shard_map/ppermute | solution.py:720
  473.6 3.0 copy-start.7
  473.6 3.0 copy-start.36
  473.6 3.0 copy-start.44
  473.6 59.6 %collective-permute-start.16 = (bf16[2,256,1536]{2,1,0:T(8,128)(2,1)}, bf16[2,256,1536]{2,1,0:T(8,128)(2,1)}, u32[]{:S(2)}, u32[]{:S(2)}) collective-permute-start(bf16[2,256,1536]{2,1,0:T(8,128)(2,1)} %get-tuple-element.115), channel_id=1, source_target_pairs={{0,4},{2,6},{4,0},{6,2},{1,5},{3,7},{5,1},{7,3},{8,12},{10,14},{12... | collective-permute-start | bytes 4718600 | tf_op jit(solution)/shard_map/ppermute | solution.py:720
  479.1 7.3 %copy-start.13 = (f32[512,1536]{1,0:T(8,128)}, f32[512,1536]{1,0:T(8,128)S(1)}, u32[]{:S(2)}) copy-start(f32[512,1536]{1,0:T(8,128)S(1)} %subtract_add_fusion) | copy-start | bytes 9437188
  509.1 10.5 %copy-start.27 = (bf16[512,2560]{1,0:T(8,128)(2,1)}, bf16[512,2560]{1,0:T(8,128)(2,1)S(1)}, u32[]{:S(2)}) copy-start(bf16[512,2560]{1,0:T(8,128)(2,1)S(1)} %constant_dynamic-update-slice_fusion.8) | copy-start | bytes 7864324
  524.0 3.0 copy-start.22
  536.4 17.2 %collective-permute-start.17 = (bf16[256,1536]{1,0:T(8,128)(2,1)}, bf16[256,1536]{1,0:T(8,128)(2,1)}, u32[]{:S(2)}, u32[]{:S(2)}) collective-permute-start(bf16[256,1536]{1,0:T(8,128)(2,1)} %get-tuple-element.113), channel_id=1, source_target_pairs={{0,4},{2,6},{4,0},{6,2},{1,5},{3,7},{5,1},{7,3},{8,12},{10,14},{12... | collective-permute-start | bytes 2359304 | tf_op jit(solution)/shard_map/ppermute | solution.py:720
  537.3 16.3 %collective-permute-start.18 = (bf16[256,1536]{1,0:T(8,128)(2,1)S(1)}, bf16[256,1536]{1,0:T(8,128)(2,1)}, u32[]{:S(2)}, u32[]{:S(2)}) collective-permute-start(bf16[256,1536]{1,0:T(8,128)(2,1)S(1)} %get-tuple-element.112), channel_id=1, source_target_pairs={{0,2},{2,0},{4,6},{6,4},{1,3},{3,1},{5,7},{7,5},{8,10},{10,8},{12,... | collective-permute-start | bytes 2359304 | tf_op jit(solution)/shard_map/ppermute | solution.py:720
  538.7 6.7 slice-start
  538.7 6.7 slice-start.1
  551.0 2.6 copy-start.16
  553.6 2.8 copy-start.8
  560.1 131.6 %copy-start.50 = (s32[1024]{0:T(1024)S(1)}, s32[1024]{0:T(1024)}, u32[]{:S(2)}) copy-start(s32[1024]{0:T(1024)} %pad_clamp_fusion) | copy-start | bytes 12292
  688.1 3.7 copy-start.5
  691.7 2.9 copy-start.4
  694.7 9.5 %copy-start.1 = (bf16[512,1536]{1,0:T(8,128)(2,1)S(1)}, bf16[512,1536]{1,0:T(8,128)(2,1)}, u32[]{:S(2)}) copy-start(bf16[512,1536]{1,0:T(8,128)(2,1)} %param.12) | copy-start | bytes 4718596
  (15 other events, 20.0 us)
Sparse Core Ops, SparseCore 0:
  9.7 78.6 all-gather.4
  193.6 112.5 all-gather.6
  365.6 65.6 reduce-scatter.2
  433.5 127.6 reduce-scatter.4
